TPU v7x, 32 devices: a whole 2x2x4 slice. The times are simulated.
32 devices in a mesh: seq: 8 (over z, x), head: 4 (over y, core).
Axes of the slice: x: 2, y: 2, z: 4, core: 2. Of those that a mesh axis runs over, the one named last changes fastest.
Arguments:
- queries: bfloat16 [8192, 4096], P('seq', 'head'), may hold values from -6 to 6
- keys: bfloat16 [8192, 4096], P('seq', 'head'), may hold values from -6 to 6
- values: bfloat16 [8192, 4096], P('seq', 'head'), may hold values from -120 to 120
- gain: float32 [4096], P('head'), may hold values from 0.1 to 1.9
- out_grad: bfloat16 [8192, 4096], P('seq', 'head'), may hold values from -6 to 6
Outputs:
- mixed: bfloat16 [8192, 4096], P('seq', 'head')
- query_grad: bfloat16 [8192, 4096], P('seq', 'head')
- key_grad: bfloat16 [8192, 4096], P('seq', 'head')
- value_grad: bfloat16 [8192, 4096], P('seq', 'head')
All inputs are finite; a program needn't handle non-finite values.
Results may differ from a plain program's by a relative error of at most 0.0058.
Values sent between devices are 32-bit elements; how exact they have to be, the bound alone decides.
No kernel may reach another device: no remote copies, remote signals or barrier semaphores. Data moves between devices by JAX's collectives and lax.ppermute only.
A program may use at most 128 MiB of HBM per device.

v0:
```python
import jax
import jax.numpy as jnp
from jax import lax
from jax.sharding import PartitionSpec as P

HEAD_DIM = 128
BLOCK = 128
WIDTH = 4096


epsilon = 1e-05


def body(queries, keys, values, gain, out_grad):
    row_count, local_width = queries.shape
    blocks = row_count // BLOCK
    head_count = local_width // HEAD_DIM
    own_index = lax.axis_index("seq")
    causal = jnp.tril(jnp.ones((BLOCK, BLOCK), dtype=bool))
    query_blocks = queries.reshape(blocks, BLOCK, head_count, HEAD_DIM)
    key_blocks = keys.reshape(blocks, BLOCK, head_count, HEAD_DIM)
    value_blocks = values.reshape(blocks, BLOCK, head_count, HEAD_DIM)
    zero_state = jnp.zeros((head_count, HEAD_DIM, HEAD_DIM), jnp.float32)
    kv_states = jnp.einsum(
        "nthd,nthe->nhde", key_blocks, value_blocks, preferred_element_type=jnp.float32
    )
    kv_running = jnp.cumsum(kv_states, axis=0)
    running = kv_running[-1]
    local_prefix = jnp.concatenate([zero_state[None], kv_running[:-1]], axis=0)
    shards = lax.all_gather(running[None], "seq", axis=0, tiled=True)
    shard_order = jnp.arange(shards.shape[0], dtype=jnp.int32)
    chosen = (shard_order < own_index)[:, None, None, None]
    incoming = jnp.sum(jnp.where(chosen, shards, 0.0), axis=0)
    prefixes = (incoming[None] + local_prefix).astype(jnp.bfloat16)
    scores = jnp.einsum(
        "nihd,njhd->nhij", query_blocks, key_blocks, preferred_element_type=jnp.float32
    )
    weights = jnp.where(causal, scores, 0.0).astype(jnp.bfloat16)
    within = jnp.einsum(
        "nhij,njhd->nihd", weights, value_blocks, preferred_element_type=jnp.float32
    )
    across = jnp.einsum(
        "nihd,nhde->nihe", query_blocks, prefixes, preferred_element_type=jnp.float32
    )
    attended = (within + across).reshape(row_count, local_width)
    scaled = gain[None, :] * out_grad.astype(jnp.float32)
    squares, dots = lax.psum(
        (jnp.sum(attended * attended, axis=1), jnp.sum(scaled * attended, axis=1)), "head"
    )
    inverse = lax.rsqrt(squares / WIDTH + epsilon)
    mixed = (gain[None, :] * attended * inverse[:, None]).astype(jnp.bfloat16)
    grad_attn = (
        inverse[:, None] * scaled - (inverse**3 * dots / WIDTH)[:, None] * attended
    ).astype(jnp.bfloat16)
    grad_blocks = grad_attn.reshape(blocks, BLOCK, head_count, HEAD_DIM)
    qg_states = jnp.einsum(
        "nthd,nthe->nhde", query_blocks, grad_blocks, preferred_element_type=jnp.float32
    )
    qg_running = jnp.cumsum(qg_states[::-1], axis=0)[::-1]
    backlog = qg_running[0]
    local_suffix = jnp.concatenate([qg_running[1:], zero_state[None]], axis=0)
    shards = lax.all_gather(backlog[None], "seq", axis=0, tiled=True)
    shard_order = jnp.arange(shards.shape[0], dtype=jnp.int32)
    chosen = (shard_order > own_index)[:, None, None, None]
    arriving = jnp.sum(jnp.where(chosen, shards, 0.0), axis=0)
    suffixes = (arriving[None] + local_suffix).astype(jnp.bfloat16)
    back_scores = jnp.einsum(
        "nihe,njhe->nhij", grad_blocks, value_blocks, preferred_element_type=jnp.float32
    )
    back_weights = jnp.where(causal, back_scores, 0.0).astype(jnp.bfloat16)
    query_part = jnp.einsum(
        "nhij,njhd->nihd", back_weights, key_blocks, preferred_element_type=jnp.float32
    ) + jnp.einsum("nihe,nhde->nihd", grad_blocks, prefixes, preferred_element_type=jnp.float32)
    key_part = jnp.einsum(
        "nhij,nihd->njhd", back_weights, query_blocks, preferred_element_type=jnp.float32
    ) + jnp.einsum("njhe,nhde->njhd", value_blocks, suffixes, preferred_element_type=jnp.float32)
    value_part = jnp.einsum(
        "nhij,nihe->njhe", weights, grad_blocks, preferred_element_type=jnp.float32
    ) + jnp.einsum("njhd,nhde->njhe", key_blocks, suffixes, preferred_element_type=jnp.float32)
    query_grad = query_part.reshape(row_count, local_width).astype(jnp.bfloat16)
    key_grad = key_part.reshape(row_count, local_width).astype(jnp.bfloat16)
    value_grad = value_part.reshape(row_count, local_width).astype(jnp.bfloat16)
    return (mixed, query_grad, key_grad, value_grad)


def solution(mesh):
    placed = (P("seq", "head"), P("seq", "head"), P("seq", "head"), P("head"), P("seq", "head"))
    return jax.shard_map(
        body,
        mesh=mesh,
        in_specs=placed,
        out_specs=(P("seq", "head"), P("seq", "head"), P("seq", "head"), P("seq", "head")),
        check_vma=False,
    )
```

profile of v0, /device:TPU:0, one launch (start us, length us, event | category | flops | bytes accessed | tf_op | source)
XLA Modules:
  0.0 248.3 jit_solution(14316147562952953138)
XLA Ops:
  12.4 3.9 %fusion.31 = f32[8,8,128,128]{3,2,1,0:T(8,128)S(1)} fusion(f32[8,8,128,128]{3,2,1,0:T(8,128)S(1)} %fusion.13), kind=kOutput, calls=%fused_computation.55 | output fusion | flops 7340032 | bytes 8388608 | tf_op jit(solution)/shard_map/jit(cumsum)/reduce_window_sum | solution.py:27
  19.3 4.5 %slice.22 = f32[7,8,128,128]{3,2,1,0:T(8,128)} slice(f32[8,8,128,128]{3,2,1,0:T(8,128)} %copy-done.7), slice={[0:7], [0:8], [0:128], [0:128]} | slice | bytes 7340032 | tf_op jit(solution)/shard_map/slice | solution.py:29
  25.8 3.8 %select_convert_fusion.1 = bf16[8,8,128,128]{3,2,1,0:T(8,128)(2,1)S(1)} fusion(pred[128,128]{1,0:T(8,128)(4,1)S(1)} %iota_compare_fusion, bf16[8,128,8,128]{3,2,1,0:T(8,128)(2,1)} %bitcast.82, bf16[8,128,8,128]{3,2,1,0:T(8,128)(2,1)} %bitcast.85), kind=kOutput, calls=%fused_computation.21 | convolution fusion | flops 270532608 | bytes 6307840 | tf_op jit(solution)/shard_map/nihd,njhd->nhij/dot_general | solution.py:35
  30.9 3.7 %fusion.9 = f32[8,8,128,128]{2,3,1,0:T(8,128)} fusion(bf16[8,8,128,128]{3,2,1,0:T(8,128)(2,1)S(1)} %select_convert_fusion.1, bf16[8,128,8,128]{3,2,1,0:T(8,128)(2,1)S(1)} %bitcast.78), kind=kOutput, calls=%fused_computation.28 | convolution fusion | flops 268435456 | bytes 8388608 | tf_op jit(solution)/shard_map/nhij,njhd->nihd/dot_general | solution.py:39
  34.6 60.9 %all-gather.3.cloned.1.call-done = f32[8,8,128,128]{3,2,1,0:T(8,128)} async-done(((f32[1,8,128,128]{3,2,1,0:T(8,128)}), f32[8,8,128,128]{3,2,1,0:T(8,128)}) %all-gather.3.cloned.1.call-update) | async-done | bytes 4194320 | tf_op jit(solution)/shard_map/all_gather | solution.py:30
  95.5 2.9 %select_reduce_fusion.1 = f32[8,128,128]{2,1,0:T(8,128)S(1)} fusion(f32[8,8,128,128]{3,2,1,0:T(8,128)} %all-gather.3.cloned.1.call-done, pred[8]{0:T(512)(128)(4,1)S(1)} %iota_compare_fusion.2), kind=kLoop, calls=%fused_computation.20 | loop fusion | flops 1966080 | bytes 4718600 | tf_op jit(solution)/shard_map/reduce_sum | solution.py:33
  98.4 7.0 %multiply_reduce_fusion = (f32[8,128]{1,0:T(8,128)S(1)}, f32[8,128,8,128]{1,3,2,0:T(8,128)}) fusion(bf16[8,128,8,128]{3,2,1,0:T(8,128)(2,1)S(1)} %bitcast.87, f32[7,8,128,128]{3,2,1,0:T(8,128)} %slice.22, f32[8,128,128]{2,1,0:T(8,128)S(1)} %select_reduce_fusion.1, f32[8,8,128,128]{2,3,1,0:T(8,128)} %fusion.9), kind=kOutput, calls=%fused_computation.18 | convolution fusion | flops 273677312 | bytes 14684160 | tf_op jit(solution)/shard_map/nihd,nhde->nihe/dot_general | solution.py:42
  105.4 5.4 %copy.90 = f32[8,128,8,128]{3,2,1,0:T(8,128)} copy(f32[8,128,8,128]{1,3,2,0:T(8,128)} %get-tuple-element.11) | data formatting | bytes 8388608 | tf_op jit(solution)/shard_map/add | solution.py:45
  110.8 3.6 %fusion.2 = f32[1024]{0:T(1024)S(1)} fusion(bf16[1024,1024]{1,0:T(8,128)(2,1)} %param.9, f32[128,8,8,128]{3,2,1,0:T(8,128)} %bitcast.75, f32[1024]{0:T(1024)S(1)} %copy-done.14), kind=kLoop, calls=%fused_computation.5 | loop fusion | flops 4193280 | bytes 6299648 | tf_op jit(solution)/shard_map/reduce_sum | solution.py:48
  114.4 5.8 %all-reduce.2 = (f32[1024]{0:T(1024)S(1)}, f32[1024]{0:T(1024)S(1)}) all-reduce(f32[1024]{0:T(1024)S(1)} %bitcast.97, f32[1024]{0:T(1024)S(1)} %fusion.2), channel_id=1, replica_groups=mesh['seq'=8,'head'=4] {'head'}, use_global_device_ids=true, to_apply=%region_3.4 | all-reduce | flops 2048 | bytes 16384 | tf_op jit(solution)/shard_map/psum | solution.py:47
  120.2 4.9 %fusion.7 = (bf16[128,8,8,128]{3,1,2,0:T(8,128)(2,1)S(1)}, bf16[1024,1024]{1,0:T(8,128)(2,1)}) fusion(f32[128,8,8,128]{3,2,1,0:T(8,128)} %bitcast.76, bf16[1024,1024]{1,0:T(8,128)(2,1)} %param.9, f32[1024]{0:T(1024)S(1)} %get-tuple-element.8, f32[1024]{0:T(1024)S(1)} %get-tuple-element.9, f32[1024]{0:T(1024)S(1)} %copy-done.14), kind=kLoop, calls=%fused_computation.23 | loop fusion | flops 9437184 | bytes 10498048
  127.0 4.1 %copy.99 = bf16[8,128,8,128]{1,3,2,0:T(8,128)(2,1)} copy(bf16[8,128,8,128]{3,2,1,0:T(8,128)(2,1)} %bitcast.89) | data formatting | bytes 4194304 | tf_op jit(solution)/shard_map/reshape | solution.py:55
  131.1 5.0 %convolution_bitcast_fusion = f32[8,8,128,128]{2,3,1,0:T(8,128)} fusion(bf16[8,128,8,128]{1,3,2,0:T(8,128)(2,1)} %copy.99, bf16[8,128,8,128]{3,2,1,0:T(8,128)(2,1)} %bitcast.86), kind=kOutput, calls=%fused_computation.22 | convolution fusion | flops 268435456 | bytes 8388608 | tf_op jit(solution)/shard_map/nthd,nthe->nhde/dot_general | solution.py:56
  136.1 4.6 %rev.4 = f32[8,8,128,128]{2,3,1,0:T(8,128)} reverse(f32[8,8,128,128]{2,3,1,0:T(8,128)} %convolution_bitcast_fusion), dimensions={0} | reverse | bytes 8388608 | tf_op jit(solution)/shard_map/rev | solution.py:59
  146.3 4.4 %slice.24 = f32[7,8,128,128]{2,3,1,0:T(8,128)} slice(f32[8,8,128,128]{2,3,1,0:T(8,128)} %copy-done.6), slice={[0:7], [0:8], [0:128], [0:128]} | slice | bytes 7340032 | tf_op jit(solution)/shard_map/slice | solution.py:61
  160.7 4.3 %slice.20 = f32[7,8,128,128]{2,3,1,0:T(8,128)} reverse(f32[7,8,128,128]{2,3,1,0:T(8,128)} %slice.24), dimensions={0} | reverse | bytes 7340032 | tf_op jit(solution)/shard_map/slice | solution.py:61
  165.1 5.0 %fusion.33 = f32[8,8,128,128]{3,2,1,0:T(8,128)} fusion(bf16[8,128,8,128]{1,3,2,0:T(8,128)(2,1)} %copy.99, bf16[8,8,128,128]{3,2,1,0:T(8,128)(2,1)} %copy-done.9), kind=kOutput, calls=%fused_computation.57 | convolution fusion | flops 268435456 | bytes 8388608 | tf_op jit(solution)/shard_map/nhij,nihe->njhe/dot_general | solution.py:77
  170.1 2.8 %fusion.21 = f32[8,8,128,128]{3,2,1,0:T(8,128)} fusion(bf16[8,8,128,128]{3,2,1,0:T(8,128)(2,1)S(1)} %copy-done.11, bf16[8,128,8,128]{3,2,1,0:T(8,128)(2,1)S(1)} %bitcast.88), kind=kOutput, calls=%fused_computation.40 | convolution fusion | flops 268435456 | bytes 8388608 | tf_op jit(solution)/shard_map/nhij,nihd->njhd/dot_general | solution.py:74
  172.9 45.5 %all-gather.5.cloned.1.call-done = f32[8,8,128,128]{3,2,1,0:T(8,128)} async-done(((f32[1,8,128,128]{3,2,1,0:T(8,128)}), f32[8,8,128,128]{3,2,1,0:T(8,128)}) %all-gather.5.cloned.1.call-update) | async-done | bytes 4194320 | tf_op jit(solution)/shard_map/all_gather | solution.py:62
  218.4 2.7 %select_reduce_fusion = f32[8,128,128]{2,1,0:T(8,128)S(1)} fusion(f32[8,8,128,128]{3,2,1,0:T(8,128)} %all-gather.5.cloned.1.call-done, pred[8]{0:T(512)(128)(4,1)S(1)} %iota_compare_fusion.1), kind=kLoop, calls=%fused_computation.15 | loop fusion | flops 1966080 | bytes 4718600 | tf_op jit(solution)/shard_map/reduce_sum | solution.py:65
  221.3 6.8 %fusion.8 = bf16[8,128,8,128]{1,3,2,0:T(8,128)(2,1)} fusion(f32[8,8,128,128]{3,2,1,0:T(8,128)} %fusion.33, bf16[8,128,8,128]{3,2,1,0:T(8,128)(2,1)} %bitcast.83, f32[7,8,128,128]{2,3,1,0:T(8,128)} %slice.20, f32[8,128,128]{1,2,0:T(8,128)S(1)} %copy.102), kind=kOutput, calls=%fused_computation.27 | convolution fusion | flops 272629760 | bytes 12582912 | tf_op jit(solution)/shard_map/njhd,nhde->njhe/dot_general | solution.py:79
  228.1 4.1 %copy.109 = bf16[8,128,8,128]{3,2,1,0:T(8,128)(2,1)} copy(bf16[8,128,8,128]{1,3,2,0:T(8,128)(2,1)} %fusion.8) | data formatting | bytes 4194304 | tf_op jit(solution)/shard_map/convert_element_type | solution.py:82
  232.2 4.2 %fusion.5 = bf16[8,128,8,128]{3,1,2,0:T(8,128)(2,1)S(1)} fusion(f32[8,8,128,128]{3,2,1,0:T(8,128)} %fusion.21, bf16[8,128,8,128]{3,2,1,0:T(8,128)(2,1)S(1)} %bitcast.80, f32[7,8,128,128]{2,3,1,0:T(8,128)} %slice.20, f32[8,128,128]{1,2,0:T(8,128)S(1)} %copy.102), kind=kOutput, calls=%fused_computation.9 | convolution fusion | flops 272629760 | bytes 12582912 | tf_op jit(solution)/shard_map/njhe,nhde->njhd/dot_general | solution.py:76
  238.1 3.3 %copy_bitcast_fusion = (bf16[1024,1024]{1,0:T(8,128)(2,1)}, bf16[1024,1024]{1,0:T(8,128)(2,1)}) fusion(bf16[128,8,8,128]{3,2,1,0:T(8,128)(2,1)S(1)} %bitcast.91, bf16[128,8,8,128]{3,2,1,0:T(8,128)(2,1)S(1)} %bitcast.92), kind=kLoop, calls=%fused_computation.24 | loop fusion | bytes 8388608 | tf_op jit(solution)/shard_map/convert_element_type | solution.py:82
  (54 shorter events, 30.7 us)
Async XLA Ops:
  7.2 88.3 %all-gather.3.cloned.1.call-start = ((), (), s32[]{:S(2)}) async-start(), calls=%async_computation | async-start | bytes 4718592 | tf_op jit(solution)/shard_map/all_gather | solution.py:30
  7.2 2.4 copy-start.12
  10.2 1.3 copy-start
  16.3 2.1 copy-start.7
  19.2 199.2 %all-gather.5.cloned.1.call-start = ((), (), s32[]{:S(2)}) async-start(), calls=%async_computation.1 | async-start | bytes 4718592 | tf_op jit(solution)/shard_map/all_gather | solution.py:62
  19.3 4.5 %copy-start.13 = (bf16[1024,1024]{1,0:T(8,128)(2,1)S(1)}, bf16[1024,1024]{1,0:T(8,128)(2,1)}, u32[]{:S(2)}) copy-start(bf16[1024,1024]{1,0:T(8,128)(2,1)} %param.5) | copy-start | bytes 6291460
  29.6 1.3 copy-start.9
  95.5 2.9 %copy-start.2 = (bf16[128,8,8,128]{3,2,1,0:T(8,128)(2,1)S(1)}, bf16[128,8,8,128]{3,2,1,0:T(8,128)(2,1)}, u32[]{:S(2)}) copy-start(bf16[128,8,8,128]{3,2,1,0:T(8,128)(2,1)} %copy.115) | copy-start | bytes 6291460
  105.4 5.4 %copy-start.14 = (f32[1024]{0:T(1024)S(1)}, f32[1024]{0:T(1024)}, u32[]{:S(2)}) copy-start(f32[1024]{0:T(1024)} %param.8) | copy-start | bytes 12292
  143.3 2.0 copy-start.6
  146.3 4.4 %copy-start.4 = (bf16[8,128,8,128]{1,3,2,0:T(8,128)(2,1)S(1)}, bf16[8,128,8,128]{1,3,2,0:T(8,128)(2,1)}, u32[]{:S(2)}) copy-start(bf16[8,128,8,128]{1,3,2,0:T(8,128)(2,1)} %copy.99) | copy-start | bytes 6291460
  150.7 3.0 %copy-start.1 = (bf16[128,8,8,128]{3,2,1,0:T(8,128)(2,1)S(1)}, bf16[128,8,8,128]{3,2,1,0:T(8,128)(2,1)}, u32[]{:S(2)}) copy-start(bf16[128,8,8,128]{3,2,1,0:T(8,128)(2,1)} %copy-done) | copy-start | bytes 6291460
  152.3 1.3 copy-start.10
  153.7 2.1 copy-start.5
  165.0 5.0 %copy-start.3 = (bf16[128,8,8,128]{3,2,1,0:T(8,128)(2,1)S(1)}, bf16[128,8,8,128]{3,2,1,0:T(8,128)(2,1)}, u32[]{:S(2)}) copy-start(bf16[128,8,8,128]{3,2,1,0:T(8,128)(2,1)} %copy.115) | copy-start | bytes 6291460
  165.0 5.0 %copy-start.11 = (bf16[8,8,128,128]{3,2,1,0:T(8,128)(2,1)S(1)}, bf16[8,8,128,128]{3,2,1,0:T(8,128)(2,1)}, u32[]{:S(2)}) copy-start(bf16[8,8,128,128]{3,2,1,0:T(8,128)(2,1)} %copy-done.10) | copy-start | bytes 6291460
  236.5 1.6 copy-start.8
Sparse Core Ops, SparseCore 0:
  19.4 76.0 all-gather.2
  146.4 71.9 all-gather.4
where the time goes:
time: 249 us; the launch traced here: 248 us
  waiting for transfers between devices  106 us (43%)
  local copies, waits for them, and re-layouts  58.1 us (23%)
  matrix products  43.1 us (17%)
  other arithmetic  20.6 us (8%)
  between operations  14.3 us (6%)
  blocking collectives  5.77 us (2%)
    all_gather x1, waiting for transfers between devices, body(): shards = lax.all_gather(running[None], 'seq', axis=0, tiled=True)  60.9 us
    all_gather x1, waiting for transfers between devices, body(): shards = lax.all_gather(backlog[None], 'seq', axis=0, tiled=True)  45.5 us
    unnamed x35, local copies, waits for them, and re-layouts  18.5 us
    slice x2, local copies, waits for them, and re-layouts, body(): local_suffix = jnp.concatenate([qg_running[1:], zero_state[None]], axis=0)  8.75 us
    convert_element_type x2, local copies, waits for them, and re-layouts, body(): value_grad = value_part.reshape(row_count, local_width).astype(jnp.bfloat16)  7.43 us
    dot_general x1, matrix products, body(): jnp.einsum('nihd,nhde->nihe', query_blocks, prefixes, preferred_element_t...  7.01 us
    dot_general x1, matrix products, body(): jnp.einsum('njhd,nhde->njhe', key_blocks, suffixes, preferred_element_typ...  6.8 us
    psum x1, blocking collectives, body(): lax.psum((jnp.sum(attended * attended, axis=1), jnp.sum(scaled * attended...  5.77 us
  transfers between devices with their start and end apart: 2, of which 2 were waited for; matrix products, arithmetic and copies ran while one was open for 15% of the time, Pallas kernels for 0%

commit v1 on v0

v1 whole, which is shorter than its diff:
```python
import functools

import jax
import jax.numpy as jnp
from jax import lax
from jax.experimental import pallas as pl
from jax.experimental.pallas import tpu as pltpu
from jax.sharding import PartitionSpec as P

HEAD_DIM = 128
BLOCK = 128
WIDTH = 4096
epsilon = 1e-05

F32 = jnp.float32
BF16 = jnp.bfloat16


def dot(a, b, ca, cb):
    return lax.dot_general(a, b, (((ca,), (cb,)), ((), ())), preferred_element_type=F32)


def causal_mask():
    row = lax.broadcasted_iota(jnp.int32, (BLOCK, BLOCK), 0)
    col = lax.broadcasted_iota(jnp.int32, (BLOCK, BLOCK), 1)
    return col <= row


def rows_of(n):
    return pl.ds(n * BLOCK, BLOCK)


def state_kernel(k_ref, v_ref, t_ref):
    t_ref[0] = dot(k_ref[...], v_ref[...], 0, 0)


def local_kernel(blocks, q_ref, k_ref, v_ref, w_ref, a_ref):
    causal = causal_mask()
    prefix = jnp.zeros((HEAD_DIM, HEAD_DIM), F32)
    for n in range(blocks):
        q, k, v = q_ref[rows_of(n), :], k_ref[rows_of(n), :], v_ref[rows_of(n), :]
        w = jnp.where(causal, dot(q, k, 1, 1), 0.0).astype(BF16)
        w_ref[rows_of(n), :] = w
        out = dot(w, v, 1, 0)
        if n > 0:
            out = out + dot(q, prefix.astype(BF16), 1, 0)
        a_ref[rows_of(n), :] = out
        if n + 1 < blocks:
            prefix = prefix + dot(k, v, 0, 0)


def stats_kernel(a_in, q_ref, p_ref, og_ref, gain_ref, a_ref, s_ref, sq, dt):
    h = pl.program_id(0)
    att = a_in[...] + dot(q_ref[...], p_ref[0].astype(BF16), 1, 0)
    a_ref[...] = att
    scaled = gain_ref[...] * og_ref[...].astype(F32)

    @pl.when(h == 0)
    def _():
        sq[...] = att * att
        dt[...] = scaled * att

    @pl.when(h > 0)
    def _():
        sq[...] += att * att
        dt[...] += scaled * att

    @pl.when(h == pl.num_programs(0) - 1)
    def _():
        for n in range(att.shape[0] // BLOCK):
            cols = pl.ds(n * BLOCK, BLOCK)
            s_ref[0:1, cols] = jnp.sum(sq[rows_of(n), :].T, axis=0, keepdims=True)
            s_ref[1:2, cols] = jnp.sum(dt[rows_of(n), :].T, axis=0, keepdims=True)


def norm_kernel(a_ref, q_ref, og_ref, gain_ref, s_ref, m_ref, g_ref, t_ref, inv, coef):
    h = pl.program_id(0)

    @pl.when(h == 0)
    def _():
        inverse = lax.rsqrt(s_ref[0:1, :] / WIDTH + epsilon)
        factor = inverse * inverse * inverse * s_ref[1:2, :] / WIDTH
        for n in range(a_ref.shape[0] // BLOCK):
            lo, hi = n * BLOCK, (n + 1) * BLOCK
            inv[rows_of(n), :] = jnp.broadcast_to(inverse[:, lo:hi], (BLOCK, BLOCK)).T
            coef[rows_of(n), :] = jnp.broadcast_to(factor[:, lo:hi], (BLOCK, BLOCK)).T

    att = a_ref[...]
    gain = gain_ref[...]
    m_ref[...] = (gain * att * inv[...]).astype(BF16)
    grad = (inv[...] * (gain * og_ref[...].astype(F32)) - coef[...] * att).astype(BF16)
    g_ref[...] = grad
    t_ref[0] = dot(q_ref[...], grad, 0, 0)


def back_kernel(blocks, q_ref, k_ref, v_ref, w_ref, g_ref, p_ref, qg_ref, kl_ref, vl_ref, bw):
    causal = causal_mask()
    prefix = p_ref[0]
    for n in range(blocks):
        k, v, g = k_ref[rows_of(n), :], v_ref[rows_of(n), :], g_ref[rows_of(n), :]
        b = jnp.where(causal, dot(g, v, 1, 1), 0.0).astype(BF16)
        bw[rows_of(n), :] = b
        qg_ref[rows_of(n), :] = (dot(b, k, 1, 0) + dot(g, prefix.astype(BF16), 1, 1)).astype(BF16)
        if n + 1 < blocks:
            prefix = prefix + dot(k, v, 0, 0)
    suffix = jnp.zeros((HEAD_DIM, HEAD_DIM), F32)
    for n in reversed(range(blocks)):
        q, k, v = q_ref[rows_of(n), :], k_ref[rows_of(n), :], v_ref[rows_of(n), :]
        g = g_ref[rows_of(n), :]
        kp = dot(bw[rows_of(n), :], q, 0, 0)
        vp = dot(w_ref[rows_of(n), :], g, 0, 0)
        if n + 1 < blocks:
            low = suffix.astype(BF16)
            kp = kp + dot(v, low, 1, 1)
            vp = vp + dot(k, low, 1, 0)
        kl_ref[rows_of(n), :] = kp
        vl_ref[rows_of(n), :] = vp
        if n > 0:
            suffix = suffix + dot(q, g, 0, 0)


def last_kernel(k_ref, v_ref, kl_ref, vl_ref, s_ref, kg_ref, vg_ref):
    low = s_ref[0].astype(BF16)
    kg_ref[...] = (kl_ref[...] + dot(v_ref[...], low, 1, 1)).astype(BF16)
    vg_ref[...] = (vl_ref[...] + dot(k_ref[...], low, 1, 0)).astype(BF16)


def call(kernel, heads, rows, ins, outs, scratch=(), flops=0, nbytes=0, vmem=16):
    specs = {
        "tok": pl.BlockSpec((rows, HEAD_DIM), lambda h: (0, h)),
        "state": pl.BlockSpec((1, HEAD_DIM, HEAD_DIM), lambda h: (h, 0, 0)),
        "gain": pl.BlockSpec((1, HEAD_DIM), lambda h: (0, h)),
        "row": pl.BlockSpec((2, rows), lambda h: (0, 0)),
    }
    shapes = {
        "tok": (rows, heads * HEAD_DIM),
        "state": (heads, HEAD_DIM, HEAD_DIM),
        "row": (2, rows),
    }
    return pl.pallas_call(
        kernel,
        grid=(heads,),
        in_specs=[specs[kind] for kind, _ in ins],
        out_specs=tuple(specs[kind] for kind, _ in outs),
        out_shape=tuple(jax.ShapeDtypeStruct(shapes[kind], dtype) for kind, dtype in outs),
        scratch_shapes=list(scratch),
        compiler_params=pltpu.CompilerParams(vmem_limit_bytes=vmem << 20),
        cost_estimate=pl.CostEstimate(flops=flops, bytes_accessed=nbytes, transcendentals=0),
    )(*[a for _, a in ins])


def seq_scan(states, size, own, reverse):
    place = (lambda i: size - 1 - i) if reverse else (lambda i: i)
    send = lambda a, pairs: lax.ppermute(a, "seq", [(place(i), place(j)) for i, j in pairs])
    if size % 2:
        raise ValueError("odd seq")
    outer = size // 2
    swap = [(i, i ^ 1) for i in range(size)]
    parity = own % 2
    low = parity == 0
    first = (parity == 1) if reverse else low
    outs = []
    for t in states:
        half = t.shape[0] // 2
        mine = jnp.where(low, t[:half], t[half:])
        other = jnp.where(low, t[half:], t[:half])
        got = send(other, swap)
        pair = mine + got
        if outer <= 4:
            running, total = pair, jnp.zeros_like(pair)
            for hop in range(outer - 1):
                r = send(running, [(2 * hop, 2 * hop + 2), (2 * hop + 1, 2 * hop + 3)])
                total = total + r
                running = r + pair
        else:
            total = send(pair, [(i, i + 2) for i in range(size - 2)])
            step = 1
            while step < outer - 1:
                total = total + send(total, [(i, i + 2 * step) for i in range(size - 2 * step)])
                step *= 2
        answer = send(jnp.where(first, total + mine, total), swap)
        kept = jnp.where(first, total, total + got)
        outs.append(jnp.concatenate([jnp.where(low, kept, answer), jnp.where(low, answer, kept)], axis=0))
    return outs


def head_sum(a, size):
    step = 1
    while step < size:
        a = a + lax.ppermute(a, "head", [(i, i ^ step) for i in range(size)])
        step *= 2
    return a


def body(seq_size, head_size, queries, keys, values, gain, out_grad):
    rows, width = queries.shape
    blocks, heads = rows // BLOCK, width // HEAD_DIM
    own = lax.axis_index("seq")
    gain = gain.reshape(1, width)
    run = functools.partial(call, heads=heads, rows=rows)
    unit = 2 * rows * HEAD_DIM * HEAD_DIM * heads
    tok = rows * width
    chunk = max(2, 2 * (heads // 8))

    def split(t):
        return [t[i : i + chunk] for i in range(0, heads, chunk)]

    (state,) = run(state_kernel, ins=[("tok", keys), ("tok", values)], outs=[("state", F32)], flops=unit, nbytes=4 * tok)
    weights, local = run(
        functools.partial(local_kernel, blocks),
        ins=[("tok", queries), ("tok", keys), ("tok", values)],
        outs=[("tok", BF16), ("tok", F32)],
        flops=4 * unit,
        nbytes=12 * tok,
    )
    prefix = jnp.concatenate(seq_scan(split(state), seq_size, own, False), axis=0)
    attended, sums = run(
        stats_kernel,
        ins=[("tok", local), ("tok", queries), ("state", prefix), ("tok", out_grad), ("gain", gain)],
        outs=[("tok", F32), ("row", F32)],
        scratch=[pltpu.VMEM((rows, HEAD_DIM), F32)] * 2,
        flops=unit,
        nbytes=12 * tok,
    )
    sums = head_sum(sums, head_size)
    mixed, grad, back = run(
        norm_kernel,
        ins=[("tok", attended), ("tok", queries), ("tok", out_grad), ("gain", gain), ("row", sums)],
        outs=[("tok", BF16), ("tok", BF16), ("state", F32)],
        scratch=[pltpu.VMEM((rows, HEAD_DIM), F32)] * 2,
        flops=unit,
        nbytes=12 * tok,
    )
    query_grad, key_local, value_local = run(
        functools.partial(back_kernel, blocks),
        ins=[("tok", queries), ("tok", keys), ("tok", values), ("tok", weights), ("tok", grad), ("state", prefix)],
        outs=[("tok", BF16), ("tok", F32), ("tok", F32)],
        scratch=[pltpu.VMEM((rows, BLOCK), BF16)],
        flops=9 * unit,
        nbytes=20 * tok,
    )
    suffix = jnp.concatenate(seq_scan(split(back), seq_size, own, True), axis=0)
    key_grad, value_grad = run(
        last_kernel,
        ins=[("tok", keys), ("tok", values), ("tok", key_local), ("tok", value_local), ("state", suffix)],
        outs=[("tok", BF16), ("tok", BF16)],
        flops=2 * unit,
        nbytes=16 * tok,
    )
    return mixed, query_grad, key_grad, value_grad


def solution(mesh):
    placed = (P("seq", "head"), P("seq", "head"), P("seq", "head"), P("head"), P("seq", "head"))
    return jax.shard_map(
        functools.partial(body, mesh.shape["seq"], mesh.shape["head"]),
        mesh=mesh,
        in_specs=placed,
        out_specs=(P("seq", "head"),) * 4,
        check_vma=False,
    )
```

time: 249 us -> 163 us (0.65)
  waiting for transfers between devices: 106 us -> 45.1 us
  Pallas kernels: 0 us -> 54.5 us
  starting transfers between devices: 0.08 us -> 47.6 us
  local copies, waits for them, and re-layouts: 58.1 us -> 10.6 us
  matrix products: 43.1 us -> 0 us
  other arithmetic: 20.6 us -> 2.83 us
  between operations: 14.3 us -> 1.35 us
  blocking collectives: 5.77 us -> 0 us
    all_gather x2 -> x0, waiting for transfers between devices: 106 us -> none  [the longest x1 60.9 us: body(): shards = lax.all_gather(running[None], 'seq', axis=0, tiled=True)]
    pallas_call x0 -> x6, Pallas kernels: none -> 54.5 us  [call(): pl.pallas_call(kernel, grid=(heads,), in_specs=[specs[kind] for kind, _ i...]
    ppermute x0 -> x42, starting transfers between devices: none -> 47.6 us  [the longest x40 46 us: seq_scan(): lax.ppermute(a, 'seq', [(place(i), place(j)) for i, j in pairs])]
    ppermute x0 -> x42, waiting for transfers between devices: none -> 45.1 us  [the longest x40 41.8 us: seq_scan(): lax.ppermute(a, 'seq', [(place(i), place(j)) for i, j in pairs])]
    dot_general x12 -> x0, matrix products: 43.1 us -> none  [the longest x1 7.01 us: body(): jnp.einsum('nihd,nhde->nihe', query_blocks, prefixes, preferred_element_t...]
    slice x6 -> x0, local copies, waits for them, and re-layouts: 15.1 us -> none  [the longest x2 8.75 us: body(): local_suffix = jnp.concatenate([qg_running[1:], zero_state[None]], axis=0)]
    convert_element_type x4 -> x0, local copies, waits for them, and re-layouts: 10.2 us -> none  [the longest x2 7.43 us: body(): value_grad = value_part.reshape(row_count, local_width).astype(jnp.bfloat16)]
    reduce_sum x3 -> x0, other arithmetic: 9.19 us -> none  [the longest x1 3.57 us: body(): jnp.sum(scaled * attended, axis=1)]
  transfers between devices with their start and end apart: 2 -> 42, of which waited for: 2 -> 16; matrix products, arithmetic and copies ran while one was open for 15% -> 1% of each run, Pallas kernels for 0% -> 21%
where the time goes in v1:
time: 163 us; the launch traced here: 162 us
  Pallas kernels  54.5 us (33%)
  starting transfers between devices  47.6 us (29%)
  waiting for transfers between devices  45.1 us (28%)
  local copies, waits for them, and re-layouts  10.6 us (7%)
  other arithmetic  2.83 us (2%)
    pallas_call x6, Pallas kernels, call(): pl.pallas_call(kernel, grid=(heads,), in_specs=[specs[kind] for kind, _ i...  54.5 us
    ppermute x40, starting transfers between devices, seq_scan(): lax.ppermute(a, 'seq', [(place(i), place(j)) for i, j in pairs])  46 us
    ppermute x40, waiting for transfers between devices, seq_scan(): lax.ppermute(a, 'seq', [(place(i), place(j)) for i, j in pairs])  41.8 us
    unnamed x24, local copies, waits for them, and re-layouts  10.6 us
    ppermute x2, waiting for transfers between devices, head_sum(): a = a + lax.ppermute(a, 'head', [(i, i ^ step) for i in range(size)])  3.29 us
  transfers between devices with their start and end apart: 42, of which 16 were waited for; matrix products, arithmetic and copies ran while one was open for 1% of the time, Pallas kernels for 21%

profile of v1, /device:TPU:0, one launch (start us, length us, event | category | flops | bytes accessed | tf_op | source)
XLA Modules:
  0.0 161.9 jit_solution(6913632844724065429)
XLA Ops:
  0.7 1.6 copy-done
  2.2 1.6 copy-done.2
  3.8 3.3 %shard_map.85 = f32[8,128,128]{2,1,0:T(8,128)S(1)} custom-call(bf16[1024,1024]{1,0:T(8,128)(2,1)S(1)} %copy-done, bf16[1024,1024]{1,0:T(8,128)(2,1)S(1)} %copy-done.2), custom_call_target="tpu_custom_call" | custom-call | flops 268435456 | bytes 4194304 | tf_op jit(solution)/shard_map/pallas_call | solution.py:140
  7.2 3.0 %collective-permute-start.15 = (f32[1,128,128]{2,1,0:T(8,128)S(1)}, f32[1,128,128]{2,1,0:T(8,128)S(1)}, u32[]{:S(2)}, u32[]{:S(2)}) collective-permute-start(f32[1,128,128]{2,1,0:T(8,128)S(1)} %slice_select_fusion), channel_id=1, source_target_pairs={{0,4},{4,0},{8,12},{12,8},{16,20},{20,16},{24,28},{28,24},{1,5},{5... | collective-permute-start | bytes 196616 | tf_op jit(solution)/shard_map/ppermute | solution.py:154
  10.2 2.2 %collective-permute-done.15 = f32[1,128,128]{2,1,0:T(8,128)S(1)} collective-permute-done((f32[1,128,128]{2,1,0:T(8,128)S(1)}, f32[1,128,128]{2,1,0:T(8,128)S(1)}, u32[]{:S(2)}, u32[]{:S(2)}) %collective-permute-start.15) | collective-permute-done | bytes 65568 | tf_op jit(solution)/shard_map/ppermute | solution.py:154
  12.5 4.0 %collective-permute-start.16 = (f32[1,128,128]{2,1,0:T(8,128)S(1)}, f32[1,128,128]{2,1,0:T(8,128)S(1)}, u32[]{:S(2)}, u32[]{:S(2)}) collective-permute-start(f32[1,128,128]{2,1,0:T(8,128)S(1)} %get-tuple-element.58), channel_id=1, source_target_pairs={{0,8},{4,12},{1,9},{5,13},{2,10},{6,14},{3,11},{7,15}} | collective-permute-start | bytes 196616 | tf_op jit(solution)/shard_map/ppermute | solution.py:154
  16.5 1.9 %collective-permute-done.16 = f32[1,128,128]{2,1,0:T(8,128)S(1)} collective-permute-done((f32[1,128,128]{2,1,0:T(8,128)S(1)}, f32[1,128,128]{2,1,0:T(8,128)S(1)}, u32[]{:S(2)}, u32[]{:S(2)}) %collective-permute-start.16) | collective-permute-done | bytes 65568 | tf_op jit(solution)/shard_map/ppermute | solution.py:154
  23.4 2.0 %collective-permute-done.5 = f32[1,128,128]{2,1,0:T(8,128)S(1)} collective-permute-done((f32[1,128,128]{2,1,0:T(8,128)S(1)}, f32[1,128,128]{2,1,0:T(8,128)S(1)}, u32[]{:S(2)}, u32[]{:S(2)}) %collective-permute-start.5) | collective-permute-done | bytes 65568 | tf_op jit(solution)/shard_map/ppermute | solution.py:154
  26.3 4.9 %collective-permute-start.6 = (f32[1,128,128]{2,1,0:T(8,128)S(1)}, f32[1,128,128]{2,1,0:T(8,128)S(1)}, u32[]{:S(2)}, u32[]{:S(2)}) collective-permute-start(f32[1,128,128]{2,1,0:T(8,128)S(1)} %get-tuple-element.55), channel_id=1, source_target_pairs={{0,8},{4,12},{1,9},{5,13},{2,10},{6,14},{3,11},{7,15}} | collective-permute-start | bytes 196616 | tf_op jit(solution)/shard_map/ppermute | solution.py:154
  32.6 1.8 %collective-permute-start.1 = (f32[1,128,128]{2,1,0:T(8,128)S(1)}, f32[1,128,128]{2,1,0:T(8,128)S(1)}, u32[]{:S(2)}, u32[]{:S(2)}) collective-permute-start(f32[1,128,128]{2,1,0:T(8,128)S(1)} %fusion), channel_id=1, source_target_pairs={{0,8},{4,12},{1,9},{5,13},{2,10},{6,14},{3,11},{7,15}} | collective-permute-start | bytes 196616 | tf_op jit(solution)/shard_map/ppermute | solution.py:154
  40.4 13.6 %shard_map.84 = (bf16[1024,1024]{1,0:T(8,128)(2,1)S(1)}, f32[1024,1024]{1,0:T(8,128)S(1)}) custom-call(bf16[1024,1024]{1,0:T(8,128)(2,1)S(1)} %copy-done.4, bf16[1024,1024]{1,0:T(8,128)(2,1)S(1)} %copy-done.1, bf16[1024,1024]{1,0:T(8,128)(2,1)S(1)} %copy-done.2), custom_call_target="tpu_custom_call" | custom-call | flops 1073741824 | bytes 12582912 | tf_op jit(solution)/shard_map/pallas_call | solution.py:140
  58.3 3.4 %collective-permute-done.9 = f32[1,128,128]{2,1,0:T(8,128)S(1)} collective-permute-done((f32[1,128,128]{2,1,0:T(8,128)S(1)}, f32[1,128,128]{2,1,0:T(8,128)S(1)}, u32[]{:S(2)}, u32[]{:S(2)}) %collective-permute-start.9) | collective-permute-done | bytes 65568 | tf_op jit(solution)/shard_map/ppermute | solution.py:154
  61.9 5.5 %shard_map.86 = (f32[1024,1024]{1,0:T(8,128)S(1)}, f32[2,1024]{1,0:T(2,128)S(1)}) custom-call(f32[1024,1024]{1,0:T(8,128)S(1)} %get-tuple-element.16.a_in, bf16[1024,1024]{1,0:T(8,128)(2,1)S(1)} %copy-done.4, f32[8,128,128]{2,1,0:T(8,128)S(1)} %select_dynamic-update-slice_fusion.8.p_ref, bf16[1024,1024]{1,0:T(8,128)(2,1)S(1)} %copy-done.6, f32[1,1024]{1,0:T(1,128)S(1)} %bitcast.1), custom_call_target="tpu_custom_call" | custom-call | flops 268435456 | bytes 12582912 | tf_op jit(solution)/shard_map/pallas_call | solution.py:140
  70.1 2.1 %collective-permute-done.21 = f32[2,1024]{1,0:T(2,128)S(1)} collective-permute-done((f32[2,1024]{1,0:T(2,128)S(1)}, f32[2,1024]{1,0:T(2,128)S(1)}, u32[]{:S(2)}, u32[]{:S(2)}) %collective-permute-start.21) | collective-permute-done | bytes 8224 | tf_op jit(solution)/shard_map/ppermute | solution.py:190
  72.2 5.7 %shard_map.87 = (bf16[1024,1024]{1,0:T(8,128)(2,1)}, bf16[1024,1024]{1,0:T(8,128)(2,1)S(1)}, f32[8,128,128]{2,1,0:T(8,128)S(1)}) custom-call(f32[1024,1024]{1,0:T(8,128)S(1)} %get-tuple-element.17.a_ref, bf16[1024,1024]{1,0:T(8,128)(2,1)S(1)} %copy-done.4, bf16[1024,1024]{1,0:T(8,128)(2,1)S(1)} %copy-done.6, f32[1,1024]{1,0:T(1,128)S(1)} %bitcast.2, ...), custom_call_target="tpu_custom_call" | custom-call | flops 268435456 | bytes 12582912 | tf_op jit(solution)/shard_map/pallas_call | solution.py:140
  80.2 3.4 %collective-permute-done.37 = f32[1,128,128]{2,1,0:T(8,128)S(1)} collective-permute-done((f32[1,128,128]{2,1,0:T(8,128)S(1)}, f32[1,128,128]{2,1,0:T(8,128)S(1)}, u32[]{:S(2)}, u32[]{:S(2)}) %collective-permute-start.37) | collective-permute-done | bytes 65568 | tf_op jit(solution)/shard_map/ppermute | solution.py:154
  92.3 14.5 %collective-permute-done.40 = f32[1,128,128]{2,1,0:T(8,128)} collective-permute-done((f32[1,128,128]{2,1,0:T(8,128)}, f32[1,128,128]{2,1,0:T(8,128)}, u32[]{:S(2)}, u32[]{:S(2)}) %collective-permute-start.40) | collective-permute-done | bytes 65568 | tf_op jit(solution)/shard_map/ppermute | solution.py:154
  115.8 5.0 %collective-permute-done.35 = f32[1,128,128]{2,1,0:T(8,128)S(1)} collective-permute-done((f32[1,128,128]{2,1,0:T(8,128)S(1)}, f32[1,128,128]{2,1,0:T(8,128)S(1)}, u32[]{:S(2)}, u32[]{:S(2)}) %collective-permute-start.35) | collective-permute-done | bytes 65568 | tf_op jit(solution)/shard_map/ppermute | solution.py:154
  124.4 1.6 copy-done.5
  126.0 1.6 copy-done.8
  127.6 1.6 copy-done.10
  129.2 20.1 %shard_map.88 = (bf16[1024,1024]{1,0:T(8,128)(2,1)}, f32[1024,1024]{1,0:T(8,128)S(1)}, f32[1024,1024]{1,0:T(8,128)S(1)}) custom-call(bf16[1024,1024]{1,0:T(8,128)(2,1)S(1)} %copy-done.5, bf16[1024,1024]{1,0:T(8,128)(2,1)S(1)} %copy-done.1, bf16[1024,1024]{1,0:T(8,128)(2,1)S(1)} %copy-done.3, bf16[1024,1024]{1,0:T(8,128)(2,1)S(1)} %copy-done.8, ...), custom_call_target="tpu_custom_call" | custom-call | flops 2415919104 | bytes 20971520 | tf_op jit(solution)/shard_map/pallas_call | solution.py:140
  152.5 3.1 %collective-permute-done.31 = f32[1,128,128]{2,1,0:T(8,128)S(1)} collective-permute-done((f32[1,128,128]{2,1,0:T(8,128)S(1)}, f32[1,128,128]{2,1,0:T(8,128)S(1)}, u32[]{:S(2)}, u32[]{:S(2)}) %collective-permute-start.31) | collective-permute-done | bytes 65568 | tf_op jit(solution)/shard_map/ppermute | solution.py:154
  155.7 6.2 %shard_map.89 = (bf16[1024,1024]{1,0:T(8,128)(2,1)}, bf16[1024,1024]{1,0:T(8,128)(2,1)}) custom-call(bf16[1024,1024]{1,0:T(8,128)(2,1)S(1)} %copy-done.1, bf16[1024,1024]{1,0:T(8,128)(2,1)S(1)} %copy-done.3, f32[1024,1024]{1,0:T(8,128)S(1)} %get-tuple-element.23.kl_ref, f32[1024,1024]{1,0:T(8,128)S(1)} %get-tuple-element.24.vl_ref, ...), custom_call_target="tpu_custom_call" | custom-call | flops 536870912 | bytes 16777216 | tf_op jit(solution)/shard_map/pallas_call | solution.py:140
  (133 shorter events, 46.8 us)
Async XLA Ops:
  7.2 5.2 %collective-permute-start.15 = (f32[1,128,128]{2,1,0:T(8,128)S(1)}, f32[1,128,128]{2,1,0:T(8,128)S(1)}, u32[]{:S(2)}, u32[]{:S(2)}) collective-permute-start(f32[1,128,128]{2,1,0:T(8,128)S(1)} %slice_select_fusion), channel_id=1, source_target_pairs={{0,4},{4,0},{8,12},{12,8},{16,20},{20,16},{24,28},{28,24},{1,5},{5... | collective-permute-start | bytes 196616 | tf_op jit(solution)/shard_map/ppermute | solution.py:154
  12.5 5.9 %collective-permute-start.16 = (f32[1,128,128]{2,1,0:T(8,128)S(1)}, f32[1,128,128]{2,1,0:T(8,128)S(1)}, u32[]{:S(2)}, u32[]{:S(2)}) collective-permute-start(f32[1,128,128]{2,1,0:T(8,128)S(1)} %get-tuple-element.58), channel_id=1, source_target_pairs={{0,8},{4,12},{1,9},{5,13},{2,10},{6,14},{3,11},{7,15}} | collective-permute-start | bytes 196616 | tf_op jit(solution)/shard_map/ppermute | solution.py:154
  19.1 4.3 %collective-permute-start.10 = (f32[1,128,128]{2,1,0:T(8,128)S(1)}, f32[1,128,128]{2,1,0:T(8,128)S(1)}, u32[]{:S(2)}, u32[]{:S(2)}) collective-permute-start(f32[1,128,128]{2,1,0:T(8,128)S(1)} %get-tuple-element.59), channel_id=1, source_target_pairs={{0,4},{4,0},{8,12},{12,8},{16,20},{20,16},{24,28},{28,24},{1,5},{5... | collective-permute-start | bytes 196616 | tf_op jit(solution)/shard_map/ppermute | solution.py:154
  20.6 4.8 %collective-permute-start.5 = (f32[1,128,128]{2,1,0:T(8,128)S(1)}, f32[1,128,128]{2,1,0:T(8,128)S(1)}, u32[]{:S(2)}, u32[]{:S(2)}) collective-permute-start(f32[1,128,128]{2,1,0:T(8,128)S(1)} %get-tuple-element.60), channel_id=1, source_target_pairs={{0,4},{4,0},{8,12},{12,8},{16,20},{20,16},{24,28},{28,24},{1,5},{5... | collective-permute-start | bytes 196616 | tf_op jit(solution)/shard_map/ppermute | solution.py:154
  21.2 4.2 %collective-permute-start.18 = (f32[1,128,128]{2,1,0:T(8,128)S(1)}, f32[1,128,128]{2,1,0:T(8,128)S(1)}, u32[]{:S(2)}, u32[]{:S(2)}) collective-permute-start(f32[1,128,128]{2,1,0:T(8,128)S(1)} %add.204), channel_id=1, source_target_pairs={{16,24},{20,28},{17,25},{21,29},{18,26},{22,30},{19,27},{23,31}} | collective-permute-start | bytes 196616 | tf_op jit(solution)/shard_map/ppermute | solution.py:154
  25.5 7.1 %collective-permute-start = (f32[1,128,128]{2,1,0:T(8,128)S(1)}, f32[1,128,128]{2,1,0:T(8,128)S(1)}, u32[]{:S(2)}, u32[]{:S(2)}) collective-permute-start(f32[1,128,128]{2,1,0:T(8,128)S(1)} %get-tuple-element.56), channel_id=1, source_target_pairs={{0,4},{4,0},{8,12},{12,8},{16,20},{20,16},{24,28},{28,24},{1,5},{5... | collective-permute-start | bytes 196616 | tf_op jit(solution)/shard_map/ppermute | solution.py:154
  26.3 8.1 %collective-permute-start.6 = (f32[1,128,128]{2,1,0:T(8,128)S(1)}, f32[1,128,128]{2,1,0:T(8,128)S(1)}, u32[]{:S(2)}, u32[]{:S(2)}) collective-permute-start(f32[1,128,128]{2,1,0:T(8,128)S(1)} %get-tuple-element.55), channel_id=1, source_target_pairs={{0,8},{4,12},{1,9},{5,13},{2,10},{6,14},{3,11},{7,15}} | collective-permute-start | bytes 196616 | tf_op jit(solution)/shard_map/ppermute | solution.py:154
  31.3 3.8 %collective-permute-start.11 = (f32[1,128,128]{2,1,0:T(8,128)S(1)}, f32[1,128,128]{2,1,0:T(8,128)S(1)}, u32[]{:S(2)}, u32[]{:S(2)}) collective-permute-start(f32[1,128,128]{2,1,0:T(8,128)S(1)} %get-tuple-element.57), channel_id=1, source_target_pairs={{0,8},{4,12},{1,9},{5,13},{2,10},{6,14},{3,11},{7,15}} | collective-permute-start | bytes 196616 | tf_op jit(solution)/shard_map/ppermute | solution.py:154
  39.2 19.1 %collective-permute-start.4 = (f32[1,128,128]{2,1,0:T(8,128)S(1)}, f32[1,128,128]{2,1,0:T(8,128)S(1)}, u32[]{:S(2)}, u32[]{:S(2)}) collective-permute-start(f32[1,128,128]{2,1,0:T(8,128)S(1)} %get-tuple-element.63), channel_id=1, source_target_pairs={{0,4},{4,0},{8,12},{12,8},{16,20},{20,16},{24,28},{28,24},{1,5},{5... | collective-permute-start | bytes 196616 | tf_op jit(solution)/shard_map/ppermute | solution.py:154
  55.4 6.4 %collective-permute-start.19 = (f32[1,128,128]{2,1,0:T(8,128)S(1)}, f32[1,128,128]{2,1,0:T(8,128)S(1)}, u32[]{:S(2)}, u32[]{:S(2)}) collective-permute-start(f32[1,128,128]{2,1,0:T(8,128)S(1)} %get-tuple-element.36), channel_id=1, source_target_pairs={{0,4},{4,0},{8,12},{12,8},{16,20},{20,16},{24,28},{28,24},{1,5},{5... | collective-permute-start | bytes 196616 | tf_op jit(solution)/shard_map/ppermute | solution.py:154
  56.3 5.5 %collective-permute-start.14 = (f32[1,128,128]{2,1,0:T(8,128)S(1)}, f32[1,128,128]{2,1,0:T(8,128)S(1)}, u32[]{:S(2)}, u32[]{:S(2)}) collective-permute-start(f32[1,128,128]{2,1,0:T(8,128)S(1)} %get-tuple-element.38), channel_id=1, source_target_pairs={{0,4},{4,0},{8,12},{12,8},{16,20},{20,16},{24,28},{28,24},{1,5},{5... | collective-permute-start | bytes 196616 | tf_op jit(solution)/shard_map/ppermute | solution.py:154
  57.4 4.3 %collective-permute-start.9 = (f32[1,128,128]{2,1,0:T(8,128)S(1)}, f32[1,128,128]{2,1,0:T(8,128)S(1)}, u32[]{:S(2)}, u32[]{:S(2)}) collective-permute-start(f32[1,128,128]{2,1,0:T(8,128)S(1)} %get-tuple-element.61), channel_id=1, source_target_pairs={{0,4},{4,0},{8,12},{12,8},{16,20},{20,16},{24,28},{28,24},{1,5},{5... | collective-permute-start | bytes 196616 | tf_op jit(solution)/shard_map/ppermute | solution.py:154
  79.3 4.3 %collective-permute-start.37 = (f32[1,128,128]{2,1,0:T(8,128)S(1)}, f32[1,128,128]{2,1,0:T(8,128)S(1)}, u32[]{:S(2)}, u32[]{:S(2)}) collective-permute-start(f32[1,128,128]{2,1,0:T(8,128)S(1)} %slice_select_fusion.8), channel_id=1, source_target_pairs={{28,24},{24,28},{20,16},{16,20},{12,8},{8,12},{4,0},{0,4},{29,25},... | collective-permute-start | bytes 196616 | tf_op jit(solution)/shard_map/ppermute | solution.py:154
  85.7 4.9 %collective-permute-start.32 = (f32[1,128,128]{2,1,0:T(8,128)}, f32[1,128,128]{2,1,0:T(8,128)S(1)}, u32[]{:S(2)}, u32[]{:S(2)}) collective-permute-start(f32[1,128,128]{2,1,0:T(8,128)} %get-tuple-element.48), channel_id=1, source_target_pairs={{28,24},{24,28},{20,16},{16,20},{12,8},{8,12},{4,0},{0,4},{29,25},... | collective-permute-start | bytes 196616 | tf_op jit(solution)/shard_map/ppermute | solution.py:154
  86.6 4.5 %collective-permute-start.27 = (f32[1,128,128]{2,1,0:T(8,128)}, f32[1,128,128]{2,1,0:T(8,128)S(1)}, u32[]{:S(2)}, u32[]{:S(2)}) collective-permute-start(f32[1,128,128]{2,1,0:T(8,128)} %get-tuple-element.49), channel_id=1, source_target_pairs={{28,24},{24,28},{20,16},{16,20},{12,8},{8,12},{4,0},{0,4},{29,25},... | collective-permute-start | bytes 196616 | tf_op jit(solution)/shard_map/ppermute | solution.py:154
  87.8 4.5 %collective-permute-start.22 = (f32[1,128,128]{2,1,0:T(8,128)}, f32[1,128,128]{2,1,0:T(8,128)S(1)}, u32[]{:S(2)}, u32[]{:S(2)}) collective-permute-start(f32[1,128,128]{2,1,0:T(8,128)} %get-tuple-element.50), channel_id=1, source_target_pairs={{28,24},{24,28},{20,16},{16,20},{12,8},{8,12},{4,0},{0,4},{29,25},... | collective-permute-start | bytes 196616 | tf_op jit(solution)/shard_map/ppermute | solution.py:154
  89.3 17.5 %collective-permute-start.40 = (f32[1,128,128]{2,1,0:T(8,128)}, f32[1,128,128]{2,1,0:T(8,128)}, u32[]{:S(2)}, u32[]{:S(2)}) collective-permute-start(f32[1,128,128]{2,1,0:T(8,128)} %add.234), channel_id=1, source_target_pairs={{12,4},{8,0},{13,5},{9,1},{14,6},{10,2},{15,7},{11,3}} | collective-permute-start | bytes 196616 | tf_op jit(solution)/shard_map/ppermute | solution.py:154
  111.8 9.0 %collective-permute-start.35 = (f32[1,128,128]{2,1,0:T(8,128)S(1)}, f32[1,128,128]{2,1,0:T(8,128)S(1)}, u32[]{:S(2)}, u32[]{:S(2)}) collective-permute-start(f32[1,128,128]{2,1,0:T(8,128)S(1)} %add.227), channel_id=1, source_target_pairs={{12,4},{8,0},{13,5},{9,1},{14,6},{10,2},{15,7},{11,3}} | collective-permute-start | bytes 196616 | tf_op jit(solution)/shard_map/ppermute | solution.py:154
  113.1 9.0 %collective-permute-start.30 = (f32[1,128,128]{2,1,0:T(8,128)S(1)}, f32[1,128,128]{2,1,0:T(8,128)S(1)}, u32[]{:S(2)}, u32[]{:S(2)}) collective-permute-start(f32[1,128,128]{2,1,0:T(8,128)S(1)} %add.220), channel_id=1, source_target_pairs={{12,4},{8,0},{13,5},{9,1},{14,6},{10,2},{15,7},{11,3}} | collective-permute-start | bytes 196616 | tf_op jit(solution)/shard_map/ppermute | solution.py:154
  114.5 9.0 %collective-permute-start.25 = (f32[1,128,128]{2,1,0:T(8,128)S(1)}, f32[1,128,128]{2,1,0:T(8,128)S(1)}, u32[]{:S(2)}, u32[]{:S(2)}) collective-permute-start(f32[1,128,128]{2,1,0:T(8,128)S(1)} %add.213), channel_id=1, source_target_pairs={{12,4},{8,0},{13,5},{9,1},{14,6},{10,2},{15,7},{11,3}} | collective-permute-start | bytes 196616 | tf_op jit(solution)/shard_map/ppermute | solution.py:154
  123.5 29.0 %collective-permute-start.26 = (f32[1,128,128]{2,1,0:T(8,128)S(1)}, f32[1,128,128]{2,1,0:T(8,128)S(1)}, u32[]{:S(2)}, u32[]{:S(2)}) collective-permute-start(f32[1,128,128]{2,1,0:T(8,128)S(1)} %get-tuple-element.51), channel_id=1, source_target_pairs={{28,24},{24,28},{20,16},{16,20},{12,8},{8,12},{4,0},{0,4},{29,25},... | collective-permute-start | bytes 196616 | tf_op jit(solution)/shard_map/ppermute | solution.py:154
  149.3 6.4 %collective-permute-start.41 = (f32[1,128,128]{2,1,0:T(8,128)S(1)}, f32[1,128,128]{2,1,0:T(8,128)S(1)}, u32[]{:S(2)}, u32[]{:S(2)}) collective-permute-start(f32[1,128,128]{2,1,0:T(8,128)S(1)} %get-tuple-element.28), channel_id=1, source_target_pairs={{28,24},{24,28},{20,16},{16,20},{12,8},{8,12},{4,0},{0,4},{29,25},... | collective-permute-start | bytes 196616 | tf_op jit(solution)/shard_map/ppermute | solution.py:154
  150.4 5.2 %collective-permute-start.36 = (f32[1,128,128]{2,1,0:T(8,128)S(1)}, f32[1,128,128]{2,1,0:T(8,128)S(1)}, u32[]{:S(2)}, u32[]{:S(2)}) collective-permute-start(f32[1,128,128]{2,1,0:T(8,128)S(1)} %get-tuple-element.30), channel_id=1, source_target_pairs={{28,24},{24,28},{20,16},{16,20},{12,8},{8,12},{4,0},{0,4},{29,25},... | collective-permute-start | bytes 196616 | tf_op jit(solution)/shard_map/ppermute | solution.py:154
  151.3 4.3 %collective-permute-start.31 = (f32[1,128,128]{2,1,0:T(8,128)S(1)}, f32[1,128,128]{2,1,0:T(8,128)S(1)}, u32[]{:S(2)}, u32[]{:S(2)}) collective-permute-start(f32[1,128,128]{2,1,0:T(8,128)S(1)} %get-tuple-element.53), channel_id=1, source_target_pairs={{28,24},{24,28},{20,16},{16,20},{12,8},{8,12},{4,0},{0,4},{29,25},... | collective-permute-start | bytes 196616 | tf_op jit(solution)/shard_map/ppermute | solution.py:154
  (30 other events, 138.2 us)

commit v2 on v0

v2 whole, which is shorter than its diff:
```python
import functools

import jax
import jax.numpy as jnp
from jax import lax
from jax.experimental import pallas as pl
from jax.experimental.pallas import tpu as pltpu
from jax.sharding import PartitionSpec as P

HEAD_DIM = 128
BLOCK = 128
WIDTH = 4096
epsilon = 1e-05

F32 = jnp.float32
BF16 = jnp.bfloat16
VMEM = pl.BlockSpec(memory_space=pltpu.VMEM)
HBM = pl.BlockSpec(memory_space=pltpu.HBM)


def dot(a, b, ca, cb):
    return lax.dot_general(a, b, (((ca,), (cb,)), ((), ())), preferred_element_type=F32)


def causal_mask():
    row = lax.broadcasted_iota(jnp.int32, (BLOCK, BLOCK), 0)
    col = lax.broadcasted_iota(jnp.int32, (BLOCK, BLOCK), 1)
    return col <= row


def rows_of(n):
    return slice(n * BLOCK, (n + 1) * BLOCK)


def cols_of(h):
    return slice(h * HEAD_DIM, (h + 1) * HEAD_DIM)


def cols_at(h):
    return pl.ds(pl.multiple_of(h * HEAD_DIM, HEAD_DIM), HEAD_DIM)


def state_kernel(first, heads, k_hbm, v_hbm, k_ref, v_ref, t_ref, sems):
    copies = []
    for h in range(heads):
        for i, (src, dst) in enumerate(((k_hbm, k_ref), (v_hbm, v_ref))):
            copies.append(pltpu.make_async_copy(src.at[:, cols_of(first + h)], dst.at[:, cols_of(h)], sems.at[i, h]))
            copies[-1].start()
    for h in range(heads):
        copies[2 * h].wait()
        copies[2 * h + 1].wait()
        t_ref[h] = dot(k_ref[:, cols_of(h)], v_ref[:, cols_of(h)], 0, 0)


def local_kernel(first, heads, blocks, q_ref, k_ref, v_ref, w_ref, a_ref, low):
    causal = causal_mask()

    def head(h, carry):
        c, cq = cols_at(h), cols_at(h + first)
        for n in range(0, blocks, 2):
            if n + 1 < blocks:
                both = slice(n * BLOCK, (n + 2) * BLOCK)
                s = dot(q_ref[both, cq], k_ref[both, c], 1, 1)
                w_ref[rows_of(n), c] = jnp.where(causal, s[:BLOCK, :BLOCK], 0.0).astype(BF16)
                w_ref[rows_of(n + 1), c] = jnp.where(causal, s[BLOCK:, BLOCK:], 0.0).astype(BF16)
            else:
                s = dot(q_ref[rows_of(n), cq], k_ref[rows_of(n), c], 1, 1)
                w_ref[rows_of(n), c] = jnp.where(causal, s, 0.0).astype(BF16)
        prefix = None
        for n in range(blocks - 1):
            s = dot(k_ref[rows_of(n), c], v_ref[rows_of(n), c], 0, 0)
            prefix = s if prefix is None else prefix + s
            low[rows_of(n), :] = prefix.astype(BF16)
        a_ref[rows_of(0), c] = dot(w_ref[rows_of(0), c], v_ref[rows_of(0), c], 1, 0)
        for n in range(1, blocks):
            left = jnp.concatenate([w_ref[rows_of(n), c], q_ref[rows_of(n), cq]], axis=1)
            right = jnp.concatenate([v_ref[rows_of(n), c], low[rows_of(n - 1), :]], axis=0)
            a_ref[rows_of(n), c] = dot(left, right, 1, 0)
        return carry

    lax.fori_loop(0, heads, head, 0, unroll=2)


def stats_kernel(first, heads, blocks, a_in, q_ref, p_ref, og_ref, gain_ref, a_ref, s_ref):
    low = [p_ref[h].astype(BF16) for h in range(heads)]
    for n in range(blocks):
        r = rows_of(n)
        squares = dots = None
        for h in range(heads):
            c, cq = cols_of(h), cols_of(first + h)
            att = a_in[r, c] + dot(q_ref[r, cq], low[h], 1, 0)
            a_ref[r, c] = att
            scaled = gain_ref[:, cq] * og_ref[r, cq].astype(F32)
            squares = att * att if squares is None else squares + att * att
            dots = scaled * att if dots is None else dots + scaled * att
        s_ref[0:1, r] = jnp.sum(squares.T, axis=0, keepdims=True)
        s_ref[1:2, r] = jnp.sum(dots.T, axis=0, keepdims=True)


def factor_kernel(blocks, s_ref, inv_ref, coef_ref):
    inverse = lax.rsqrt(s_ref[0:1, :] / WIDTH + epsilon)
    factor = inverse * inverse * inverse * s_ref[1:2, :] / WIDTH
    for n in range(blocks):
        inv_ref[rows_of(n), :] = jnp.broadcast_to(inverse[:, rows_of(n)], (BLOCK, BLOCK)).T
        coef_ref[rows_of(n), :] = jnp.broadcast_to(factor[:, rows_of(n)], (BLOCK, BLOCK)).T


def grad_kernel(first, heads, a_ref, q_ref, og_ref, gain_ref, inv_ref, coef_ref, g_ref, t_ref):
    for h in range(heads):
        c, cq = cols_of(h), cols_of(first + h)
        scaled = gain_ref[:, cq] * og_ref[:, cq].astype(F32)
        grad = (inv_ref[...] * scaled - coef_ref[...] * a_ref[:, c]).astype(BF16)
        g_ref[:, c] = grad
        t_ref[h] = dot(q_ref[:, cq], grad, 0, 0)


def mixed_kernel(parts, heads, *refs):
    a_refs, (gain_ref, inv_ref, m_ref) = refs[:parts], refs[parts:]
    for p, a_ref in enumerate(a_refs):
        for h in range(heads):
            cq = cols_of(p * heads + h)
            m_ref[:, cq] = (gain_ref[:, cq] * a_ref[:, cols_of(h)] * inv_ref[...]).astype(BF16)


def back_kernel(first, inner, heads, blocks, q_ref, k_ref, v_ref, w_ref, g_ref, p_ref, *rest):
    qg_hbm, kl_ref, vl_ref, qg, bw, plow, slow, sems = rest[-8:]
    causal = causal_mask()

    def copy_out(h, c, cq):
        return pltpu.make_async_copy(qg.at[:, c], qg_hbm.at[:, cq], sems.at[h])

    def head(h, carry):
        c, ci, cq = cols_at(h), cols_at(h + inner), cols_at(h + first)
        for n in range(blocks):
            r = rows_of(n)
            bw[r, :] = jnp.where(causal, dot(g_ref[r, ci], v_ref[r, ci], 1, 1), 0.0).astype(BF16)
        prefix = p_ref[h + inner]
        plow[rows_of(0), :] = prefix.astype(BF16)
        for n in range(blocks - 1):
            prefix = prefix + dot(k_ref[rows_of(n), ci], v_ref[rows_of(n), ci], 0, 0)
            plow[rows_of(n + 1), :] = prefix.astype(BF16)
        suffix = None
        for n in reversed(range(1, blocks)):
            s = dot(q_ref[rows_of(n), cq], g_ref[rows_of(n), ci], 0, 0)
            suffix = s if suffix is None else suffix + s
            slow[rows_of(n - 1), :] = suffix.astype(BF16)
        for n in range(blocks):
            r = rows_of(n)
            q, k, v, g = q_ref[r, cq], k_ref[r, ci], v_ref[r, ci], g_ref[r, ci]
            qg[r, c] = (dot(bw[r, :], k, 1, 0) + dot(g, plow[r, :], 1, 1)).astype(BF16)
            kp, vp = dot(bw[r, :], q, 0, 0), dot(w_ref[r, ci], g, 0, 0)
            if n + 1 < blocks:
                kp, vp = kp + dot(v, slow[r, :], 1, 1), vp + dot(k, slow[r, :], 1, 0)
            kl_ref[r, c] = kp
            vl_ref[r, c] = vp
        copy_out(h, c, cq).start()
        return carry

    lax.fori_loop(0, heads, head, 0, unroll=2)
    for h in range(heads):
        copy_out(h, cols_of(h), cols_of(h + first)).wait()


def last_kernel(first, pieces, heads, k_ref, v_ref, s_ref, *rest):
    kls, vls = rest[:pieces], rest[pieces : 2 * pieces]
    kg_hbm, vg_hbm, kg, vg, sems = rest[-5:]
    copies = []
    for p in range(pieces):
        for i in range(heads):
            h = p * heads + i
            c, cq = cols_of(h), cols_of(first + h)
            low = s_ref[h].astype(BF16)
            kg[:, c] = (kls[p][:, cols_of(i)] + dot(v_ref[:, c], low, 1, 1)).astype(BF16)
            copies.append(pltpu.make_async_copy(kg.at[:, c], kg_hbm.at[:, cq], sems.at[0, h]))
            copies[-1].start()
            vg[:, c] = (vls[p][:, cols_of(i)] + dot(k_ref[:, c], low, 1, 0)).astype(BF16)
            copies.append(pltpu.make_async_copy(vg.at[:, c], vg_hbm.at[:, cq], sems.at[1, h]))
            copies[-1].start()
    for copy in copies:
        copy.wait()


def call(kernel, ins, outs, in_specs=None, out_specs=None, scratch=(), aliases=None, flops=0, vmem=6):
    nbytes = sum(a.size * a.dtype.itemsize for a in ins)
    return pl.pallas_call(
        kernel,
        in_specs=in_specs or [VMEM] * len(ins),
        out_specs=tuple(out_specs or [VMEM] * len(outs)),
        out_shape=tuple(jax.ShapeDtypeStruct(shape, dtype) for shape, dtype in outs),
        scratch_shapes=list(scratch),
        input_output_aliases=aliases or {},
        compiler_params=pltpu.CompilerParams(vmem_limit_bytes=vmem << 20),
        cost_estimate=pl.CostEstimate(flops=flops, bytes_accessed=nbytes, transcendentals=0),
    )(*ins)


def scan_stages(states, size, own, reverse):
    place = (lambda i: size - 1 - i) if reverse else (lambda i: i)
    perm = lambda pairs: [(place(i), place(j)) for i, j in pairs]
    outer = size // 2
    swap = [(i, i ^ 1) for i in range(size)]
    low = own % 2 == 0
    first = own % 2 == (1 if reverse else 0)
    half = states.shape[0] // 2
    mine = jnp.where(low, states[:half], states[half:])
    other = jnp.where(low, states[half:], states[:half])
    got = yield other, perm(swap)
    pair = mine + got
    total = None
    if outer <= 4:
        running = pair
        for hop in range(outer - 1):
            r = yield running, perm([(2 * hop, 2 * hop + 2), (2 * hop + 1, 2 * hop + 3)])
            total = r if total is None else total + r
            running = r + pair
    else:
        total = yield pair, perm([(i, i + 2) for i in range(size - 2)])
        step = 1
        while step < outer - 1:
            r = yield total, perm([(i, i + 2 * step) for i in range(size - 2 * step)])
            total = total + r
            step *= 2
    answer = yield jnp.where(first, total + mine, total), perm(swap)
    kept = jnp.where(first, total, total + got)
    return jnp.concatenate([jnp.where(low, kept, answer), jnp.where(low, answer, kept)], axis=0)


def drive(makers, pieces):
    live, done, behind, stage = {}, {}, (), 0
    while live or stage < max(len(makers), len(pieces)):
        if stage < len(makers):
            scan = makers[stage]()
            live[stage] = (scan, next(scan))
        order = sorted(live)
        operands = [live[i][1][0] for i in order]
        tied = lax.optimization_barrier((*operands, *behind))[: len(operands)] if operands else ()
        arrived = [lax.ppermute(a, "seq", live[i][1][1]) for a, i in zip(tied, order)]
        behind = pieces[stage](tied, done) if stage < len(pieces) else ()
        for i, r in zip(order, arrived):
            try:
                live[i] = (live[i][0], live[i][0].send(r))
            except StopIteration as stop:
                done[i] = stop.value
                del live[i]
        stage += 1
    return done


def after(tied, *arrays):
    return lax.optimization_barrier((*arrays, *tied))[: len(arrays)]


def head_sum(a, size):
    if size & (size - 1):
        return lax.psum(a, "head")
    step = 1
    while step < size:
        a = a + lax.ppermute(a, "head", [(i, i ^ step) for i in range(size)])
        step *= 2
    return a


def body(seq_size, head_size, queries, keys, values, gain, out_grad):
    rows, width = queries.shape
    blocks, heads = rows // BLOCK, width // HEAD_DIM
    half = heads // 2
    part = half * HEAD_DIM
    own = lax.axis_index("seq")
    gain = gain.reshape(1, width)
    unit = 2 * rows * HEAD_DIM * HEAD_DIM
    state = (half, HEAD_DIM, HEAD_DIM)
    ks, vs, ts, ws, atts, sums, grads, backs = ({} for _ in range(8))

    def make_state(i):
        ks[i], vs[i], ts[i] = call(
            functools.partial(state_kernel, i * half, half),
            [keys, values],
            [((rows, part), BF16), ((rows, part), BF16), (state, F32)],
            in_specs=[HBM, HBM],
            scratch=[pltpu.SemaphoreType.DMA((2, half))],
            flops=unit * half,
        )

    def make_local(i, tied):
        (k,) = after(tied, ks[i])
        ws[i], atts[i] = call(
            functools.partial(local_kernel, i * half, half, blocks),
            [queries, k, vs[i]],
            [((rows, part), BF16), ((rows, part), F32)],
            scratch=[pltpu.VMEM((rows, HEAD_DIM), BF16)],
            flops=4 * unit * half,
        )
        return ws[i], atts[i]

    def make_stats(i, prefix):
        atts[i], sums[i] = call(
            functools.partial(stats_kernel, i * half, half, blocks),
            [atts[i], queries, prefix, out_grad, gain],
            [((rows, part), F32), ((2, rows), F32)],
            aliases={0: 0},
            flops=unit * half,
        )

    make_state(0)

    def piece_state(tied, done):
        make_state(1)
        return (ts[1],)

    def piece_stats(tied, done):
        make_stats(0, done[0])
        return ()

    prefixes = drive(
        [lambda i=i: scan_stages(ts[i], seq_size, own, False) for i in range(2)],
        [
            piece_state,
            lambda tied, done: make_local(0, tied),
            lambda tied, done: make_local(1, tied),
        ],
    )
    make_stats(0, prefixes[0])
    make_stats(1, prefixes[1])
    total = head_sum(sums[0] + sums[1], head_size)
    inverse, coef = call(functools.partial(factor_kernel, blocks), [total], [((rows, BLOCK), F32)] * 2)

    def make_grad(i):
        grads[i], backs[i] = call(
            functools.partial(grad_kernel, i * half, half),
            [atts[i], queries, out_grad, gain, inverse, coef],
            [((rows, part), BF16), (state, F32)],
            flops=unit * half,
        )

    made = {"query": None}
    locals_ = {}
    size = max(1, half // 2)
    count = half // size

    def make_back(i, j, tied):
        (g,) = after(tied, grads[i])
        first, inner = i * half + j * size, j * size
        ins = [queries, ks[i], vs[i], ws[i], g, prefixes[i]]
        specs, aliases = [VMEM] * len(ins), {}
        if made["query"] is not None:
            aliases = {len(ins): 0}
            ins.append(made["query"])
            specs.append(HBM)
        made["query"], kl, vl = call(
            functools.partial(back_kernel, first, inner, size, blocks),
            ins,
            [((rows, width), BF16), ((rows, size * HEAD_DIM), F32), ((rows, size * HEAD_DIM), F32)],
            in_specs=specs,
            out_specs=[HBM, VMEM, VMEM],
            scratch=[pltpu.VMEM((rows, size * HEAD_DIM), BF16)]
            + [pltpu.VMEM((rows, HEAD_DIM), BF16)] * 3
            + [pltpu.SemaphoreType.DMA((size,))],
            aliases=aliases,
            flops=9 * unit * size,
        )
        locals_[i, j] = (kl, vl)
        return kl, vl

    def make_mixed(tied):
        (inv,) = after(tied, inverse)
        (made["mixed"],) = call(
            functools.partial(mixed_kernel, 2, half), [atts[0], atts[1], gain, inv], [((rows, width), BF16)]
        )
        return (made["mixed"],)

    def make_last(i, suffix):
        ins = [ks[i], vs[i], suffix]
        ins += [locals_[i, j][0] for j in range(count)] + [locals_[i, j][1] for j in range(count)]
        specs, aliases = [VMEM] * len(ins), {}
        if "key" in made:
            aliases = {len(ins): 0, len(ins) + 1: 1}
            ins += [made["key"], made["value"]]
            specs += [HBM, HBM]
        made["key"], made["value"] = call(
            functools.partial(last_kernel, i * half, count, size),
            ins,
            [((rows, width), BF16)] * 2,
            in_specs=specs,
            out_specs=[HBM, HBM],
            scratch=[pltpu.VMEM((rows, part), BF16)] * 2 + [pltpu.SemaphoreType.DMA((2, half))],
            aliases=aliases,
            flops=2 * unit * half,
            vmem=8,
        )
        return ()

    make_grad(0)

    def piece_grad(tied, done):
        make_grad(1)
        return (backs[1],)

    work = [functools.partial(make_back, i, j) for i in range(2) for j in range(count)]
    suffixes = drive(
        [lambda i=i: scan_stages(backs[i], seq_size, own, True) for i in range(2)],
        [piece_grad] + [lambda tied, done, w=w: w(tied) for w in work],
    )
    make_mixed(())
    make_last(0, suffixes[0])
    make_last(1, suffixes[1])
    return made["mixed"], made["query"], made["key"], made["value"]


def solution(mesh):
    placed = (P("seq", "head"), P("seq", "head"), P("seq", "head"), P("head"), P("seq", "head"))
    return jax.shard_map(
        functools.partial(body, mesh.shape["seq"], mesh.shape["head"]),
        mesh=mesh,
        in_specs=placed,
        out_specs=(P("seq", "head"),) * 4,
        check_vma=False,
    )
```

time: 249 us -> 102 us (0.41)
  waiting for transfers between devices: 106 us -> 21.9 us
  local copies, waits for them, and re-layouts: 58.1 us -> 12.3 us
  matrix products: 43.1 us -> 0 us
  Pallas kernels: 0 us -> 30.1 us
  starting transfers between devices: 0.08 us -> 29.6 us
  other arithmetic: 20.6 us -> 4.75 us
  between operations: 14.3 us -> 1.65 us
  blocking collectives: 5.77 us -> 0 us
    all_gather x2 -> x0, waiting for transfers between devices: 106 us -> none  [the longest x1 60.9 us: body(): shards = lax.all_gather(running[None], 'seq', axis=0, tiled=True)]
    dot_general x12 -> x0, matrix products: 43.1 us -> none  [the longest x1 7.01 us: body(): jnp.einsum('nihd,nhde->nihe', query_blocks, prefixes, preferred_element_t...]
    pallas_call x0 -> x16, Pallas kernels: none -> 30.1 us  [call(): pl.pallas_call(kernel, in_specs=in_specs or [VMEM] * len(ins), out_specs=...]
    ppermute x0 -> x22, starting transfers between devices: none -> 29.6 us  [the longest x20 28 us: drive(): lax.ppermute(a, 'seq', live[i][1][1])]
    ppermute x0 -> x22, waiting for transfers between devices: none -> 21.9 us  [the longest x20 18.7 us: drive(): lax.ppermute(a, 'seq', live[i][1][1])]
    slice x6 -> x0, local copies, waits for them, and re-layouts: 15.1 us -> none  [the longest x2 8.75 us: body(): local_suffix = jnp.concatenate([qg_running[1:], zero_state[None]], axis=0)]
    convert_element_type x4 -> x0, local copies, waits for them, and re-layouts: 10.2 us -> none  [the longest x2 7.43 us: body(): value_grad = value_part.reshape(row_count, local_width).astype(jnp.bfloat16)]
    reduce_sum x3 -> x0, other arithmetic: 9.19 us -> none  [the longest x1 3.57 us: body(): jnp.sum(scaled * attended, axis=1)]
  transfers between devices with their start and end apart: 2 -> 22, of which waited for: 2 -> 11; matrix products, arithmetic and copies ran while one was open for 15% -> 2% of each run, Pallas kernels for 0% -> 23%
where the time goes in v2:
time: 102 us; the launch traced here: 100 us
  Pallas kernels  30.1 us (30%)
  starting transfers between devices  29.6 us (29%)
  waiting for transfers between devices  21.9 us (21%)
  local copies, waits for them, and re-layouts  12.3 us (12%)
  other arithmetic  4.75 us (5%)
  between operations  1.65 us (2%)
    pallas_call x16, Pallas kernels, call(): pl.pallas_call(kernel, in_specs=in_specs or [VMEM] * len(ins), out_specs=...  30.1 us
    ppermute x20, starting transfers between devices, drive(): lax.ppermute(a, 'seq', live[i][1][1])  28 us
    ppermute x20, waiting for transfers between devices, drive(): lax.ppermute(a, 'seq', live[i][1][1])  18.7 us
    unnamed x98, local copies, waits for them, and re-layouts  12.3 us
    ppermute x2, waiting for transfers between devices, head_sum(): a = a + lax.ppermute(a, 'head', [(i, i ^ step) for i in range(size)])  3.29 us
    add x8, other arithmetic, scan_stages(): running = r + pair  2.41 us
  transfers between devices with their start and end apart: 22, of which 11 were waited for; matrix products, arithmetic and copies ran while one was open for 2% of the time, Pallas kernels for 23%

profile of v2, /device:TPU:0, one launch (start us, length us, event | category | flops | bytes accessed | tf_op | source)
XLA Modules:
  0.0 100.4 jit_solution(16458941731966814383)
XLA Ops:
  0.7 1.6 %copy-done.14 = bf16[1024,1024]{1,0:T(8,128)(2,1)S(1)} copy-done((bf16[1024,1024]{1,0:T(8,128)(2,1)S(1)}, bf16[1024,1024]{1,0:T(8,128)(2,1)}, u32[]{:S(2)}) %copy-start.14) | copy-done | bytes 2097176
  2.2 1.6 %copy-done.16 = bf16[1024,1024]{1,0:T(8,128)(2,1)S(1)} copy-done((bf16[1024,1024]{1,0:T(8,128)(2,1)S(1)}, bf16[1024,1024]{1,0:T(8,128)(2,1)}, u32[]{:S(2)}) %copy-start.16) | copy-done | bytes 2097176
  3.8 1.7 %shard_map.84 = (bf16[1024,512]{1,0:T(8,128)(2,1)S(1)}, bf16[1024,512]{1,0:T(8,128)(2,1)S(1)}, f32[4,128,128]{2,1,0:T(8,128)S(1)}) custom-call(bf16[1024,1024]{1,0:T(8,128)(2,1)S(1)} %copy-done.14, bf16[1024,1024]{1,0:T(8,128)(2,1)S(1)} %copy-done.16), custom_call_target="tpu_custom_call" | custom-call | flops 134217728 | bytes 4194304 | tf_op jit(solution)/shard_map/pallas_call | solution.py:185
  5.6 3.0 %collective-permute-start = (f32[2,128,128]{2,1,0:T(8,128)S(1)}, f32[2,128,128]{2,1,0:T(8,128)S(1)}, u32[]{:S(2)}, u32[]{:S(2)}) collective-permute-start(f32[2,128,128]{2,1,0:T(8,128)S(1)} %slice_select_fusion.6), channel_id=1, source_target_pairs={{0,4},{4,0},{8,12},{12,8},{16,20},{20,16},{24,28},{28,24},{1,5},{5... | collective-permute-start | bytes 393224 | tf_op jit(solution)/shard_map/ppermute | solution.py:237
  8.6 1.7 %shard_map.85 = (bf16[1024,512]{1,0:T(8,128)(2,1)S(1)}, bf16[1024,512]{1,0:T(8,128)(2,1)S(1)}, f32[4,128,128]{2,1,0:T(8,128)S(1)}) custom-call(bf16[1024,1024]{1,0:T(8,128)(2,1)S(1)} %copy-done.15, bf16[1024,1024]{1,0:T(8,128)(2,1)S(1)} %copy-done.17), custom_call_target="tpu_custom_call" | custom-call | flops 134217728 | bytes 4194304 | tf_op jit(solution)/shard_map/pallas_call | solution.py:185
  10.4 1.7 %collective-permute-done = f32[2,128,128]{2,1,0:T(8,128)S(1)} collective-permute-done((f32[2,128,128]{2,1,0:T(8,128)S(1)}, f32[2,128,128]{2,1,0:T(8,128)S(1)}, u32[]{:S(2)}, u32[]{:S(2)}) %collective-permute-start) | collective-permute-done | bytes 131104 | tf_op jit(solution)/shard_map/ppermute | solution.py:237
  12.1 3.7 %collective-permute-start.1 = (f32[2,128,128]{2,1,0:T(8,128)S(1)}, f32[2,128,128]{2,1,0:T(8,128)S(1)}, u32[]{:S(2)}, u32[]{:S(2)}) collective-permute-start(f32[2,128,128]{2,1,0:T(8,128)S(1)} %fusion), channel_id=1, source_target_pairs={{0,8},{4,12},{1,9},{5,13},{2,10},{6,14},{3,11},{7,15}} | collective-permute-start | bytes 393224 | tf_op jit(solution)/shard_map/ppermute | solution.py:237
  17.4 2.1 %shard_map.86 = (bf16[1024,512]{1,0:T(8,128)(2,1)S(1)}, f32[1024,512]{1,0:T(8,128)S(1)}) custom-call(bf16[1024,1024]{1,0:T(8,128)(2,1)S(1)} %copy-done, bf16[1024,512]{1,0:T(8,128)(2,1)S(1)} %get-tuple-element.68.k_ref, bf16[1024,512]{1,0:T(8,128)(2,1)S(1)} %get-tuple-element.69.v_ref), custom_call_target="tpu_custom_call" | custom-call | flops 536870912 | bytes 4194304 | tf_op jit(solution)/shard_map/pallas_call | solution.py:185
  21.6 3.5 %collective-permute-start.4 = (f32[2,128,128]{2,1,0:T(8,128)S(1)}, f32[2,128,128]{2,1,0:T(8,128)S(1)}, u32[]{:S(2)}, u32[]{:S(2)}) collective-permute-start(f32[2,128,128]{2,1,0:T(8,128)S(1)} %fusion.1), channel_id=1, source_target_pairs={{0,8},{4,12},{1,9},{5,13},{2,10},{6,14},{3,11},{7,15}} | collective-permute-start | bytes 393224 | tf_op jit(solution)/shard_map/ppermute | solution.py:237
  25.1 2.1 %shard_map.87 = (bf16[1024,512]{1,0:T(8,128)(2,1)S(1)}, f32[1024,512]{1,0:T(8,128)S(1)}) custom-call(bf16[1024,1024]{1,0:T(8,128)(2,1)S(1)} %copy-done, bf16[1024,512]{1,0:T(8,128)(2,1)S(1)} %get-tuple-element.75.k_ref, bf16[1024,512]{1,0:T(8,128)(2,1)S(1)} %get-tuple-element.76.v_ref), custom_call_target="tpu_custom_call" | custom-call | flops 536870912 | bytes 4194304 | tf_op jit(solution)/shard_map/pallas_call | solution.py:185
  29.9 1.6 %collective-permute-start.7 = (f32[2,128,128]{2,1,0:T(8,128)S(1)}, f32[2,128,128]{2,1,0:T(8,128)S(1)}, u32[]{:S(2)}, u32[]{:S(2)}) collective-permute-start(f32[2,128,128]{2,1,0:T(8,128)S(1)} %get-tuple-element.81), channel_id=1, source_target_pairs={{0,4},{4,0},{8,12},{12,8},{16,20},{20,16},{24,28},{28,24},{1,5},{5... | collective-permute-start | bytes 393224 | tf_op jit(solution)/shard_map/ppermute | solution.py:237
  32.1 2.8 %collective-permute-done.7 = f32[2,128,128]{2,1,0:T(8,128)S(1)} collective-permute-done((f32[2,128,128]{2,1,0:T(8,128)S(1)}, f32[2,128,128]{2,1,0:T(8,128)S(1)}, u32[]{:S(2)}, u32[]{:S(2)}) %collective-permute-start.7) | collective-permute-done | bytes 131104 | tf_op jit(solution)/shard_map/ppermute | solution.py:237
  40.8 2.1 %collective-permute-done.11 = f32[2,1024]{1,0:T(2,128)S(1)} collective-permute-done((f32[2,1024]{1,0:T(2,128)S(1)}, f32[2,1024]{1,0:T(2,128)S(1)}, u32[]{:S(2)}, u32[]{:S(2)}) %collective-permute-start.11) | collective-permute-done | bytes 8224 | tf_op jit(solution)/shard_map/ppermute | solution.py:258
  48.1 3.5 %collective-permute-done.12 = f32[2,128,128]{2,1,0:T(8,128)S(1)} collective-permute-done((f32[2,128,128]{2,1,0:T(8,128)S(1)}, f32[2,128,128]{2,1,0:T(8,128)S(1)}, u32[]{:S(2)}, u32[]{:S(2)}) %collective-permute-start.12) | collective-permute-done | bytes 131104 | tf_op jit(solution)/shard_map/ppermute | solution.py:237
  54.0 3.0 %shard_map.94 = (bf16[1024,1024]{1,0:T(8,128)(2,1)}, f32[1024,256]{1,0:T(8,128)S(1)}, f32[1024,256]{1,0:T(8,128)S(1)}) custom-call(bf16[1024,1024]{1,0:T(8,128)(2,1)S(1)} %copy-done, bf16[1024,512]{1,0:T(8,128)(2,1)S(1)} %get-tuple-element.68.k_ref, bf16[1024,512]{1,0:T(8,128)(2,1)S(1)} %get-tuple-element.69.v_ref, ...), custom_call_target="tpu_custom_call" | custom-call | flops 603979776 | bytes 6553600 | tf_op jit(solution)/shard_map/pallas_call | solution.py:185
  59.4 3.0 %shard_map.95 = (bf16[1024,1024]{1,0:T(8,128)(2,1)}, f32[1024,256]{1,0:T(8,128)S(1)}, f32[1024,256]{1,0:T(8,128)S(1)}) custom-call(bf16[1024,1024]{1,0:T(8,128)(2,1)S(1)} %copy-done, bf16[1024,512]{1,0:T(8,128)(2,1)S(1)} %get-tuple-element.68.k_ref, bf16[1024,512]{1,0:T(8,128)(2,1)S(1)} %get-tuple-element.69.v_ref, ...), custom_call_target="tpu_custom_call", output_to_operand_aliasing={{0}: (6, {})} | custom-call | flops 603979776 | bytes 8650752 | tf_op jit(solution)/shard_map/pallas_call | solution.py:185
  73.4 2.9 %shard_map.96 = (bf16[1024,1024]{1,0:T(8,128)(2,1)}, f32[1024,256]{1,0:T(8,128)S(1)}, f32[1024,256]{1,0:T(8,128)S(1)}) custom-call(bf16[1024,1024]{1,0:T(8,128)(2,1)S(1)} %copy-done, bf16[1024,512]{1,0:T(8,128)(2,1)S(1)} %copy-done.9, bf16[1024,512]{1,0:T(8,128)(2,1)S(1)} %copy-done.12, ...), custom_call_target="tpu_custom_call", output_to_operand_aliasing={{0}: (6, {})} | custom-call | flops 603979776 | bytes 8650752 | tf_op jit(solution)/shard_map/pallas_call | solution.py:185
  77.3 2.3 %collective-permute-done.17 = f32[2,128,128]{2,1,0:T(8,128)} collective-permute-done((f32[2,128,128]{2,1,0:T(8,128)}, f32[2,128,128]{2,1,0:T(8,128)}, u32[]{:S(2)}, u32[]{:S(2)}) %collective-permute-start.17) | collective-permute-done | bytes 131104 | tf_op jit(solution)/shard_map/ppermute | solution.py:237
  83.3 2.0 %shard_map.91 = bf16[1024,1024]{1,0:T(8,128)(2,1)} custom-call(f32[1024,512]{1,0:T(8,128)S(1)} %copy-done.3, f32[1024,512]{1,0:T(8,128)S(1)} %copy-done.5, f32[1,1024]{1,0:T(1,128)S(1)} %bitcast.5, f32[1024,128]{1,0:T(8,128)S(1)} %copy-done.19), custom_call_target="tpu_custom_call" | custom-call | bytes 4722688 | tf_op jit(solution)/shard_map/pallas_call | solution.py:185
  85.3 2.9 %shard_map.97 = (bf16[1024,1024]{1,0:T(8,128)(2,1)}, f32[1024,256]{1,0:T(8,128)S(1)}, f32[1024,256]{1,0:T(8,128)S(1)}) custom-call(bf16[1024,1024]{1,0:T(8,128)(2,1)S(1)} %copy-done, bf16[1024,512]{1,0:T(8,128)(2,1)S(1)} %copy-done.10, bf16[1024,512]{1,0:T(8,128)(2,1)S(1)} %copy-done.13, ...), custom_call_target="tpu_custom_call", output_to_operand_aliasing={{0}: (6, {})} | custom-call | flops 603979776 | bytes 8650752 | tf_op jit(solution)/shard_map/pallas_call | solution.py:185
  88.3 4.1 %collective-permute-done.19 = f32[2,128,128]{2,1,0:T(8,128)S(1)} collective-permute-done((f32[2,128,128]{2,1,0:T(8,128)S(1)}, f32[2,128,128]{2,1,0:T(8,128)S(1)}, u32[]{:S(2)}, u32[]{:S(2)}) %collective-permute-start.19) | collective-permute-done | bytes 131104 | tf_op jit(solution)/shard_map/ppermute | solution.py:237
  94.4 1.7 %shard_map.98 = (bf16[1024,1024]{1,0:T(8,128)(2,1)}, bf16[1024,1024]{1,0:T(8,128)(2,1)}) custom-call(bf16[1024,512]{1,0:T(8,128)(2,1)S(1)} %get-tuple-element.68.k_ref, bf16[1024,512]{1,0:T(8,128)(2,1)S(1)} %copy-done.7, f32[4,128,128]{2,1,0:T(8,128)S(1)} %pad_maximum_fusion.3.s_ref, f32[1024,256]{1,0:T(8,128)S(1)} %copy-done.31, ...), custom_call_target="tpu_custom_call" | custom-call | flops 268435456 | bytes 6553600 | tf_op jit(solution)/shard_map/pallas_call | solution.py:185
  96.0 2.4 %collective-permute-done.20 = f32[2,128,128]{2,1,0:T(8,128)S(1)} collective-permute-done((f32[2,128,128]{2,1,0:T(8,128)S(1)}, f32[2,128,128]{2,1,0:T(8,128)S(1)}, u32[]{:S(2)}, u32[]{:S(2)}) %collective-permute-start.20) | collective-permute-done | bytes 131104 | tf_op jit(solution)/shard_map/ppermute | solution.py:237
  98.5 1.7 %shard_map.99 = (bf16[1024,1024]{1,0:T(8,128)(2,1)}, bf16[1024,1024]{1,0:T(8,128)(2,1)}) custom-call(bf16[1024,512]{1,0:T(8,128)(2,1)S(1)} %copy-done.10, bf16[1024,512]{1,0:T(8,128)(2,1)S(1)} %copy-done.13, f32[4,128,128]{2,1,0:T(8,128)S(1)} %pad_maximum_fusion.2.s_ref, ...), custom_call_target="tpu_custom_call", output_to_operand_aliasing={{0}: (7, {}), {1}: (8, {})} | custom-call | flops 268435456 | bytes 10747904 | tf_op jit(solution)/shard_map/pallas_call | solution.py:185
  (164 shorter events, 40.0 us)
Async XLA Ops:
  5.5 53.8 %copy-start.6 = (bf16[1024,512]{1,0:T(8,128)(2,1)}, bf16[1024,512]{1,0:T(8,128)(2,1)S(1)}, u32[]{:S(2)}) copy-start(bf16[1024,512]{1,0:T(8,128)(2,1)S(1)} %get-tuple-element.69.v_ref) | copy-start | bytes 3145732
  5.6 6.5 %collective-permute-start = (f32[2,128,128]{2,1,0:T(8,128)S(1)}, f32[2,128,128]{2,1,0:T(8,128)S(1)}, u32[]{:S(2)}, u32[]{:S(2)}) collective-permute-start(f32[2,128,128]{2,1,0:T(8,128)S(1)} %slice_select_fusion.6), channel_id=1, source_target_pairs={{0,4},{4,0},{8,12},{12,8},{16,20},{20,16},{24,28},{28,24},{1,5},{5... | collective-permute-start | bytes 393224 | tf_op jit(solution)/shard_map/ppermute | solution.py:237
  10.3 14.8 %copy-start.8 = (bf16[1024,512]{1,0:T(8,128)(2,1)}, bf16[1024,512]{1,0:T(8,128)(2,1)S(1)}, u32[]{:S(2)}) copy-start(bf16[1024,512]{1,0:T(8,128)(2,1)S(1)} %get-tuple-element.75.k_ref) | copy-start | bytes 3145732
  12.1 7.4 %collective-permute-start.1 = (f32[2,128,128]{2,1,0:T(8,128)S(1)}, f32[2,128,128]{2,1,0:T(8,128)S(1)}, u32[]{:S(2)}, u32[]{:S(2)}) collective-permute-start(f32[2,128,128]{2,1,0:T(8,128)S(1)} %fusion), channel_id=1, source_target_pairs={{0,8},{4,12},{1,9},{5,13},{2,10},{6,14},{3,11},{7,15}} | collective-permute-start | bytes 393224 | tf_op jit(solution)/shard_map/ppermute | solution.py:237
  15.9 5.0 %collective-permute-start.2 = (f32[2,128,128]{2,1,0:T(8,128)S(1)}, f32[2,128,128]{2,1,0:T(8,128)S(1)}, u32[]{:S(2)}, u32[]{:S(2)}) collective-permute-start(f32[2,128,128]{2,1,0:T(8,128)S(1)} %slice_select_fusion.5), channel_id=1, source_target_pairs={{0,4},{4,0},{8,12},{12,8},{16,20},{20,16},{24,28},{28,24},{1,5},{5... | collective-permute-start | bytes 393224 | tf_op jit(solution)/shard_map/ppermute | solution.py:237
  20.9 6.4 %collective-permute-start.3 = (f32[2,128,128]{2,1,0:T(8,128)S(1)}, f32[2,128,128]{2,1,0:T(8,128)S(1)}, u32[]{:S(2)}, u32[]{:S(2)}) collective-permute-start(f32[2,128,128]{2,1,0:T(8,128)S(1)} %add.106), channel_id=1, source_target_pairs={{8,16},{12,20},{9,17},{13,21},{10,18},{14,22},{11,19},{15,23}} | collective-permute-start | bytes 393224 | tf_op jit(solution)/shard_map/ppermute | solution.py:237
  21.6 6.0 %collective-permute-start.4 = (f32[2,128,128]{2,1,0:T(8,128)S(1)}, f32[2,128,128]{2,1,0:T(8,128)S(1)}, u32[]{:S(2)}, u32[]{:S(2)}) collective-permute-start(f32[2,128,128]{2,1,0:T(8,128)S(1)} %fusion.1), channel_id=1, source_target_pairs={{0,8},{4,12},{1,9},{5,13},{2,10},{6,14},{3,11},{7,15}} | collective-permute-start | bytes 393224 | tf_op jit(solution)/shard_map/ppermute | solution.py:237
  27.6 1.5 %collective-permute-start.5 = (f32[2,128,128]{2,1,0:T(8,128)S(1)}, f32[2,128,128]{2,1,0:T(8,128)S(1)}, u32[]{:S(2)}, u32[]{:S(2)}) collective-permute-start(f32[2,128,128]{2,1,0:T(8,128)S(1)} %add.109), channel_id=1, source_target_pairs={{16,24},{20,28},{17,25},{21,29},{18,26},{22,30},{19,27},{23,31}} | collective-permute-start | bytes 393224 | tf_op jit(solution)/shard_map/ppermute | solution.py:237
  28.4 0.7 collective-permute-start.6
  29.2 2.2 %collective-permute-start.8 = (f32[2,128,128]{2,1,0:T(8,128)S(1)}, f32[2,128,128]{2,1,0:T(8,128)S(1)}, u32[]{:S(2)}, u32[]{:S(2)}) collective-permute-start(f32[2,128,128]{2,1,0:T(8,128)S(1)} %add.114), channel_id=1, source_target_pairs={{16,24},{20,28},{17,25},{21,29},{18,26},{22,30},{19,27},{23,31}} | collective-permute-start | bytes 393224 | tf_op jit(solution)/shard_map/ppermute | solution.py:237
  29.9 5.0 %collective-permute-start.7 = (f32[2,128,128]{2,1,0:T(8,128)S(1)}, f32[2,128,128]{2,1,0:T(8,128)S(1)}, u32[]{:S(2)}, u32[]{:S(2)}) collective-permute-start(f32[2,128,128]{2,1,0:T(8,128)S(1)} %get-tuple-element.81), channel_id=1, source_target_pairs={{0,4},{4,0},{8,12},{12,8},{16,20},{20,16},{24,28},{28,24},{1,5},{5... | collective-permute-start | bytes 393224 | tf_op jit(solution)/shard_map/ppermute | solution.py:237
  31.5 5.0 %collective-permute-start.9 = (f32[2,128,128]{2,1,0:T(8,128)S(1)}, f32[2,128,128]{2,1,0:T(8,128)S(1)}, u32[]{:S(2)}, u32[]{:S(2)}) collective-permute-start(f32[2,128,128]{2,1,0:T(8,128)S(1)} %get-tuple-element.126), channel_id=1, source_target_pairs={{0,4},{4,0},{8,12},{12,8},{16,20},{20,16},{24,28},{28,24},{1,5},{5... | collective-permute-start | bytes 393224 | tf_op jit(solution)/shard_map/ppermute | solution.py:237
  38.0 1.2 %collective-permute-start.10 = (f32[2,1024]{1,0:T(2,128)S(1)}, f32[2,1024]{1,0:T(2,128)S(1)}, u32[]{:S(2)}, u32[]{:S(2)}) collective-permute-start(f32[2,1024]{1,0:T(2,128)S(1)} %add.119), channel_id=1, source_target_pairs={{0,1},{1,0},{2,3},{3,2},{4,5},{5,4},{6,7},{7,6},{8,9},{9,8},{10,11... | collective-permute-start | bytes 24584 | tf_op jit(solution)/shard_map/ppermute | solution.py:258
  39.3 3.7 %collective-permute-start.11 = (f32[2,1024]{1,0:T(2,128)S(1)}, f32[2,1024]{1,0:T(2,128)S(1)}, u32[]{:S(2)}, u32[]{:S(2)}) collective-permute-start(f32[2,1024]{1,0:T(2,128)S(1)} %add.120), channel_id=1, source_target_pairs={{0,2},{1,3},{2,0},{3,1},{4,6},{5,7},{6,4},{7,5},{8,10},{9,11},{10,... | collective-permute-start | bytes 24584 | tf_op jit(solution)/shard_map/ppermute | solution.py:258
  46.6 5.0 %collective-permute-start.12 = (f32[2,128,128]{2,1,0:T(8,128)S(1)}, f32[2,128,128]{2,1,0:T(8,128)S(1)}, u32[]{:S(2)}, u32[]{:S(2)}) collective-permute-start(f32[2,128,128]{2,1,0:T(8,128)S(1)} %slice_select_fusion.2), channel_id=1, source_target_pairs={{28,24},{24,28},{20,16},{16,20},{12,8},{8,12},{4,0},{0,4},{29,25},... | collective-permute-start | bytes 393224 | tf_op jit(solution)/shard_map/ppermute | solution.py:237
  51.6 6.3 %collective-permute-start.13 = (f32[2,128,128]{2,1,0:T(8,128)S(1)}, f32[2,128,128]{2,1,0:T(8,128)S(1)}, u32[]{:S(2)}, u32[]{:S(2)}) collective-permute-start(f32[2,128,128]{2,1,0:T(8,128)S(1)} %fusion.2), channel_id=1, source_target_pairs={{28,20},{24,16},{29,21},{25,17},{30,22},{26,18},{31,23},{27,19}} | collective-permute-start | bytes 393224 | tf_op jit(solution)/shard_map/ppermute | solution.py:237
  52.5 5.4 %collective-permute-start.14 = (f32[2,128,128]{2,1,0:T(8,128)S(1)}, f32[2,128,128]{2,1,0:T(8,128)S(1)}, u32[]{:S(2)}, u32[]{:S(2)}) collective-permute-start(f32[2,128,128]{2,1,0:T(8,128)S(1)} %slice_select_fusion.1), channel_id=1, source_target_pairs={{28,24},{24,28},{20,16},{16,20},{12,8},{8,12},{4,0},{0,4},{29,25},... | collective-permute-start | bytes 393224 | tf_op jit(solution)/shard_map/ppermute | solution.py:237
  58.0 6.4 %collective-permute-start.15 = (f32[2,128,128]{2,1,0:T(8,128)S(1)}, f32[2,128,128]{2,1,0:T(8,128)S(1)}, u32[]{:S(2)}, u32[]{:S(2)}) collective-permute-start(f32[2,128,128]{2,1,0:T(8,128)S(1)} %add.123), channel_id=1, source_target_pairs={{20,12},{16,8},{21,13},{17,9},{22,14},{18,10},{23,15},{19,11}} | collective-permute-start | bytes 393224 | tf_op jit(solution)/shard_map/ppermute | solution.py:237
  58.7 6.5 %collective-permute-start.16 = (f32[2,128,128]{2,1,0:T(8,128)S(1)}, f32[2,128,128]{2,1,0:T(8,128)S(1)}, u32[]{:S(2)}, u32[]{:S(2)}) collective-permute-start(f32[2,128,128]{2,1,0:T(8,128)S(1)} %fusion.3), channel_id=1, source_target_pairs={{28,20},{24,16},{29,21},{25,17},{30,22},{26,18},{31,23},{27,19}} | collective-permute-start | bytes 393224 | tf_op jit(solution)/shard_map/ppermute | solution.py:237
  65.8 10.5 %collective-permute-start.18 = (f32[2,128,128]{2,1,0:T(8,128)}, f32[2,128,128]{2,1,0:T(8,128)}, u32[]{:S(2)}, u32[]{:S(2)}) collective-permute-start(f32[2,128,128]{2,1,0:T(8,128)} %add.127), channel_id=1, source_target_pairs={{20,12},{16,8},{21,13},{17,9},{22,14},{18,10},{23,15},{19,11}} | collective-permute-start | bytes 393224 | tf_op jit(solution)/shard_map/ppermute | solution.py:237
  67.1 12.4 %collective-permute-start.17 = (f32[2,128,128]{2,1,0:T(8,128)}, f32[2,128,128]{2,1,0:T(8,128)}, u32[]{:S(2)}, u32[]{:S(2)}) collective-permute-start(f32[2,128,128]{2,1,0:T(8,128)} %add.126), channel_id=1, source_target_pairs={{12,4},{8,0},{13,5},{9,1},{14,6},{10,2},{15,7},{11,3}} | collective-permute-start | bytes 393224 | tf_op jit(solution)/shard_map/ppermute | solution.py:237
  80.5 7.8 %collective-permute-start.21 = (f32[2,128,128]{2,1,0:T(8,128)S(1)}, f32[2,128,128]{2,1,0:T(8,128)S(1)}, u32[]{:S(2)}, u32[]{:S(2)}) collective-permute-start(f32[2,128,128]{2,1,0:T(8,128)S(1)} %get-tuple-element.110), channel_id=1, source_target_pairs={{28,24},{24,28},{20,16},{16,20},{12,8},{8,12},{4,0},{0,4},{29,25},... | collective-permute-start | bytes 393224 | tf_op jit(solution)/shard_map/ppermute | solution.py:237
  82.0 10.5 %collective-permute-start.19 = (f32[2,128,128]{2,1,0:T(8,128)S(1)}, f32[2,128,128]{2,1,0:T(8,128)S(1)}, u32[]{:S(2)}, u32[]{:S(2)}) collective-permute-start(f32[2,128,128]{2,1,0:T(8,128)S(1)} %add.130), channel_id=1, source_target_pairs={{12,4},{8,0},{13,5},{9,1},{14,6},{10,2},{15,7},{11,3}} | collective-permute-start | bytes 393224 | tf_op jit(solution)/shard_map/ppermute | solution.py:237
  93.4 5.0 %collective-permute-start.20 = (f32[2,128,128]{2,1,0:T(8,128)S(1)}, f32[2,128,128]{2,1,0:T(8,128)S(1)}, u32[]{:S(2)}, u32[]{:S(2)}) collective-permute-start(f32[2,128,128]{2,1,0:T(8,128)S(1)} %get-tuple-element.117), channel_id=1, source_target_pairs={{28,24},{24,28},{20,16},{16,20},{12,8},{8,12},{4,0},{0,4},{29,25},... | collective-permute-start | bytes 393224 | tf_op jit(solution)/shard_map/ppermute | solution.py:237
  (47 other events, 250.6 us)

commit v3 on v2

v3 whole, which is shorter than its diff:
```python
import functools

import jax
import jax.numpy as jnp
from jax import lax
from jax.experimental import pallas as pl
from jax.experimental.pallas import tpu as pltpu
from jax.sharding import PartitionSpec as P

HEAD_DIM = 128
BLOCK = 128
WIDTH = 4096
epsilon = 1e-05

F32 = jnp.float32
BF16 = jnp.bfloat16
VMEM = pl.BlockSpec(memory_space=pltpu.VMEM)
HBM = pl.BlockSpec(memory_space=pltpu.HBM)


def dot(a, b, ca, cb):
    return lax.dot_general(a, b, (((ca,), (cb,)), ((), ())), preferred_element_type=F32)


def causal_mask():
    row = lax.broadcasted_iota(jnp.int32, (BLOCK, BLOCK), 0)
    col = lax.broadcasted_iota(jnp.int32, (BLOCK, BLOCK), 1)
    return col <= row


def rows_of(n):
    return slice(n * BLOCK, (n + 1) * BLOCK)


def cols_of(h):
    return slice(h * HEAD_DIM, (h + 1) * HEAD_DIM)


def cols_at(h):
    return pl.ds(pl.multiple_of(h * HEAD_DIM, HEAD_DIM), HEAD_DIM)


def load_kernel(first, heads, k_hbm, v_hbm, k_ref, v_ref, t_ref, sems):
    copies = []
    for h in range(k_ref.shape[1] // HEAD_DIM):
        for i, (src, dst) in enumerate(((k_hbm, k_ref), (v_hbm, v_ref))):
            copies.append(pltpu.make_async_copy(src.at[:, cols_of(h)], dst.at[:, cols_of(h)], sems.at[i, h]))
            copies[-1].start()
    for h, (k_copy, v_copy) in enumerate(zip(copies[::2], copies[1::2])):
        k_copy.wait()
        v_copy.wait()
        if h < heads:
            t_ref[h] = dot(k_ref[:, cols_of(h)], v_ref[:, cols_of(h)], 0, 0)


def state_kernel(first, heads, k_ref, v_ref, t_ref):
    for h in range(heads):
        t_ref[h] = dot(k_ref[:, cols_of(first + h)], v_ref[:, cols_of(first + h)], 0, 0)


def local_kernel(first, heads, blocks, q_ref, k_ref, v_ref, w_ref, a_ref, low):
    causal = causal_mask()

    def head(h, carry):
        c, cq = cols_at(h), cols_at(h + first)
        for n in range(0, blocks, 2):
            if n + 1 < blocks:
                both = slice(n * BLOCK, (n + 2) * BLOCK)
                s = dot(q_ref[both, cq], k_ref[both, cq], 1, 1)
                w_ref[rows_of(n), c] = jnp.where(causal, s[:BLOCK, :BLOCK], 0.0).astype(BF16)
                w_ref[rows_of(n + 1), c] = jnp.where(causal, s[BLOCK:, BLOCK:], 0.0).astype(BF16)
            else:
                s = dot(q_ref[rows_of(n), cq], k_ref[rows_of(n), cq], 1, 1)
                w_ref[rows_of(n), c] = jnp.where(causal, s, 0.0).astype(BF16)
        prefix = None
        for n in range(blocks - 1):
            s = dot(k_ref[rows_of(n), cq], v_ref[rows_of(n), cq], 0, 0)
            prefix = s if prefix is None else prefix + s
            low[rows_of(n), :] = prefix.astype(BF16)
        a_ref[rows_of(0), c] = dot(w_ref[rows_of(0), c], v_ref[rows_of(0), cq], 1, 0)
        for n in range(1, blocks):
            left = jnp.concatenate([w_ref[rows_of(n), c], q_ref[rows_of(n), cq]], axis=1)
            right = jnp.concatenate([v_ref[rows_of(n), cq], low[rows_of(n - 1), :]], axis=0)
            a_ref[rows_of(n), c] = dot(left, right, 1, 0)
        return carry

    lax.fori_loop(0, heads, head, 0, unroll=min(2, heads))


def stats_kernel(first, parts, size, blocks, *refs):
    a_ins, (q_ref, p_ref, og_ref, gain_ref, a_ref, s_ref) = refs[:parts], refs[parts:]
    low = [p_ref[h].astype(BF16) for h in range(parts * size)]
    for n in range(blocks):
        r = rows_of(n)
        squares = dots = None
        for h in range(parts * size):
            c, cq = cols_of(h), cols_of(first + h)
            att = a_ins[h // size][r, cols_of(h % size)] + dot(q_ref[r, cq], low[h], 1, 0)
            a_ref[r, c] = att
            scaled = gain_ref[:, cq] * og_ref[r, cq].astype(F32)
            squares = att * att if squares is None else squares + att * att
            dots = scaled * att if dots is None else dots + scaled * att
        s_ref[0:1, r] = jnp.sum(squares.T, axis=0, keepdims=True)
        s_ref[1:2, r] = jnp.sum(dots.T, axis=0, keepdims=True)


def factor_kernel(blocks, s_ref, inv_ref, coef_ref):
    inverse = lax.rsqrt(s_ref[0:1, :] / WIDTH + epsilon)
    factor = inverse * inverse * inverse * s_ref[1:2, :] / WIDTH
    for n in range(blocks):
        inv_ref[rows_of(n), :] = jnp.broadcast_to(inverse[:, rows_of(n)], (BLOCK, BLOCK)).T
        coef_ref[rows_of(n), :] = jnp.broadcast_to(factor[:, rows_of(n)], (BLOCK, BLOCK)).T


def grad_kernel(first, heads, a_ref, q_ref, og_ref, gain_ref, inv_ref, coef_ref, g_ref, t_ref):
    for h in range(heads):
        c, cq = cols_of(h), cols_of(first + h)
        scaled = gain_ref[:, cq] * og_ref[:, cq].astype(F32)
        grad = (inv_ref[...] * scaled - coef_ref[...] * a_ref[:, c]).astype(BF16)
        g_ref[:, c] = grad
        t_ref[h] = dot(q_ref[:, cq], grad, 0, 0)


def mixed_kernel(parts, heads, *refs):
    a_refs, (gain_ref, inv_ref, m_ref) = refs[:parts], refs[parts:]
    for p, a_ref in enumerate(a_refs):
        for h in range(heads):
            cq = cols_of(p * heads + h)
            m_ref[:, cq] = (gain_ref[:, cq] * a_ref[:, cols_of(h)] * inv_ref[...]).astype(BF16)


def back_kernel(first, inner, winner, heads, blocks, q_ref, k_ref, v_ref, w_ref, g_ref, p_ref, *rest):
    qg_hbm, kl_ref, vl_ref, qg, bw, plow, slow, sems = rest[-8:]
    causal = causal_mask()

    def copy_out(h, c, cq):
        return pltpu.make_async_copy(qg.at[:, c], qg_hbm.at[:, cq], sems.at[h])

    def head(h, carry):
        c, ci, cw, cq = cols_at(h), cols_at(h + inner), cols_at(h + winner), cols_at(h + first)
        for n in range(blocks):
            r = rows_of(n)
            bw[r, :] = jnp.where(causal, dot(g_ref[r, ci], v_ref[r, cq], 1, 1), 0.0).astype(BF16)
        prefix = p_ref[h + inner]
        plow[rows_of(0), :] = prefix.astype(BF16)
        for n in range(blocks - 1):
            prefix = prefix + dot(k_ref[rows_of(n), cq], v_ref[rows_of(n), cq], 0, 0)
            plow[rows_of(n + 1), :] = prefix.astype(BF16)
        suffix = None
        for n in reversed(range(1, blocks)):
            s = dot(q_ref[rows_of(n), cq], g_ref[rows_of(n), ci], 0, 0)
            suffix = s if suffix is None else suffix + s
            slow[rows_of(n - 1), :] = suffix.astype(BF16)
        for n in range(blocks):
            r = rows_of(n)
            q, k, v, g = q_ref[r, cq], k_ref[r, cq], v_ref[r, cq], g_ref[r, ci]
            qg[r, c] = (dot(bw[r, :], k, 1, 0) + dot(g, plow[r, :], 1, 1)).astype(BF16)
            kp, vp = dot(bw[r, :], q, 0, 0), dot(w_ref[r, cw], g, 0, 0)
            if n + 1 < blocks:
                kp, vp = kp + dot(v, slow[r, :], 1, 1), vp + dot(k, slow[r, :], 1, 0)
            kl_ref[r, c] = kp
            vl_ref[r, c] = vp
        copy_out(h, c, cq).start()
        return carry

    lax.fori_loop(0, heads, head, 0, unroll=min(2, heads))
    for h in range(heads):
        copy_out(h, cols_of(h), cols_of(h + first)).wait()


def last_kernel(first, pieces, heads, k_ref, v_ref, s_ref, *rest):
    kls, vls = rest[:pieces], rest[pieces : 2 * pieces]
    kg_hbm, vg_hbm, kg, vg, sems = rest[-5:]
    copies = []
    for p in range(pieces):
        for i in range(heads):
            h = p * heads + i
            c, cq = cols_of(h), cols_of(first + h)
            low = s_ref[h].astype(BF16)
            kg[:, c] = (kls[p][:, cols_of(i)] + dot(v_ref[:, cq], low, 1, 1)).astype(BF16)
            copies.append(pltpu.make_async_copy(kg.at[:, c], kg_hbm.at[:, cq], sems.at[0, h]))
            copies[-1].start()
            vg[:, c] = (vls[p][:, cols_of(i)] + dot(k_ref[:, cq], low, 1, 0)).astype(BF16)
            copies.append(pltpu.make_async_copy(vg.at[:, c], vg_hbm.at[:, cq], sems.at[1, h]))
            copies[-1].start()
    for copy in copies:
        copy.wait()


def call(kernel, ins, outs, in_specs=None, out_specs=None, scratch=(), aliases=None, flops=0, vmem=6):
    nbytes = sum(a.size * a.dtype.itemsize for a in ins)
    return pl.pallas_call(
        kernel,
        in_specs=in_specs or [VMEM] * len(ins),
        out_specs=tuple(out_specs or [VMEM] * len(outs)),
        out_shape=tuple(jax.ShapeDtypeStruct(shape, dtype) for shape, dtype in outs),
        scratch_shapes=list(scratch),
        input_output_aliases=aliases or {},
        compiler_params=pltpu.CompilerParams(vmem_limit_bytes=vmem << 20),
        cost_estimate=pl.CostEstimate(flops=flops, bytes_accessed=nbytes, transcendentals=0),
    )(*ins)


def scan_stages(states, size, low, reverse):
    place = (lambda i: size - 1 - i) if reverse else (lambda i: i)
    perm = lambda pairs: [(place(i), place(j)) for i, j in pairs]
    outer = size // 2
    swap = [(i, i ^ 1) for i in range(size)]
    at_first = (lambda a, b: jnp.where(low, b, a)) if reverse else (lambda a, b: jnp.where(low, a, b))
    half = states.shape[0] // 2
    mine = jnp.where(low, states[:half], states[half:])
    other = jnp.where(low, states[half:], states[:half])
    got = yield other, perm(swap)
    pair = mine + got
    total = None
    if outer <= 4:
        running = pair
        for hop in range(outer - 1):
            r = yield running, perm([(2 * hop, 2 * hop + 2), (2 * hop + 1, 2 * hop + 3)])
            total = r if total is None else total + r
            running = r + pair
    else:
        total = yield pair, perm([(i, i + 2) for i in range(size - 2)])
        step = 1
        while step < outer - 1:
            r = yield total, perm([(i, i + 2 * step) for i in range(size - 2 * step)])
            total = total + r
            step *= 2
    answer = yield at_first(total + mine, total), perm(swap)
    kept = at_first(total, total + got)
    return jnp.concatenate([jnp.where(low, kept, answer), jnp.where(low, answer, kept)], axis=0)


def drive(makers, pieces, finish):
    live, arrived, behind, settled, event = [], [], (), (), 0
    waiting = list(makers)
    while waiting or live:
        if waiting:
            scan = waiting.pop(0)()
            name, request = len(makers) - len(waiting) - 1, next(scan)
        else:
            name, scan, result = live.pop(0)
            if settled:
                result = after(settled, result)[0]
            try:
                request = scan.send(result)
            except StopIteration as stop:
                settled = finish(name, stop.value)
                continue
        ordered = arrived[-len(makers) - 1 : -len(makers)]
        operand, *_ = lax.optimization_barrier((request[0], *ordered, *behind))
        arrived.append(lax.ppermute(operand, "seq", request[1]))
        live.append((name, scan, arrived[-1]))
        behind = pieces[event]((operand,)) if event < len(pieces) else ()
        event += 1
    for piece in pieces[event:]:
        piece(())


def after(tied, *arrays):
    return lax.optimization_barrier((*arrays, *tied))[: len(arrays)]


def head_sum(a, size):
    if size & (size - 1):
        return lax.psum(a, "head")
    step = 1
    while step < size:
        a = a + lax.ppermute(a, "head", [(i, i ^ step) for i in range(size)])
        step *= 2
    return a


def body(seq_size, head_size, queries, keys, values, gain, out_grad):
    rows, width = queries.shape
    blocks, heads = rows // BLOCK, width // HEAD_DIM
    half = heads // 2
    part = half * HEAD_DIM
    low = lax.axis_index("seq") % 2 == 0
    gain = gain.reshape(1, width)
    unit = 2 * rows * HEAD_DIM * HEAD_DIM
    whole = ((rows, width), BF16)
    state = ((half, HEAD_DIM, HEAD_DIM), F32)

    k, v, t0 = call(
        functools.partial(load_kernel, 0, half),
        [keys, values],
        [whole, whole, state],
        in_specs=[HBM, HBM],
        scratch=[pltpu.SemaphoreType.DMA((2, heads))],
        flops=unit * half,
        vmem=48,
    )
    states = [t0]

    def piece_state(tied):
        (kt,) = after(tied, k)
        states.extend(call(functools.partial(state_kernel, half, half), [kt, v], [state], flops=unit * half))
        return (states[1],)

    size = min(2, half)
    weights, attended = {}, {}

    def piece_local(first, tied):
        (qt,) = after(tied, queries)
        weights[first], attended[first] = call(
            functools.partial(local_kernel, first, size, blocks),
            [qt, k, v],
            [((rows, size * HEAD_DIM), BF16), ((rows, size * HEAD_DIM), F32)],
            scratch=[pltpu.VMEM((rows, HEAD_DIM), BF16)],
            flops=4 * unit * size,
        )
        return weights[first], attended[first]

    prefixes, atts, sums = [], [], []

    def make_stats(i, prefix):
        parts = [attended[first] for first in range(i * half, (i + 1) * half, size)]
        att, s = call(
            functools.partial(stats_kernel, i * half, len(parts), size, blocks),
            [*parts, queries, prefix, out_grad, gain],
            [((rows, part), F32), ((2, rows), F32)],
            flops=unit * half,
        )
        prefixes.append(prefix)
        atts.append(att)
        sums.append(s)
        return att, s

    drive(
        [lambda i=i: scan_stages(states[i], seq_size, low, False) for i in range(2)],
        [piece_state] + [functools.partial(piece_local, first) for first in range(0, heads, size)],
        make_stats,
    )
    total = head_sum(sums[0] + sums[1], head_size)
    inverse, coef = call(functools.partial(factor_kernel, blocks), [total], [((rows, BLOCK), F32)] * 2)

    grads, backs = [], []

    def piece_grad(i, tied):
        (qt,) = after(tied, queries)
        grad, back = call(
            functools.partial(grad_kernel, i * half, half),
            [atts[i], qt, out_grad, gain, inverse, coef],
            [((rows, part), BF16), state],
            flops=unit * half,
        )
        grads.append(grad)
        backs.append(back)
        return (back,)

    made, inner = {}, {}

    def piece_back(h, tied):
        i = h // half
        (qt,) = after(tied, queries)
        ins = [qt, k, v, weights[h // size * size], grads[i], prefixes[i]]
        specs, aliases = [VMEM] * len(ins), {}
        if "query" in made:
            aliases = {len(ins): 0}
            ins.append(made["query"])
            specs.append(HBM)
        made["query"], kl, vl = call(
            functools.partial(back_kernel, h, h % half, h % size, 1, blocks),
            ins,
            [whole, ((rows, HEAD_DIM), F32), ((rows, HEAD_DIM), F32)],
            in_specs=specs,
            out_specs=[HBM, VMEM, VMEM],
            scratch=[pltpu.VMEM((rows, HEAD_DIM), BF16)] * 4 + [pltpu.SemaphoreType.DMA((1,))],
            aliases=aliases,
            flops=9 * unit,
        )
        inner[h] = (kl, vl)
        return kl, vl

    def piece_mixed(tied):
        (inv,) = after(tied, inverse)
        (made["mixed"],) = call(functools.partial(mixed_kernel, 2, half), [*atts, gain, inv], [whole])
        return (made["mixed"],)

    def make_last(i, suffix):
        mine = [inner[h] for h in range(i * half, (i + 1) * half)]
        ins = [k, v, suffix] + [kl for kl, _ in mine] + [vl for _, vl in mine]
        specs, aliases = [VMEM] * len(ins), {}
        if "key" in made:
            aliases = {len(ins): 0, len(ins) + 1: 1}
            ins += [made["key"], made["value"]]
            specs += [HBM, HBM]
        made["key"], made["value"] = call(
            functools.partial(last_kernel, i * half, half, 1),
            ins,
            [whole, whole],
            in_specs=specs,
            out_specs=[HBM, HBM],
            scratch=[pltpu.VMEM((rows, part), BF16)] * 2 + [pltpu.SemaphoreType.DMA((2, half))],
            aliases=aliases,
            flops=2 * unit * half,
        )
        return made["key"], made["value"]

    piece_grad(0, ())
    drive(
        [lambda i=i: scan_stages(backs[i], seq_size, low, True) for i in range(2)],
        [functools.partial(piece_grad, 1)]
        + [functools.partial(piece_back, h) for h in range(heads)]
        + [piece_mixed],
        make_last,
    )
    return made["mixed"], made["query"], made["key"], made["value"]


def solution(mesh):
    placed = (P("seq", "head"), P("seq", "head"), P("seq", "head"), P("head"), P("seq", "head"))
    return jax.shard_map(
        functools.partial(body, mesh.shape["seq"], mesh.shape["head"]),
        mesh=mesh,
        in_specs=placed,
        out_specs=(P("seq", "head"),) * 4,
        check_vma=False,
    )
```

time: 102 us -> 84.5 us (0.83); the launches traced: 100 us -> 84.1 us
  local copies, waits for them, and re-layouts: 12.3 us -> 0.87 us
  other arithmetic: 4.75 us -> 0.7 us
  starting transfers between devices: 29.6 us -> 26.3 us
  Pallas kernels: 30.1 us -> 33 us
    unnamed x98 -> x6, local copies, waits for them, and re-layouts: 12.3 us -> 0.87 us
    ppermute x20, starting transfers between devices: 28 us -> 24.7 us  [drive(): arrived.append(lax.ppermute(operand, 'seq', request[1]))]
    pallas_call x16 -> x22, Pallas kernels: 30.1 us -> 33 us  [call(): pl.pallas_call(kernel, in_specs=in_specs or [VMEM] * len(ins), out_specs=...]
    add x8, other arithmetic: 2.41 us -> 0.14 us  [scan_stages(): running = r + pair]
    select_n x4, other arithmetic: 2.03 us -> 0.18 us  [the longest x2 0.09 us: scan_stages(): jnp.where(low, a, b)]
  transfers between devices with their start and end apart: 22 -> 22, of which waited for: 11 -> 11; matrix products, arithmetic and copies ran while one was open for 2% -> 1% of each run, Pallas kernels for 23% -> 32%
where the time goes in v3:
time: 84.5 us; the launch traced here: 84.1 us
  Pallas kernels  33 us (39%)
  starting transfers between devices  26.3 us (31%)
  waiting for transfers between devices  22 us (26%)
  between operations  1.32 us (2%)
  local copies, waits for them, and re-layouts  0.87 us (1%)
    pallas_call x22, Pallas kernels, call(): pl.pallas_call(kernel, in_specs=in_specs or [VMEM] * len(ins), out_specs=...  33 us
    ppermute x20, starting transfers between devices, drive(): arrived.append(lax.ppermute(operand, 'seq', request[1]))  24.7 us
    ppermute x20, waiting for transfers between devices, drive(): arrived.append(lax.ppermute(operand, 'seq', request[1]))  18.7 us
    ppermute x2, waiting for transfers between devices, head_sum(): a = a + lax.ppermute(a, 'head', [(i, i ^ step) for i in range(size)])  3.29 us
  transfers between devices with their start and end apart: 22, of which 11 were waited for; matrix products, arithmetic and copies ran while one was open for 1% of the time, Pallas kernels for 32%

profile of v3, /device:TPU:0, one launch (start us, length us, event | category | flops | bytes accessed | tf_op | source)
XLA Modules:
  0.0 84.1 jit_solution(13919868238830968220)
XLA Ops:
  0.6 2.4 %shard_map.84 = (bf16[1024,1024]{1,0:T(8,128)(2,1)S(1)}, bf16[1024,1024]{1,0:T(8,128)(2,1)S(1)}, f32[4,128,128]{2,1,0:T(8,128)S(1)}) custom-call(bf16[1024,1024]{1,0:T(8,128)(2,1)} %k_hbm.1, bf16[1024,1024]{1,0:T(8,128)(2,1)} %v_hbm.1), custom_call_target="tpu_custom_call" | custom-call | flops 134217728 | bytes 4194304 | tf_op jit(solution)/shard_map/pallas_call | solution.py:192
  3.1 3.0 %collective-permute-start = (f32[2,128,128]{2,1,0:T(8,128)S(1)}, f32[2,128,128]{2,1,0:T(8,128)S(1)}, u32[]{:S(2)}, u32[]{:S(2)}) collective-permute-start(f32[2,128,128]{2,1,0:T(8,128)S(1)} %slice_select_fusion.7), channel_id=1, source_target_pairs={{0,4},{4,0},{8,12},{12,8},{16,20},{20,16},{24,28},{28,24},{1,5},{5... | collective-permute-start | bytes 393224 | tf_op jit(solution)/shard_map/ppermute | solution.py:252
  10.2 4.1 %collective-permute-start.1 = (f32[2,128,128]{2,1,0:T(8,128)S(1)}, f32[2,128,128]{2,1,0:T(8,128)S(1)}, u32[]{:S(2)}, u32[]{:S(2)}) collective-permute-start(f32[2,128,128]{2,1,0:T(8,128)S(1)} %fusion), channel_id=1, source_target_pairs={{0,8},{4,12},{1,9},{5,13},{2,10},{6,14},{3,11},{7,15}} | collective-permute-start | bytes 393224 | tf_op jit(solution)/shard_map/ppermute | solution.py:252
  15.5 1.8 %collective-permute-start.4 = (f32[2,128,128]{2,1,0:T(8,128)S(1)}, f32[2,128,128]{2,1,0:T(8,128)S(1)}, u32[]{:S(2)}, u32[]{:S(2)}) collective-permute-start(f32[2,128,128]{2,1,0:T(8,128)S(1)} %fusion.3), channel_id=1, source_target_pairs={{0,8},{4,12},{1,9},{5,13},{2,10},{6,14},{3,11},{7,15}} | collective-permute-start | bytes 393224 | tf_op jit(solution)/shard_map/ppermute | solution.py:252
  23.5 1.6 %collective-permute-start.7 = (f32[2,128,128]{2,1,0:T(8,128)S(1)}, f32[2,128,128]{2,1,0:T(8,128)S(1)}, u32[]{:S(2)}, u32[]{:S(2)}) collective-permute-start(f32[2,128,128]{2,1,0:T(8,128)S(1)} %get-tuple-element.110), channel_id=1, source_target_pairs={{0,4},{4,0},{8,12},{12,8},{16,20},{20,16},{24,28},{28,24},{1,5},{5... | collective-permute-start | bytes 393224 | tf_op jit(solution)/shard_map/ppermute | solution.py:252
  25.7 3.3 %collective-permute-done.7 = f32[2,128,128]{2,1,0:T(8,128)S(1)} collective-permute-done((f32[2,128,128]{2,1,0:T(8,128)S(1)}, f32[2,128,128]{2,1,0:T(8,128)S(1)}, u32[]{:S(2)}, u32[]{:S(2)}) %collective-permute-start.7) | collective-permute-done | bytes 131104 | tf_op jit(solution)/shard_map/ppermute | solution.py:252
  32.5 1.5 %collective-permute-start.11 = (f32[2,1024]{1,0:T(2,128)S(1)}, f32[2,1024]{1,0:T(2,128)S(1)}, u32[]{:S(2)}, u32[]{:S(2)}) collective-permute-start(f32[2,1024]{1,0:T(2,128)S(1)} %add.113), channel_id=1, source_target_pairs={{0,2},{1,3},{2,0},{3,1},{4,6},{5,7},{6,4},{7,5},{8,10},{9,11},{10,... | collective-permute-start | bytes 24584 | tf_op jit(solution)/shard_map/ppermute | solution.py:269
  34.0 2.1 %collective-permute-done.11 = f32[2,1024]{1,0:T(2,128)S(1)} collective-permute-done((f32[2,1024]{1,0:T(2,128)S(1)}, f32[2,1024]{1,0:T(2,128)S(1)}, u32[]{:S(2)}, u32[]{:S(2)}) %collective-permute-start.11) | collective-permute-done | bytes 8224 | tf_op jit(solution)/shard_map/ppermute | solution.py:269
  37.6 1.6 %collective-permute-start.13 = (f32[2,128,128]{2,1,0:T(8,128)S(1)}, f32[2,128,128]{2,1,0:T(8,128)S(1)}, u32[]{:S(2)}, u32[]{:S(2)}) collective-permute-start(f32[2,128,128]{2,1,0:T(8,128)S(1)} %slice_select_fusion.5), channel_id=1, source_target_pairs={{28,24},{24,28},{20,16},{16,20},{12,8},{8,12},{4,0},{0,4},{29,25},... | collective-permute-start | bytes 393224 | tf_op jit(solution)/shard_map/ppermute | solution.py:252
  40.8 2.0 %shard_map.95 = (bf16[1024,1024]{1,0:T(8,128)(2,1)}, f32[1024,128]{1,0:T(8,128)S(1)}, f32[1024,128]{1,0:T(8,128)S(1)}) custom-call(bf16[1024,1024]{1,0:T(8,128)(2,1)S(1)} %copy-done, bf16[1024,1024]{1,0:T(8,128)(2,1)S(1)} %get-tuple-element.90.k_ref, bf16[1024,1024]{1,0:T(8,128)(2,1)S(1)} %get-tuple-element.91.v_ref, ...), custom_call_target="tpu_custom_call" | custom-call | flops 301989888 | bytes 8126464 | tf_op jit(solution)/shard_map/pallas_call | solution.py:192
  45.5 2.0 %shard_map.96 = (bf16[1024,1024]{1,0:T(8,128)(2,1)}, f32[1024,128]{1,0:T(8,128)S(1)}, f32[1024,128]{1,0:T(8,128)S(1)}) custom-call(bf16[1024,1024]{1,0:T(8,128)(2,1)S(1)} %copy-done, bf16[1024,1024]{1,0:T(8,128)(2,1)S(1)} %get-tuple-element.90.k_ref, bf16[1024,1024]{1,0:T(8,128)(2,1)S(1)} %get-tuple-element.91.v_ref, ...), custom_call_target="tpu_custom_call", output_to_operand_aliasing={{0}: (6, {})} | custom-call | flops 301989888 | bytes 10223616 | tf_op jit(solution)/shard_map/pallas_call | solution.py:192
  48.1 2.0 %shard_map.97 = (bf16[1024,1024]{1,0:T(8,128)(2,1)}, f32[1024,128]{1,0:T(8,128)S(1)}, f32[1024,128]{1,0:T(8,128)S(1)}) custom-call(bf16[1024,1024]{1,0:T(8,128)(2,1)S(1)} %copy-done, bf16[1024,1024]{1,0:T(8,128)(2,1)S(1)} %get-tuple-element.90.k_ref, bf16[1024,1024]{1,0:T(8,128)(2,1)S(1)} %get-tuple-element.91.v_ref, ...), custom_call_target="tpu_custom_call", output_to_operand_aliasing={{0}: (6, {})} | custom-call | flops 301989888 | bytes 10223616 | tf_op jit(solution)/shard_map/pallas_call | solution.py:192
  50.9 2.0 %shard_map.98 = (bf16[1024,1024]{1,0:T(8,128)(2,1)}, f32[1024,128]{1,0:T(8,128)S(1)}, f32[1024,128]{1,0:T(8,128)S(1)}) custom-call(bf16[1024,1024]{1,0:T(8,128)(2,1)S(1)} %copy-done, bf16[1024,1024]{1,0:T(8,128)(2,1)S(1)} %get-tuple-element.90.k_ref, bf16[1024,1024]{1,0:T(8,128)(2,1)S(1)} %get-tuple-element.91.v_ref, ...), custom_call_target="tpu_custom_call", output_to_operand_aliasing={{0}: (6, {})} | custom-call | flops 301989888 | bytes 10223616 | tf_op jit(solution)/shard_map/pallas_call | solution.py:192
  53.5 2.0 %shard_map.99 = (bf16[1024,1024]{1,0:T(8,128)(2,1)}, f32[1024,128]{1,0:T(8,128)S(1)}, f32[1024,128]{1,0:T(8,128)S(1)}) custom-call(bf16[1024,1024]{1,0:T(8,128)(2,1)S(1)} %copy-done, bf16[1024,1024]{1,0:T(8,128)(2,1)S(1)} %get-tuple-element.90.k_ref, bf16[1024,1024]{1,0:T(8,128)(2,1)S(1)} %get-tuple-element.91.v_ref, ...), custom_call_target="tpu_custom_call", output_to_operand_aliasing={{0}: (6, {})} | custom-call | flops 301989888 | bytes 10223616 | tf_op jit(solution)/shard_map/pallas_call | solution.py:192
  56.9 2.0 %shard_map.100 = (bf16[1024,1024]{1,0:T(8,128)(2,1)}, f32[1024,128]{1,0:T(8,128)S(1)}, f32[1024,128]{1,0:T(8,128)S(1)}) custom-call(bf16[1024,1024]{1,0:T(8,128)(2,1)S(1)} %copy-done, bf16[1024,1024]{1,0:T(8,128)(2,1)S(1)} %get-tuple-element.90.k_ref, bf16[1024,1024]{1,0:T(8,128)(2,1)S(1)} %get-tuple-element.91.v_ref, ...), custom_call_target="tpu_custom_call", output_to_operand_aliasing={{0}: (6, {})} | custom-call | flops 301989888 | bytes 10223616 | tf_op jit(solution)/shard_map/pallas_call | solution.py:192
  58.8 1.5 %collective-permute-start.18 = (f32[2,128,128]{2,1,0:T(8,128)S(1)}, f32[2,128,128]{2,1,0:T(8,128)S(1)}, u32[]{:S(2)}, u32[]{:S(2)}) collective-permute-start(f32[2,128,128]{2,1,0:T(8,128)S(1)} %add.120), channel_id=1, source_target_pairs={{12,4},{8,0},{13,5},{9,1},{14,6},{10,2},{15,7},{11,3}} | collective-permute-start | bytes 393224 | tf_op jit(solution)/shard_map/ppermute | solution.py:252
  60.3 2.0 %shard_map.101 = (bf16[1024,1024]{1,0:T(8,128)(2,1)}, f32[1024,128]{1,0:T(8,128)S(1)}, f32[1024,128]{1,0:T(8,128)S(1)}) custom-call(bf16[1024,1024]{1,0:T(8,128)(2,1)S(1)} %copy-done, bf16[1024,1024]{1,0:T(8,128)(2,1)S(1)} %get-tuple-element.90.k_ref, bf16[1024,1024]{1,0:T(8,128)(2,1)S(1)} %get-tuple-element.91.v_ref, ...), custom_call_target="tpu_custom_call", output_to_operand_aliasing={{0}: (6, {})} | custom-call | flops 301989888 | bytes 10223616 | tf_op jit(solution)/shard_map/pallas_call | solution.py:192
  62.3 5.3 %collective-permute-done.19 = f32[2,128,128]{2,1,0:T(8,128)S(1)} collective-permute-done((f32[2,128,128]{2,1,0:T(8,128)S(1)}, f32[2,128,128]{2,1,0:T(8,128)S(1)}, u32[]{:S(2)}, u32[]{:S(2)}) %collective-permute-start.19) | collective-permute-done | bytes 131104 | tf_op jit(solution)/shard_map/ppermute | solution.py:252
  67.6 2.0 %collective-permute-start.21 = (f32[2,128,128]{2,1,0:T(8,128)S(1)}, f32[2,128,128]{2,1,0:T(8,128)S(1)}, u32[]{:S(2)}, u32[]{:S(2)}) collective-permute-start(f32[2,128,128]{2,1,0:T(8,128)S(1)} %get-tuple-element.159), channel_id=1, source_target_pairs={{28,24},{24,28},{20,16},{16,20},{12,8},{8,12},{4,0},{0,4},{29,25},... | collective-permute-start | bytes 393224 | tf_op jit(solution)/shard_map/ppermute | solution.py:252
  69.6 5.5 %collective-permute-done.18 = f32[2,128,128]{2,1,0:T(8,128)S(1)} collective-permute-done((f32[2,128,128]{2,1,0:T(8,128)S(1)}, f32[2,128,128]{2,1,0:T(8,128)S(1)}, u32[]{:S(2)}, u32[]{:S(2)}) %collective-permute-start.18) | collective-permute-done | bytes 131104 | tf_op jit(solution)/shard_map/ppermute | solution.py:252
  75.2 2.0 %shard_map.102 = (bf16[1024,1024]{1,0:T(8,128)(2,1)}, f32[1024,128]{1,0:T(8,128)S(1)}, f32[1024,128]{1,0:T(8,128)S(1)}) custom-call(bf16[1024,1024]{1,0:T(8,128)(2,1)S(1)} %copy-done, bf16[1024,1024]{1,0:T(8,128)(2,1)S(1)} %get-tuple-element.90.k_ref, bf16[1024,1024]{1,0:T(8,128)(2,1)S(1)} %get-tuple-element.91.v_ref, ...), custom_call_target="tpu_custom_call", output_to_operand_aliasing={{0}: (6, {})} | custom-call | flops 301989888 | bytes 10223616 | tf_op jit(solution)/shard_map/pallas_call | solution.py:192
  78.2 2.1 %shard_map.103 = bf16[1024,1024]{1,0:T(8,128)(2,1)} custom-call(f32[1024,512]{1,0:T(8,128)S(1)} %get-tuple-element.111.a_ref.refs_0_, f32[1024,512]{1,0:T(8,128)S(1)} %get-tuple-element.116.a_ref.refs_1_, f32[1,1024]{1,0:T(1,128)S(1)} %bitcast.5, f32[1024,128]{1,0:T(8,128)S(1)} %get-tuple-element.165.inv_ref.refs_3_), custom_call_target="tpu_custom_call" | custom-call | bytes 4722688 | tf_op jit(solution)/shard_map/pallas_call | solution.py:192
  80.3 1.7 %shard_map.104 = (bf16[1024,1024]{1,0:T(8,128)(2,1)}, bf16[1024,1024]{1,0:T(8,128)(2,1)}) custom-call(bf16[1024,1024]{1,0:T(8,128)(2,1)S(1)} %get-tuple-element.90.k_ref, bf16[1024,1024]{1,0:T(8,128)(2,1)S(1)} %get-tuple-element.91.v_ref, f32[4,128,128]{2,1,0:T(8,128)S(1)} %pad_maximum_fusion.2.s_ref, f32[1024,128]{1,0:T(8,128)S(1)} %get-tuple-element.126.rest_0_, ...), custom_call_target="tpu_custom_call" | custom-call | flops 268435456 | bytes 8650752 | tf_op jit(solution)/shard_map/pallas_call | solution.py:192
  82.2 1.7 %shard_map.105 = (bf16[1024,1024]{1,0:T(8,128)(2,1)}, bf16[1024,1024]{1,0:T(8,128)(2,1)}) custom-call(bf16[1024,1024]{1,0:T(8,128)(2,1)S(1)} %get-tuple-element.90.k_ref, bf16[1024,1024]{1,0:T(8,128)(2,1)S(1)} %get-tuple-element.91.v_ref, f32[4,128,128]{2,1,0:T(8,128)S(1)} %pad_maximum_fusion.3.s_ref, ...), custom_call_target="tpu_custom_call", output_to_operand_aliasing={{0}: (11, {}), {1}: (12, {})} | custom-call | flops 268435456 | bytes 12845056 | tf_op jit(solution)/shard_map/pallas_call | solution.py:192
  (79 shorter events, 25.9 us)
Async XLA Ops:
  3.1 7.1 %collective-permute-start = (f32[2,128,128]{2,1,0:T(8,128)S(1)}, f32[2,128,128]{2,1,0:T(8,128)S(1)}, u32[]{:S(2)}, u32[]{:S(2)}) collective-permute-start(f32[2,128,128]{2,1,0:T(8,128)S(1)} %slice_select_fusion.7), channel_id=1, source_target_pairs={{0,4},{4,0},{8,12},{12,8},{16,20},{20,16},{24,28},{28,24},{1,5},{5... | collective-permute-start | bytes 393224 | tf_op jit(solution)/shard_map/ppermute | solution.py:252
  6.8 7.5 %collective-permute-start.2 = (f32[2,128,128]{2,1,0:T(8,128)S(1)}, f32[2,128,128]{2,1,0:T(8,128)S(1)}, u32[]{:S(2)}, u32[]{:S(2)}) collective-permute-start(f32[2,128,128]{2,1,0:T(8,128)S(1)} %slice_select_fusion.1), channel_id=1, source_target_pairs={{0,4},{4,0},{8,12},{12,8},{16,20},{20,16},{24,28},{28,24},{1,5},{5... | collective-permute-start | bytes 393224 | tf_op jit(solution)/shard_map/ppermute | solution.py:252
  10.2 8.2 %collective-permute-start.1 = (f32[2,128,128]{2,1,0:T(8,128)S(1)}, f32[2,128,128]{2,1,0:T(8,128)S(1)}, u32[]{:S(2)}, u32[]{:S(2)}) collective-permute-start(f32[2,128,128]{2,1,0:T(8,128)S(1)} %fusion), channel_id=1, source_target_pairs={{0,8},{4,12},{1,9},{5,13},{2,10},{6,14},{3,11},{7,15}} | collective-permute-start | bytes 393224 | tf_op jit(solution)/shard_map/ppermute | solution.py:252
  15.5 4.3 %collective-permute-start.4 = (f32[2,128,128]{2,1,0:T(8,128)S(1)}, f32[2,128,128]{2,1,0:T(8,128)S(1)}, u32[]{:S(2)}, u32[]{:S(2)}) collective-permute-start(f32[2,128,128]{2,1,0:T(8,128)S(1)} %fusion.3), channel_id=1, source_target_pairs={{0,8},{4,12},{1,9},{5,13},{2,10},{6,14},{3,11},{7,15}} | collective-permute-start | bytes 393224 | tf_op jit(solution)/shard_map/ppermute | solution.py:252
  18.5 3.3 %collective-permute-start.3 = (f32[2,128,128]{2,1,0:T(8,128)S(1)}, f32[2,128,128]{2,1,0:T(8,128)S(1)}, u32[]{:S(2)}, u32[]{:S(2)}) collective-permute-start(f32[2,128,128]{2,1,0:T(8,128)S(1)} %add.99), channel_id=1, source_target_pairs={{8,16},{12,20},{9,17},{13,21},{10,18},{14,22},{11,19},{15,23}} | collective-permute-start | bytes 393224 | tf_op jit(solution)/shard_map/ppermute | solution.py:252
  21.0 8.0 %copy-start.1 = (bf16[1024,1024]{1,0:T(8,128)(2,1)S(1)}, bf16[1024,1024]{1,0:T(8,128)(2,1)}, u32[]{:S(2)}) copy-start(bf16[1024,1024]{1,0:T(8,128)(2,1)} %og_ref.3) | copy-start | bytes 6291460
  21.0 8.0 %copy-start.2 = (f32[1024]{0:T(1024)S(1)}, f32[1024]{0:T(1024)}, u32[]{:S(2)}) copy-start(f32[1024]{0:T(1024)} %param.8) | copy-start | bytes 12292
  21.0 1.5 %collective-permute-start.6 = (f32[2,128,128]{2,1,0:T(8,128)S(1)}, f32[2,128,128]{2,1,0:T(8,128)S(1)}, u32[]{:S(2)}, u32[]{:S(2)}) collective-permute-start(f32[2,128,128]{2,1,0:T(8,128)S(1)} %add.106), channel_id=1, source_target_pairs={{8,16},{12,20},{9,17},{13,21},{10,18},{14,22},{11,19},{15,23}} | collective-permute-start | bytes 393224 | tf_op jit(solution)/shard_map/ppermute | solution.py:252
  21.9 1.6 %collective-permute-start.5 = (f32[2,128,128]{2,1,0:T(8,128)S(1)}, f32[2,128,128]{2,1,0:T(8,128)S(1)}, u32[]{:S(2)}, u32[]{:S(2)}) collective-permute-start(f32[2,128,128]{2,1,0:T(8,128)S(1)} %add.102), channel_id=1, source_target_pairs={{16,24},{20,28},{17,25},{21,29},{18,26},{22,30},{19,27},{23,31}} | collective-permute-start | bytes 393224 | tf_op jit(solution)/shard_map/ppermute | solution.py:252
  22.6 2.5 %collective-permute-start.8 = (f32[2,128,128]{2,1,0:T(8,128)S(1)}, f32[2,128,128]{2,1,0:T(8,128)S(1)}, u32[]{:S(2)}, u32[]{:S(2)}) collective-permute-start(f32[2,128,128]{2,1,0:T(8,128)S(1)} %add.108), channel_id=1, source_target_pairs={{16,24},{20,28},{17,25},{21,29},{18,26},{22,30},{19,27},{23,31}} | collective-permute-start | bytes 393224 | tf_op jit(solution)/shard_map/ppermute | solution.py:252
  23.5 5.5 %collective-permute-start.7 = (f32[2,128,128]{2,1,0:T(8,128)S(1)}, f32[2,128,128]{2,1,0:T(8,128)S(1)}, u32[]{:S(2)}, u32[]{:S(2)}) collective-permute-start(f32[2,128,128]{2,1,0:T(8,128)S(1)} %get-tuple-element.110), channel_id=1, source_target_pairs={{0,4},{4,0},{8,12},{12,8},{16,20},{20,16},{24,28},{28,24},{1,5},{5... | collective-permute-start | bytes 393224 | tf_op jit(solution)/shard_map/ppermute | solution.py:252
  25.1 5.3 %collective-permute-start.9 = (f32[2,128,128]{2,1,0:T(8,128)S(1)}, f32[2,128,128]{2,1,0:T(8,128)S(1)}, u32[]{:S(2)}, u32[]{:S(2)}) collective-permute-start(f32[2,128,128]{2,1,0:T(8,128)S(1)} %get-tuple-element.113), channel_id=1, source_target_pairs={{0,4},{4,0},{8,12},{12,8},{16,20},{20,16},{24,28},{28,24},{1,5},{5... | collective-permute-start | bytes 393224 | tf_op jit(solution)/shard_map/ppermute | solution.py:252
  31.3 1.2 %collective-permute-start.10 = (f32[2,1024]{1,0:T(2,128)S(1)}, f32[2,1024]{1,0:T(2,128)S(1)}, u32[]{:S(2)}, u32[]{:S(2)}) collective-permute-start(f32[2,1024]{1,0:T(2,128)S(1)} %add.112), channel_id=1, source_target_pairs={{0,1},{1,0},{2,3},{3,2},{4,5},{5,4},{6,7},{7,6},{8,9},{9,8},{10,11... | collective-permute-start | bytes 24584 | tf_op jit(solution)/shard_map/ppermute | solution.py:269
  32.5 3.7 %collective-permute-start.11 = (f32[2,1024]{1,0:T(2,128)S(1)}, f32[2,1024]{1,0:T(2,128)S(1)}, u32[]{:S(2)}, u32[]{:S(2)}) collective-permute-start(f32[2,1024]{1,0:T(2,128)S(1)} %add.113), channel_id=1, source_target_pairs={{0,2},{1,3},{2,0},{3,1},{4,6},{5,7},{6,4},{7,5},{8,10},{9,11},{10,... | collective-permute-start | bytes 24584 | tf_op jit(solution)/shard_map/ppermute | solution.py:269
  37.6 6.0 %collective-permute-start.13 = (f32[2,128,128]{2,1,0:T(8,128)S(1)}, f32[2,128,128]{2,1,0:T(8,128)S(1)}, u32[]{:S(2)}, u32[]{:S(2)}) collective-permute-start(f32[2,128,128]{2,1,0:T(8,128)S(1)} %slice_select_fusion.5), channel_id=1, source_target_pairs={{28,24},{24,28},{20,16},{16,20},{12,8},{8,12},{4,0},{0,4},{29,25},... | collective-permute-start | bytes 393224 | tf_op jit(solution)/shard_map/ppermute | solution.py:252
  40.3 5.1 %collective-permute-start.12 = (f32[2,128,128]{2,1,0:T(8,128)S(1)}, f32[2,128,128]{2,1,0:T(8,128)S(1)}, u32[]{:S(2)}, u32[]{:S(2)}) collective-permute-start(f32[2,128,128]{2,1,0:T(8,128)S(1)} %slice_select_fusion.2), channel_id=1, source_target_pairs={{28,24},{24,28},{20,16},{16,20},{12,8},{8,12},{4,0},{0,4},{29,25},... | collective-permute-start | bytes 393224 | tf_op jit(solution)/shard_map/ppermute | solution.py:252
  43.7 6.4 %collective-permute-start.15 = (f32[2,128,128]{2,1,0:T(8,128)S(1)}, f32[2,128,128]{2,1,0:T(8,128)S(1)}, u32[]{:S(2)}, u32[]{:S(2)}) collective-permute-start(f32[2,128,128]{2,1,0:T(8,128)S(1)} %fusion.1), channel_id=1, source_target_pairs={{28,20},{24,16},{29,21},{25,17},{30,22},{26,18},{31,23},{27,19}} | collective-permute-start | bytes 393224 | tf_op jit(solution)/shard_map/ppermute | solution.py:252
  47.4 3.4 %collective-permute-start.14 = (f32[2,128,128]{2,1,0:T(8,128)S(1)}, f32[2,128,128]{2,1,0:T(8,128)S(1)}, u32[]{:S(2)}, u32[]{:S(2)}) collective-permute-start(f32[2,128,128]{2,1,0:T(8,128)S(1)} %fusion.2), channel_id=1, source_target_pairs={{28,20},{24,16},{29,21},{25,17},{30,22},{26,18},{31,23},{27,19}} | collective-permute-start | bytes 393224 | tf_op jit(solution)/shard_map/ppermute | solution.py:252
  50.1 5.3 %collective-permute-start.17 = (f32[2,128,128]{2,1,0:T(8,128)S(1)}, f32[2,128,128]{2,1,0:T(8,128)S(1)}, u32[]{:S(2)}, u32[]{:S(2)}) collective-permute-start(f32[2,128,128]{2,1,0:T(8,128)S(1)} %add.118), channel_id=1, source_target_pairs={{20,12},{16,8},{21,13},{17,9},{22,14},{18,10},{23,15},{19,11}} | collective-permute-start | bytes 393224 | tf_op jit(solution)/shard_map/ppermute | solution.py:252
  52.8 4.0 %collective-permute-start.16 = (f32[2,128,128]{2,1,0:T(8,128)S(1)}, f32[2,128,128]{2,1,0:T(8,128)S(1)}, u32[]{:S(2)}, u32[]{:S(2)}) collective-permute-start(f32[2,128,128]{2,1,0:T(8,128)S(1)} %add.117), channel_id=1, source_target_pairs={{20,12},{16,8},{21,13},{17,9},{22,14},{18,10},{23,15},{19,11}} | collective-permute-start | bytes 393224 | tf_op jit(solution)/shard_map/ppermute | solution.py:252
  55.5 12.1 %collective-permute-start.19 = (f32[2,128,128]{2,1,0:T(8,128)S(1)}, f32[2,128,128]{2,1,0:T(8,128)S(1)}, u32[]{:S(2)}, u32[]{:S(2)}) collective-permute-start(f32[2,128,128]{2,1,0:T(8,128)S(1)} %add.121), channel_id=1, source_target_pairs={{12,4},{8,0},{13,5},{9,1},{14,6},{10,2},{15,7},{11,3}} | collective-permute-start | bytes 393224 | tf_op jit(solution)/shard_map/ppermute | solution.py:252
  58.8 16.3 %collective-permute-start.18 = (f32[2,128,128]{2,1,0:T(8,128)S(1)}, f32[2,128,128]{2,1,0:T(8,128)S(1)}, u32[]{:S(2)}, u32[]{:S(2)}) collective-permute-start(f32[2,128,128]{2,1,0:T(8,128)S(1)} %add.120), channel_id=1, source_target_pairs={{12,4},{8,0},{13,5},{9,1},{14,6},{10,2},{15,7},{11,3}} | collective-permute-start | bytes 393224 | tf_op jit(solution)/shard_map/ppermute | solution.py:252
  67.6 12.6 %collective-permute-start.21 = (f32[2,128,128]{2,1,0:T(8,128)S(1)}, f32[2,128,128]{2,1,0:T(8,128)S(1)}, u32[]{:S(2)}, u32[]{:S(2)}) collective-permute-start(f32[2,128,128]{2,1,0:T(8,128)S(1)} %get-tuple-element.159), channel_id=1, source_target_pairs={{28,24},{24,28},{20,16},{16,20},{12,8},{8,12},{4,0},{0,4},{29,25},... | collective-permute-start | bytes 393224 | tf_op jit(solution)/shard_map/ppermute | solution.py:252
  77.1 5.0 %collective-permute-start.20 = (f32[2,128,128]{2,1,0:T(8,128)S(1)}, f32[2,128,128]{2,1,0:T(8,128)S(1)}, u32[]{:S(2)}, u32[]{:S(2)}) collective-permute-start(f32[2,128,128]{2,1,0:T(8,128)S(1)} %get-tuple-element.164), channel_id=1, source_target_pairs={{28,24},{24,28},{20,16},{16,20},{12,8},{8,12},{4,0},{0,4},{29,25},... | collective-permute-start | bytes 393224 | tf_op jit(solution)/shard_map/ppermute | solution.py:252
  (1 other events, 1.6 us)

commit v4 on v3

--- a/solution.py
+++ b/solution.py
@@ -121,51 +121,61 @@
         t_ref[h] = dot(q_ref[:, cq], grad, 0, 0)
 
 
-def mixed_kernel(parts, heads, *refs):
-    a_refs, (gain_ref, inv_ref, m_ref) = refs[:parts], refs[parts:]
-    for p, a_ref in enumerate(a_refs):
-        for h in range(heads):
-            cq = cols_of(p * heads + h)
-            m_ref[:, cq] = (gain_ref[:, cq] * a_ref[:, cols_of(h)] * inv_ref[...]).astype(BF16)
-
-
-def back_kernel(first, inner, winner, heads, blocks, q_ref, k_ref, v_ref, w_ref, g_ref, p_ref, *rest):
-    qg_hbm, kl_ref, vl_ref, qg, bw, plow, slow, sems = rest[-8:]
+def back_kernel(first, inner, heads, blocks, q_ref, k_ref, v_ref, w_ref, g_ref, p_ref, a_ref, gain_ref, inv_ref, *rest):
+    m_hbm, qg_hbm, kl_ref, vl_ref, mixed, qg, bw, plow, slow, sems = rest[-10:]
     causal = causal_mask()
-
-    def copy_out(h, c, cq):
-        return pltpu.make_async_copy(qg.at[:, c], qg_hbm.at[:, cq], sems.at[h])
-
-    def head(h, carry):
-        c, ci, cw, cq = cols_at(h), cols_at(h + inner), cols_at(h + winner), cols_at(h + first)
+    here = [(h, cols_of(h), cols_of(h + inner), cols_of(h + first)) for h in range(heads)]
+    copies = []
+
+    def copy_out(i, h, src, dst):
+        copies.append(pltpu.make_async_copy(src.at[:, cols_of(h)], dst.at[:, cols_of(h + first)], sems.at[i, h]))
+        copies[-1].start()
+
+    for h, c, ci, cq in here:
+        mixed[:, c] = (gain_ref[:, cq] * a_ref[:, ci] * inv_ref[...]).astype(BF16)
+        copy_out(0, h, mixed, m_hbm)
+    for h, c, ci, cq in here:
+        for n in range(0, blocks, 2):
+            r = slice(n * BLOCK, min(n + 2, blocks) * BLOCK)
+            s = dot(g_ref[r, ci], v_ref[r, cq], 1, 1)
+            for m in range(n, min(n + 2, blocks)):
+                inside = rows_of(m - n)
+                bw[rows_of(m), c] = jnp.where(causal, s[inside, inside], 0.0).astype(BF16)
+    for h, c, ci, cq in here:
+        prefix = p_ref[h + inner].T
+        plow[rows_of(0), c] = prefix.astype(BF16)
+        for n in range(blocks - 1):
+            prefix = prefix + dot(v_ref[rows_of(n), cq], k_ref[rows_of(n), cq], 0, 0)
+            plow[rows_of(n + 1), c] = prefix.astype(BF16)
+    for h, c, ci, cq in here:
         for n in range(blocks):
             r = rows_of(n)
-            bw[r, :] = jnp.where(causal, dot(g_ref[r, ci], v_ref[r, cq], 1, 1), 0.0).astype(BF16)
-        prefix = p_ref[h + inner]
-        plow[rows_of(0), :] = prefix.astype(BF16)
-        for n in range(blocks - 1):
-            prefix = prefix + dot(k_ref[rows_of(n), cq], v_ref[rows_of(n), cq], 0, 0)
-            plow[rows_of(n + 1), :] = prefix.astype(BF16)
+            left = jnp.concatenate([bw[r, c], g_ref[r, ci]], axis=1)
+            right = jnp.concatenate([k_ref[r, cq], plow[r, c]], axis=0)
+            qg[r, c] = dot(left, right, 1, 0).astype(BF16)
+        copy_out(1, h, qg, qg_hbm)
+    for h, c, ci, cq in here:
         suffix = None
         for n in reversed(range(1, blocks)):
-            s = dot(q_ref[rows_of(n), cq], g_ref[rows_of(n), ci], 0, 0)
+            s = dot(g_ref[rows_of(n), ci], q_ref[rows_of(n), cq], 0, 0)
             suffix = s if suffix is None else suffix + s
-            slow[rows_of(n - 1), :] = suffix.astype(BF16)
+            slow[rows_of(n - 1), c] = suffix.astype(BF16)
+    for h, c, ci, cq in here:
         for n in range(blocks):
             r = rows_of(n)
             q, k, v, g = q_ref[r, cq], k_ref[r, cq], v_ref[r, cq], g_ref[r, ci]
-            qg[r, c] = (dot(bw[r, :], k, 1, 0) + dot(g, plow[r, :], 1, 1)).astype(BF16)
-            kp, vp = dot(bw[r, :], q, 0, 0), dot(w_ref[r, cw], g, 0, 0)
+            vp = dot(w_ref[r, c], g, 0, 0)
             if n + 1 < blocks:
-                kp, vp = kp + dot(v, slow[r, :], 1, 1), vp + dot(k, slow[r, :], 1, 0)
+                left = jnp.concatenate([bw[r, c].T, v], axis=1)
+                right = jnp.concatenate([q, slow[r, c]], axis=0)
+                kp = dot(left, right, 1, 0)
+                vp = vp + dot(k, slow[r, c], 1, 1)
+            else:
+                kp = dot(bw[r, c], q, 0, 0)
             kl_ref[r, c] = kp
             vl_ref[r, c] = vp
-        copy_out(h, c, cq).start()
-        return carry
-
-    lax.fori_loop(0, heads, head, 0, unroll=min(2, heads))
-    for h in range(heads):
-        copy_out(h, cols_of(h), cols_of(h + first)).wait()
+    for copy in copies:
+        copy.wait()
 
 
 def last_kernel(first, pieces, heads, k_ref, v_ref, s_ref, *rest):
@@ -210,23 +220,29 @@
     half = states.shape[0] // 2
     mine = jnp.where(low, states[:half], states[half:])
     other = jnp.where(low, states[half:], states[:half])
-    got = yield other, perm(swap)
+    got = yield other, perm(swap), False
     pair = mine + got
     total = None
-    if outer <= 4:
+    if outer == 4 and not reverse:
+        r = yield pair, perm([(0, 2), (1, 3), (4, 6), (5, 7)]), False
+        both = pair + r
+        far = yield both, perm([(2, 6), (3, 7)]), False
+        (both,) = after((far,), both)
+        total = r + far + (yield both, perm([(2, 4), (3, 5)]), True)
+    elif outer <= 4:
         running = pair
         for hop in range(outer - 1):
-            r = yield running, perm([(2 * hop, 2 * hop + 2), (2 * hop + 1, 2 * hop + 3)])
+            r = yield running, perm([(2 * hop, 2 * hop + 2), (2 * hop + 1, 2 * hop + 3)]), False
             total = r if total is None else total + r
             running = r + pair
     else:
-        total = yield pair, perm([(i, i + 2) for i in range(size - 2)])
+        total = yield pair, perm([(i, i + 2) for i in range(size - 2)]), False
         step = 1
         while step < outer - 1:
-            r = yield total, perm([(i, i + 2 * step) for i in range(size - 2 * step)])
+            r = yield total, perm([(i, i + 2 * step) for i in range(size - 2 * step)]), False
             total = total + r
             step *= 2
-    answer = yield at_first(total + mine, total), perm(swap)
+    answer = yield at_first(total + mine, total), perm(swap), False
     kept = at_first(total, total + got)
     return jnp.concatenate([jnp.where(low, kept, answer), jnp.where(low, answer, kept)], axis=0)
 
@@ -247,13 +263,14 @@
             except StopIteration as stop:
                 settled = finish(name, stop.value)
                 continue
-        ordered = arrived[-len(makers) - 1 : -len(makers)]
+        back = 1 + name if request[2] else 1 + len(makers)
+        ordered = arrived[-back:][:1] if len(arrived) >= back else []
         operand, *_ = lax.optimization_barrier((request[0], *ordered, *behind))
         arrived.append(lax.ppermute(operand, "seq", request[1]))
         live.append((name, scan, arrived[-1]))
-        behind = pieces[event]((operand,)) if event < len(pieces) else ()
+        behind = pieces.pop(event)((operand,)) if event in pieces else ()
         event += 1
-    for piece in pieces[event:]:
+    for piece in pieces.values():
         piece(())
 
 
@@ -296,7 +313,7 @@
     def piece_state(tied):
         (kt,) = after(tied, k)
         states.extend(call(functools.partial(state_kernel, half, half), [kt, v], [state], flops=unit * half))
-        return (states[1],)
+        return (states[1], *piece_local(0, (states[1],)))
 
     size = min(2, half)
     weights, attended = {}, {}
@@ -329,7 +346,7 @@
 
     drive(
         [lambda i=i: scan_stages(states[i], seq_size, low, False) for i in range(2)],
-        [piece_state] + [functools.partial(piece_local, first) for first in range(0, heads, size)],
+        {0: piece_state, **{2 * i: functools.partial(piece_local, i * size) for i in range(1, heads // size)}},
         make_stats,
     )
     total = head_sum(sums[0] + sums[1], head_size)
@@ -351,35 +368,31 @@
 
     made, inner = {}, {}
 
-    def piece_back(h, tied):
-        i = h // half
+    def piece_back(first, tied):
+        i = first // half
         (qt,) = after(tied, queries)
-        ins = [qt, k, v, weights[h // size * size], grads[i], prefixes[i]]
+        ins = [qt, k, v, weights[first], grads[i], prefixes[i], atts[i], gain, inverse]
         specs, aliases = [VMEM] * len(ins), {}
         if "query" in made:
-            aliases = {len(ins): 0}
-            ins.append(made["query"])
-            specs.append(HBM)
-        made["query"], kl, vl = call(
-            functools.partial(back_kernel, h, h % half, h % size, 1, blocks),
+            aliases = {len(ins): 0, len(ins) + 1: 1}
+            ins += [made["mixed"], made["query"]]
+            specs += [HBM, HBM]
+        own = ((rows, size * HEAD_DIM), F32)
+        made["mixed"], made["query"], kl, vl = call(
+            functools.partial(back_kernel, first, first % half, size, blocks),
             ins,
-            [whole, ((rows, HEAD_DIM), F32), ((rows, HEAD_DIM), F32)],
+            [whole, whole, own, own],
             in_specs=specs,
-            out_specs=[HBM, VMEM, VMEM],
-            scratch=[pltpu.VMEM((rows, HEAD_DIM), BF16)] * 4 + [pltpu.SemaphoreType.DMA((1,))],
+            out_specs=[HBM, HBM, VMEM, VMEM],
+            scratch=[pltpu.VMEM((rows, size * HEAD_DIM), BF16)] * 5 + [pltpu.SemaphoreType.DMA((2, size))],
             aliases=aliases,
-            flops=9 * unit,
+            flops=9 * unit * size,
         )
-        inner[h] = (kl, vl)
+        inner[first] = (kl, vl)
         return kl, vl
 
-    def piece_mixed(tied):
-        (inv,) = after(tied, inverse)
-        (made["mixed"],) = call(functools.partial(mixed_kernel, 2, half), [*atts, gain, inv], [whole])
-        return (made["mixed"],)
-
     def make_last(i, suffix):
-        mine = [inner[h] for h in range(i * half, (i + 1) * half)]
+        mine = [inner[first] for first in range(i * half, (i + 1) * half, size)]
         ins = [k, v, suffix] + [kl for kl, _ in mine] + [vl for _, vl in mine]
         specs, aliases = [VMEM] * len(ins), {}
         if "key" in made:
@@ -387,7 +400,7 @@
             ins += [made["key"], made["value"]]
             specs += [HBM, HBM]
         made["key"], made["value"] = call(
-            functools.partial(last_kernel, i * half, half, 1),
+            functools.partial(last_kernel, i * half, len(mine), size),
             ins,
             [whole, whole],
             in_specs=specs,
@@ -401,9 +414,10 @@
     piece_grad(0, ())
     drive(
         [lambda i=i: scan_stages(backs[i], seq_size, low, True) for i in range(2)],
-        [functools.partial(piece_grad, 1)]
-        + [functools.partial(piece_back, h) for h in range(heads)]
-        + [piece_mixed],
+        {
+            0: functools.partial(piece_grad, 1),
+            **{2 * i + 2: functools.partial(piece_back, i * size) for i in range(heads // size)},
+        },
         make_last,
     )
     return made["mixed"], made["query"], made["key"], made["value"]

time: 84.5 us -> 92 us (1.089)
  waiting for transfers between devices: 22 us -> 38.6 us
  Pallas kernels: 33 us -> 23.6 us
    ppermute x20, waiting for transfers between devices: 18.7 us -> 35.3 us  [drive(): arrived.append(lax.ppermute(operand, 'seq', request[1]))]
    pallas_call x22 -> x17, Pallas kernels: 33 us -> 23.6 us  [call(): pl.pallas_call(kernel, in_specs=in_specs or [VMEM] * len(ins), out_specs=...]
  transfers between devices with their start and end apart: 22 -> 22, of which waited for: 11 -> 12; matrix products, arithmetic and copies ran while one was open for 1% -> 1% of each run, Pallas kernels for 32% -> 19%
where the time goes in v4:
time: 92 us; the launch traced here: 91.7 us
  waiting for transfers between devices  38.6 us (42%)
  starting transfers between devices  26.6 us (29%)
  Pallas kernels  23.6 us (26%)
  between operations  1.22 us (1%)
  local copies, waits for them, and re-layouts  0.98 us (1%)
    ppermute x20, waiting for transfers between devices, drive(): arrived.append(lax.ppermute(operand, 'seq', request[1]))  35.3 us
    ppermute x20, starting transfers between devices, drive(): arrived.append(lax.ppermute(operand, 'seq', request[1]))  25 us
    pallas_call x17, Pallas kernels, call(): pl.pallas_call(kernel, in_specs=in_specs or [VMEM] * len(ins), out_specs=...  23.6 us
    ppermute x2, waiting for transfers between devices, head_sum(): a = a + lax.ppermute(a, 'head', [(i, i ^ step) for i in range(size)])  3.29 us
  transfers between devices with their start and end apart: 22, of which 12 were waited for; matrix products, arithmetic and copies ran while one was open for 1% of the time, Pallas kernels for 19%

profile of v4, /device:TPU:0, one launch (start us, length us, event | category | flops | bytes accessed | tf_op | source)
XLA Modules:
  0.0 91.7 jit_solution(908510372811309548)
XLA Ops:
  0.6 2.4 %shard_map.84 = (bf16[1024,1024]{1,0:T(8,128)(2,1)S(1)}, bf16[1024,1024]{1,0:T(8,128)(2,1)S(1)}, f32[4,128,128]{2,1,0:T(8,128)S(1)}) custom-call(bf16[1024,1024]{1,0:T(8,128)(2,1)} %k_hbm.1, bf16[1024,1024]{1,0:T(8,128)(2,1)} %v_hbm.1), custom_call_target="tpu_custom_call" | custom-call | flops 134217728 | bytes 4194304 | tf_op jit(solution)/shard_map/pallas_call | solution.py:202
  3.1 3.0 %collective-permute-start = (f32[2,128,128]{2,1,0:T(8,128)S(1)}, f32[2,128,128]{2,1,0:T(8,128)S(1)}, u32[]{:S(2)}, u32[]{:S(2)}) collective-permute-start(f32[2,128,128]{2,1,0:T(8,128)S(1)} %slice_select_fusion.7), channel_id=1, source_target_pairs={{0,4},{4,0},{8,12},{12,8},{16,20},{20,16},{24,28},{28,24},{1,5},{5... | collective-permute-start | bytes 393224 | tf_op jit(solution)/shard_map/ppermute | solution.py:269
  7.7 1.2 %shard_map.86 = (bf16[1024,256]{1,0:T(8,128)(2,1)S(1)}, f32[1024,256]{1,0:T(8,128)S(1)}) custom-call(bf16[1024,1024]{1,0:T(8,128)(2,1)S(1)} %copy-done, bf16[1024,1024]{1,0:T(8,128)(2,1)S(1)} %get-tuple-element.77.k_ref, bf16[1024,1024]{1,0:T(8,128)(2,1)S(1)} %get-tuple-element.78.v_ref), custom_call_target="tpu_custom_call" | custom-call | flops 268435456 | bytes 6291456 | tf_op jit(solution)/shard_map/pallas_call | solution.py:202
  9.6 3.7 %collective-permute-start.1 = (f32[2,128,128]{2,1,0:T(8,128)S(1)}, f32[2,128,128]{2,1,0:T(8,128)S(1)}, u32[]{:S(2)}, u32[]{:S(2)}) collective-permute-start(f32[2,128,128]{2,1,0:T(8,128)S(1)} %fusion), channel_id=1, source_target_pairs={{0,8},{4,12},{16,24},{20,28},{1,9},{5,13},{17,25},{21,29},{2,10},{... | collective-permute-start | bytes 393224 | tf_op jit(solution)/shard_map/ppermute | solution.py:269
  13.9 1.2 %shard_map.87 = (bf16[1024,256]{1,0:T(8,128)(2,1)S(1)}, f32[1024,256]{1,0:T(8,128)S(1)}) custom-call(bf16[1024,1024]{1,0:T(8,128)(2,1)S(1)} %copy-done, bf16[1024,1024]{1,0:T(8,128)(2,1)S(1)} %get-tuple-element.77.k_ref, bf16[1024,1024]{1,0:T(8,128)(2,1)S(1)} %get-tuple-element.78.v_ref), custom_call_target="tpu_custom_call" | custom-call | flops 268435456 | bytes 6291456 | tf_op jit(solution)/shard_map/pallas_call | solution.py:202
  15.1 3.5 %collective-permute-start.4 = (f32[2,128,128]{2,1,0:T(8,128)S(1)}, f32[2,128,128]{2,1,0:T(8,128)S(1)}, u32[]{:S(2)}, u32[]{:S(2)}) collective-permute-start(f32[2,128,128]{2,1,0:T(8,128)S(1)} %fusion.3), channel_id=1, source_target_pairs={{0,8},{4,12},{16,24},{20,28},{1,9},{5,13},{17,25},{21,29},{2,10},{... | collective-permute-start | bytes 393224 | tf_op jit(solution)/shard_map/ppermute | solution.py:269
  25.2 1.6 %collective-permute-start.9 = (f32[2,128,128]{2,1,0:T(8,128)S(1)}, f32[2,128,128]{2,1,0:T(8,128)S(1)}, u32[]{:S(2)}, u32[]{:S(2)}) collective-permute-start(f32[2,128,128]{2,1,0:T(8,128)S(1)} %get-tuple-element.102), channel_id=1, source_target_pairs={{0,4},{4,0},{8,12},{12,8},{16,20},{20,16},{24,28},{28,24},{1,5},{5... | collective-permute-start | bytes 393224 | tf_op jit(solution)/shard_map/ppermute | solution.py:269
  26.7 2.8 %collective-permute-done.7 = f32[2,128,128]{2,1,0:T(8,128)S(1)} collective-permute-done((f32[2,128,128]{2,1,0:T(8,128)S(1)}, f32[2,128,128]{2,1,0:T(8,128)S(1)}, u32[]{:S(2)}, u32[]{:S(2)}) %collective-permute-start.7) | collective-permute-done | bytes 131104 | tf_op jit(solution)/shard_map/ppermute | solution.py:269
  32.0 1.2 %collective-permute-done.10 = f32[2,1024]{1,0:T(2,128)S(1)} collective-permute-done((f32[2,1024]{1,0:T(2,128)S(1)}, f32[2,1024]{1,0:T(2,128)S(1)}, u32[]{:S(2)}, u32[]{:S(2)}) %collective-permute-start.10) | collective-permute-done | bytes 8224 | tf_op jit(solution)/shard_map/ppermute | solution.py:286
  33.2 1.5 %collective-permute-start.11 = (f32[2,1024]{1,0:T(2,128)S(1)}, f32[2,1024]{1,0:T(2,128)S(1)}, u32[]{:S(2)}, u32[]{:S(2)}) collective-permute-start(f32[2,1024]{1,0:T(2,128)S(1)} %add.105), channel_id=1, source_target_pairs={{0,2},{1,3},{2,0},{3,1},{4,6},{5,7},{6,4},{7,5},{8,10},{9,11},{10,... | collective-permute-start | bytes 24584 | tf_op jit(solution)/shard_map/ppermute | solution.py:286
  34.7 2.1 %collective-permute-done.11 = f32[2,1024]{1,0:T(2,128)S(1)} collective-permute-done((f32[2,1024]{1,0:T(2,128)S(1)}, f32[2,1024]{1,0:T(2,128)S(1)}, u32[]{:S(2)}, u32[]{:S(2)}) %collective-permute-start.11) | collective-permute-done | bytes 8224 | tf_op jit(solution)/shard_map/ppermute | solution.py:286
  40.1 1.4 %collective-permute-start.14 = (f32[2,128,128]{2,1,0:T(8,128)S(1)}, f32[2,128,128]{2,1,0:T(8,128)S(1)}, u32[]{:S(2)}, u32[]{:S(2)}) collective-permute-start(f32[2,128,128]{2,1,0:T(8,128)S(1)} %slice_select_fusion.3), channel_id=1, source_target_pairs={{28,24},{24,28},{20,16},{16,20},{12,8},{8,12},{4,0},{0,4},{29,25},... | collective-permute-start | bytes 393224 | tf_op jit(solution)/shard_map/ppermute | solution.py:269
  41.4 2.8 %collective-permute-done.12 = f32[2,128,128]{2,1,0:T(8,128)S(1)} collective-permute-done((f32[2,128,128]{2,1,0:T(8,128)S(1)}, f32[2,128,128]{2,1,0:T(8,128)S(1)}, u32[]{:S(2)}, u32[]{:S(2)}) %collective-permute-start.12) | collective-permute-done | bytes 131104 | tf_op jit(solution)/shard_map/ppermute | solution.py:269
  45.7 2.0 %shard_map.95 = (bf16[1024,1024]{1,0:T(8,128)(2,1)}, bf16[1024,1024]{1,0:T(8,128)(2,1)}, f32[1024,256]{1,0:T(8,128)S(1)}, f32[1024,256]{1,0:T(8,128)S(1)}) custom-call(bf16[1024,1024]{1,0:T(8,128)(2,1)S(1)} %copy-done, bf16[1024,1024]{1,0:T(8,128)(2,1)S(1)} %get-tuple-element.77.k_ref, bf16[1024,1024]{1,0:T(8,128)(2,1)S(1)} %get-tuple-element.78.v_ref, ...), custom_call_target="tpu_custom_call" | custom-call | flops 603979776 | bytes 10752000 | tf_op jit(solution)/shard_map/pallas_call | solution.py:202
  49.2 2.0 %shard_map.96 = (bf16[1024,1024]{1,0:T(8,128)(2,1)}, bf16[1024,1024]{1,0:T(8,128)(2,1)}, f32[1024,256]{1,0:T(8,128)S(1)}, f32[1024,256]{1,0:T(8,128)S(1)}) custom-call(bf16[1024,1024]{1,0:T(8,128)(2,1)S(1)} %copy-done, bf16[1024,1024]{1,0:T(8,128)(2,1)S(1)} %get-tuple-element.77.k_ref, ...), custom_call_target="tpu_custom_call", output_to_operand_aliasing={{0}: (9, {}), {1}: (10, {})} | custom-call | flops 603979776 | bytes 14946304 | tf_op jit(solution)/shard_map/pallas_call | solution.py:202
  52.0 1.3 %collective-permute-start.17 = (f32[2,128,128]{2,1,0:T(8,128)S(1)}, f32[2,128,128]{2,1,0:T(8,128)S(1)}, u32[]{:S(2)}, u32[]{:S(2)}) collective-permute-start(f32[2,128,128]{2,1,0:T(8,128)S(1)} %add.110), channel_id=1, source_target_pairs={{12,4},{8,0},{13,5},{9,1},{14,6},{10,2},{15,7},{11,3}} | collective-permute-start | bytes 393224 | tf_op jit(solution)/shard_map/ppermute | solution.py:269
  53.3 2.1 %shard_map.97 = (bf16[1024,1024]{1,0:T(8,128)(2,1)}, bf16[1024,1024]{1,0:T(8,128)(2,1)}, f32[1024,256]{1,0:T(8,128)S(1)}, f32[1024,256]{1,0:T(8,128)S(1)}) custom-call(bf16[1024,1024]{1,0:T(8,128)(2,1)S(1)} %copy-done, bf16[1024,1024]{1,0:T(8,128)(2,1)S(1)} %get-tuple-element.77.k_ref, ...), custom_call_target="tpu_custom_call", output_to_operand_aliasing={{0}: (9, {}), {1}: (10, {})} | custom-call | flops 603979776 | bytes 14946304 | tf_op jit(solution)/shard_map/pallas_call | solution.py:202
  55.4 1.3 %collective-permute-start.19 = (f32[2,128,128]{2,1,0:T(8,128)S(1)}, f32[2,128,128]{2,1,0:T(8,128)S(1)}, u32[]{:S(2)}, u32[]{:S(2)}) collective-permute-start(f32[2,128,128]{2,1,0:T(8,128)S(1)} %add.116), channel_id=1, source_target_pairs={{12,4},{8,0},{13,5},{9,1},{14,6},{10,2},{15,7},{11,3}} | collective-permute-start | bytes 393224 | tf_op jit(solution)/shard_map/ppermute | solution.py:269
  56.7 18.5 %collective-permute-done.17 = f32[2,128,128]{2,1,0:T(8,128)S(1)} collective-permute-done((f32[2,128,128]{2,1,0:T(8,128)S(1)}, f32[2,128,128]{2,1,0:T(8,128)S(1)}, u32[]{:S(2)}, u32[]{:S(2)}) %collective-permute-start.17) | collective-permute-done | bytes 131104 | tf_op jit(solution)/shard_map/ppermute | solution.py:269
  76.2 6.3 %collective-permute-done.19 = f32[2,128,128]{2,1,0:T(8,128)S(1)} collective-permute-done((f32[2,128,128]{2,1,0:T(8,128)S(1)}, f32[2,128,128]{2,1,0:T(8,128)S(1)}, u32[]{:S(2)}, u32[]{:S(2)}) %collective-permute-start.19) | collective-permute-done | bytes 131104 | tf_op jit(solution)/shard_map/ppermute | solution.py:269
  82.5 2.1 %shard_map.98 = (bf16[1024,1024]{1,0:T(8,128)(2,1)}, bf16[1024,1024]{1,0:T(8,128)(2,1)}, f32[1024,256]{1,0:T(8,128)S(1)}, f32[1024,256]{1,0:T(8,128)S(1)}) custom-call(bf16[1024,1024]{1,0:T(8,128)(2,1)S(1)} %copy-done, bf16[1024,1024]{1,0:T(8,128)(2,1)S(1)} %get-tuple-element.77.k_ref, ...), custom_call_target="tpu_custom_call", output_to_operand_aliasing={{0}: (9, {}), {1}: (10, {})} | custom-call | flops 603979776 | bytes 14946304 | tf_op jit(solution)/shard_map/pallas_call | solution.py:202
  85.8 1.8 %shard_map.99 = (bf16[1024,1024]{1,0:T(8,128)(2,1)}, bf16[1024,1024]{1,0:T(8,128)(2,1)}) custom-call(bf16[1024,1024]{1,0:T(8,128)(2,1)S(1)} %get-tuple-element.77.k_ref, bf16[1024,1024]{1,0:T(8,128)(2,1)S(1)} %get-tuple-element.78.v_ref, f32[4,128,128]{2,1,0:T(8,128)S(1)} %pad_maximum_fusion.2.s_ref, f32[1024,256]{1,0:T(8,128)S(1)} %get-tuple-element.115.rest_0_, ...), custom_call_target="tpu_custom_call" | custom-call | flops 268435456 | bytes 8650752 | tf_op jit(solution)/shard_map/pallas_call | solution.py:202
  87.6 2.0 %collective-permute-done.20 = f32[2,128,128]{2,1,0:T(8,128)S(1)} collective-permute-done((f32[2,128,128]{2,1,0:T(8,128)S(1)}, f32[2,128,128]{2,1,0:T(8,128)S(1)}, u32[]{:S(2)}, u32[]{:S(2)}) %collective-permute-start.20) | collective-permute-done | bytes 131104 | tf_op jit(solution)/shard_map/ppermute | solution.py:269
  89.7 1.8 %shard_map.100 = (bf16[1024,1024]{1,0:T(8,128)(2,1)}, bf16[1024,1024]{1,0:T(8,128)(2,1)}) custom-call(bf16[1024,1024]{1,0:T(8,128)(2,1)S(1)} %get-tuple-element.77.k_ref, bf16[1024,1024]{1,0:T(8,128)(2,1)S(1)} %get-tuple-element.78.v_ref, f32[4,128,128]{2,1,0:T(8,128)S(1)} %pad_maximum_fusion.3.s_ref, ...), custom_call_target="tpu_custom_call", output_to_operand_aliasing={{0}: (7, {}), {1}: (8, {})} | custom-call | flops 268435456 | bytes 12845056 | tf_op jit(solution)/shard_map/pallas_call | solution.py:202
  (72 shorter events, 20.9 us)
Async XLA Ops:
  3.1 6.5 %collective-permute-start = (f32[2,128,128]{2,1,0:T(8,128)S(1)}, f32[2,128,128]{2,1,0:T(8,128)S(1)}, u32[]{:S(2)}, u32[]{:S(2)}) collective-permute-start(f32[2,128,128]{2,1,0:T(8,128)S(1)} %slice_select_fusion.7), channel_id=1, source_target_pairs={{0,4},{4,0},{8,12},{12,8},{16,20},{20,16},{24,28},{28,24},{1,5},{5... | collective-permute-start | bytes 393224 | tf_op jit(solution)/shard_map/ppermute | solution.py:269
  8.9 5.0 %collective-permute-start.2 = (f32[2,128,128]{2,1,0:T(8,128)S(1)}, f32[2,128,128]{2,1,0:T(8,128)S(1)}, u32[]{:S(2)}, u32[]{:S(2)}) collective-permute-start(f32[2,128,128]{2,1,0:T(8,128)S(1)} %slice_select_fusion.1), channel_id=1, source_target_pairs={{0,4},{4,0},{8,12},{12,8},{16,20},{20,16},{24,28},{28,24},{1,5},{5... | collective-permute-start | bytes 393224 | tf_op jit(solution)/shard_map/ppermute | solution.py:269
  9.6 9.0 %collective-permute-start.1 = (f32[2,128,128]{2,1,0:T(8,128)S(1)}, f32[2,128,128]{2,1,0:T(8,128)S(1)}, u32[]{:S(2)}, u32[]{:S(2)}) collective-permute-start(f32[2,128,128]{2,1,0:T(8,128)S(1)} %fusion), channel_id=1, source_target_pairs={{0,8},{4,12},{16,24},{20,28},{1,9},{5,13},{17,25},{21,29},{2,10},{... | collective-permute-start | bytes 393224 | tf_op jit(solution)/shard_map/ppermute | solution.py:269
  15.1 6.0 %collective-permute-start.4 = (f32[2,128,128]{2,1,0:T(8,128)S(1)}, f32[2,128,128]{2,1,0:T(8,128)S(1)}, u32[]{:S(2)}, u32[]{:S(2)}) collective-permute-start(f32[2,128,128]{2,1,0:T(8,128)S(1)} %fusion.3), channel_id=1, source_target_pairs={{0,8},{4,12},{16,24},{20,28},{1,9},{5,13},{17,25},{21,29},{2,10},{... | collective-permute-start | bytes 393224 | tf_op jit(solution)/shard_map/ppermute | solution.py:269
  18.6 3.2 %collective-permute-start.3 = (f32[2,128,128]{2,1,0:T(8,128)S(1)}, f32[2,128,128]{2,1,0:T(8,128)S(1)}, u32[]{:S(2)}, u32[]{:S(2)}) collective-permute-start(f32[2,128,128]{2,1,0:T(8,128)S(1)} %add.93), channel_id=1, source_target_pairs={{8,24},{12,28},{9,25},{13,29},{10,26},{14,30},{11,27},{15,31}} | collective-permute-start | bytes 393224 | tf_op jit(solution)/shard_map/ppermute | solution.py:269
  21.1 0.7 collective-permute-start.5
  21.8 2.7 %collective-permute-start.6 = (f32[2,128,128]{2,1,0:T(8,128)S(1)}, f32[2,128,128]{2,1,0:T(8,128)S(1)}, u32[]{:S(2)}, u32[]{:S(2)}) collective-permute-start(f32[2,128,128]{2,1,0:T(8,128)S(1)} %add.93), channel_id=1, source_target_pairs={{8,16},{12,20},{9,17},{13,21},{10,18},{14,22},{11,19},{15,23}} | collective-permute-start | bytes 393224 | tf_op jit(solution)/shard_map/ppermute | solution.py:269
  23.6 6.0 %copy-start.1 = (bf16[1024,1024]{1,0:T(8,128)(2,1)S(1)}, bf16[1024,1024]{1,0:T(8,128)(2,1)}, u32[]{:S(2)}) copy-start(bf16[1024,1024]{1,0:T(8,128)(2,1)} %og_ref.3) | copy-start | bytes 6291460
  23.6 6.0 %copy-start.2 = (f32[1024]{0:T(1024)S(1)}, f32[1024]{0:T(1024)}, u32[]{:S(2)}) copy-start(f32[1024]{0:T(1024)} %param.8) | copy-start | bytes 12292
  23.7 1.5 %collective-permute-start.8 = (f32[2,128,128]{2,1,0:T(8,128)S(1)}, f32[2,128,128]{2,1,0:T(8,128)S(1)}, u32[]{:S(2)}, u32[]{:S(2)}) collective-permute-start(f32[2,128,128]{2,1,0:T(8,128)S(1)} %add.96), channel_id=1, source_target_pairs={{8,16},{12,20},{9,17},{13,21},{10,18},{14,22},{11,19},{15,23}} | collective-permute-start | bytes 393224 | tf_op jit(solution)/shard_map/ppermute | solution.py:269
  24.5 5.0 %collective-permute-start.7 = (f32[2,128,128]{2,1,0:T(8,128)S(1)}, f32[2,128,128]{2,1,0:T(8,128)S(1)}, u32[]{:S(2)}, u32[]{:S(2)}) collective-permute-start(f32[2,128,128]{2,1,0:T(8,128)S(1)} %get-tuple-element.94), channel_id=1, source_target_pairs={{0,4},{4,0},{8,12},{12,8},{16,20},{20,16},{24,28},{28,24},{1,5},{5... | collective-permute-start | bytes 393224 | tf_op jit(solution)/shard_map/ppermute | solution.py:269
  25.2 5.8 %collective-permute-start.9 = (f32[2,128,128]{2,1,0:T(8,128)S(1)}, f32[2,128,128]{2,1,0:T(8,128)S(1)}, u32[]{:S(2)}, u32[]{:S(2)}) collective-permute-start(f32[2,128,128]{2,1,0:T(8,128)S(1)} %get-tuple-element.102), channel_id=1, source_target_pairs={{0,4},{4,0},{8,12},{12,8},{16,20},{20,16},{24,28},{28,24},{1,5},{5... | collective-permute-start | bytes 393224 | tf_op jit(solution)/shard_map/ppermute | solution.py:269
  31.9 1.2 %collective-permute-start.10 = (f32[2,1024]{1,0:T(2,128)S(1)}, f32[2,1024]{1,0:T(2,128)S(1)}, u32[]{:S(2)}, u32[]{:S(2)}) collective-permute-start(f32[2,1024]{1,0:T(2,128)S(1)} %add.104), channel_id=1, source_target_pairs={{0,1},{1,0},{2,3},{3,2},{4,5},{5,4},{6,7},{7,6},{8,9},{9,8},{10,11... | collective-permute-start | bytes 24584 | tf_op jit(solution)/shard_map/ppermute | solution.py:286
  33.2 3.7 %collective-permute-start.11 = (f32[2,1024]{1,0:T(2,128)S(1)}, f32[2,1024]{1,0:T(2,128)S(1)}, u32[]{:S(2)}, u32[]{:S(2)}) collective-permute-start(f32[2,1024]{1,0:T(2,128)S(1)} %add.105), channel_id=1, source_target_pairs={{0,2},{1,3},{2,0},{3,1},{4,6},{5,7},{6,4},{7,5},{8,10},{9,11},{10,... | collective-permute-start | bytes 24584 | tf_op jit(solution)/shard_map/ppermute | solution.py:286
  38.2 6.0 %collective-permute-start.12 = (f32[2,128,128]{2,1,0:T(8,128)S(1)}, f32[2,128,128]{2,1,0:T(8,128)S(1)}, u32[]{:S(2)}, u32[]{:S(2)}) collective-permute-start(f32[2,128,128]{2,1,0:T(8,128)S(1)} %slice_select_fusion.4), channel_id=1, source_target_pairs={{28,24},{24,28},{20,16},{16,20},{12,8},{8,12},{4,0},{0,4},{29,25},... | collective-permute-start | bytes 393224 | tf_op jit(solution)/shard_map/ppermute | solution.py:269
  40.1 5.6 %collective-permute-start.14 = (f32[2,128,128]{2,1,0:T(8,128)S(1)}, f32[2,128,128]{2,1,0:T(8,128)S(1)}, u32[]{:S(2)}, u32[]{:S(2)}) collective-permute-start(f32[2,128,128]{2,1,0:T(8,128)S(1)} %slice_select_fusion.3), channel_id=1, source_target_pairs={{28,24},{24,28},{20,16},{16,20},{12,8},{8,12},{4,0},{0,4},{29,25},... | collective-permute-start | bytes 393224 | tf_op jit(solution)/shard_map/ppermute | solution.py:269
  44.3 4.1 %collective-permute-start.13 = (f32[2,128,128]{2,1,0:T(8,128)S(1)}, f32[2,128,128]{2,1,0:T(8,128)S(1)}, u32[]{:S(2)}, u32[]{:S(2)}) collective-permute-start(f32[2,128,128]{2,1,0:T(8,128)S(1)} %fusion.1), channel_id=1, source_target_pairs={{28,20},{24,16},{29,21},{25,17},{30,22},{26,18},{31,23},{27,19}} | collective-permute-start | bytes 393224 | tf_op jit(solution)/shard_map/ppermute | solution.py:269
  47.8 1.4 %collective-permute-start.16 = (f32[2,128,128]{2,1,0:T(8,128)S(1)}, f32[2,128,128]{2,1,0:T(8,128)S(1)}, u32[]{:S(2)}, u32[]{:S(2)}) collective-permute-start(f32[2,128,128]{2,1,0:T(8,128)S(1)} %fusion.2), channel_id=1, source_target_pairs={{28,20},{24,16},{29,21},{25,17},{30,22},{26,18},{31,23},{27,19}} | collective-permute-start | bytes 393224 | tf_op jit(solution)/shard_map/ppermute | solution.py:269
  48.5 3.4 %collective-permute-start.15 = (f32[2,128,128]{2,1,0:T(8,128)S(1)}, f32[2,128,128]{2,1,0:T(8,128)S(1)}, u32[]{:S(2)}, u32[]{:S(2)}) collective-permute-start(f32[2,128,128]{2,1,0:T(8,128)S(1)} %add.108), channel_id=1, source_target_pairs={{20,12},{16,8},{21,13},{17,9},{22,14},{18,10},{23,15},{19,11}} | collective-permute-start | bytes 393224 | tf_op jit(solution)/shard_map/ppermute | solution.py:269
  51.2 2.0 %collective-permute-start.18 = (f32[2,128,128]{2,1,0:T(8,128)S(1)}, f32[2,128,128]{2,1,0:T(8,128)S(1)}, u32[]{:S(2)}, u32[]{:S(2)}) collective-permute-start(f32[2,128,128]{2,1,0:T(8,128)S(1)} %add.114), channel_id=1, source_target_pairs={{20,12},{16,8},{21,13},{17,9},{22,14},{18,10},{23,15},{19,11}} | collective-permute-start | bytes 393224 | tf_op jit(solution)/shard_map/ppermute | solution.py:269
  52.0 23.2 %collective-permute-start.17 = (f32[2,128,128]{2,1,0:T(8,128)S(1)}, f32[2,128,128]{2,1,0:T(8,128)S(1)}, u32[]{:S(2)}, u32[]{:S(2)}) collective-permute-start(f32[2,128,128]{2,1,0:T(8,128)S(1)} %add.110), channel_id=1, source_target_pairs={{12,4},{8,0},{13,5},{9,1},{14,6},{10,2},{15,7},{11,3}} | collective-permute-start | bytes 393224 | tf_op jit(solution)/shard_map/ppermute | solution.py:269
  55.4 27.1 %collective-permute-start.19 = (f32[2,128,128]{2,1,0:T(8,128)S(1)}, f32[2,128,128]{2,1,0:T(8,128)S(1)}, u32[]{:S(2)}, u32[]{:S(2)}) collective-permute-start(f32[2,128,128]{2,1,0:T(8,128)S(1)} %add.116), channel_id=1, source_target_pairs={{12,4},{8,0},{13,5},{9,1},{14,6},{10,2},{15,7},{11,3}} | collective-permute-start | bytes 393224 | tf_op jit(solution)/shard_map/ppermute | solution.py:269
  75.2 10.5 %collective-permute-start.21 = (f32[2,128,128]{2,1,0:T(8,128)S(1)}, f32[2,128,128]{2,1,0:T(8,128)S(1)}, u32[]{:S(2)}, u32[]{:S(2)}) collective-permute-start(f32[2,128,128]{2,1,0:T(8,128)S(1)} %get-tuple-element.125), channel_id=1, source_target_pairs={{28,24},{24,28},{20,16},{16,20},{12,8},{8,12},{4,0},{0,4},{29,25},... | collective-permute-start | bytes 393224 | tf_op jit(solution)/shard_map/ppermute | solution.py:269
  84.6 5.0 %collective-permute-start.20 = (f32[2,128,128]{2,1,0:T(8,128)S(1)}, f32[2,128,128]{2,1,0:T(8,128)S(1)}, u32[]{:S(2)}, u32[]{:S(2)}) collective-permute-start(f32[2,128,128]{2,1,0:T(8,128)S(1)} %get-tuple-element.140), channel_id=1, source_target_pairs={{28,24},{24,28},{20,16},{16,20},{12,8},{8,12},{4,0},{0,4},{29,25},... | collective-permute-start | bytes 393224 | tf_op jit(solution)/shard_map/ppermute | solution.py:269
  (1 other events, 1.6 us)

commit v5 on v4

--- a/solution.py
+++ b/solution.py
@@ -121,7 +121,7 @@
         t_ref[h] = dot(q_ref[:, cq], grad, 0, 0)
 
 
-def back_kernel(first, inner, heads, blocks, q_ref, k_ref, v_ref, w_ref, g_ref, p_ref, a_ref, gain_ref, inv_ref, *rest):
+def back_kernel(first, inner, winner, heads, blocks, q_ref, k_ref, v_ref, w_ref, g_ref, p_ref, a_ref, gain_ref, inv_ref, *rest):
     m_hbm, qg_hbm, kl_ref, vl_ref, mixed, qg, bw, plow, slow, sems = rest[-10:]
     causal = causal_mask()
     here = [(h, cols_of(h), cols_of(h + inner), cols_of(h + first)) for h in range(heads)]
@@ -164,7 +164,7 @@
         for n in range(blocks):
             r = rows_of(n)
             q, k, v, g = q_ref[r, cq], k_ref[r, cq], v_ref[r, cq], g_ref[r, ci]
-            vp = dot(w_ref[r, c], g, 0, 0)
+            vp = dot(w_ref[r, cols_of(h + winner)], g, 0, 0)
             if n + 1 < blocks:
                 left = jnp.concatenate([bw[r, c].T, v], axis=1)
                 right = jnp.concatenate([q, slow[r, c]], axis=0)
@@ -220,54 +220,42 @@
     half = states.shape[0] // 2
     mine = jnp.where(low, states[:half], states[half:])
     other = jnp.where(low, states[half:], states[:half])
-    got = yield other, perm(swap), False
+    got = yield other, perm(swap)
     pair = mine + got
     total = None
-    if outer == 4 and not reverse:
-        r = yield pair, perm([(0, 2), (1, 3), (4, 6), (5, 7)]), False
-        both = pair + r
-        far = yield both, perm([(2, 6), (3, 7)]), False
-        (both,) = after((far,), both)
-        total = r + far + (yield both, perm([(2, 4), (3, 5)]), True)
-    elif outer <= 4:
+    if outer <= 4:
         running = pair
         for hop in range(outer - 1):
-            r = yield running, perm([(2 * hop, 2 * hop + 2), (2 * hop + 1, 2 * hop + 3)]), False
+            r = yield running, perm([(2 * hop, 2 * hop + 2), (2 * hop + 1, 2 * hop + 3)])
             total = r if total is None else total + r
             running = r + pair
     else:
-        total = yield pair, perm([(i, i + 2) for i in range(size - 2)]), False
+        total = yield pair, perm([(i, i + 2) for i in range(size - 2)])
         step = 1
         while step < outer - 1:
-            r = yield total, perm([(i, i + 2 * step) for i in range(size - 2 * step)]), False
+            r = yield total, perm([(i, i + 2 * step) for i in range(size - 2 * step)])
             total = total + r
             step *= 2
-    answer = yield at_first(total + mine, total), perm(swap), False
+    answer = yield at_first(total + mine, total), perm(swap)
     kept = at_first(total, total + got)
     return jnp.concatenate([jnp.where(low, kept, answer), jnp.where(low, answer, kept)], axis=0)
 
 
 def drive(makers, pieces, finish):
-    live, arrived, behind, settled, event = [], [], (), (), 0
+    live, behind, event = [], (), 0
     waiting = list(makers)
     while waiting or live:
         if waiting:
             scan = waiting.pop(0)()
-            name, request = len(makers) - len(waiting) - 1, next(scan)
+            name, (operand, pairs) = len(makers) - len(waiting) - 1, next(scan)
         else:
             name, scan, result = live.pop(0)
-            if settled:
-                result = after(settled, result)[0]
             try:
-                request = scan.send(result)
+                operand, pairs = scan.send(after(behind, result)[0])
             except StopIteration as stop:
-                settled = finish(name, stop.value)
+                behind = finish(name, stop.value)
                 continue
-        back = 1 + name if request[2] else 1 + len(makers)
-        ordered = arrived[-back:][:1] if len(arrived) >= back else []
-        operand, *_ = lax.optimization_barrier((request[0], *ordered, *behind))
-        arrived.append(lax.ppermute(operand, "seq", request[1]))
-        live.append((name, scan, arrived[-1]))
+        live.append((name, scan, lax.ppermute(operand, "seq", pairs)))
         behind = pieces.pop(event)((operand,)) if event in pieces else ()
         event += 1
     for piece in pieces.values():
@@ -275,7 +263,7 @@
 
 
 def after(tied, *arrays):
-    return lax.optimization_barrier((*arrays, *tied))[: len(arrays)]
+    return lax.optimization_barrier((*arrays, *tied))[: len(arrays)] if tied else arrays
 
 
 def head_sum(a, size):
@@ -313,7 +301,7 @@
     def piece_state(tied):
         (kt,) = after(tied, k)
         states.extend(call(functools.partial(state_kernel, half, half), [kt, v], [state], flops=unit * half))
-        return (states[1], *piece_local(0, (states[1],)))
+        return (states[1],)
 
     size = min(2, half)
     weights, attended = {}, {}
@@ -346,7 +334,7 @@
 
     drive(
         [lambda i=i: scan_stages(states[i], seq_size, low, False) for i in range(2)],
-        {0: piece_state, **{2 * i: functools.partial(piece_local, i * size) for i in range(1, heads // size)}},
+        {0: piece_state, **{i + 1: functools.partial(piece_local, i * size) for i in range(heads // size)}},
         make_stats,
     )
     total = head_sum(sums[0] + sums[1], head_size)
@@ -371,28 +359,28 @@
     def piece_back(first, tied):
         i = first // half
         (qt,) = after(tied, queries)
-        ins = [qt, k, v, weights[first], grads[i], prefixes[i], atts[i], gain, inverse]
+        ins = [qt, k, v, weights[first // size * size], grads[i], prefixes[i], atts[i], gain, inverse]
         specs, aliases = [VMEM] * len(ins), {}
         if "query" in made:
             aliases = {len(ins): 0, len(ins) + 1: 1}
             ins += [made["mixed"], made["query"]]
             specs += [HBM, HBM]
-        own = ((rows, size * HEAD_DIM), F32)
+        own = ((rows, HEAD_DIM), F32)
         made["mixed"], made["query"], kl, vl = call(
-            functools.partial(back_kernel, first, first % half, size, blocks),
+            functools.partial(back_kernel, first, first % half, first % size, 1, blocks),
             ins,
             [whole, whole, own, own],
             in_specs=specs,
             out_specs=[HBM, HBM, VMEM, VMEM],
-            scratch=[pltpu.VMEM((rows, size * HEAD_DIM), BF16)] * 5 + [pltpu.SemaphoreType.DMA((2, size))],
+            scratch=[pltpu.VMEM((rows, HEAD_DIM), BF16)] * 5 + [pltpu.SemaphoreType.DMA((2, 1))],
             aliases=aliases,
-            flops=9 * unit * size,
+            flops=9 * unit,
         )
         inner[first] = (kl, vl)
         return kl, vl
 
     def make_last(i, suffix):
-        mine = [inner[first] for first in range(i * half, (i + 1) * half, size)]
+        mine = [inner[first] for first in range(i * half, (i + 1) * half)]
         ins = [k, v, suffix] + [kl for kl, _ in mine] + [vl for _, vl in mine]
         specs, aliases = [VMEM] * len(ins), {}
         if "key" in made:
@@ -400,7 +388,7 @@
             ins += [made["key"], made["value"]]
             specs += [HBM, HBM]
         made["key"], made["value"] = call(
-            functools.partial(last_kernel, i * half, len(mine), size),
+            functools.partial(last_kernel, i * half, half, 1),
             ins,
             [whole, whole],
             in_specs=specs,
@@ -416,7 +404,7 @@
         [lambda i=i: scan_stages(backs[i], seq_size, low, True) for i in range(2)],
         {
             0: functools.partial(piece_grad, 1),
-            **{2 * i + 2: functools.partial(piece_back, i * size) for i in range(heads // size)},
+            **{i + 1: functools.partial(piece_back, i) for i in range(heads)},
         },
         make_last,
     )

time: 92 us -> 80.8 us (0.88)
  waiting for transfers between devices: 38.6 us -> 21.3 us
  Pallas kernels: 23.6 us -> 31.6 us
  starting transfers between devices: 26.6 us -> 24.7 us
    ppermute x20, waiting for transfers between devices: 35.3 us -> 18 us  [drive(): live.append((name, scan, lax.ppermute(operand, 'seq', pairs)))]
    pallas_call x17 -> x21, Pallas kernels: 23.6 us -> 31.6 us  [call(): pl.pallas_call(kernel, in_specs=in_specs or [VMEM] * len(ins), out_specs=...]
    ppermute x20, starting transfers between devices: 25 us -> 23.1 us  [drive(): live.append((name, scan, lax.ppermute(operand, 'seq', pairs)))]
  transfers between devices with their start and end apart: 22 -> 22, of which waited for: 12 -> 11; matrix products, arithmetic and copies ran while one was open for 1% -> 1% of each run, Pallas kernels for 19% -> 31%
where the time goes in v5:
time: 80.8 us; the launch traced here: 80.5 us
  Pallas kernels  31.6 us (39%)
  starting transfers between devices  24.7 us (31%)
  waiting for transfers between devices  21.3 us (26%)
  between operations  1.3 us (2%)
  local copies, waits for them, and re-layouts  0.87 us (1%)
    pallas_call x21, Pallas kernels, call(): pl.pallas_call(kernel, in_specs=in_specs or [VMEM] * len(ins), out_specs=...  31.6 us
    ppermute x20, starting transfers between devices, drive(): live.append((name, scan, lax.ppermute(operand, 'seq', pairs)))  23.1 us
    ppermute x20, waiting for transfers between devices, drive(): live.append((name, scan, lax.ppermute(operand, 'seq', pairs)))  18 us
    ppermute x2, waiting for transfers between devices, head_sum(): a = a + lax.ppermute(a, 'head', [(i, i ^ step) for i in range(size)])  3.28 us
  transfers between devices with their start and end apart: 22, of which 11 were waited for; matrix products, arithmetic and copies ran while one was open for 1% of the time, Pallas kernels for 31%

profile of v5, /device:TPU:0, one launch (start us, length us, event | category | flops | bytes accessed | tf_op | source)
XLA Modules:
  0.0 80.5 jit_solution(2420919098046516967)
XLA Ops:
  0.6 2.4 %shard_map.84 = (bf16[1024,1024]{1,0:T(8,128)(2,1)S(1)}, bf16[1024,1024]{1,0:T(8,128)(2,1)S(1)}, f32[4,128,128]{2,1,0:T(8,128)S(1)}) custom-call(bf16[1024,1024]{1,0:T(8,128)(2,1)} %k_hbm.1, bf16[1024,1024]{1,0:T(8,128)(2,1)} %v_hbm.1), custom_call_target="tpu_custom_call" | custom-call | flops 134217728 | bytes 4194304 | tf_op jit(solution)/shard_map/pallas_call | solution.py:202
  3.1 3.0 %collective-permute-start = (f32[2,128,128]{2,1,0:T(8,128)S(1)}, f32[2,128,128]{2,1,0:T(8,128)S(1)}, u32[]{:S(2)}, u32[]{:S(2)}) collective-permute-start(f32[2,128,128]{2,1,0:T(8,128)S(1)} %slice_select_fusion.7), channel_id=1, source_target_pairs={{0,4},{4,0},{8,12},{12,8},{16,20},{20,16},{24,28},{28,24},{1,5},{5... | collective-permute-start | bytes 393224 | tf_op jit(solution)/shard_map/ppermute | solution.py:258
  8.9 1.3 %collective-permute-done = f32[2,128,128]{2,1,0:T(8,128)S(1)} collective-permute-done((f32[2,128,128]{2,1,0:T(8,128)S(1)}, f32[2,128,128]{2,1,0:T(8,128)S(1)}, u32[]{:S(2)}, u32[]{:S(2)}) %collective-permute-start) | collective-permute-done | bytes 131104 | tf_op jit(solution)/shard_map/ppermute | solution.py:258
  10.2 4.1 %collective-permute-start.1 = (f32[2,128,128]{2,1,0:T(8,128)S(1)}, f32[2,128,128]{2,1,0:T(8,128)S(1)}, u32[]{:S(2)}, u32[]{:S(2)}) collective-permute-start(f32[2,128,128]{2,1,0:T(8,128)S(1)} %fusion), channel_id=1, source_target_pairs={{0,8},{4,12},{1,9},{5,13},{2,10},{6,14},{3,11},{7,15}} | collective-permute-start | bytes 393224 | tf_op jit(solution)/shard_map/ppermute | solution.py:258
  15.5 1.3 %collective-permute-start.6 = (f32[2,128,128]{2,1,0:T(8,128)S(1)}, f32[2,128,128]{2,1,0:T(8,128)S(1)}, u32[]{:S(2)}, u32[]{:S(2)}) collective-permute-start(f32[2,128,128]{2,1,0:T(8,128)S(1)} %fusion.3), channel_id=1, source_target_pairs={{0,8},{4,12},{1,9},{5,13},{2,10},{6,14},{3,11},{7,15}} | collective-permute-start | bytes 393224 | tf_op jit(solution)/shard_map/ppermute | solution.py:258
  22.4 1.7 %collective-permute-start.5 = (f32[2,128,128]{2,1,0:T(8,128)S(1)}, f32[2,128,128]{2,1,0:T(8,128)S(1)}, u32[]{:S(2)}, u32[]{:S(2)}) collective-permute-start(f32[2,128,128]{2,1,0:T(8,128)S(1)} %get-tuple-element.180), channel_id=1, source_target_pairs={{0,4},{4,0},{8,12},{12,8},{16,20},{20,16},{24,28},{28,24},{1,5},{5... | collective-permute-start | bytes 393224 | tf_op jit(solution)/shard_map/ppermute | solution.py:258
  24.6 3.1 %collective-permute-done.5 = f32[2,128,128]{2,1,0:T(8,128)S(1)} collective-permute-done((f32[2,128,128]{2,1,0:T(8,128)S(1)}, f32[2,128,128]{2,1,0:T(8,128)S(1)}, u32[]{:S(2)}, u32[]{:S(2)}) %collective-permute-start.5) | collective-permute-done | bytes 131104 | tf_op jit(solution)/shard_map/ppermute | solution.py:258
  31.5 1.5 %collective-permute-start.11 = (f32[2,1024]{1,0:T(2,128)S(1)}, f32[2,1024]{1,0:T(2,128)S(1)}, u32[]{:S(2)}, u32[]{:S(2)}) collective-permute-start(f32[2,1024]{1,0:T(2,128)S(1)} %add.113), channel_id=1, source_target_pairs={{0,2},{1,3},{2,0},{3,1},{4,6},{5,7},{6,4},{7,5},{8,10},{9,11},{10,... | collective-permute-start | bytes 24584 | tf_op jit(solution)/shard_map/ppermute | solution.py:274
  33.0 2.1 %collective-permute-done.11 = f32[2,1024]{1,0:T(2,128)S(1)} collective-permute-done((f32[2,1024]{1,0:T(2,128)S(1)}, f32[2,1024]{1,0:T(2,128)S(1)}, u32[]{:S(2)}, u32[]{:S(2)}) %collective-permute-start.11) | collective-permute-done | bytes 8224 | tf_op jit(solution)/shard_map/ppermute | solution.py:274
  36.5 1.4 %collective-permute-start.12 = (f32[2,128,128]{2,1,0:T(8,128)S(1)}, f32[2,128,128]{2,1,0:T(8,128)S(1)}, u32[]{:S(2)}, u32[]{:S(2)}) collective-permute-start(f32[2,128,128]{2,1,0:T(8,128)S(1)} %slice_select_fusion.4), channel_id=1, source_target_pairs={{28,24},{24,28},{20,16},{16,20},{12,8},{8,12},{4,0},{0,4},{29,25},... | collective-permute-start | bytes 393224 | tf_op jit(solution)/shard_map/ppermute | solution.py:258
  39.7 2.0 %shard_map.95 = (bf16[1024,1024]{1,0:T(8,128)(2,1)}, bf16[1024,1024]{1,0:T(8,128)(2,1)}, f32[1024,128]{1,0:T(8,128)S(1)}, f32[1024,128]{1,0:T(8,128)S(1)}) custom-call(bf16[1024,1024]{1,0:T(8,128)(2,1)S(1)} %copy-done, bf16[1024,1024]{1,0:T(8,128)(2,1)S(1)} %get-tuple-element.91.k_ref, bf16[1024,1024]{1,0:T(8,128)(2,1)S(1)} %get-tuple-element.92.v_ref, ...), custom_call_target="tpu_custom_call" | custom-call | flops 301989888 | bytes 10752000 | tf_op jit(solution)/shard_map/pallas_call | solution.py:202
  43.5 2.0 %shard_map.96 = (bf16[1024,1024]{1,0:T(8,128)(2,1)}, bf16[1024,1024]{1,0:T(8,128)(2,1)}, f32[1024,128]{1,0:T(8,128)S(1)}, f32[1024,128]{1,0:T(8,128)S(1)}) custom-call(bf16[1024,1024]{1,0:T(8,128)(2,1)S(1)} %copy-done, bf16[1024,1024]{1,0:T(8,128)(2,1)S(1)} %get-tuple-element.91.k_ref, ...), custom_call_target="tpu_custom_call", output_to_operand_aliasing={{0}: (9, {}), {1}: (10, {})} | custom-call | flops 301989888 | bytes 14946304 | tf_op jit(solution)/shard_map/pallas_call | solution.py:202
  46.3 2.0 %shard_map.97 = (bf16[1024,1024]{1,0:T(8,128)(2,1)}, bf16[1024,1024]{1,0:T(8,128)(2,1)}, f32[1024,128]{1,0:T(8,128)S(1)}, f32[1024,128]{1,0:T(8,128)S(1)}) custom-call(bf16[1024,1024]{1,0:T(8,128)(2,1)S(1)} %copy-done, bf16[1024,1024]{1,0:T(8,128)(2,1)S(1)} %get-tuple-element.91.k_ref, ...), custom_call_target="tpu_custom_call", output_to_operand_aliasing={{0}: (9, {}), {1}: (10, {})} | custom-call | flops 301989888 | bytes 14946304 | tf_op jit(solution)/shard_map/pallas_call | solution.py:202
  49.0 2.0 %shard_map.98 = (bf16[1024,1024]{1,0:T(8,128)(2,1)}, bf16[1024,1024]{1,0:T(8,128)(2,1)}, f32[1024,128]{1,0:T(8,128)S(1)}, f32[1024,128]{1,0:T(8,128)S(1)}) custom-call(bf16[1024,1024]{1,0:T(8,128)(2,1)S(1)} %copy-done, bf16[1024,1024]{1,0:T(8,128)(2,1)S(1)} %get-tuple-element.91.k_ref, ...), custom_call_target="tpu_custom_call", output_to_operand_aliasing={{0}: (9, {}), {1}: (10, {})} | custom-call | flops 301989888 | bytes 14946304 | tf_op jit(solution)/shard_map/pallas_call | solution.py:202
  51.7 2.0 %shard_map.99 = (bf16[1024,1024]{1,0:T(8,128)(2,1)}, bf16[1024,1024]{1,0:T(8,128)(2,1)}, f32[1024,128]{1,0:T(8,128)S(1)}, f32[1024,128]{1,0:T(8,128)S(1)}) custom-call(bf16[1024,1024]{1,0:T(8,128)(2,1)S(1)} %copy-done, bf16[1024,1024]{1,0:T(8,128)(2,1)S(1)} %get-tuple-element.91.k_ref, ...), custom_call_target="tpu_custom_call", output_to_operand_aliasing={{0}: (9, {}), {1}: (10, {})} | custom-call | flops 301989888 | bytes 14946304 | tf_op jit(solution)/shard_map/pallas_call | solution.py:202
  53.8 1.3 %collective-permute-start.17 = (f32[2,128,128]{2,1,0:T(8,128)S(1)}, f32[2,128,128]{2,1,0:T(8,128)S(1)}, u32[]{:S(2)}, u32[]{:S(2)}) collective-permute-start(f32[2,128,128]{2,1,0:T(8,128)S(1)} %add.120), channel_id=1, source_target_pairs={{12,4},{8,0},{13,5},{9,1},{14,6},{10,2},{15,7},{11,3}} | collective-permute-start | bytes 393224 | tf_op jit(solution)/shard_map/ppermute | solution.py:258
  55.1 2.0 %shard_map.100 = (bf16[1024,1024]{1,0:T(8,128)(2,1)}, bf16[1024,1024]{1,0:T(8,128)(2,1)}, f32[1024,128]{1,0:T(8,128)S(1)}, f32[1024,128]{1,0:T(8,128)S(1)}) custom-call(bf16[1024,1024]{1,0:T(8,128)(2,1)S(1)} %copy-done, bf16[1024,1024]{1,0:T(8,128)(2,1)S(1)} %get-tuple-element.91.k_ref, ...), custom_call_target="tpu_custom_call", output_to_operand_aliasing={{0}: (9, {}), {1}: (10, {})} | custom-call | flops 301989888 | bytes 14946304 | tf_op jit(solution)/shard_map/pallas_call | solution.py:202
  57.1 1.5 %collective-permute-start.19 = (f32[2,128,128]{2,1,0:T(8,128)S(1)}, f32[2,128,128]{2,1,0:T(8,128)S(1)}, u32[]{:S(2)}, u32[]{:S(2)}) collective-permute-start(f32[2,128,128]{2,1,0:T(8,128)S(1)} %add.121), channel_id=1, source_target_pairs={{12,4},{8,0},{13,5},{9,1},{14,6},{10,2},{15,7},{11,3}} | collective-permute-start | bytes 393224 | tf_op jit(solution)/shard_map/ppermute | solution.py:258
  58.7 2.0 %shard_map.101 = (bf16[1024,1024]{1,0:T(8,128)(2,1)}, bf16[1024,1024]{1,0:T(8,128)(2,1)}, f32[1024,128]{1,0:T(8,128)S(1)}, f32[1024,128]{1,0:T(8,128)S(1)}) custom-call(bf16[1024,1024]{1,0:T(8,128)(2,1)S(1)} %copy-done, bf16[1024,1024]{1,0:T(8,128)(2,1)S(1)} %get-tuple-element.91.k_ref, ...), custom_call_target="tpu_custom_call", output_to_operand_aliasing={{0}: (9, {}), {1}: (10, {})} | custom-call | flops 301989888 | bytes 14946304 | tf_op jit(solution)/shard_map/pallas_call | solution.py:202
  60.7 9.6 %collective-permute-done.17 = f32[2,128,128]{2,1,0:T(8,128)S(1)} collective-permute-done((f32[2,128,128]{2,1,0:T(8,128)S(1)}, f32[2,128,128]{2,1,0:T(8,128)S(1)}, u32[]{:S(2)}, u32[]{:S(2)}) %collective-permute-start.17) | collective-permute-done | bytes 131104 | tf_op jit(solution)/shard_map/ppermute | solution.py:258
  71.0 2.0 %shard_map.102 = (bf16[1024,1024]{1,0:T(8,128)(2,1)}, bf16[1024,1024]{1,0:T(8,128)(2,1)}, f32[1024,128]{1,0:T(8,128)S(1)}, f32[1024,128]{1,0:T(8,128)S(1)}) custom-call(bf16[1024,1024]{1,0:T(8,128)(2,1)S(1)} %copy-done, bf16[1024,1024]{1,0:T(8,128)(2,1)S(1)} %get-tuple-element.91.k_ref, ...), custom_call_target="tpu_custom_call", output_to_operand_aliasing={{0}: (9, {}), {1}: (10, {})} | custom-call | flops 301989888 | bytes 14946304 | tf_op jit(solution)/shard_map/pallas_call | solution.py:202
  75.4 1.8 %shard_map.103 = (bf16[1024,1024]{1,0:T(8,128)(2,1)}, bf16[1024,1024]{1,0:T(8,128)(2,1)}) custom-call(bf16[1024,1024]{1,0:T(8,128)(2,1)S(1)} %get-tuple-element.91.k_ref, bf16[1024,1024]{1,0:T(8,128)(2,1)S(1)} %get-tuple-element.92.v_ref, f32[4,128,128]{2,1,0:T(8,128)S(1)} %pad_maximum_fusion.2.s_ref, f32[1024,128]{1,0:T(8,128)S(1)} %get-tuple-element.121.rest_0_, ...), custom_call_target="tpu_custom_call" | custom-call | flops 268435456 | bytes 8650752 | tf_op jit(solution)/shard_map/pallas_call | solution.py:202
  77.2 1.2 %collective-permute-done.20 = f32[2,128,128]{2,1,0:T(8,128)S(1)} collective-permute-done((f32[2,128,128]{2,1,0:T(8,128)S(1)}, f32[2,128,128]{2,1,0:T(8,128)S(1)}, u32[]{:S(2)}, u32[]{:S(2)}) %collective-permute-start.20) | collective-permute-done | bytes 131104 | tf_op jit(solution)/shard_map/ppermute | solution.py:258
  78.5 1.8 %shard_map.104 = (bf16[1024,1024]{1,0:T(8,128)(2,1)}, bf16[1024,1024]{1,0:T(8,128)(2,1)}) custom-call(bf16[1024,1024]{1,0:T(8,128)(2,1)S(1)} %get-tuple-element.91.k_ref, bf16[1024,1024]{1,0:T(8,128)(2,1)S(1)} %get-tuple-element.92.v_ref, f32[4,128,128]{2,1,0:T(8,128)S(1)} %pad_maximum_fusion.3.s_ref, ...), custom_call_target="tpu_custom_call", output_to_operand_aliasing={{0}: (11, {}), {1}: (12, {})} | custom-call | flops 268435456 | bytes 12845056 | tf_op jit(solution)/shard_map/pallas_call | solution.py:202
  (78 shorter events, 23.8 us)
Async XLA Ops:
  3.1 7.1 %collective-permute-start = (f32[2,128,128]{2,1,0:T(8,128)S(1)}, f32[2,128,128]{2,1,0:T(8,128)S(1)}, u32[]{:S(2)}, u32[]{:S(2)}) collective-permute-start(f32[2,128,128]{2,1,0:T(8,128)S(1)} %slice_select_fusion.7), channel_id=1, source_target_pairs={{0,4},{4,0},{8,12},{12,8},{16,20},{20,16},{24,28},{28,24},{1,5},{5... | collective-permute-start | bytes 393224 | tf_op jit(solution)/shard_map/ppermute | solution.py:258
  6.8 8.7 %collective-permute-start.2 = (f32[2,128,128]{2,1,0:T(8,128)S(1)}, f32[2,128,128]{2,1,0:T(8,128)S(1)}, u32[]{:S(2)}, u32[]{:S(2)}) collective-permute-start(f32[2,128,128]{2,1,0:T(8,128)S(1)} %slice_select_fusion.1), channel_id=1, source_target_pairs={{0,4},{4,0},{8,12},{12,8},{16,20},{20,16},{24,28},{28,24},{1,5},{5... | collective-permute-start | bytes 393224 | tf_op jit(solution)/shard_map/ppermute | solution.py:258
  10.2 7.8 %collective-permute-start.1 = (f32[2,128,128]{2,1,0:T(8,128)S(1)}, f32[2,128,128]{2,1,0:T(8,128)S(1)}, u32[]{:S(2)}, u32[]{:S(2)}) collective-permute-start(f32[2,128,128]{2,1,0:T(8,128)S(1)} %fusion), channel_id=1, source_target_pairs={{0,8},{4,12},{1,9},{5,13},{2,10},{6,14},{3,11},{7,15}} | collective-permute-start | bytes 393224 | tf_op jit(solution)/shard_map/ppermute | solution.py:258
  15.5 4.4 %collective-permute-start.6 = (f32[2,128,128]{2,1,0:T(8,128)S(1)}, f32[2,128,128]{2,1,0:T(8,128)S(1)}, u32[]{:S(2)}, u32[]{:S(2)}) collective-permute-start(f32[2,128,128]{2,1,0:T(8,128)S(1)} %fusion.3), channel_id=1, source_target_pairs={{0,8},{4,12},{1,9},{5,13},{2,10},{6,14},{3,11},{7,15}} | collective-permute-start | bytes 393224 | tf_op jit(solution)/shard_map/ppermute | solution.py:258
  18.1 2.7 %collective-permute-start.3 = (f32[2,128,128]{2,1,0:T(8,128)S(1)}, f32[2,128,128]{2,1,0:T(8,128)S(1)}, u32[]{:S(2)}, u32[]{:S(2)}) collective-permute-start(f32[2,128,128]{2,1,0:T(8,128)S(1)} %add.100), channel_id=1, source_target_pairs={{8,16},{12,20},{9,17},{13,21},{10,18},{14,22},{11,19},{15,23}} | collective-permute-start | bytes 393224 | tf_op jit(solution)/shard_map/ppermute | solution.py:258
  19.9 7.9 %copy-start.1 = (bf16[1024,1024]{1,0:T(8,128)(2,1)S(1)}, bf16[1024,1024]{1,0:T(8,128)(2,1)}, u32[]{:S(2)}) copy-start(bf16[1024,1024]{1,0:T(8,128)(2,1)} %og_ref.3) | copy-start | bytes 6291460
  19.9 7.9 %copy-start.2 = (f32[1024]{0:T(1024)S(1)}, f32[1024]{0:T(1024)}, u32[]{:S(2)}) copy-start(f32[1024]{0:T(1024)} %param.8) | copy-start | bytes 12292
  19.9 1.5 %collective-permute-start.7 = (f32[2,128,128]{2,1,0:T(8,128)S(1)}, f32[2,128,128]{2,1,0:T(8,128)S(1)}, u32[]{:S(2)}, u32[]{:S(2)}) collective-permute-start(f32[2,128,128]{2,1,0:T(8,128)S(1)} %add.106), channel_id=1, source_target_pairs={{8,16},{12,20},{9,17},{13,21},{10,18},{14,22},{11,19},{15,23}} | collective-permute-start | bytes 393224 | tf_op jit(solution)/shard_map/ppermute | solution.py:258
  20.8 1.6 %collective-permute-start.4 = (f32[2,128,128]{2,1,0:T(8,128)S(1)}, f32[2,128,128]{2,1,0:T(8,128)S(1)}, u32[]{:S(2)}, u32[]{:S(2)}) collective-permute-start(f32[2,128,128]{2,1,0:T(8,128)S(1)} %add.102), channel_id=1, source_target_pairs={{16,24},{20,28},{17,25},{21,29},{18,26},{22,30},{19,27},{23,31}} | collective-permute-start | bytes 393224 | tf_op jit(solution)/shard_map/ppermute | solution.py:258
  21.5 2.6 %collective-permute-start.8 = (f32[2,128,128]{2,1,0:T(8,128)S(1)}, f32[2,128,128]{2,1,0:T(8,128)S(1)}, u32[]{:S(2)}, u32[]{:S(2)}) collective-permute-start(f32[2,128,128]{2,1,0:T(8,128)S(1)} %add.108), channel_id=1, source_target_pairs={{16,24},{20,28},{17,25},{21,29},{18,26},{22,30},{19,27},{23,31}} | collective-permute-start | bytes 393224 | tf_op jit(solution)/shard_map/ppermute | solution.py:258
  22.4 5.3 %collective-permute-start.5 = (f32[2,128,128]{2,1,0:T(8,128)S(1)}, f32[2,128,128]{2,1,0:T(8,128)S(1)}, u32[]{:S(2)}, u32[]{:S(2)}) collective-permute-start(f32[2,128,128]{2,1,0:T(8,128)S(1)} %get-tuple-element.180), channel_id=1, source_target_pairs={{0,4},{4,0},{8,12},{12,8},{16,20},{20,16},{24,28},{28,24},{1,5},{5... | collective-permute-start | bytes 393224 | tf_op jit(solution)/shard_map/ppermute | solution.py:258
  24.2 5.0 %collective-permute-start.9 = (f32[2,128,128]{2,1,0:T(8,128)S(1)}, f32[2,128,128]{2,1,0:T(8,128)S(1)}, u32[]{:S(2)}, u32[]{:S(2)}) collective-permute-start(f32[2,128,128]{2,1,0:T(8,128)S(1)} %get-tuple-element.178), channel_id=1, source_target_pairs={{0,4},{4,0},{8,12},{12,8},{16,20},{20,16},{24,28},{28,24},{1,5},{5... | collective-permute-start | bytes 393224 | tf_op jit(solution)/shard_map/ppermute | solution.py:258
  30.2 1.2 %collective-permute-start.10 = (f32[2,1024]{1,0:T(2,128)S(1)}, f32[2,1024]{1,0:T(2,128)S(1)}, u32[]{:S(2)}, u32[]{:S(2)}) collective-permute-start(f32[2,1024]{1,0:T(2,128)S(1)} %add.112), channel_id=1, source_target_pairs={{0,1},{1,0},{2,3},{3,2},{4,5},{5,4},{6,7},{7,6},{8,9},{9,8},{10,11... | collective-permute-start | bytes 24584 | tf_op jit(solution)/shard_map/ppermute | solution.py:274
  31.5 3.7 %collective-permute-start.11 = (f32[2,1024]{1,0:T(2,128)S(1)}, f32[2,1024]{1,0:T(2,128)S(1)}, u32[]{:S(2)}, u32[]{:S(2)}) collective-permute-start(f32[2,1024]{1,0:T(2,128)S(1)} %add.113), channel_id=1, source_target_pairs={{0,2},{1,3},{2,0},{3,1},{4,6},{5,7},{6,4},{7,5},{8,10},{9,11},{10,... | collective-permute-start | bytes 24584 | tf_op jit(solution)/shard_map/ppermute | solution.py:274
  36.5 6.3 %collective-permute-start.12 = (f32[2,128,128]{2,1,0:T(8,128)S(1)}, f32[2,128,128]{2,1,0:T(8,128)S(1)}, u32[]{:S(2)}, u32[]{:S(2)}) collective-permute-start(f32[2,128,128]{2,1,0:T(8,128)S(1)} %slice_select_fusion.4), channel_id=1, source_target_pairs={{28,24},{24,28},{20,16},{16,20},{12,8},{8,12},{4,0},{0,4},{29,25},... | collective-permute-start | bytes 393224 | tf_op jit(solution)/shard_map/ppermute | solution.py:258
  38.9 6.6 %collective-permute-start.14 = (f32[2,128,128]{2,1,0:T(8,128)S(1)}, f32[2,128,128]{2,1,0:T(8,128)S(1)}, u32[]{:S(2)}, u32[]{:S(2)}) collective-permute-start(f32[2,128,128]{2,1,0:T(8,128)S(1)} %slice_select_fusion.3), channel_id=1, source_target_pairs={{28,24},{24,28},{20,16},{16,20},{12,8},{8,12},{4,0},{0,4},{29,25},... | collective-permute-start | bytes 393224 | tf_op jit(solution)/shard_map/ppermute | solution.py:258
  42.8 5.5 %collective-permute-start.13 = (f32[2,128,128]{2,1,0:T(8,128)S(1)}, f32[2,128,128]{2,1,0:T(8,128)S(1)}, u32[]{:S(2)}, u32[]{:S(2)}) collective-permute-start(f32[2,128,128]{2,1,0:T(8,128)S(1)} %fusion.1), channel_id=1, source_target_pairs={{28,20},{24,16},{29,21},{25,17},{30,22},{26,18},{31,23},{27,19}} | collective-permute-start | bytes 393224 | tf_op jit(solution)/shard_map/ppermute | solution.py:258
  45.6 5.4 %collective-permute-start.16 = (f32[2,128,128]{2,1,0:T(8,128)S(1)}, f32[2,128,128]{2,1,0:T(8,128)S(1)}, u32[]{:S(2)}, u32[]{:S(2)}) collective-permute-start(f32[2,128,128]{2,1,0:T(8,128)S(1)} %fusion.2), channel_id=1, source_target_pairs={{28,20},{24,16},{29,21},{25,17},{30,22},{26,18},{31,23},{27,19}} | collective-permute-start | bytes 393224 | tf_op jit(solution)/shard_map/ppermute | solution.py:258
  48.3 5.4 %collective-permute-start.15 = (f32[2,128,128]{2,1,0:T(8,128)S(1)}, f32[2,128,128]{2,1,0:T(8,128)S(1)}, u32[]{:S(2)}, u32[]{:S(2)}) collective-permute-start(f32[2,128,128]{2,1,0:T(8,128)S(1)} %add.117), channel_id=1, source_target_pairs={{20,12},{16,8},{21,13},{17,9},{22,14},{18,10},{23,15},{19,11}} | collective-permute-start | bytes 393224 | tf_op jit(solution)/shard_map/ppermute | solution.py:258
  51.0 6.1 %collective-permute-start.18 = (f32[2,128,128]{2,1,0:T(8,128)S(1)}, f32[2,128,128]{2,1,0:T(8,128)S(1)}, u32[]{:S(2)}, u32[]{:S(2)}) collective-permute-start(f32[2,128,128]{2,1,0:T(8,128)S(1)} %add.118), channel_id=1, source_target_pairs={{20,12},{16,8},{21,13},{17,9},{22,14},{18,10},{23,15},{19,11}} | collective-permute-start | bytes 393224 | tf_op jit(solution)/shard_map/ppermute | solution.py:258
  53.8 16.5 %collective-permute-start.17 = (f32[2,128,128]{2,1,0:T(8,128)S(1)}, f32[2,128,128]{2,1,0:T(8,128)S(1)}, u32[]{:S(2)}, u32[]{:S(2)}) collective-permute-start(f32[2,128,128]{2,1,0:T(8,128)S(1)} %add.120), channel_id=1, source_target_pairs={{12,4},{8,0},{13,5},{9,1},{14,6},{10,2},{15,7},{11,3}} | collective-permute-start | bytes 393224 | tf_op jit(solution)/shard_map/ppermute | solution.py:258
  57.1 16.2 %collective-permute-start.19 = (f32[2,128,128]{2,1,0:T(8,128)S(1)}, f32[2,128,128]{2,1,0:T(8,128)S(1)}, u32[]{:S(2)}, u32[]{:S(2)}) collective-permute-start(f32[2,128,128]{2,1,0:T(8,128)S(1)} %add.121), channel_id=1, source_target_pairs={{12,4},{8,0},{13,5},{9,1},{14,6},{10,2},{15,7},{11,3}} | collective-permute-start | bytes 393224 | tf_op jit(solution)/shard_map/ppermute | solution.py:258
  70.3 5.0 %collective-permute-start.21 = (f32[2,128,128]{2,1,0:T(8,128)S(1)}, f32[2,128,128]{2,1,0:T(8,128)S(1)}, u32[]{:S(2)}, u32[]{:S(2)}) collective-permute-start(f32[2,128,128]{2,1,0:T(8,128)S(1)} %get-tuple-element.176), channel_id=1, source_target_pairs={{28,24},{24,28},{20,16},{16,20},{12,8},{8,12},{4,0},{0,4},{29,25},... | collective-permute-start | bytes 393224 | tf_op jit(solution)/shard_map/ppermute | solution.py:258
  73.4 5.0 %collective-permute-start.20 = (f32[2,128,128]{2,1,0:T(8,128)S(1)}, f32[2,128,128]{2,1,0:T(8,128)S(1)}, u32[]{:S(2)}, u32[]{:S(2)}) collective-permute-start(f32[2,128,128]{2,1,0:T(8,128)S(1)} %get-tuple-element.174), channel_id=1, source_target_pairs={{28,24},{24,28},{20,16},{16,20},{12,8},{8,12},{4,0},{0,4},{29,25},... | collective-permute-start | bytes 393224 | tf_op jit(solution)/shard_map/ppermute | solution.py:258
  (1 other events, 1.6 us)

commit v6 on v5

v6 whole, which is shorter than its diff:
```python
import functools

import jax
import jax.numpy as jnp
from jax import lax
from jax.experimental import pallas as pl
from jax.experimental.pallas import tpu as pltpu
from jax.sharding import PartitionSpec as P

HEAD_DIM = 128
BLOCK = 128
WIDTH = 4096
epsilon = 1e-05

F32 = jnp.float32
BF16 = jnp.bfloat16
VMEM = pl.BlockSpec(memory_space=pltpu.VMEM)
HBM = pl.BlockSpec(memory_space=pltpu.HBM)


def dot(a, b, ca, cb):
    return lax.dot_general(a, b, (((ca,), (cb,)), ((), ())), preferred_element_type=F32)


def causal_mask():
    row = lax.broadcasted_iota(jnp.int32, (BLOCK, BLOCK), 0)
    col = lax.broadcasted_iota(jnp.int32, (BLOCK, BLOCK), 1)
    return col <= row


def rows_of(n):
    return slice(n * BLOCK, (n + 1) * BLOCK)


def cols_of(h):
    return slice(h * HEAD_DIM, (h + 1) * HEAD_DIM)


def cols_at(h):
    return pl.ds(pl.multiple_of(h * HEAD_DIM, HEAD_DIM), HEAD_DIM)


def load_kernel(first, heads, k_hbm, v_hbm, k_ref, v_ref, t_ref, sems):
    copies = []
    for h in range(heads):
        for i, (src, dst) in enumerate(((k_hbm, k_ref), (v_hbm, v_ref))):
            copies.append(pltpu.make_async_copy(src.at[:, cols_of(first + h)], dst.at[:, cols_of(h)], sems.at[i, h]))
            copies[-1].start()
    for h in range(heads):
        copies[2 * h].wait()
        copies[2 * h + 1].wait()
        t_ref[h] = dot(k_ref[:, cols_of(h)], v_ref[:, cols_of(h)], 0, 0)


def local_kernel(first, inner, heads, blocks, q_ref, k_ref, v_ref, w_ref, a_ref, low):
    causal = causal_mask()

    def head(h, carry):
        c, ci, cq = cols_at(h), cols_at(h + inner), cols_at(h + first)
        for n in range(0, blocks, 2):
            if n + 1 < blocks:
                both = slice(n * BLOCK, (n + 2) * BLOCK)
                s = dot(q_ref[both, cq], k_ref[both, ci], 1, 1)
                w_ref[rows_of(n), c] = jnp.where(causal, s[:BLOCK, :BLOCK], 0.0).astype(BF16)
                w_ref[rows_of(n + 1), c] = jnp.where(causal, s[BLOCK:, BLOCK:], 0.0).astype(BF16)
            else:
                s = dot(q_ref[rows_of(n), cq], k_ref[rows_of(n), ci], 1, 1)
                w_ref[rows_of(n), c] = jnp.where(causal, s, 0.0).astype(BF16)
        prefix = None
        for n in range(blocks - 1):
            s = dot(k_ref[rows_of(n), ci], v_ref[rows_of(n), ci], 0, 0)
            prefix = s if prefix is None else prefix + s
            low[rows_of(n), :] = prefix.astype(BF16)
        a_ref[rows_of(0), c] = dot(w_ref[rows_of(0), c], v_ref[rows_of(0), ci], 1, 0)
        for n in range(1, blocks):
            left = jnp.concatenate([w_ref[rows_of(n), c], q_ref[rows_of(n), cq]], axis=1)
            right = jnp.concatenate([v_ref[rows_of(n), ci], low[rows_of(n - 1), :]], axis=0)
            a_ref[rows_of(n), c] = dot(left, right, 1, 0)
        return carry

    lax.fori_loop(0, heads, head, 0, unroll=min(2, heads))


def stats_kernel(first, parts, size, blocks, *refs):
    a_ins, (q_ref, p_ref, og_ref, gain_ref, a_ref, s_ref) = refs[:parts], refs[parts:]
    low = [p_ref[h].astype(BF16) for h in range(parts * size)]
    for n in range(blocks):
        r = rows_of(n)
        squares = dots = None
        for h in range(parts * size):
            c, cq = cols_of(h), cols_of(first + h)
            att = a_ins[h // size][r, cols_of(h % size)] + dot(q_ref[r, cq], low[h], 1, 0)
            a_ref[r, c] = att
            scaled = gain_ref[:, cq] * og_ref[r, cq].astype(F32)
            squares = att * att if squares is None else squares + att * att
            dots = scaled * att if dots is None else dots + scaled * att
        s_ref[0:1, r] = jnp.sum(squares.T, axis=0, keepdims=True)
        s_ref[1:2, r] = jnp.sum(dots.T, axis=0, keepdims=True)


def grad_kernel(first, heads, blocks, a_ref, q_ref, og_ref, gain_ref, *rest):
    if len(rest) == 5:
        s_ref, g_ref, t_ref, inv_ref, coef_ref = rest
        inverse = lax.rsqrt(s_ref[0:1, :] / WIDTH + epsilon)
        factor = inverse * inverse * inverse * s_ref[1:2, :] / WIDTH
        for n in range(blocks):
            inv_ref[rows_of(n), :] = jnp.broadcast_to(inverse[:, rows_of(n)], (BLOCK, BLOCK)).T
            coef_ref[rows_of(n), :] = jnp.broadcast_to(factor[:, rows_of(n)], (BLOCK, BLOCK)).T
    else:
        inv_ref, coef_ref, g_ref, t_ref = rest
    for h in range(heads):
        c, cq = cols_of(h), cols_of(first + h)
        scaled = gain_ref[:, cq] * og_ref[:, cq].astype(F32)
        grad = (inv_ref[...] * scaled - coef_ref[...] * a_ref[:, c]).astype(BF16)
        g_ref[:, c] = grad
        t_ref[h] = dot(q_ref[:, cq], grad, 0, 0)


def flush(pairs, sems):
    copies = [pltpu.make_async_copy(src, dst, sems.at[i]) for i, (src, dst) in enumerate(pairs)]
    for copy in copies:
        copy.start()
    return copies


def back_kernel(h, inner, winner, blocks, before, q_ref, k_ref, v_ref, w_ref, g_ref, p_ref, a_ref, gain_ref, inv_ref, *rest):
    copies = []
    if before is not None:
        old_m, old_q = rest[:2]
        m_ref, qg_ref, kl_ref, vl_ref, m_hbm, q_hbm, bw, plow, slow, sems = rest[-10:]
        copies = flush([(old_m, m_hbm.at[:, cols_of(before)]), (old_q, q_hbm.at[:, cols_of(before)])], sems)
    else:
        m_ref, qg_ref, kl_ref, vl_ref, bw, plow, slow = rest
    causal = causal_mask()
    ci, cw, cq = cols_of(inner), cols_of(winner), cols_of(h)
    m_ref[...] = (gain_ref[:, cq] * a_ref[:, ci] * inv_ref[...]).astype(BF16)
    for n in range(0, blocks, 2):
        r = slice(n * BLOCK, min(n + 2, blocks) * BLOCK)
        s = dot(g_ref[r, ci], v_ref[r, ci], 1, 1)
        for m in range(n, min(n + 2, blocks)):
            inside = rows_of(m - n)
            bw[rows_of(m), :] = jnp.where(causal, s[inside, inside], 0.0).astype(BF16)
    prefix = p_ref[inner].T
    plow[rows_of(0), :] = prefix.astype(BF16)
    for n in range(blocks - 1):
        prefix = prefix + dot(v_ref[rows_of(n), ci], k_ref[rows_of(n), ci], 0, 0)
        plow[rows_of(n + 1), :] = prefix.astype(BF16)
    suffix = None
    for n in reversed(range(1, blocks)):
        s = dot(g_ref[rows_of(n), ci], q_ref[rows_of(n), cq], 0, 0)
        suffix = s if suffix is None else suffix + s
        slow[rows_of(n - 1), :] = suffix.astype(BF16)
    for n in range(blocks):
        r = rows_of(n)
        q, k, v, g = q_ref[r, cq], k_ref[r, ci], v_ref[r, ci], g_ref[r, ci]
        left = jnp.concatenate([bw[r, :], g], axis=1)
        right = jnp.concatenate([k, plow[r, :]], axis=0)
        qg_ref[r, :] = dot(left, right, 1, 0).astype(BF16)
        vp = dot(w_ref[r, cw], g, 0, 0)
        if n + 1 < blocks:
            left = jnp.concatenate([bw[r, :].T, v], axis=1)
            right = jnp.concatenate([q, slow[r, :]], axis=0)
            kp = dot(left, right, 1, 0)
            vp = vp + dot(k, slow[r, :], 1, 1)
        else:
            kp = dot(bw[r, :], q, 0, 0)
        kl_ref[r, :] = kp
        vl_ref[r, :] = vp
    for copy in copies:
        copy.wait()


def last_kernel(heads, before, k_ref, v_ref, s_ref, *rest):
    kls, vls, rest = rest[:heads], rest[heads : 2 * heads], rest[2 * heads :]
    old_a, old_b = rest[:2]
    if before is not None:
        kg, vg, a_hbm, b_hbm, sems = rest[-5:]
        copies = flush([(old_a, a_hbm.at[:, cols_of(before)]), (old_b, b_hbm.at[:, cols_of(before)])], sems.at[0])
    else:
        a_hbm, b_hbm, kg, vg, sems = rest[-5:]
        there = slice(0, heads * HEAD_DIM)
        copies = flush([(old_a, a_hbm.at[:, there]), (old_b, b_hbm.at[:, there])], sems.at[0])
    for h in range(heads):
        c = cols_of(h)
        low = s_ref[h].astype(BF16)
        kg[:, c] = (kls[h][...] + dot(v_ref[:, c], low, 1, 1)).astype(BF16)
        vg[:, c] = (vls[h][...] + dot(k_ref[:, c], low, 1, 0)).astype(BF16)
        if before is None:
            to = cols_of(heads + h)
            copies += flush([(kg.at[:, c], a_hbm.at[:, to]), (vg.at[:, c], b_hbm.at[:, to])], sems.at[1 + h])
    for copy in copies:
        copy.wait()


def call(kernel, ins, outs, in_specs=None, out_specs=None, scratch=(), aliases=None, flops=0, vmem=6):
    nbytes = sum(a.size * a.dtype.itemsize for a in ins)
    return pl.pallas_call(
        kernel,
        in_specs=in_specs or [VMEM] * len(ins),
        out_specs=tuple(out_specs or [VMEM] * len(outs)),
        out_shape=tuple(jax.ShapeDtypeStruct(shape, dtype) for shape, dtype in outs),
        scratch_shapes=list(scratch),
        input_output_aliases=aliases or {},
        compiler_params=pltpu.CompilerParams(vmem_limit_bytes=vmem << 20),
        cost_estimate=pl.CostEstimate(flops=flops, bytes_accessed=nbytes, transcendentals=0),
    )(*ins)


def scan_stages(states, size, low, reverse):
    place = (lambda i: size - 1 - i) if reverse else (lambda i: i)
    perm = lambda pairs: [(place(i), place(j)) for i, j in pairs]
    outer = size // 2
    swap = [(i, i ^ 1) for i in range(size)]
    at_first = (lambda a, b: jnp.where(low, b, a)) if reverse else (lambda a, b: jnp.where(low, a, b))
    half = states.shape[0] // 2
    mine = jnp.where(low, states[:half], states[half:])
    other = jnp.where(low, states[half:], states[:half])
    got = yield other, perm(swap)
    pair = mine + got
    total = None
    if outer <= 4:
        running = pair
        for hop in range(outer - 1):
            r = yield running, perm([(2 * hop, 2 * hop + 2), (2 * hop + 1, 2 * hop + 3)])
            total = r if total is None else total + r
            running = r + pair
    else:
        total = yield pair, perm([(i, i + 2) for i in range(size - 2)])
        step = 1
        while step < outer - 1:
            r = yield total, perm([(i, i + 2 * step) for i in range(size - 2 * step)])
            total = total + r
            step *= 2
    answer = yield at_first(total + mine, total), perm(swap)
    kept = at_first(total, total + got)
    return jnp.concatenate([jnp.where(low, kept, answer), jnp.where(low, answer, kept)], axis=0)


def drive(makers, pieces, finish):
    live, behind, event = [], (), 0
    waiting = list(makers)
    while waiting or live:
        if waiting:
            scan = waiting.pop(0)()
            name, (operand, pairs) = len(makers) - len(waiting) - 1, next(scan)
        else:
            name, scan, result = live.pop(0)
            try:
                operand, pairs = scan.send(after(behind, result)[0])
            except StopIteration as stop:
                behind = finish(name, stop.value)
                continue
        live.append((name, scan, lax.ppermute(operand, "seq", pairs)))
        behind = pieces.pop(event)((operand,)) if event in pieces else ()
        event += 1
    for piece in pieces.values():
        piece(())


def after(tied, *arrays):
    return lax.optimization_barrier((*arrays, *tied))[: len(arrays)] if tied else arrays


def head_sum(a, size):
    if size & (size - 1):
        return lax.psum(a, "head")
    step = 1
    while step < size:
        a = a + lax.ppermute(a, "head", [(i, i ^ step) for i in range(size)])
        step *= 2
    return a


def body(seq_size, head_size, queries, keys, values, gain, out_grad):
    rows, width = queries.shape
    blocks, heads = rows // BLOCK, width // HEAD_DIM
    half = heads // 2
    part = half * HEAD_DIM
    low = lax.axis_index("seq") % 2 == 0
    gain = gain.reshape(1, width)
    unit = 2 * rows * HEAD_DIM * HEAD_DIM
    whole = ((rows, width), BF16)
    state = ((half, HEAD_DIM, HEAD_DIM), F32)

    ks, vs, states = [], [], []

    def piece_state(i, tied):
        k, v, t = call(
            functools.partial(load_kernel, i * half, half),
            after(tied, keys, values),
            [((rows, part), BF16), ((rows, part), BF16), state],
            in_specs=[HBM, HBM],
            scratch=[pltpu.SemaphoreType.DMA((2, half))],
            flops=unit * half,
            vmem=50,
        )
        ks.append(k)
        vs.append(v)
        states.append(t)
        return (t,)

    piece_state(0, ())

    size = min(2, half)
    weights, attended = {}, {}

    def piece_local(first, tied):
        (qt,) = after(tied, queries)
        weights[first], attended[first] = call(
            functools.partial(local_kernel, first, first % half, size, blocks),
            [qt, ks[first // half], vs[first // half]],
            [((rows, size * HEAD_DIM), BF16), ((rows, size * HEAD_DIM), F32)],
            scratch=[pltpu.VMEM((rows, HEAD_DIM), BF16)],
            flops=4 * unit * size,
        )
        return weights[first], attended[first]

    prefixes, atts, sums = [], [], []

    def make_stats(i, prefix):
        parts = [attended[first] for first in range(i * half, (i + 1) * half, size)]
        att, s = call(
            functools.partial(stats_kernel, i * half, len(parts), size, blocks),
            [*parts, queries, prefix, out_grad, gain],
            [((rows, part), F32), ((2, rows), F32)],
            flops=unit * half,
        )
        prefixes.append(prefix)
        atts.append(att)
        sums.append(s)
        return att, s

    drive(
        [lambda i=i: scan_stages(states[i], seq_size, low, False) for i in range(2)],
        {0: functools.partial(piece_state, 1), **{i + 1: functools.partial(piece_local, i * size) for i in range(heads // size)}},
        make_stats,
    )
    total = head_sum(sums[0] + sums[1], head_size)

    grads, backs, factors = [], [], []

    def piece_grad(i, tied):
        (qt,) = after(tied, queries)
        grad, back, *new = call(
            functools.partial(grad_kernel, i * half, half, blocks),
            [atts[i], qt, out_grad, gain, *(factors or [total])],
            [((rows, part), BF16), state] + ([] if factors else [((rows, BLOCK), F32)] * 2),
            flops=unit * half,
        )
        factors.extend(new)
        grads.append(grad)
        backs.append(back)
        return (back,)

    column = (rows, HEAD_DIM)
    inner, made, fresh = {}, [], []

    def piece_back(h, tied):
        i = h // half
        (qt,) = after(tied, queries)
        ins = [qt, ks[i], vs[i], weights[h // size * size], grads[i], prefixes[i], atts[i], gain, factors[0], *fresh]
        specs, outs, aliases = [VMEM] * len(ins), [(column, BF16)] * 2 + [(column, F32)] * 2, {}
        out_specs, scratch = [VMEM] * 4, [pltpu.VMEM(column, BF16)] * 3
        if fresh:
            aliases = {len(ins) + n: 4 + n for n in range(len(made))}
            ins, specs = ins + made, specs + [HBM] * len(made)
            outs, out_specs = outs + [whole] * 2, out_specs + [HBM] * 2
            scratch.append(pltpu.SemaphoreType.DMA((2,)))
        m, q, *others = call(
            functools.partial(back_kernel, h, h % half, h % size, blocks, h - 1 if fresh else None),
            ins,
            outs,
            in_specs=specs,
            out_specs=out_specs,
            scratch=scratch,
            aliases=aliases,
            flops=9 * unit,
        )
        inner[h], made[:] = others[:2], others[2:]
        fresh[:] = [m, q]
        return tuple(inner[h])

    results = []

    def make_last(i, suffix):
        mine = [inner[h] for h in range(i * half, (i + 1) * half)]
        ins = [ks[i], vs[i], suffix] + [kl for kl, _ in mine] + [vl for _, vl in mine] + (results if i else fresh)
        specs, aliases = [VMEM] * len(ins), {}
        here = [((rows, part), BF16)] * 2
        if i:
            outs, out_specs, scratch = [whole] * 2, [HBM] * 2, [pltpu.VMEM(*pair) for pair in here]
        else:
            aliases = {len(ins) + n: 2 + n for n in range(len(made))}
            ins, specs = ins + made, specs + [HBM] * len(made)
            outs, out_specs, scratch = here + [whole] * 2, [VMEM] * 2 + [HBM] * 2, []
        results.clear()
        got = call(
            functools.partial(last_kernel, half, None if i else heads - 1),
            ins,
            outs,
            in_specs=specs,
            out_specs=out_specs,
            scratch=scratch + [pltpu.SemaphoreType.DMA((1 + half, 2))],
            aliases=aliases,
            flops=2 * unit * half,
        )
        results.extend(got[:2])
        if i == 0:
            made[:] = got[2:]
        return tuple(got)

    piece_grad(0, ())
    drive(
        [lambda i=i: scan_stages(backs[i], seq_size, low, True) for i in range(2)],
        {
            0: functools.partial(piece_grad, 1),
            **{i + 1: functools.partial(piece_back, i) for i in range(heads)},
        },
        make_last,
    )
    return (*made, *results)


def solution(mesh):
    placed = (P("seq", "head"), P("seq", "head"), P("seq", "head"), P("head"), P("seq", "head"))
    return jax.shard_map(
        functools.partial(body, mesh.shape["seq"], mesh.shape["head"]),
        mesh=mesh,
        in_specs=placed,
        out_specs=(P("seq", "head"),) * 4,
        check_vma=False,
    )
```

time: 80.8 us -> 79.3 us (0.981)
  Pallas kernels: 31.6 us -> 29.7 us
  starting transfers between devices: 24.7 us -> 26.5 us
  local copies, waits for them, and re-layouts: 0.87 us -> 0.02 us
    pallas_call x21 -> x20, Pallas kernels: 31.6 us -> 29.7 us  [call(): pl.pallas_call(kernel, in_specs=in_specs or [VMEM] * len(ins), out_specs=...]
    ppermute x20, starting transfers between devices: 23.1 us -> 24.9 us  [drive(): live.append((name, scan, lax.ppermute(operand, 'seq', pairs)))]
    unnamed x6, local copies, waits for them, and re-layouts: 0.87 us -> 0.02 us
  transfers between devices with their start and end apart: 22 -> 22, of which waited for: 11 -> 8; matrix products, arithmetic and copies ran while one was open for 1% -> 1% of each run, Pallas kernels for 31% -> 29%
where the time goes in v6:
time: 79.3 us; the launch traced here: 79 us
  Pallas kernels  29.7 us (37%)
  starting transfers between devices  26.5 us (33%)
  waiting for transfers between devices  20.7 us (26%)
  between operations  1.33 us (2%)
    pallas_call x20, Pallas kernels, call(): pl.pallas_call(kernel, in_specs=in_specs or [VMEM] * len(ins), out_specs=...  29.7 us
    ppermute x20, starting transfers between devices, drive(): live.append((name, scan, lax.ppermute(operand, 'seq', pairs)))  24.9 us
    ppermute x20, waiting for transfers between devices, drive(): live.append((name, scan, lax.ppermute(operand, 'seq', pairs)))  17.4 us
    ppermute x2, waiting for transfers between devices, head_sum(): a = a + lax.ppermute(a, 'head', [(i, i ^ step) for i in range(size)])  3.29 us
    ppermute x2, starting transfers between devices, head_sum(): a = a + lax.ppermute(a, 'head', [(i, i ^ step) for i in range(size)])  1.59 us
  transfers between devices with their start and end apart: 22, of which 8 were waited for; matrix products, arithmetic and copies ran while one was open for 1% of the time, Pallas kernels for 29%

profile of v6, /device:TPU:0, one launch (start us, length us, event | category | flops | bytes accessed | tf_op | source)
XLA Modules:
  0.0 79.0 jit_solution(1813824189679983903)
XLA Ops:
  0.6 2.2 %shard_map.84 = (bf16[1024,512]{1,0:T(8,128)(2,1)S(1)}, bf16[1024,512]{1,0:T(8,128)(2,1)S(1)}, f32[4,128,128]{2,1,0:T(8,128)S(1)}) custom-call(bf16[1024,1024]{1,0:T(8,128)(2,1)} %k_hbm.2, bf16[1024,1024]{1,0:T(8,128)(2,1)} %v_hbm.2), custom_call_target="tpu_custom_call" | custom-call | flops 134217728 | bytes 4194304 | tf_op jit(solution)/shard_map/pallas_call | solution.py:197
  2.9 3.0 %collective-permute-start = (f32[2,128,128]{2,1,0:T(8,128)S(1)}, f32[2,128,128]{2,1,0:T(8,128)S(1)}, u32[]{:S(2)}, u32[]{:S(2)}) collective-permute-start(f32[2,128,128]{2,1,0:T(8,128)S(1)} %slice_select_fusion.7), channel_id=1, source_target_pairs={{0,4},{4,0},{8,12},{12,8},{16,20},{20,16},{24,28},{28,24},{1,5},{5... | collective-permute-start | bytes 393224 | tf_op jit(solution)/shard_map/ppermute | solution.py:253
  5.9 2.2 %shard_map.85 = (bf16[1024,512]{1,0:T(8,128)(2,1)S(1)}, bf16[1024,512]{1,0:T(8,128)(2,1)S(1)}, f32[4,128,128]{2,1,0:T(8,128)S(1)}) custom-call(bf16[1024,1024]{1,0:T(8,128)(2,1)} %k_hbm.2, bf16[1024,1024]{1,0:T(8,128)(2,1)} %v_hbm.2), custom_call_target="tpu_custom_call" | custom-call | flops 134217728 | bytes 4194304 | tf_op jit(solution)/shard_map/pallas_call | solution.py:197
  9.4 3.9 %collective-permute-start.1 = (f32[2,128,128]{2,1,0:T(8,128)S(1)}, f32[2,128,128]{2,1,0:T(8,128)S(1)}, u32[]{:S(2)}, u32[]{:S(2)}) collective-permute-start(f32[2,128,128]{2,1,0:T(8,128)S(1)} %fusion), channel_id=1, source_target_pairs={{0,8},{4,12},{1,9},{5,13},{2,10},{6,14},{3,11},{7,15}} | collective-permute-start | bytes 393224 | tf_op jit(solution)/shard_map/ppermute | solution.py:253
  14.4 2.3 %collective-permute-start.6 = (f32[2,128,128]{2,1,0:T(8,128)S(1)}, f32[2,128,128]{2,1,0:T(8,128)S(1)}, u32[]{:S(2)}, u32[]{:S(2)}) collective-permute-start(f32[2,128,128]{2,1,0:T(8,128)S(1)} %fusion.1), channel_id=1, source_target_pairs={{0,8},{4,12},{1,9},{5,13},{2,10},{6,14},{3,11},{7,15}} | collective-permute-start | bytes 393224 | tf_op jit(solution)/shard_map/ppermute | solution.py:253
  22.7 1.3 %collective-permute-start.9 = (f32[2,128,128]{2,1,0:T(8,128)S(1)}, f32[2,128,128]{2,1,0:T(8,128)S(1)}, u32[]{:S(2)}, u32[]{:S(2)}) collective-permute-start(f32[2,128,128]{2,1,0:T(8,128)S(1)} %get-tuple-element.218), channel_id=1, source_target_pairs={{0,4},{4,0},{8,12},{12,8},{16,20},{20,16},{24,28},{28,24},{1,5},{5... | collective-permute-start | bytes 393224 | tf_op jit(solution)/shard_map/ppermute | solution.py:253
  24.0 2.8 %collective-permute-done.5 = f32[2,128,128]{2,1,0:T(8,128)S(1)} collective-permute-done((f32[2,128,128]{2,1,0:T(8,128)S(1)}, f32[2,128,128]{2,1,0:T(8,128)S(1)}, u32[]{:S(2)}, u32[]{:S(2)}) %collective-permute-start.5) | collective-permute-done | bytes 131104 | tf_op jit(solution)/shard_map/ppermute | solution.py:253
  30.5 1.5 %collective-permute-start.11 = (f32[2,1024]{1,0:T(2,128)S(1)}, f32[2,1024]{1,0:T(2,128)S(1)}, u32[]{:S(2)}, u32[]{:S(2)}) collective-permute-start(f32[2,1024]{1,0:T(2,128)S(1)} %add.113), channel_id=1, source_target_pairs={{0,2},{1,3},{2,0},{3,1},{4,6},{5,7},{6,4},{7,5},{8,10},{9,11},{10,... | collective-permute-start | bytes 24584 | tf_op jit(solution)/shard_map/ppermute | solution.py:269
  32.0 2.1 %collective-permute-done.11 = f32[2,1024]{1,0:T(2,128)S(1)} collective-permute-done((f32[2,1024]{1,0:T(2,128)S(1)}, f32[2,1024]{1,0:T(2,128)S(1)}, u32[]{:S(2)}, u32[]{:S(2)}) %collective-permute-start.11) | collective-permute-done | bytes 8224 | tf_op jit(solution)/shard_map/ppermute | solution.py:269
  35.4 1.4 %collective-permute-start.12 = (f32[2,128,128]{2,1,0:T(8,128)S(1)}, f32[2,128,128]{2,1,0:T(8,128)S(1)}, u32[]{:S(2)}, u32[]{:S(2)}) collective-permute-start(f32[2,128,128]{2,1,0:T(8,128)S(1)} %slice_select_fusion.2), channel_id=1, source_target_pairs={{28,24},{24,28},{20,16},{16,20},{12,8},{8,12},{4,0},{0,4},{29,25},... | collective-permute-start | bytes 393224 | tf_op jit(solution)/shard_map/ppermute | solution.py:253
  39.8 1.9 %collective-permute-done.12 = f32[2,128,128]{2,1,0:T(8,128)S(1)} collective-permute-done((f32[2,128,128]{2,1,0:T(8,128)S(1)}, f32[2,128,128]{2,1,0:T(8,128)S(1)}, u32[]{:S(2)}, u32[]{:S(2)}) %collective-permute-start.12) | collective-permute-done | bytes 131104 | tf_op jit(solution)/shard_map/ppermute | solution.py:253
  42.6 1.8 %shard_map.95 = (bf16[1024,128]{1,0:T(8,128)(2,1)S(1)}, bf16[1024,128]{1,0:T(8,128)(2,1)S(1)}, f32[1024,128]{1,0:T(8,128)S(1)}, f32[1024,128]{1,0:T(8,128)S(1)},...) custom-call(bf16[1024,1024]{1,0:T(8,128)(2,1)S(1)} %copy-done, bf16[1024,512]{1,0:T(8,128)(2,1)S(1)} %get-tuple-element.109.k_ref, ...), custom_call_target="tpu_custom_call" | custom-call | flops 301989888 | bytes 9179136 | tf_op jit(solution)/shard_map/pallas_call | solution.py:197
  45.0 1.7 %shard_map.96 = (bf16[1024,128]{1,0:T(8,128)(2,1)S(1)}, bf16[1024,128]{1,0:T(8,128)(2,1)S(1)}, f32[1024,128]{1,0:T(8,128)S(1)}, f32[1024,128]{1,0:T(8,128)S(1)},...) custom-call(bf16[1024,1024]{1,0:T(8,128)(2,1)S(1)} %copy-done, ...), custom_call_target="tpu_custom_call", output_to_operand_aliasing={{4}: (11, {}), {5}: (12, {})} | custom-call | flops 301989888 | bytes 13373440 | tf_op jit(solution)/shard_map/pallas_call | solution.py:197
  47.5 1.7 %shard_map.97 = (bf16[1024,128]{1,0:T(8,128)(2,1)S(1)}, bf16[1024,128]{1,0:T(8,128)(2,1)S(1)}, f32[1024,128]{1,0:T(8,128)S(1)}, f32[1024,128]{1,0:T(8,128)S(1)},...) custom-call(bf16[1024,1024]{1,0:T(8,128)(2,1)S(1)} %copy-done, ...), custom_call_target="tpu_custom_call", output_to_operand_aliasing={{4}: (11, {}), {5}: (12, {})} | custom-call | flops 301989888 | bytes 13373440 | tf_op jit(solution)/shard_map/pallas_call | solution.py:197
  50.0 1.8 %shard_map.98 = (bf16[1024,128]{1,0:T(8,128)(2,1)S(1)}, bf16[1024,128]{1,0:T(8,128)(2,1)S(1)}, f32[1024,128]{1,0:T(8,128)S(1)}, f32[1024,128]{1,0:T(8,128)S(1)},...) custom-call(bf16[1024,1024]{1,0:T(8,128)(2,1)S(1)} %copy-done, ...), custom_call_target="tpu_custom_call", output_to_operand_aliasing={{4}: (11, {}), {5}: (12, {})} | custom-call | flops 301989888 | bytes 13373440 | tf_op jit(solution)/shard_map/pallas_call | solution.py:197
  53.1 1.8 %shard_map.99 = (bf16[1024,128]{1,0:T(8,128)(2,1)S(1)}, bf16[1024,128]{1,0:T(8,128)(2,1)S(1)}, f32[1024,128]{1,0:T(8,128)S(1)}, f32[1024,128]{1,0:T(8,128)S(1)},...) custom-call(bf16[1024,1024]{1,0:T(8,128)(2,1)S(1)} %copy-done, ...), custom_call_target="tpu_custom_call", output_to_operand_aliasing={{4}: (11, {}), {5}: (12, {})} | custom-call | flops 301989888 | bytes 13373440 | tf_op jit(solution)/shard_map/pallas_call | solution.py:197
  56.2 1.7 %shard_map.100 = (bf16[1024,128]{1,0:T(8,128)(2,1)S(1)}, bf16[1024,128]{1,0:T(8,128)(2,1)S(1)}, f32[1024,128]{1,0:T(8,128)S(1)}, f32[1024,128]{1,0:T(8,128)S(1)}...) custom-call(bf16[1024,1024]{1,0:T(8,128)(2,1)S(1)} %copy-done, ...), custom_call_target="tpu_custom_call", output_to_operand_aliasing={{4}: (11, {}), {5}: (12, {})} | custom-call | flops 301989888 | bytes 13373440 | tf_op jit(solution)/shard_map/pallas_call | solution.py:197
  57.9 10.2 %collective-permute-done.17 = f32[2,128,128]{2,1,0:T(8,128)S(1)} collective-permute-done((f32[2,128,128]{2,1,0:T(8,128)S(1)}, f32[2,128,128]{2,1,0:T(8,128)S(1)}, u32[]{:S(2)}, u32[]{:S(2)}) %collective-permute-start.17) | collective-permute-done | bytes 131104 | tf_op jit(solution)/shard_map/ppermute | solution.py:253
  68.2 1.7 %collective-permute-start.19 = (f32[2,128,128]{2,1,0:T(8,128)S(1)}, f32[2,128,128]{2,1,0:T(8,128)S(1)}, u32[]{:S(2)}, u32[]{:S(2)}) collective-permute-start(f32[2,128,128]{2,1,0:T(8,128)S(1)} %get-tuple-element.216), channel_id=1, source_target_pairs={{28,24},{24,28},{20,16},{16,20},{12,8},{8,12},{4,0},{0,4},{29,25},... | collective-permute-start | bytes 393224 | tf_op jit(solution)/shard_map/ppermute | solution.py:253
  69.8 1.7 %shard_map.101 = (bf16[1024,128]{1,0:T(8,128)(2,1)S(1)}, bf16[1024,128]{1,0:T(8,128)(2,1)S(1)}, f32[1024,128]{1,0:T(8,128)S(1)}, f32[1024,128]{1,0:T(8,128)S(1)}...) custom-call(bf16[1024,1024]{1,0:T(8,128)(2,1)S(1)} %copy-done, ...), custom_call_target="tpu_custom_call", output_to_operand_aliasing={{4}: (11, {}), {5}: (12, {})} | custom-call | flops 301989888 | bytes 13373440 | tf_op jit(solution)/shard_map/pallas_call | solution.py:197
  71.6 1.3 %collective-permute-start.21 = (f32[2,128,128]{2,1,0:T(8,128)S(1)}, f32[2,128,128]{2,1,0:T(8,128)S(1)}, u32[]{:S(2)}, u32[]{:S(2)}) collective-permute-start(f32[2,128,128]{2,1,0:T(8,128)S(1)} %get-tuple-element.214), channel_id=1, source_target_pairs={{28,24},{24,28},{20,16},{16,20},{12,8},{8,12},{4,0},{0,4},{29,25},... | collective-permute-start | bytes 393224 | tf_op jit(solution)/shard_map/ppermute | solution.py:253
  73.2 1.6 %shard_map.102 = (bf16[1024,512]{1,0:T(8,128)(2,1)S(1)}, bf16[1024,512]{1,0:T(8,128)(2,1)S(1)}, bf16[1024,1024]{1,0:T(8,128)(2,1)}, bf16[1024,1024]{1,0:T(8,128)(2,1)}) custom-call(bf16[1024,512]{1,0:T(8,128)(2,1)S(1)} %get-tuple-element.109.k_ref, bf16[1024,512]{1,0:T(8,128)(2,1)S(1)} %get-tuple-element.110.v_ref, ...), custom_call_target="tpu_custom_call", output_to_operand_aliasing={{2}: (13, {}), {3}: (14, {})} | custom-call | flops 268435456 | bytes 11272192 | tf_op jit(solution)/shard_map/pallas_call | solution.py:197
  74.8 1.9 %collective-permute-done.21 = f32[2,128,128]{2,1,0:T(8,128)S(1)} collective-permute-done((f32[2,128,128]{2,1,0:T(8,128)S(1)}, f32[2,128,128]{2,1,0:T(8,128)S(1)}, u32[]{:S(2)}, u32[]{:S(2)}) %collective-permute-start.21) | collective-permute-done | bytes 131104 | tf_op jit(solution)/shard_map/ppermute | solution.py:253
  76.7 2.1 %shard_map.103 = (bf16[1024,1024]{1,0:T(8,128)(2,1)}, bf16[1024,1024]{1,0:T(8,128)(2,1)}) custom-call(bf16[1024,512]{1,0:T(8,128)(2,1)S(1)} %get-tuple-element.124.k_ref, bf16[1024,512]{1,0:T(8,128)(2,1)S(1)} %get-tuple-element.125.v_ref, f32[4,128,128]{2,1,0:T(8,128)S(1)} %pad_maximum_fusion.3.s_ref, f32[1024,128]{1,0:T(8,128)S(1)} %get-tuple-element.176.rest_0_, ...), custom_call_target="tpu_custom_call" | custom-call | flops 268435456 | bytes 8650752 | tf_op jit(solution)/shard_map/pallas_call | solution.py:197
  (77 shorter events, 22.1 us)
Async XLA Ops:
  2.9 6.5 %collective-permute-start = (f32[2,128,128]{2,1,0:T(8,128)S(1)}, f32[2,128,128]{2,1,0:T(8,128)S(1)}, u32[]{:S(2)}, u32[]{:S(2)}) collective-permute-start(f32[2,128,128]{2,1,0:T(8,128)S(1)} %slice_select_fusion.7), channel_id=1, source_target_pairs={{0,4},{4,0},{8,12},{12,8},{16,20},{20,16},{24,28},{28,24},{1,5},{5... | collective-permute-start | bytes 393224 | tf_op jit(solution)/shard_map/ppermute | solution.py:253
  8.1 6.2 %collective-permute-start.2 = (f32[2,128,128]{2,1,0:T(8,128)S(1)}, f32[2,128,128]{2,1,0:T(8,128)S(1)}, u32[]{:S(2)}, u32[]{:S(2)}) collective-permute-start(f32[2,128,128]{2,1,0:T(8,128)S(1)} %slice_select_fusion.5), channel_id=1, source_target_pairs={{0,4},{4,0},{8,12},{12,8},{16,20},{20,16},{24,28},{28,24},{1,5},{5... | collective-permute-start | bytes 393224 | tf_op jit(solution)/shard_map/ppermute | solution.py:253
  9.4 8.3 %collective-permute-start.1 = (f32[2,128,128]{2,1,0:T(8,128)S(1)}, f32[2,128,128]{2,1,0:T(8,128)S(1)}, u32[]{:S(2)}, u32[]{:S(2)}) collective-permute-start(f32[2,128,128]{2,1,0:T(8,128)S(1)} %fusion), channel_id=1, source_target_pairs={{0,8},{4,12},{1,9},{5,13},{2,10},{6,14},{3,11},{7,15}} | collective-permute-start | bytes 393224 | tf_op jit(solution)/shard_map/ppermute | solution.py:253
  14.4 5.0 %collective-permute-start.6 = (f32[2,128,128]{2,1,0:T(8,128)S(1)}, f32[2,128,128]{2,1,0:T(8,128)S(1)}, u32[]{:S(2)}, u32[]{:S(2)}) collective-permute-start(f32[2,128,128]{2,1,0:T(8,128)S(1)} %fusion.1), channel_id=1, source_target_pairs={{0,8},{4,12},{1,9},{5,13},{2,10},{6,14},{3,11},{7,15}} | collective-permute-start | bytes 393224 | tf_op jit(solution)/shard_map/ppermute | solution.py:253
  17.8 2.6 %collective-permute-start.3 = (f32[2,128,128]{2,1,0:T(8,128)S(1)}, f32[2,128,128]{2,1,0:T(8,128)S(1)}, u32[]{:S(2)}, u32[]{:S(2)}) collective-permute-start(f32[2,128,128]{2,1,0:T(8,128)S(1)} %add.100), channel_id=1, source_target_pairs={{8,16},{12,20},{9,17},{13,21},{10,18},{14,22},{11,19},{15,23}} | collective-permute-start | bytes 393224 | tf_op jit(solution)/shard_map/ppermute | solution.py:253
  19.5 7.4 %copy-start.1 = (bf16[1024,1024]{1,0:T(8,128)(2,1)S(1)}, bf16[1024,1024]{1,0:T(8,128)(2,1)}, u32[]{:S(2)}) copy-start(bf16[1024,1024]{1,0:T(8,128)(2,1)} %og_ref.3) | copy-start | bytes 6291460
  19.5 7.4 %copy-start.2 = (f32[1024]{0:T(1024)S(1)}, f32[1024]{0:T(1024)}, u32[]{:S(2)}) copy-start(f32[1024]{0:T(1024)} %param.8) | copy-start | bytes 12292
  19.5 1.5 %collective-permute-start.7 = (f32[2,128,128]{2,1,0:T(8,128)S(1)}, f32[2,128,128]{2,1,0:T(8,128)S(1)}, u32[]{:S(2)}, u32[]{:S(2)}) collective-permute-start(f32[2,128,128]{2,1,0:T(8,128)S(1)} %add.106), channel_id=1, source_target_pairs={{8,16},{12,20},{9,17},{13,21},{10,18},{14,22},{11,19},{15,23}} | collective-permute-start | bytes 393224 | tf_op jit(solution)/shard_map/ppermute | solution.py:253
  20.4 1.4 %collective-permute-start.4 = (f32[2,128,128]{2,1,0:T(8,128)S(1)}, f32[2,128,128]{2,1,0:T(8,128)S(1)}, u32[]{:S(2)}, u32[]{:S(2)}) collective-permute-start(f32[2,128,128]{2,1,0:T(8,128)S(1)} %add.102), channel_id=1, source_target_pairs={{16,24},{20,28},{17,25},{21,29},{18,26},{22,30},{19,27},{23,31}} | collective-permute-start | bytes 393224 | tf_op jit(solution)/shard_map/ppermute | solution.py:253
  21.1 1.6 %collective-permute-start.8 = (f32[2,128,128]{2,1,0:T(8,128)S(1)}, f32[2,128,128]{2,1,0:T(8,128)S(1)}, u32[]{:S(2)}, u32[]{:S(2)}) collective-permute-start(f32[2,128,128]{2,1,0:T(8,128)S(1)} %add.108), channel_id=1, source_target_pairs={{16,24},{20,28},{17,25},{21,29},{18,26},{22,30},{19,27},{23,31}} | collective-permute-start | bytes 393224 | tf_op jit(solution)/shard_map/ppermute | solution.py:253
  21.8 5.0 %collective-permute-start.5 = (f32[2,128,128]{2,1,0:T(8,128)S(1)}, f32[2,128,128]{2,1,0:T(8,128)S(1)}, u32[]{:S(2)}, u32[]{:S(2)}) collective-permute-start(f32[2,128,128]{2,1,0:T(8,128)S(1)} %get-tuple-element.220), channel_id=1, source_target_pairs={{0,4},{4,0},{8,12},{12,8},{16,20},{20,16},{24,28},{28,24},{1,5},{5... | collective-permute-start | bytes 393224 | tf_op jit(solution)/shard_map/ppermute | solution.py:253
  22.7 5.5 %collective-permute-start.9 = (f32[2,128,128]{2,1,0:T(8,128)S(1)}, f32[2,128,128]{2,1,0:T(8,128)S(1)}, u32[]{:S(2)}, u32[]{:S(2)}) collective-permute-start(f32[2,128,128]{2,1,0:T(8,128)S(1)} %get-tuple-element.218), channel_id=1, source_target_pairs={{0,4},{4,0},{8,12},{12,8},{16,20},{20,16},{24,28},{28,24},{1,5},{5... | collective-permute-start | bytes 393224 | tf_op jit(solution)/shard_map/ppermute | solution.py:253
  29.2 1.2 %collective-permute-start.10 = (f32[2,1024]{1,0:T(2,128)S(1)}, f32[2,1024]{1,0:T(2,128)S(1)}, u32[]{:S(2)}, u32[]{:S(2)}) collective-permute-start(f32[2,1024]{1,0:T(2,128)S(1)} %add.112), channel_id=1, source_target_pairs={{0,1},{1,0},{2,3},{3,2},{4,5},{5,4},{6,7},{7,6},{8,9},{9,8},{10,11... | collective-permute-start | bytes 24584 | tf_op jit(solution)/shard_map/ppermute | solution.py:269
  30.5 3.7 %collective-permute-start.11 = (f32[2,1024]{1,0:T(2,128)S(1)}, f32[2,1024]{1,0:T(2,128)S(1)}, u32[]{:S(2)}, u32[]{:S(2)}) collective-permute-start(f32[2,1024]{1,0:T(2,128)S(1)} %add.113), channel_id=1, source_target_pairs={{0,2},{1,3},{2,0},{3,1},{4,6},{5,7},{6,4},{7,5},{8,10},{9,11},{10,... | collective-permute-start | bytes 24584 | tf_op jit(solution)/shard_map/ppermute | solution.py:269
  35.4 6.2 %collective-permute-start.12 = (f32[2,128,128]{2,1,0:T(8,128)S(1)}, f32[2,128,128]{2,1,0:T(8,128)S(1)}, u32[]{:S(2)}, u32[]{:S(2)}) collective-permute-start(f32[2,128,128]{2,1,0:T(8,128)S(1)} %slice_select_fusion.2), channel_id=1, source_target_pairs={{28,24},{24,28},{20,16},{16,20},{12,8},{8,12},{4,0},{0,4},{29,25},... | collective-permute-start | bytes 393224 | tf_op jit(solution)/shard_map/ppermute | solution.py:253
  37.9 6.5 %collective-permute-start.14 = (f32[2,128,128]{2,1,0:T(8,128)S(1)}, f32[2,128,128]{2,1,0:T(8,128)S(1)}, u32[]{:S(2)}, u32[]{:S(2)}) collective-permute-start(f32[2,128,128]{2,1,0:T(8,128)S(1)} %slice_select_fusion.1), channel_id=1, source_target_pairs={{28,24},{24,28},{20,16},{16,20},{12,8},{8,12},{4,0},{0,4},{29,25},... | collective-permute-start | bytes 393224 | tf_op jit(solution)/shard_map/ppermute | solution.py:253
  41.7 5.1 %collective-permute-start.13 = (f32[2,128,128]{2,1,0:T(8,128)S(1)}, f32[2,128,128]{2,1,0:T(8,128)S(1)}, u32[]{:S(2)}, u32[]{:S(2)}) collective-permute-start(f32[2,128,128]{2,1,0:T(8,128)S(1)} %fusion.2), channel_id=1, source_target_pairs={{28,20},{24,16},{29,21},{25,17},{30,22},{26,18},{31,23},{27,19}} | collective-permute-start | bytes 393224 | tf_op jit(solution)/shard_map/ppermute | solution.py:253
  44.4 4.9 %collective-permute-start.16 = (f32[2,128,128]{2,1,0:T(8,128)S(1)}, f32[2,128,128]{2,1,0:T(8,128)S(1)}, u32[]{:S(2)}, u32[]{:S(2)}) collective-permute-start(f32[2,128,128]{2,1,0:T(8,128)S(1)} %fusion.3), channel_id=1, source_target_pairs={{28,20},{24,16},{29,21},{25,17},{30,22},{26,18},{31,23},{27,19}} | collective-permute-start | bytes 393224 | tf_op jit(solution)/shard_map/ppermute | solution.py:253
  46.8 4.9 %collective-permute-start.15 = (f32[2,128,128]{2,1,0:T(8,128)S(1)}, f32[2,128,128]{2,1,0:T(8,128)S(1)}, u32[]{:S(2)}, u32[]{:S(2)}) collective-permute-start(f32[2,128,128]{2,1,0:T(8,128)S(1)} %add.117), channel_id=1, source_target_pairs={{20,12},{16,8},{21,13},{17,9},{22,14},{18,10},{23,15},{19,11}} | collective-permute-start | bytes 393224 | tf_op jit(solution)/shard_map/ppermute | solution.py:253
  49.3 5.6 %collective-permute-start.18 = (f32[2,128,128]{2,1,0:T(8,128)S(1)}, f32[2,128,128]{2,1,0:T(8,128)S(1)}, u32[]{:S(2)}, u32[]{:S(2)}) collective-permute-start(f32[2,128,128]{2,1,0:T(8,128)S(1)} %add.118), channel_id=1, source_target_pairs={{20,12},{16,8},{21,13},{17,9},{22,14},{18,10},{23,15},{19,11}} | collective-permute-start | bytes 393224 | tf_op jit(solution)/shard_map/ppermute | solution.py:253
  51.8 16.3 %collective-permute-start.17 = (f32[2,128,128]{2,1,0:T(8,128)S(1)}, f32[2,128,128]{2,1,0:T(8,128)S(1)}, u32[]{:S(2)}, u32[]{:S(2)}) collective-permute-start(f32[2,128,128]{2,1,0:T(8,128)S(1)} %add.120), channel_id=1, source_target_pairs={{12,4},{8,0},{13,5},{9,1},{14,6},{10,2},{15,7},{11,3}} | collective-permute-start | bytes 393224 | tf_op jit(solution)/shard_map/ppermute | solution.py:253
  54.9 16.7 %collective-permute-start.20 = (f32[2,128,128]{2,1,0:T(8,128)S(1)}, f32[2,128,128]{2,1,0:T(8,128)S(1)}, u32[]{:S(2)}, u32[]{:S(2)}) collective-permute-start(f32[2,128,128]{2,1,0:T(8,128)S(1)} %add.121), channel_id=1, source_target_pairs={{12,4},{8,0},{13,5},{9,1},{14,6},{10,2},{15,7},{11,3}} | collective-permute-start | bytes 393224 | tf_op jit(solution)/shard_map/ppermute | solution.py:253
  68.2 5.0 %collective-permute-start.19 = (f32[2,128,128]{2,1,0:T(8,128)S(1)}, f32[2,128,128]{2,1,0:T(8,128)S(1)}, u32[]{:S(2)}, u32[]{:S(2)}) collective-permute-start(f32[2,128,128]{2,1,0:T(8,128)S(1)} %get-tuple-element.216), channel_id=1, source_target_pairs={{28,24},{24,28},{20,16},{16,20},{12,8},{8,12},{4,0},{0,4},{29,25},... | collective-permute-start | bytes 393224 | tf_op jit(solution)/shard_map/ppermute | solution.py:253
  71.6 5.0 %collective-permute-start.21 = (f32[2,128,128]{2,1,0:T(8,128)S(1)}, f32[2,128,128]{2,1,0:T(8,128)S(1)}, u32[]{:S(2)}, u32[]{:S(2)}) collective-permute-start(f32[2,128,128]{2,1,0:T(8,128)S(1)} %get-tuple-element.214), channel_id=1, source_target_pairs={{28,24},{24,28},{20,16},{16,20},{12,8},{8,12},{4,0},{0,4},{29,25},... | collective-permute-start | bytes 393224 | tf_op jit(solution)/shard_map/ppermute | solution.py:253
  (1 other events, 5.5 us)

commit v7 on v6

--- a/solution.py
+++ b/solution.py
@@ -123,71 +123,80 @@
     return copies
 
 
-def back_kernel(h, inner, winner, blocks, before, q_ref, k_ref, v_ref, w_ref, g_ref, p_ref, a_ref, gain_ref, inv_ref, *rest):
+def back_kernel(first, heads, inner, winner, blocks, before, q_ref, k_ref, v_ref, w_ref, g_ref, p_ref, a_ref, gain_ref, inv_ref, *rest):
     copies = []
     if before is not None:
         old_m, old_q = rest[:2]
         m_ref, qg_ref, kl_ref, vl_ref, m_hbm, q_hbm, bw, plow, slow, sems = rest[-10:]
-        copies = flush([(old_m, m_hbm.at[:, cols_of(before)]), (old_q, q_hbm.at[:, cols_of(before)])], sems)
+        copies = flush([(old_m, m_hbm.at[:, before]), (old_q, q_hbm.at[:, before])], sems)
     else:
         m_ref, qg_ref, kl_ref, vl_ref, bw, plow, slow = rest
     causal = causal_mask()
-    ci, cw, cq = cols_of(inner), cols_of(winner), cols_of(h)
-    m_ref[...] = (gain_ref[:, cq] * a_ref[:, ci] * inv_ref[...]).astype(BF16)
-    for n in range(0, blocks, 2):
-        r = slice(n * BLOCK, min(n + 2, blocks) * BLOCK)
-        s = dot(g_ref[r, ci], v_ref[r, ci], 1, 1)
-        for m in range(n, min(n + 2, blocks)):
-            inside = rows_of(m - n)
-            bw[rows_of(m), :] = jnp.where(causal, s[inside, inside], 0.0).astype(BF16)
-    prefix = p_ref[inner].T
-    plow[rows_of(0), :] = prefix.astype(BF16)
-    for n in range(blocks - 1):
-        prefix = prefix + dot(v_ref[rows_of(n), ci], k_ref[rows_of(n), ci], 0, 0)
-        plow[rows_of(n + 1), :] = prefix.astype(BF16)
-    suffix = None
-    for n in reversed(range(1, blocks)):
-        s = dot(g_ref[rows_of(n), ci], q_ref[rows_of(n), cq], 0, 0)
-        suffix = s if suffix is None else suffix + s
-        slow[rows_of(n - 1), :] = suffix.astype(BF16)
-    for n in range(blocks):
-        r = rows_of(n)
-        q, k, v, g = q_ref[r, cq], k_ref[r, ci], v_ref[r, ci], g_ref[r, ci]
-        left = jnp.concatenate([bw[r, :], g], axis=1)
-        right = jnp.concatenate([k, plow[r, :]], axis=0)
-        qg_ref[r, :] = dot(left, right, 1, 0).astype(BF16)
-        vp = dot(w_ref[r, cw], g, 0, 0)
-        if n + 1 < blocks:
-            left = jnp.concatenate([bw[r, :].T, v], axis=1)
-            right = jnp.concatenate([q, slow[r, :]], axis=0)
-            kp = dot(left, right, 1, 0)
-            vp = vp + dot(k, slow[r, :], 1, 1)
-        else:
-            kp = dot(bw[r, :], q, 0, 0)
-        kl_ref[r, :] = kp
-        vl_ref[r, :] = vp
+    here = [(h, cols_of(h), cols_of(h + inner), cols_of(h + winner), cols_of(h + first)) for h in range(heads)]
+    for h, c, ci, cw, cq in here:
+        m_ref[:, c] = (gain_ref[:, cq] * a_ref[:, ci] * inv_ref[...]).astype(BF16)
+    for h, c, ci, cw, cq in here:
+        for n in range(0, blocks, 2):
+            r = slice(n * BLOCK, min(n + 2, blocks) * BLOCK)
+            s = dot(g_ref[r, ci], v_ref[r, ci], 1, 1)
+            for m in range(n, min(n + 2, blocks)):
+                inside = rows_of(m - n)
+                bw[rows_of(m), c] = jnp.where(causal, s[inside, inside], 0.0).astype(BF16)
+    for h, c, ci, cw, cq in here:
+        prefix = p_ref[h + inner].T
+        plow[rows_of(0), c] = prefix.astype(BF16)
+        for n in range(blocks - 1):
+            prefix = prefix + dot(v_ref[rows_of(n), ci], k_ref[rows_of(n), ci], 0, 0)
+            plow[rows_of(n + 1), c] = prefix.astype(BF16)
+    for h, c, ci, cw, cq in here:
+        suffix = None
+        for n in reversed(range(1, blocks)):
+            s = dot(g_ref[rows_of(n), ci], q_ref[rows_of(n), cq], 0, 0)
+            suffix = s if suffix is None else suffix + s
+            slow[rows_of(n - 1), c] = suffix.astype(BF16)
+    for h, c, ci, cw, cq in here:
+        for n in range(blocks):
+            r = rows_of(n)
+            q, k, v, g = q_ref[r, cq], k_ref[r, ci], v_ref[r, ci], g_ref[r, ci]
+            left = jnp.concatenate([bw[r, c], g], axis=1)
+            right = jnp.concatenate([k, plow[r, c]], axis=0)
+            qg_ref[r, c] = dot(left, right, 1, 0).astype(BF16)
+            vp = dot(w_ref[r, cw], g, 0, 0)
+            if n + 1 < blocks:
+                left = jnp.concatenate([bw[r, c].T, v], axis=1)
+                right = jnp.concatenate([q, slow[r, c]], axis=0)
+                kp = dot(left, right, 1, 0)
+                vp = vp + dot(k, slow[r, c], 1, 1)
+            else:
+                kp = dot(bw[r, c], q, 0, 0)
+            kl_ref[r, c] = kp
+            vl_ref[r, c] = vp
     for copy in copies:
         copy.wait()
 
 
-def last_kernel(heads, before, k_ref, v_ref, s_ref, *rest):
-    kls, vls, rest = rest[:heads], rest[heads : 2 * heads], rest[2 * heads :]
+def last_kernel(counts, before, k_ref, v_ref, s_ref, *rest):
+    kls, vls, rest = rest[: len(counts)], rest[len(counts) : 2 * len(counts)], rest[2 * len(counts) :]
     old_a, old_b = rest[:2]
+    heads = sum(counts)
     if before is not None:
         kg, vg, a_hbm, b_hbm, sems = rest[-5:]
-        copies = flush([(old_a, a_hbm.at[:, cols_of(before)]), (old_b, b_hbm.at[:, cols_of(before)])], sems.at[0])
+        copies = flush([(old_a, a_hbm.at[:, before]), (old_b, b_hbm.at[:, before])], sems.at[0])
     else:
         a_hbm, b_hbm, kg, vg, sems = rest[-5:]
         there = slice(0, heads * HEAD_DIM)
         copies = flush([(old_a, a_hbm.at[:, there]), (old_b, b_hbm.at[:, there])], sems.at[0])
-    for h in range(heads):
-        c = cols_of(h)
-        low = s_ref[h].astype(BF16)
-        kg[:, c] = (kls[h][...] + dot(v_ref[:, c], low, 1, 1)).astype(BF16)
-        vg[:, c] = (vls[h][...] + dot(k_ref[:, c], low, 1, 0)).astype(BF16)
-        if before is None:
-            to = cols_of(heads + h)
-            copies += flush([(kg.at[:, c], a_hbm.at[:, to]), (vg.at[:, c], b_hbm.at[:, to])], sems.at[1 + h])
+    h = 0
+    for kl, vl, count in zip(kls, vls, counts):
+        for i in range(count):
+            c, ci = cols_of(h), cols_of(i)
+            low = s_ref[h].astype(BF16)
+            kg[:, c] = (kl[:, ci] + dot(v_ref[:, c], low, 1, 1)).astype(BF16)
+            vg[:, c] = (vl[:, ci] + dot(k_ref[:, c], low, 1, 0)).astype(BF16)
+            h += 1
+            if before is None:
+                to = cols_of(heads + h - 1)
+                copies += flush([(kg.at[:, c], a_hbm.at[:, to]), (vg.at[:, c], b_hbm.at[:, to])], sems.at[h])
     for copy in copies:
         copy.wait()
 
@@ -352,39 +361,39 @@
         backs.append(back)
         return (back,)
 
-    column = (rows, HEAD_DIM)
-    inner, made, fresh = {}, [], []
-
-    def piece_back(h, tied):
-        i = h // half
+    inner, made, fresh, before = {}, [], [], [None]
+
+    def piece_back(first, count, tied):
+        i = first // half
         (qt,) = after(tied, queries)
-        ins = [qt, ks[i], vs[i], weights[h // size * size], grads[i], prefixes[i], atts[i], gain, factors[0], *fresh]
-        specs, outs, aliases = [VMEM] * len(ins), [(column, BF16)] * 2 + [(column, F32)] * 2, {}
-        out_specs, scratch = [VMEM] * 4, [pltpu.VMEM(column, BF16)] * 3
+        ins = [qt, ks[i], vs[i], weights[first // size * size], grads[i], prefixes[i], atts[i], gain, factors[0], *fresh]
+        own = (rows, count * HEAD_DIM)
+        specs, outs, aliases = [VMEM] * len(ins), [(own, BF16)] * 2 + [(own, F32)] * 2, {}
+        out_specs, scratch = [VMEM] * 4, [pltpu.VMEM(own, BF16)] * 3
         if fresh:
             aliases = {len(ins) + n: 4 + n for n in range(len(made))}
             ins, specs = ins + made, specs + [HBM] * len(made)
             outs, out_specs = outs + [whole] * 2, out_specs + [HBM] * 2
             scratch.append(pltpu.SemaphoreType.DMA((2,)))
         m, q, *others = call(
-            functools.partial(back_kernel, h, h % half, h % size, blocks, h - 1 if fresh else None),
+            functools.partial(back_kernel, first, count, first % half, first % size, blocks, before[0]),
             ins,
             outs,
             in_specs=specs,
             out_specs=out_specs,
             scratch=scratch,
             aliases=aliases,
-            flops=9 * unit,
-        )
-        inner[h], made[:] = others[:2], others[2:]
-        fresh[:] = [m, q]
-        return tuple(inner[h])
+            flops=9 * unit * count,
+        )
+        inner[first], made[:] = (count, *others[:2]), others[2:]
+        fresh[:], before[0] = [m, q], slice(first * HEAD_DIM, (first + count) * HEAD_DIM)
+        return tuple(others[:2])
 
     results = []
 
     def make_last(i, suffix):
-        mine = [inner[h] for h in range(i * half, (i + 1) * half)]
-        ins = [ks[i], vs[i], suffix] + [kl for kl, _ in mine] + [vl for _, vl in mine] + (results if i else fresh)
+        mine = [inner[first] for first in sorted(inner) if first // half == i]
+        ins = [ks[i], vs[i], suffix] + [kl for _, kl, _ in mine] + [vl for _, _, vl in mine] + (results if i else fresh)
         specs, aliases = [VMEM] * len(ins), {}
         here = [((rows, part), BF16)] * 2
         if i:
@@ -395,7 +404,7 @@
             outs, out_specs, scratch = here + [whole] * 2, [VMEM] * 2 + [HBM] * 2, []
         results.clear()
         got = call(
-            functools.partial(last_kernel, half, None if i else heads - 1),
+            functools.partial(last_kernel, [count for count, _, _ in mine], None if i else before[0]),
             ins,
             outs,
             in_specs=specs,
@@ -410,12 +419,19 @@
         return tuple(got)
 
     piece_grad(0, ())
+    groups = [(0, 1), (1, 1)] + [(first, size) for first in range(2, heads, size)] if size == 2 else [(0, 1), (1, 1)]
+    under = {0: [functools.partial(piece_grad, 1)]}
+    for n, group in enumerate(groups):
+        under.setdefault((1, 2, 3, 5)[min(n, 3)], []).append(functools.partial(piece_back, *group))
+
+    def in_turn(works, tied):
+        for work in works:
+            tied = work(tied)
+        return tied
+
     drive(
         [lambda i=i: scan_stages(backs[i], seq_size, low, True) for i in range(2)],
-        {
-            0: functools.partial(piece_grad, 1),
-            **{i + 1: functools.partial(piece_back, i) for i in range(heads)},
-        },
+        {event: functools.partial(in_turn, works) for event, works in under.items()},
         make_last,
     )
     return (*made, *results)

time: 79.3 us -> 77.9 us (0.982)
  Pallas kernels: 29.7 us -> 27 us
  waiting for transfers between devices: 20.7 us -> 21.6 us
    pallas_call x20 -> x17, Pallas kernels: 29.7 us -> 27 us  [call(): pl.pallas_call(kernel, in_specs=in_specs or [VMEM] * len(ins), out_specs=...]
    ppermute x20, waiting for transfers between devices: 17.4 us -> 18.3 us  [drive(): live.append((name, scan, lax.ppermute(operand, 'seq', pairs)))]
  transfers between devices with their start and end apart: 22 -> 22, of which waited for: 8 -> 8; matrix products, arithmetic and copies ran while one was open for 1% -> 1% of each run, Pallas kernels for 29% -> 26%
where the time goes in v7:
time: 77.9 us; the launch traced here: 77.6 us
  Pallas kernels  27 us (35%)
  starting transfers between devices  27 us (35%)
  waiting for transfers between devices  21.6 us (28%)
  between operations  1.3 us (2%)
    pallas_call x17, Pallas kernels, call(): pl.pallas_call(kernel, in_specs=in_specs or [VMEM] * len(ins), out_specs=...  27 us
    ppermute x20, starting transfers between devices, drive(): live.append((name, scan, lax.ppermute(operand, 'seq', pairs)))  25.4 us
    ppermute x20, waiting for transfers between devices, drive(): live.append((name, scan, lax.ppermute(operand, 'seq', pairs)))  18.3 us
    ppermute x2, waiting for transfers between devices, head_sum(): a = a + lax.ppermute(a, 'head', [(i, i ^ step) for i in range(size)])  3.29 us
    ppermute x2, starting transfers between devices, head_sum(): a = a + lax.ppermute(a, 'head', [(i, i ^ step) for i in range(size)])  1.59 us
  transfers between devices with their start and end apart: 22, of which 8 were waited for; matrix products, arithmetic and copies ran while one was open for 1% of the time, Pallas kernels for 26%

profile of v7, /device:TPU:0, one launch (start us, length us, event | category | flops | bytes accessed | tf_op | source)
XLA Modules:
  0.0 77.6 jit_solution(14955761001827082421)
XLA Ops:
  0.6 2.2 %shard_map.84 = (bf16[1024,512]{1,0:T(8,128)(2,1)S(1)}, bf16[1024,512]{1,0:T(8,128)(2,1)S(1)}, f32[4,128,128]{2,1,0:T(8,128)S(1)}) custom-call(bf16[1024,1024]{1,0:T(8,128)(2,1)} %k_hbm.2, bf16[1024,1024]{1,0:T(8,128)(2,1)} %v_hbm.2), custom_call_target="tpu_custom_call" | custom-call | flops 134217728 | bytes 4194304 | tf_op jit(solution)/shard_map/pallas_call | solution.py:206
  2.9 3.0 %collective-permute-start = (f32[2,128,128]{2,1,0:T(8,128)S(1)}, f32[2,128,128]{2,1,0:T(8,128)S(1)}, u32[]{:S(2)}, u32[]{:S(2)}) collective-permute-start(f32[2,128,128]{2,1,0:T(8,128)S(1)} %slice_select_fusion.7), channel_id=1, source_target_pairs={{0,4},{4,0},{8,12},{12,8},{16,20},{20,16},{24,28},{28,24},{1,5},{5... | collective-permute-start | bytes 393224 | tf_op jit(solution)/shard_map/ppermute | solution.py:262
  5.9 2.2 %shard_map.85 = (bf16[1024,512]{1,0:T(8,128)(2,1)S(1)}, bf16[1024,512]{1,0:T(8,128)(2,1)S(1)}, f32[4,128,128]{2,1,0:T(8,128)S(1)}) custom-call(bf16[1024,1024]{1,0:T(8,128)(2,1)} %k_hbm.2, bf16[1024,1024]{1,0:T(8,128)(2,1)} %v_hbm.2), custom_call_target="tpu_custom_call" | custom-call | flops 134217728 | bytes 4194304 | tf_op jit(solution)/shard_map/pallas_call | solution.py:206
  9.4 3.9 %collective-permute-start.1 = (f32[2,128,128]{2,1,0:T(8,128)S(1)}, f32[2,128,128]{2,1,0:T(8,128)S(1)}, u32[]{:S(2)}, u32[]{:S(2)}) collective-permute-start(f32[2,128,128]{2,1,0:T(8,128)S(1)} %fusion), channel_id=1, source_target_pairs={{0,8},{4,12},{1,9},{5,13},{2,10},{6,14},{3,11},{7,15}} | collective-permute-start | bytes 393224 | tf_op jit(solution)/shard_map/ppermute | solution.py:262
  14.4 2.3 %collective-permute-start.6 = (f32[2,128,128]{2,1,0:T(8,128)S(1)}, f32[2,128,128]{2,1,0:T(8,128)S(1)}, u32[]{:S(2)}, u32[]{:S(2)}) collective-permute-start(f32[2,128,128]{2,1,0:T(8,128)S(1)} %fusion.1), channel_id=1, source_target_pairs={{0,8},{4,12},{1,9},{5,13},{2,10},{6,14},{3,11},{7,15}} | collective-permute-start | bytes 393224 | tf_op jit(solution)/shard_map/ppermute | solution.py:262
  22.7 1.3 %collective-permute-start.9 = (f32[2,128,128]{2,1,0:T(8,128)S(1)}, f32[2,128,128]{2,1,0:T(8,128)S(1)}, u32[]{:S(2)}, u32[]{:S(2)}) collective-permute-start(f32[2,128,128]{2,1,0:T(8,128)S(1)} %get-tuple-element.168), channel_id=1, source_target_pairs={{0,4},{4,0},{8,12},{12,8},{16,20},{20,16},{24,28},{28,24},{1,5},{5... | collective-permute-start | bytes 393224 | tf_op jit(solution)/shard_map/ppermute | solution.py:262
  24.0 2.8 %collective-permute-done.5 = f32[2,128,128]{2,1,0:T(8,128)S(1)} collective-permute-done((f32[2,128,128]{2,1,0:T(8,128)S(1)}, f32[2,128,128]{2,1,0:T(8,128)S(1)}, u32[]{:S(2)}, u32[]{:S(2)}) %collective-permute-start.5) | collective-permute-done | bytes 131104 | tf_op jit(solution)/shard_map/ppermute | solution.py:262
  30.5 1.5 %collective-permute-start.11 = (f32[2,1024]{1,0:T(2,128)S(1)}, f32[2,1024]{1,0:T(2,128)S(1)}, u32[]{:S(2)}, u32[]{:S(2)}) collective-permute-start(f32[2,1024]{1,0:T(2,128)S(1)} %add.113), channel_id=1, source_target_pairs={{0,2},{1,3},{2,0},{3,1},{4,6},{5,7},{6,4},{7,5},{8,10},{9,11},{10,... | collective-permute-start | bytes 24584 | tf_op jit(solution)/shard_map/ppermute | solution.py:278
  32.0 2.1 %collective-permute-done.11 = f32[2,1024]{1,0:T(2,128)S(1)} collective-permute-done((f32[2,1024]{1,0:T(2,128)S(1)}, f32[2,1024]{1,0:T(2,128)S(1)}, u32[]{:S(2)}, u32[]{:S(2)}) %collective-permute-start.11) | collective-permute-done | bytes 8224 | tf_op jit(solution)/shard_map/ppermute | solution.py:278
  34.1 1.3 %shard_map.92 = (bf16[1024,512]{1,0:T(8,128)(2,1)S(1)}, f32[4,128,128]{2,1,0:T(8,128)S(1)}, f32[1024,128]{1,0:T(8,128)S(1)}, f32[1024,128]{1,0:T(8,128)S(1)}) custom-call(f32[1024,512]{1,0:T(8,128)S(1)} %get-tuple-element.104.a_ref, bf16[1024,1024]{1,0:T(8,128)(2,1)S(1)} %copy-done, bf16[1024,1024]{1,0:T(8,128)(2,1)S(1)} %copy-done.1, ...), custom_call_target="tpu_custom_call" | custom-call | flops 134217728 | bytes 6303744 | tf_op jit(solution)/shard_map/pallas_call | solution.py:206
  35.5 1.4 %collective-permute-start.12 = (f32[2,128,128]{2,1,0:T(8,128)S(1)}, f32[2,128,128]{2,1,0:T(8,128)S(1)}, u32[]{:S(2)}, u32[]{:S(2)}) collective-permute-start(f32[2,128,128]{2,1,0:T(8,128)S(1)} %slice_select_fusion.2), channel_id=1, source_target_pairs={{28,24},{24,28},{20,16},{16,20},{12,8},{8,12},{4,0},{0,4},{29,25},... | collective-permute-start | bytes 393224 | tf_op jit(solution)/shard_map/ppermute | solution.py:262
  39.9 1.8 %collective-permute-done.12 = f32[2,128,128]{2,1,0:T(8,128)S(1)} collective-permute-done((f32[2,128,128]{2,1,0:T(8,128)S(1)}, f32[2,128,128]{2,1,0:T(8,128)S(1)}, u32[]{:S(2)}, u32[]{:S(2)}) %collective-permute-start.12) | collective-permute-done | bytes 131104 | tf_op jit(solution)/shard_map/ppermute | solution.py:262
  42.6 1.8 %shard_map.95 = (bf16[1024,128]{1,0:T(8,128)(2,1)S(1)}, bf16[1024,128]{1,0:T(8,128)(2,1)S(1)}, f32[1024,128]{1,0:T(8,128)S(1)}, f32[1024,128]{1,0:T(8,128)S(1)},...) custom-call(bf16[1024,1024]{1,0:T(8,128)(2,1)S(1)} %copy-done, bf16[1024,512]{1,0:T(8,128)(2,1)S(1)} %get-tuple-element.84.k_ref, ...), custom_call_target="tpu_custom_call" | custom-call | flops 301989888 | bytes 9179136 | tf_op jit(solution)/shard_map/pallas_call | solution.py:206
  45.0 2.4 %shard_map.96 = (bf16[1024,256]{1,0:T(8,128)(2,1)S(1)}, bf16[1024,256]{1,0:T(8,128)(2,1)S(1)}, f32[1024,256]{1,0:T(8,128)S(1)}, f32[1024,256]{1,0:T(8,128)S(1)},...) custom-call(bf16[1024,1024]{1,0:T(8,128)(2,1)S(1)} %copy-done, ...), custom_call_target="tpu_custom_call", output_to_operand_aliasing={{4}: (11, {}), {5}: (12, {})} | custom-call | flops 603979776 | bytes 13373440 | tf_op jit(solution)/shard_map/pallas_call | solution.py:206
  48.9 2.5 %shard_map.97 = (bf16[1024,256]{1,0:T(8,128)(2,1)S(1)}, bf16[1024,256]{1,0:T(8,128)(2,1)S(1)}, f32[1024,256]{1,0:T(8,128)S(1)}, f32[1024,256]{1,0:T(8,128)S(1)},...) custom-call(bf16[1024,1024]{1,0:T(8,128)(2,1)S(1)} %copy-done, ...), custom_call_target="tpu_custom_call", output_to_operand_aliasing={{4}: (11, {}), {5}: (12, {})} | custom-call | flops 603979776 | bytes 13897728 | tf_op jit(solution)/shard_map/pallas_call | solution.py:206
  51.4 2.5 %shard_map.98 = (bf16[1024,256]{1,0:T(8,128)(2,1)S(1)}, bf16[1024,256]{1,0:T(8,128)(2,1)S(1)}, f32[1024,256]{1,0:T(8,128)S(1)}, f32[1024,256]{1,0:T(8,128)S(1)},...) custom-call(bf16[1024,1024]{1,0:T(8,128)(2,1)S(1)} %copy-done, ...), custom_call_target="tpu_custom_call", output_to_operand_aliasing={{4}: (11, {}), {5}: (12, {})} | custom-call | flops 603979776 | bytes 13897728 | tf_op jit(solution)/shard_map/pallas_call | solution.py:206
  54.0 1.3 %collective-permute-start.17 = (f32[2,128,128]{2,1,0:T(8,128)S(1)}, f32[2,128,128]{2,1,0:T(8,128)S(1)}, u32[]{:S(2)}, u32[]{:S(2)}) collective-permute-start(f32[2,128,128]{2,1,0:T(8,128)S(1)} %add.120), channel_id=1, source_target_pairs={{12,4},{8,0},{13,5},{9,1},{14,6},{10,2},{15,7},{11,3}} | collective-permute-start | bytes 393224 | tf_op jit(solution)/shard_map/ppermute | solution.py:262
  55.3 1.3 %collective-permute-start.20 = (f32[2,128,128]{2,1,0:T(8,128)S(1)}, f32[2,128,128]{2,1,0:T(8,128)S(1)}, u32[]{:S(2)}, u32[]{:S(2)}) collective-permute-start(f32[2,128,128]{2,1,0:T(8,128)S(1)} %add.125), channel_id=1, source_target_pairs={{12,4},{8,0},{13,5},{9,1},{14,6},{10,2},{15,7},{11,3}} | collective-permute-start | bytes 393224 | tf_op jit(solution)/shard_map/ppermute | solution.py:262
  56.6 11.7 %collective-permute-done.17 = f32[2,128,128]{2,1,0:T(8,128)S(1)} collective-permute-done((f32[2,128,128]{2,1,0:T(8,128)S(1)}, f32[2,128,128]{2,1,0:T(8,128)S(1)}, u32[]{:S(2)}, u32[]{:S(2)}) %collective-permute-start.17) | collective-permute-done | bytes 131104 | tf_op jit(solution)/shard_map/ppermute | solution.py:262
  68.3 1.6 %collective-permute-start.18 = (f32[2,128,128]{2,1,0:T(8,128)S(1)}, f32[2,128,128]{2,1,0:T(8,128)S(1)}, u32[]{:S(2)}, u32[]{:S(2)}) collective-permute-start(f32[2,128,128]{2,1,0:T(8,128)S(1)} %get-tuple-element.166), channel_id=1, source_target_pairs={{28,24},{24,28},{20,16},{16,20},{12,8},{8,12},{4,0},{0,4},{29,25},... | collective-permute-start | bytes 393224 | tf_op jit(solution)/shard_map/ppermute | solution.py:262
  70.1 1.9 %collective-permute-start.21 = (f32[2,128,128]{2,1,0:T(8,128)S(1)}, f32[2,128,128]{2,1,0:T(8,128)S(1)}, u32[]{:S(2)}, u32[]{:S(2)}) collective-permute-start(f32[2,128,128]{2,1,0:T(8,128)S(1)} %get-tuple-element.164), channel_id=1, source_target_pairs={{28,24},{24,28},{20,16},{16,20},{12,8},{8,12},{4,0},{0,4},{29,25},... | collective-permute-start | bytes 393224 | tf_op jit(solution)/shard_map/ppermute | solution.py:262
  72.0 1.4 %collective-permute-done.18 = f32[2,128,128]{2,1,0:T(8,128)S(1)} collective-permute-done((f32[2,128,128]{2,1,0:T(8,128)S(1)}, f32[2,128,128]{2,1,0:T(8,128)S(1)}, u32[]{:S(2)}, u32[]{:S(2)}) %collective-permute-start.18) | collective-permute-done | bytes 131104 | tf_op jit(solution)/shard_map/ppermute | solution.py:262
  73.4 1.8 %shard_map.99 = (bf16[1024,512]{1,0:T(8,128)(2,1)S(1)}, bf16[1024,512]{1,0:T(8,128)(2,1)S(1)}, bf16[1024,1024]{1,0:T(8,128)(2,1)}, bf16[1024,1024]{1,0:T(8,128)(2,1)}) custom-call(bf16[1024,512]{1,0:T(8,128)(2,1)S(1)} %get-tuple-element.84.k_ref, bf16[1024,512]{1,0:T(8,128)(2,1)S(1)} %get-tuple-element.85.v_ref, ...), custom_call_target="tpu_custom_call", output_to_operand_aliasing={{2}: (11, {}), {3}: (12, {})} | custom-call | flops 268435456 | bytes 11796480 | tf_op jit(solution)/shard_map/pallas_call | solution.py:206
  75.3 2.1 %shard_map.100 = (bf16[1024,1024]{1,0:T(8,128)(2,1)}, bf16[1024,1024]{1,0:T(8,128)(2,1)}) custom-call(bf16[1024,512]{1,0:T(8,128)(2,1)S(1)} %get-tuple-element.99.k_ref, bf16[1024,512]{1,0:T(8,128)(2,1)S(1)} %get-tuple-element.100.v_ref, f32[4,128,128]{2,1,0:T(8,128)S(1)} %pad_maximum_fusion.3.s_ref, f32[1024,256]{1,0:T(8,128)S(1)} %get-tuple-element.143.rest_0_, ...), custom_call_target="tpu_custom_call" | custom-call | flops 268435456 | bytes 8650752 | tf_op jit(solution)/shard_map/pallas_call | solution.py:206
  (74 shorter events, 18.2 us)
Async XLA Ops:
  2.9 6.5 %collective-permute-start = (f32[2,128,128]{2,1,0:T(8,128)S(1)}, f32[2,128,128]{2,1,0:T(8,128)S(1)}, u32[]{:S(2)}, u32[]{:S(2)}) collective-permute-start(f32[2,128,128]{2,1,0:T(8,128)S(1)} %slice_select_fusion.7), channel_id=1, source_target_pairs={{0,4},{4,0},{8,12},{12,8},{16,20},{20,16},{24,28},{28,24},{1,5},{5... | collective-permute-start | bytes 393224 | tf_op jit(solution)/shard_map/ppermute | solution.py:262
  8.1 6.2 %collective-permute-start.2 = (f32[2,128,128]{2,1,0:T(8,128)S(1)}, f32[2,128,128]{2,1,0:T(8,128)S(1)}, u32[]{:S(2)}, u32[]{:S(2)}) collective-permute-start(f32[2,128,128]{2,1,0:T(8,128)S(1)} %slice_select_fusion.5), channel_id=1, source_target_pairs={{0,4},{4,0},{8,12},{12,8},{16,20},{20,16},{24,28},{28,24},{1,5},{5... | collective-permute-start | bytes 393224 | tf_op jit(solution)/shard_map/ppermute | solution.py:262
  9.4 8.3 %collective-permute-start.1 = (f32[2,128,128]{2,1,0:T(8,128)S(1)}, f32[2,128,128]{2,1,0:T(8,128)S(1)}, u32[]{:S(2)}, u32[]{:S(2)}) collective-permute-start(f32[2,128,128]{2,1,0:T(8,128)S(1)} %fusion), channel_id=1, source_target_pairs={{0,8},{4,12},{1,9},{5,13},{2,10},{6,14},{3,11},{7,15}} | collective-permute-start | bytes 393224 | tf_op jit(solution)/shard_map/ppermute | solution.py:262
  14.4 5.0 %collective-permute-start.6 = (f32[2,128,128]{2,1,0:T(8,128)S(1)}, f32[2,128,128]{2,1,0:T(8,128)S(1)}, u32[]{:S(2)}, u32[]{:S(2)}) collective-permute-start(f32[2,128,128]{2,1,0:T(8,128)S(1)} %fusion.1), channel_id=1, source_target_pairs={{0,8},{4,12},{1,9},{5,13},{2,10},{6,14},{3,11},{7,15}} | collective-permute-start | bytes 393224 | tf_op jit(solution)/shard_map/ppermute | solution.py:262
  17.8 2.6 %collective-permute-start.3 = (f32[2,128,128]{2,1,0:T(8,128)S(1)}, f32[2,128,128]{2,1,0:T(8,128)S(1)}, u32[]{:S(2)}, u32[]{:S(2)}) collective-permute-start(f32[2,128,128]{2,1,0:T(8,128)S(1)} %add.100), channel_id=1, source_target_pairs={{8,16},{12,20},{9,17},{13,21},{10,18},{14,22},{11,19},{15,23}} | collective-permute-start | bytes 393224 | tf_op jit(solution)/shard_map/ppermute | solution.py:262
  19.5 7.4 %copy-start.1 = (bf16[1024,1024]{1,0:T(8,128)(2,1)S(1)}, bf16[1024,1024]{1,0:T(8,128)(2,1)}, u32[]{:S(2)}) copy-start(bf16[1024,1024]{1,0:T(8,128)(2,1)} %og_ref.3) | copy-start | bytes 6291460
  19.5 7.4 %copy-start.2 = (f32[1024]{0:T(1024)S(1)}, f32[1024]{0:T(1024)}, u32[]{:S(2)}) copy-start(f32[1024]{0:T(1024)} %param.8) | copy-start | bytes 12292
  19.5 1.5 %collective-permute-start.7 = (f32[2,128,128]{2,1,0:T(8,128)S(1)}, f32[2,128,128]{2,1,0:T(8,128)S(1)}, u32[]{:S(2)}, u32[]{:S(2)}) collective-permute-start(f32[2,128,128]{2,1,0:T(8,128)S(1)} %add.106), channel_id=1, source_target_pairs={{8,16},{12,20},{9,17},{13,21},{10,18},{14,22},{11,19},{15,23}} | collective-permute-start | bytes 393224 | tf_op jit(solution)/shard_map/ppermute | solution.py:262
  20.4 1.4 %collective-permute-start.4 = (f32[2,128,128]{2,1,0:T(8,128)S(1)}, f32[2,128,128]{2,1,0:T(8,128)S(1)}, u32[]{:S(2)}, u32[]{:S(2)}) collective-permute-start(f32[2,128,128]{2,1,0:T(8,128)S(1)} %add.102), channel_id=1, source_target_pairs={{16,24},{20,28},{17,25},{21,29},{18,26},{22,30},{19,27},{23,31}} | collective-permute-start | bytes 393224 | tf_op jit(solution)/shard_map/ppermute | solution.py:262
  21.1 1.6 %collective-permute-start.8 = (f32[2,128,128]{2,1,0:T(8,128)S(1)}, f32[2,128,128]{2,1,0:T(8,128)S(1)}, u32[]{:S(2)}, u32[]{:S(2)}) collective-permute-start(f32[2,128,128]{2,1,0:T(8,128)S(1)} %add.108), channel_id=1, source_target_pairs={{16,24},{20,28},{17,25},{21,29},{18,26},{22,30},{19,27},{23,31}} | collective-permute-start | bytes 393224 | tf_op jit(solution)/shard_map/ppermute | solution.py:262
  21.8 5.0 %collective-permute-start.5 = (f32[2,128,128]{2,1,0:T(8,128)S(1)}, f32[2,128,128]{2,1,0:T(8,128)S(1)}, u32[]{:S(2)}, u32[]{:S(2)}) collective-permute-start(f32[2,128,128]{2,1,0:T(8,128)S(1)} %get-tuple-element.170), channel_id=1, source_target_pairs={{0,4},{4,0},{8,12},{12,8},{16,20},{20,16},{24,28},{28,24},{1,5},{5... | collective-permute-start | bytes 393224 | tf_op jit(solution)/shard_map/ppermute | solution.py:262
  22.7 5.5 %collective-permute-start.9 = (f32[2,128,128]{2,1,0:T(8,128)S(1)}, f32[2,128,128]{2,1,0:T(8,128)S(1)}, u32[]{:S(2)}, u32[]{:S(2)}) collective-permute-start(f32[2,128,128]{2,1,0:T(8,128)S(1)} %get-tuple-element.168), channel_id=1, source_target_pairs={{0,4},{4,0},{8,12},{12,8},{16,20},{20,16},{24,28},{28,24},{1,5},{5... | collective-permute-start | bytes 393224 | tf_op jit(solution)/shard_map/ppermute | solution.py:262
  29.2 1.2 %collective-permute-start.10 = (f32[2,1024]{1,0:T(2,128)S(1)}, f32[2,1024]{1,0:T(2,128)S(1)}, u32[]{:S(2)}, u32[]{:S(2)}) collective-permute-start(f32[2,1024]{1,0:T(2,128)S(1)} %add.112), channel_id=1, source_target_pairs={{0,1},{1,0},{2,3},{3,2},{4,5},{5,4},{6,7},{7,6},{8,9},{9,8},{10,11... | collective-permute-start | bytes 24584 | tf_op jit(solution)/shard_map/ppermute | solution.py:278
  30.5 3.7 %collective-permute-start.11 = (f32[2,1024]{1,0:T(2,128)S(1)}, f32[2,1024]{1,0:T(2,128)S(1)}, u32[]{:S(2)}, u32[]{:S(2)}) collective-permute-start(f32[2,1024]{1,0:T(2,128)S(1)} %add.113), channel_id=1, source_target_pairs={{0,2},{1,3},{2,0},{3,1},{4,6},{5,7},{6,4},{7,5},{8,10},{9,11},{10,... | collective-permute-start | bytes 24584 | tf_op jit(solution)/shard_map/ppermute | solution.py:278
  35.5 6.2 %collective-permute-start.12 = (f32[2,128,128]{2,1,0:T(8,128)S(1)}, f32[2,128,128]{2,1,0:T(8,128)S(1)}, u32[]{:S(2)}, u32[]{:S(2)}) collective-permute-start(f32[2,128,128]{2,1,0:T(8,128)S(1)} %slice_select_fusion.2), channel_id=1, source_target_pairs={{28,24},{24,28},{20,16},{16,20},{12,8},{8,12},{4,0},{0,4},{29,25},... | collective-permute-start | bytes 393224 | tf_op jit(solution)/shard_map/ppermute | solution.py:262
  38.0 6.3 %collective-permute-start.14 = (f32[2,128,128]{2,1,0:T(8,128)S(1)}, f32[2,128,128]{2,1,0:T(8,128)S(1)}, u32[]{:S(2)}, u32[]{:S(2)}) collective-permute-start(f32[2,128,128]{2,1,0:T(8,128)S(1)} %slice_select_fusion.1), channel_id=1, source_target_pairs={{28,24},{24,28},{20,16},{16,20},{12,8},{8,12},{4,0},{0,4},{29,25},... | collective-permute-start | bytes 393224 | tf_op jit(solution)/shard_map/ppermute | solution.py:262
  41.7 5.8 %collective-permute-start.13 = (f32[2,128,128]{2,1,0:T(8,128)S(1)}, f32[2,128,128]{2,1,0:T(8,128)S(1)}, u32[]{:S(2)}, u32[]{:S(2)}) collective-permute-start(f32[2,128,128]{2,1,0:T(8,128)S(1)} %fusion.2), channel_id=1, source_target_pairs={{28,20},{24,16},{29,21},{25,17},{30,22},{26,18},{31,23},{27,19}} | collective-permute-start | bytes 393224 | tf_op jit(solution)/shard_map/ppermute | solution.py:262
  44.4 3.8 %collective-permute-start.16 = (f32[2,128,128]{2,1,0:T(8,128)S(1)}, f32[2,128,128]{2,1,0:T(8,128)S(1)}, u32[]{:S(2)}, u32[]{:S(2)}) collective-permute-start(f32[2,128,128]{2,1,0:T(8,128)S(1)} %fusion.3), channel_id=1, source_target_pairs={{28,20},{24,16},{29,21},{25,17},{30,22},{26,18},{31,23},{27,19}} | collective-permute-start | bytes 393224 | tf_op jit(solution)/shard_map/ppermute | solution.py:262
  47.5 6.4 %collective-permute-start.15 = (f32[2,128,128]{2,1,0:T(8,128)S(1)}, f32[2,128,128]{2,1,0:T(8,128)S(1)}, u32[]{:S(2)}, u32[]{:S(2)}) collective-permute-start(f32[2,128,128]{2,1,0:T(8,128)S(1)} %add.117), channel_id=1, source_target_pairs={{20,12},{16,8},{21,13},{17,9},{22,14},{18,10},{23,15},{19,11}} | collective-permute-start | bytes 393224 | tf_op jit(solution)/shard_map/ppermute | solution.py:262
  48.2 7.0 %collective-permute-start.19 = (f32[2,128,128]{2,1,0:T(8,128)S(1)}, f32[2,128,128]{2,1,0:T(8,128)S(1)}, u32[]{:S(2)}, u32[]{:S(2)}) collective-permute-start(f32[2,128,128]{2,1,0:T(8,128)S(1)} %add.118), channel_id=1, source_target_pairs={{20,12},{16,8},{21,13},{17,9},{22,14},{18,10},{23,15},{19,11}} | collective-permute-start | bytes 393224 | tf_op jit(solution)/shard_map/ppermute | solution.py:262
  54.0 14.3 %collective-permute-start.17 = (f32[2,128,128]{2,1,0:T(8,128)S(1)}, f32[2,128,128]{2,1,0:T(8,128)S(1)}, u32[]{:S(2)}, u32[]{:S(2)}) collective-permute-start(f32[2,128,128]{2,1,0:T(8,128)S(1)} %add.120), channel_id=1, source_target_pairs={{12,4},{8,0},{13,5},{9,1},{14,6},{10,2},{15,7},{11,3}} | collective-permute-start | bytes 393224 | tf_op jit(solution)/shard_map/ppermute | solution.py:262
  55.3 14.8 %collective-permute-start.20 = (f32[2,128,128]{2,1,0:T(8,128)S(1)}, f32[2,128,128]{2,1,0:T(8,128)S(1)}, u32[]{:S(2)}, u32[]{:S(2)}) collective-permute-start(f32[2,128,128]{2,1,0:T(8,128)S(1)} %add.125), channel_id=1, source_target_pairs={{12,4},{8,0},{13,5},{9,1},{14,6},{10,2},{15,7},{11,3}} | collective-permute-start | bytes 393224 | tf_op jit(solution)/shard_map/ppermute | solution.py:262
  68.3 5.0 %collective-permute-start.18 = (f32[2,128,128]{2,1,0:T(8,128)S(1)}, f32[2,128,128]{2,1,0:T(8,128)S(1)}, u32[]{:S(2)}, u32[]{:S(2)}) collective-permute-start(f32[2,128,128]{2,1,0:T(8,128)S(1)} %get-tuple-element.166), channel_id=1, source_target_pairs={{28,24},{24,28},{20,16},{16,20},{12,8},{8,12},{4,0},{0,4},{29,25},... | collective-permute-start | bytes 393224 | tf_op jit(solution)/shard_map/ppermute | solution.py:262
  70.1 5.1 %collective-permute-start.21 = (f32[2,128,128]{2,1,0:T(8,128)S(1)}, f32[2,128,128]{2,1,0:T(8,128)S(1)}, u32[]{:S(2)}, u32[]{:S(2)}) collective-permute-start(f32[2,128,128]{2,1,0:T(8,128)S(1)} %get-tuple-element.164), channel_id=1, source_target_pairs={{28,24},{24,28},{20,16},{16,20},{12,8},{8,12},{4,0},{0,4},{29,25},... | collective-permute-start | bytes 393224 | tf_op jit(solution)/shard_map/ppermute | solution.py:262
  (1 other events, 5.5 us)

commit v8 on v7

v8 whole, which is shorter than its diff:
```python
import functools

import jax
import jax.numpy as jnp
from jax import lax
from jax.experimental import pallas as pl
from jax.experimental.pallas import tpu as pltpu
from jax.sharding import PartitionSpec as P

HEAD_DIM = 128
BLOCK = 128
WIDTH = 4096
epsilon = 1e-05

F32 = jnp.float32
BF16 = jnp.bfloat16
VMEM = pl.BlockSpec(memory_space=pltpu.VMEM)
HBM = pl.BlockSpec(memory_space=pltpu.HBM)


def dot(a, b, ca, cb):
    return lax.dot_general(a, b, (((ca,), (cb,)), ((), ())), preferred_element_type=F32)


def causal_mask():
    row = lax.broadcasted_iota(jnp.int32, (BLOCK, BLOCK), 0)
    col = lax.broadcasted_iota(jnp.int32, (BLOCK, BLOCK), 1)
    return col <= row


def rows_of(n):
    return slice(n * BLOCK, (n + 1) * BLOCK)


def cols_of(h):
    return slice(h * HEAD_DIM, (h + 1) * HEAD_DIM)


def places(size):
    low = 1 - lax.rem(lax.axis_index("seq"), 2)

    def columns(group, h=0, heads=1):
        chunk, own = divmod(group, 2)
        half = 2 * chunk + (1 - low if own else low)
        return pl.ds(pl.multiple_of((half * size + h) * HEAD_DIM, HEAD_DIM), heads * HEAD_DIM)

    return columns


def flush(pairs, sems):
    copies = [pltpu.make_async_copy(src, dst, sems.at[i]) for i, (src, dst) in enumerate(pairs)]
    for copy in copies:
        copy.start()
    return copies


def load_kernel(groups, size, k_hbm, v_hbm, *rest):
    count = len(groups)
    k_refs, v_refs, t_refs, sems = rest[:count], rest[count : 2 * count], rest[2 * count : 3 * count], rest[-1]
    at = places(size)
    copies = [
        flush([(k_hbm.at[:, at(g, 0, size)], k_ref), (v_hbm.at[:, at(g, 0, size)], v_ref)], sems.at[n])
        for n, (g, k_ref, v_ref) in enumerate(zip(groups, k_refs, v_refs))
    ]
    for group, k_ref, v_ref, t_ref in zip(copies, k_refs, v_refs, t_refs):
        for copy in group:
            copy.wait()
        for h in range(size):
            t_ref[h] = dot(k_ref[:, cols_of(h)], v_ref[:, cols_of(h)], 0, 0)


def local_kernel(group, size, blocks, q_ref, k_ref, v_ref, w_ref, a_ref, low):
    causal = causal_mask()
    at = places(size)
    here = [(cols_of(h), at(group, h)) for h in range(size)]
    for c, cq in here:
        for n in range(0, blocks, 2):
            r = slice(n * BLOCK, min(n + 2, blocks) * BLOCK)
            s = dot(q_ref[r, cq], k_ref[r, c], 1, 1)
            for m in range(n, min(n + 2, blocks)):
                inside = rows_of(m - n)
                w_ref[rows_of(m), c] = jnp.where(causal, s[inside, inside], 0.0).astype(BF16)
    for c, cq in here:
        prefix = None
        for n in range(blocks - 1):
            s = dot(k_ref[rows_of(n), c], v_ref[rows_of(n), c], 0, 0)
            prefix = s if prefix is None else prefix + s
            low[rows_of(n), c] = prefix.astype(BF16)
    for c, cq in here:
        a_ref[rows_of(0), c] = dot(w_ref[rows_of(0), c], v_ref[rows_of(0), c], 1, 0)
        for n in range(1, blocks):
            left = jnp.concatenate([w_ref[rows_of(n), c], q_ref[rows_of(n), cq]], axis=1)
            right = jnp.concatenate([v_ref[rows_of(n), c], low[rows_of(n - 1), c]], axis=0)
            a_ref[rows_of(n), c] = dot(left, right, 1, 0)


def stats_kernel(group, size, blocks, a_in, q_ref, p_ref, og_ref, gain_ref, a_ref, s_ref):
    at = places(size)
    low = [p_ref[h].astype(BF16) for h in range(size)]
    for n in range(blocks):
        r = rows_of(n)
        squares = dots = None
        for h in range(size):
            c, cq = cols_of(h), at(group, h)
            att = a_in[r, c] + dot(q_ref[r, cq], low[h], 1, 0)
            a_ref[r, c] = att
            scaled = gain_ref[:, cq] * og_ref[r, cq].astype(F32)
            squares = att * att if squares is None else squares + att * att
            dots = scaled * att if dots is None else dots + scaled * att
        s_ref[0:1, r] = jnp.sum(squares.T, axis=0, keepdims=True)
        s_ref[1:2, r] = jnp.sum(dots.T, axis=0, keepdims=True)


def grad_kernel(group, size, blocks, a_ref, q_ref, og_ref, gain_ref, *rest):
    if len(rest) == 5:
        s_ref, g_ref, t_ref, inv_ref, coef_ref = rest
        inverse = lax.rsqrt(s_ref[0:1, :] / WIDTH + epsilon)
        factor = inverse * inverse * inverse * s_ref[1:2, :] / WIDTH
        for n in range(blocks):
            inv_ref[rows_of(n), :] = jnp.broadcast_to(inverse[:, rows_of(n)], (BLOCK, BLOCK)).T
            coef_ref[rows_of(n), :] = jnp.broadcast_to(factor[:, rows_of(n)], (BLOCK, BLOCK)).T
    else:
        inv_ref, coef_ref, g_ref, t_ref = rest
    at = places(size)
    for h in range(size):
        c, cq = cols_of(h), at(group, h)
        scaled = gain_ref[:, cq] * og_ref[:, cq].astype(F32)
        grad = (inv_ref[...] * scaled - coef_ref[...] * a_ref[:, c]).astype(BF16)
        g_ref[:, c] = grad
        t_ref[h] = dot(q_ref[:, cq], grad, 0, 0)


def back_kernel(here, before, size, blocks, q_ref, k_ref, v_ref, w_ref, g_ref, p_ref, a_ref, gain_ref, inv_ref, *rest):
    at = places(size)
    copies = []
    if before is not None:
        old_m, old_q = rest[:2]
        m_ref, qg_ref, kl_ref, vl_ref, m_hbm, q_hbm, bw, plow, slow, sems = rest[-10:]
        there = at(*before)
        copies = flush([(old_m, m_hbm.at[:, there]), (old_q, q_hbm.at[:, there])], sems)
    else:
        m_ref, qg_ref, kl_ref, vl_ref, bw, plow, slow = rest
    causal = causal_mask()
    group, first, heads = here
    each = [(h, cols_of(h), cols_of(h + first), at(group, h + first)) for h in range(heads)]
    for h, c, ci, cq in each:
        m_ref[:, c] = (gain_ref[:, cq] * a_ref[:, ci] * inv_ref[...]).astype(BF16)
    for h, c, ci, cq in each:
        for n in range(0, blocks, 2):
            r = slice(n * BLOCK, min(n + 2, blocks) * BLOCK)
            s = dot(g_ref[r, ci], v_ref[r, ci], 1, 1)
            for m in range(n, min(n + 2, blocks)):
                inside = rows_of(m - n)
                bw[rows_of(m), c] = jnp.where(causal, s[inside, inside], 0.0).astype(BF16)
    for h, c, ci, cq in each:
        prefix = p_ref[h + first].T
        plow[rows_of(0), c] = prefix.astype(BF16)
        for n in range(blocks - 1):
            prefix = prefix + dot(v_ref[rows_of(n), ci], k_ref[rows_of(n), ci], 0, 0)
            plow[rows_of(n + 1), c] = prefix.astype(BF16)
    for h, c, ci, cq in each:
        suffix = None
        for n in reversed(range(1, blocks)):
            s = dot(g_ref[rows_of(n), ci], q_ref[rows_of(n), cq], 0, 0)
            suffix = s if suffix is None else suffix + s
            slow[rows_of(n - 1), c] = suffix.astype(BF16)
    for h, c, ci, cq in each:
        for n in range(blocks):
            r = rows_of(n)
            q, k, v, g = q_ref[r, cq], k_ref[r, ci], v_ref[r, ci], g_ref[r, ci]
            left = jnp.concatenate([bw[r, c], g], axis=1)
            right = jnp.concatenate([k, plow[r, c]], axis=0)
            qg_ref[r, c] = dot(left, right, 1, 0).astype(BF16)
            vp = dot(w_ref[r, ci], g, 0, 0)
            if n + 1 < blocks:
                left = jnp.concatenate([bw[r, c].T, v], axis=1)
                right = jnp.concatenate([q, slow[r, c]], axis=0)
                kp = dot(left, right, 1, 0)
                vp = vp + dot(k, slow[r, c], 1, 1)
            else:
                kp = dot(bw[r, c], q, 0, 0)
            kl_ref[r, c] = kp
            vl_ref[r, c] = vp
    for copy in copies:
        copy.wait()


def flush_kernel(here, size, a_ref, b_ref, *rest):
    a_hbm, b_hbm, sems = rest[-3:]
    there = places(size)(*here)
    for copy in flush([(a_ref, a_hbm.at[:, there]), (b_ref, b_hbm.at[:, there])], sems):
        copy.wait()


def last_kernel(group, counts, size, k_ref, v_ref, s_ref, *rest):
    kls, vls = rest[: len(counts)], rest[len(counts) : 2 * len(counts)]
    k_hbm, v_hbm, kg, vg, sems = rest[-5:]
    at = places(size)
    copies, h = [], 0
    for kl, vl, count in zip(kls, vls, counts):
        for i in range(count):
            c, ci, to = cols_of(h), cols_of(i), at(group, h)
            low = s_ref[h].astype(BF16)
            kg[:, c] = (kl[:, ci] + dot(v_ref[:, c], low, 1, 1)).astype(BF16)
            copies += flush([(kg.at[:, c], k_hbm.at[:, to])], sems.at[0, h : h + 1])
            vg[:, c] = (vl[:, ci] + dot(k_ref[:, c], low, 1, 0)).astype(BF16)
            copies += flush([(vg.at[:, c], v_hbm.at[:, to])], sems.at[1, h : h + 1])
            h += 1
    for copy in copies:
        copy.wait()


def call(kernel, ins, outs, in_specs=None, out_specs=None, scratch=(), aliases=None, flops=0, vmem=6):
    nbytes = sum(a.size * a.dtype.itemsize for a in ins)
    return pl.pallas_call(
        kernel,
        in_specs=in_specs or [VMEM] * len(ins),
        out_specs=tuple(out_specs or [VMEM] * len(outs)),
        out_shape=tuple(jax.ShapeDtypeStruct(shape, dtype) for shape, dtype in outs),
        scratch_shapes=list(scratch),
        input_output_aliases=aliases or {},
        compiler_params=pltpu.CompilerParams(vmem_limit_bytes=vmem << 20),
        cost_estimate=pl.CostEstimate(flops=flops, bytes_accessed=nbytes, transcendentals=0),
    )(*ins)


def scan_stages(other, mine, size, low, reverse):
    place = (lambda i: size - 1 - i) if reverse else (lambda i: i)
    perm = lambda pairs: [(place(i), place(j)) for i, j in pairs]
    at_first = (lambda a, b: jnp.where(low, b, a)) if reverse else (lambda a, b: jnp.where(low, a, b))
    outer = size // 2
    swap = [(i, i ^ 1) for i in range(size)]
    got = yield other, perm(swap), None
    mine = mine()
    pair = mine + got
    total = None
    if outer <= 4:
        running = pair
        for hop in range(outer - 1):
            r = yield running, perm([(2 * hop, 2 * hop + 2), (2 * hop + 1, 2 * hop + 3)]), None
            total = r if total is None else total + r
            running = r + pair
    else:
        total = yield pair, perm([(i, i + 2) for i in range(size - 2)]), None
        step = 1
        while step < outer - 1:
            r = yield total, perm([(i, i + 2 * step) for i in range(size - 2 * step)]), None
            total = total + r
            step *= 2
    return (yield at_first(total + mine, total), perm(swap), at_first(total, total + got))


def after(tied, *arrays):
    return lax.optimization_barrier((*arrays, *tied))[: len(arrays)] if tied else arrays


def drive(makers, pieces, early, finish):
    live, behind, event = [], (), 0
    waiting = list(makers)
    while waiting or live:
        if waiting:
            scan = waiting.pop(0)()
            name, (operand, pairs, answer) = len(makers) - len(waiting) - 1, next(scan)
        else:
            name, scan, result = live.pop(0)
            try:
                operand, pairs, answer = scan.send(after(behind, result)[0])
            except StopIteration as stop:
                behind = finish(name, stop.value)
                continue
        if answer is not None:
            early(name, answer)
        live.append((name, scan, lax.ppermute(operand, "seq", pairs)))
        behind = pieces.pop(event)((operand,)) if event in pieces else ()
        event += 1
    for piece in pieces.values():
        piece(())


def in_events(events):
    def in_turn(works, tied):
        for work in works:
            tied = work(tied)
        return tied

    return {event: functools.partial(in_turn, works) for event, works in sorted(events.items())}


def head_sum(a, size):
    if size & (size - 1):
        return lax.psum(a, "head")
    step = 1
    while step < size:
        a = a + lax.ppermute(a, "head", [(i, i ^ step) for i in range(size)])
        step *= 2
    return a


def body(seq_size, head_size, queries, keys, values, gain, out_grad):
    rows, width = queries.shape
    blocks, heads = rows // BLOCK, width // HEAD_DIM
    size = heads // 4
    low = lax.axis_index("seq") % 2 == 0
    gain = gain.reshape(1, width)
    unit = 2 * rows * HEAD_DIM * HEAD_DIM
    whole = ((rows, width), BF16)
    part = (rows, size * HEAD_DIM)
    state = ((size, HEAD_DIM, HEAD_DIM), F32)
    ks, vs, states, weights, atts, sums, prefixes, grads, backs = ({} for _ in range(9))

    outer = seq_size // 2
    last = 2 * (2 + (outer - 1 if outer <= 4 else (outer - 2).bit_length() + 1)) - 1


    def piece_load(groups, tied):
        got = call(
            functools.partial(load_kernel, groups, size),
            after(tied, keys, values),
            [(part, BF16)] * (2 * len(groups)) + [state] * len(groups),
            in_specs=[HBM, HBM],
            scratch=[pltpu.SemaphoreType.DMA((len(groups), 2))],
            flops=unit * size * len(groups),
            vmem=52 if len(groups) == 1 else 50,
        )
        count = len(groups)
        for n, g in enumerate(groups):
            ks[g], vs[g], states[g] = got[n], got[count + n], got[2 * count + n]
        return tuple(states[g] for g in groups)

    def piece_local(g, tied):
        (q,) = after(tied, queries)
        weights[g], atts[g] = call(
            functools.partial(local_kernel, g, size, blocks),
            [q, ks[g], vs[g]],
            [(part, BF16), (part, F32)],
            scratch=[pltpu.VMEM(part, BF16)],
            flops=4 * unit * size,
        )
        return weights[g], atts[g]

    def piece_stats(g, tied):
        (q,) = after(tied, queries)
        atts[g], sums[g] = call(
            functools.partial(stats_kernel, g, size, blocks),
            [atts[g], q, prefixes[g], out_grad, gain],
            [(part, F32), ((2, rows), F32)],
            flops=unit * size,
        )
        return atts[g], sums[g]

    def end_stats(i, answer):
        prefixes[2 * i] = answer
        return piece_stats(2 * i, ())

    piece_load([0], (low,))
    drive(
        [lambda i=i: scan_stages(states[2 * i], lambda: states[2 * i + 1], seq_size, low, False) for i in range(2)],
        in_events({
            0: [functools.partial(piece_load, [1, 2, 3])],
            2: [functools.partial(piece_local, 0)],
            3: [functools.partial(piece_local, 1)],
            4: [functools.partial(piece_local, 2)],
            5: [functools.partial(piece_local, 3)],
            last: [functools.partial(piece_stats, 1), functools.partial(piece_stats, 3)],
        }),
        lambda i, answer: prefixes.update({2 * i + 1: answer}),
        end_stats,
    )
    total = head_sum(sum(sums[g] for g in range(1, 4)) + sums[0], head_size)

    factors, inner, made, fresh, before, suffixes, results = [], {}, [], [], [None], {}, []

    def piece_grad(g, tied):
        (q,) = after(tied, queries)
        grads[g], backs[g], *new = call(
            functools.partial(grad_kernel, g, size, blocks),
            [atts[g], q, out_grad, gain, *(factors or [total])],
            [(part, BF16), state] + ([] if factors else [((rows, BLOCK), F32)] * 2),
            flops=unit * size,
        )
        factors.extend(new)
        return (backs[g],)

    def piece_back(g, first, count, tied):
        (q,) = after(tied, queries)
        ins = [q, ks[g], vs[g], weights[g], grads[g], prefixes[g], atts[g], gain, factors[0], *fresh]
        own = (rows, count * HEAD_DIM)
        specs, outs, aliases = [VMEM] * len(ins), [(own, BF16)] * 2 + [(own, F32)] * 2, {}
        out_specs, scratch = [VMEM] * 4, [pltpu.VMEM(own, BF16)] * 3
        if fresh:
            aliases = {len(ins) + n: 4 + n for n in range(len(made))}
            ins, specs = ins + made, specs + [HBM] * len(made)
            outs, out_specs = outs + [whole] * 2, out_specs + [HBM] * 2
            scratch.append(pltpu.SemaphoreType.DMA((2,)))
        m, q, *others = call(
            functools.partial(back_kernel, (g, first, count), before[0], size, blocks),
            ins,
            outs,
            in_specs=specs,
            out_specs=out_specs,
            scratch=scratch,
            aliases=aliases,
            flops=9 * unit * count,
        )
        inner[g, first], made[:] = (count, *others[:2]), others[2:]
        fresh[:], before[0] = [m, q], (g, first, count)
        return tuple(others[:2])

    def piece_flush(tied):
        ins, into = [*after(tied, fresh[0]), fresh[1]], list(made)
        made[:] = call(
            functools.partial(flush_kernel, before[0], size),
            ins + into,
            [whole] * 2,
            in_specs=[VMEM] * 2 + [HBM] * len(into),
            out_specs=[HBM] * 2,
            scratch=[pltpu.SemaphoreType.DMA((2,))],
            aliases={2 + n: n for n in range(len(into))},
        )
        return tuple(made)

    def piece_last(g, tied):
        mine = [inner[key] for key in sorted(inner) if key[0] == g]
        ins = [*after(tied, ks[g]), vs[g], suffixes[g]] + [kl for _, kl, _ in mine] + [vl for _, _, vl in mine]
        results[:] = call(
            functools.partial(last_kernel, g, [count for count, _, _ in mine], size),
            ins + results,
            [whole] * 2,
            in_specs=[VMEM] * len(ins) + [HBM] * len(results),
            out_specs=[HBM] * 2,
            scratch=[pltpu.VMEM(part, BF16)] * 2 + [pltpu.SemaphoreType.DMA((2, size))],
            aliases={len(ins) + n: n for n in range(len(results))},
            flops=2 * unit * size,
        )
        return tuple(results)

    def end_last(i, answer):
        suffixes[2 * i] = answer
        return piece_last(2 * i, ())

    piece_grad(0, ())
    drive(
        [lambda i=i: scan_stages(backs[2 * i], lambda: backs[2 * i + 1], seq_size, low, True) for i in range(2)],
        in_events({
            0: [functools.partial(piece_grad, 2)],
            1: [functools.partial(piece_grad, 1), functools.partial(piece_grad, 3)],
            2: [functools.partial(piece_back, 0, 0, size)],
            3: [functools.partial(piece_back, 1, 0, size)],
            5: [functools.partial(piece_back, 2, 0, size), functools.partial(piece_back, 3, 0, size), piece_flush],
            last: [functools.partial(piece_last, 1), functools.partial(piece_last, 3)],
        }),
        lambda i, answer: suffixes.update({2 * i + 1: answer}),
        end_last,
    )
    return (*made, *results)


def solution(mesh):
    placed = (P("seq", "head"), P("seq", "head"), P("seq", "head"), P("head"), P("seq", "head"))
    return jax.shard_map(
        functools.partial(body, mesh.shape["seq"], mesh.shape["head"]),
        mesh=mesh,
        in_specs=placed,
        out_specs=(P("seq", "head"),) * 4,
        check_vma=False,
    )
```

time: 77.9 us -> 74.9 us (0.961)
  waiting for transfers between devices: 21.6 us -> 17.5 us
  Pallas kernels: 27 us -> 29 us
    ppermute x20, waiting for transfers between devices: 18.3 us -> 14.3 us  [drive(): live.append((name, scan, lax.ppermute(operand, 'seq', pairs)))]
    pallas_call x17 -> x23, Pallas kernels: 27 us -> 29 us  [call(): pl.pallas_call(kernel, in_specs=in_specs or [VMEM] * len(ins), out_specs=...]
  transfers between devices with their start and end apart: 22 -> 22, of which waited for: 8 -> 9; matrix products, arithmetic and copies ran while one was open for 1% -> 1% of each run, Pallas kernels for 26% -> 33%
where the time goes in v8:
time: 74.9 us; the launch traced here: 74.6 us
  Pallas kernels  29 us (39%)
  starting transfers between devices  26.4 us (35%)
  waiting for transfers between devices  17.5 us (23%)
  between operations  1.29 us (2%)
    pallas_call x23, Pallas kernels, call(): pl.pallas_call(kernel, in_specs=in_specs or [VMEM] * len(ins), out_specs=...  29 us
    ppermute x20, starting transfers between devices, drive(): live.append((name, scan, lax.ppermute(operand, 'seq', pairs)))  24.8 us
    ppermute x20, waiting for transfers between devices, drive(): live.append((name, scan, lax.ppermute(operand, 'seq', pairs)))  14.3 us
    ppermute x2, waiting for transfers between devices, head_sum(): a = a + lax.ppermute(a, 'head', [(i, i ^ step) for i in range(size)])  3.29 us
    ppermute x2, starting transfers between devices, head_sum(): a = a + lax.ppermute(a, 'head', [(i, i ^ step) for i in range(size)])  1.59 us
  transfers between devices with their start and end apart: 22, of which 9 were waited for; matrix products, arithmetic and copies ran while one was open for 1% of the time, Pallas kernels for 33%

profile of v8, /device:TPU:0, one launch (start us, length us, event | category | flops | bytes accessed | tf_op | source)
XLA Modules:
  0.0 74.6 jit_solution(4818026846487635555)
XLA Ops:
  0.6 1.6 %shard_map.84 = (bf16[1024,256]{1,0:T(8,128)(2,1)S(1)}, bf16[1024,256]{1,0:T(8,128)(2,1)S(1)}, f32[2,128,128]{2,1,0:T(8,128)S(1)}) custom-call(bf16[1024,1024]{1,0:T(8,128)(2,1)} %k_hbm.1, bf16[1024,1024]{1,0:T(8,128)(2,1)} %v_hbm.1), custom_call_target="tpu_custom_call" | custom-call | flops 67108864 | bytes 4194304 | tf_op jit(solution)/shard_map/pallas_call | solution.py:215
  2.2 3.0 %collective-permute-start.1 = (f32[2,128,128]{2,1,0:T(8,128)S(1)}, f32[2,128,128]{2,1,0:T(8,128)S(1)}, u32[]{:S(2)}, u32[]{:S(2)}) collective-permute-start(f32[2,128,128]{2,1,0:T(8,128)S(1)} %get-tuple-element.108), channel_id=1, source_target_pairs={{0,4},{4,0},{8,12},{12,8},{16,20},{20,16},{24,28},{28,24},{1,5},{5... | collective-permute-start | bytes 393224 | tf_op jit(solution)/shard_map/ppermute | solution.py:273
  5.2 2.3 %shard_map.85 = (bf16[1024,256]{1,0:T(8,128)(2,1)S(1)}, bf16[1024,256]{1,0:T(8,128)(2,1)S(1)}, bf16[1024,256]{1,0:T(8,128)(2,1)S(1)}, bf16[1024,256]{1,0:T(8,128...) custom-call(bf16[1024,1024]{1,0:T(8,128)(2,1)} %k_hbm.1, ...), custom_call_target="tpu_custom_call" | custom-call | flops 201326592 | bytes 4194304 | tf_op jit(solution)/shard_map/pallas_call | solution.py:215
  8.8 3.7 %collective-permute-start.3 = (f32[2,128,128]{2,1,0:T(8,128)S(1)}, f32[2,128,128]{2,1,0:T(8,128)S(1)}, u32[]{:S(2)}, u32[]{:S(2)}) collective-permute-start(f32[2,128,128]{2,1,0:T(8,128)S(1)} %add.104), channel_id=1, source_target_pairs={{0,8},{4,12},{1,9},{5,13},{2,10},{6,14},{3,11},{7,15}} | collective-permute-start | bytes 393224 | tf_op jit(solution)/shard_map/ppermute | solution.py:273
  13.4 2.6 %collective-permute-start.2 = (f32[2,128,128]{2,1,0:T(8,128)S(1)}, f32[2,128,128]{2,1,0:T(8,128)S(1)}, u32[]{:S(2)}, u32[]{:S(2)}) collective-permute-start(f32[2,128,128]{2,1,0:T(8,128)S(1)} %add.105), channel_id=1, source_target_pairs={{0,8},{4,12},{1,9},{5,13},{2,10},{6,14},{3,11},{7,15}} | collective-permute-start | bytes 393224 | tf_op jit(solution)/shard_map/ppermute | solution.py:273
  22.7 1.4 %collective-permute-start.8 = (f32[2,128,128]{2,1,0:T(8,128)S(1)}, f32[2,128,128]{2,1,0:T(8,128)S(1)}, u32[]{:S(2)}, u32[]{:S(2)}) collective-permute-start(f32[2,128,128]{2,1,0:T(8,128)S(1)} %get-tuple-element.215), channel_id=1, source_target_pairs={{0,4},{4,0},{8,12},{12,8},{16,20},{20,16},{24,28},{28,24},{1,5},{5... | collective-permute-start | bytes 393224 | tf_op jit(solution)/shard_map/ppermute | solution.py:273
  25.3 1.6 %collective-permute-done.9.p_ref = f32[2,128,128]{2,1,0:T(8,128)S(1)} collective-permute-done((f32[2,128,128]{2,1,0:T(8,128)S(1)}, f32[2,128,128]{2,1,0:T(8,128)S(1)}, u32[]{:S(2)}, u32[]{:S(2)}) %collective-permute-start.9) | collective-permute-done | bytes 131104 | tf_op jit(solution)/shard_map/ppermute | solution.py:273
  29.1 1.2 %collective-permute-done.10 = f32[2,1024]{1,0:T(2,128)S(1)} collective-permute-done((f32[2,1024]{1,0:T(2,128)S(1)}, f32[2,1024]{1,0:T(2,128)S(1)}, u32[]{:S(2)}, u32[]{:S(2)}) %collective-permute-start.10) | collective-permute-done | bytes 8224 | tf_op jit(solution)/shard_map/ppermute | solution.py:294
  30.2 1.5 %collective-permute-start.11 = (f32[2,1024]{1,0:T(2,128)S(1)}, f32[2,1024]{1,0:T(2,128)S(1)}, u32[]{:S(2)}, u32[]{:S(2)}) collective-permute-start(f32[2,1024]{1,0:T(2,128)S(1)} %add.121), channel_id=1, source_target_pairs={{0,2},{1,3},{2,0},{3,1},{4,6},{5,7},{6,4},{7,5},{8,10},{9,11},{10,... | collective-permute-start | bytes 24584 | tf_op jit(solution)/shard_map/ppermute | solution.py:294
  31.7 2.1 %collective-permute-done.11 = f32[2,1024]{1,0:T(2,128)S(1)} collective-permute-done((f32[2,1024]{1,0:T(2,128)S(1)}, f32[2,1024]{1,0:T(2,128)S(1)}, u32[]{:S(2)}, u32[]{:S(2)}) %collective-permute-start.11) | collective-permute-done | bytes 8224 | tf_op jit(solution)/shard_map/ppermute | solution.py:294
  34.7 1.2 %collective-permute-start.13 = (f32[2,128,128]{2,1,0:T(8,128)S(1)}, f32[2,128,128]{2,1,0:T(8,128)S(1)}, u32[]{:S(2)}, u32[]{:S(2)}) collective-permute-start(f32[2,128,128]{2,1,0:T(8,128)S(1)} %get-tuple-element.150), channel_id=1, source_target_pairs={{28,24},{24,28},{20,16},{16,20},{12,8},{8,12},{4,0},{0,4},{29,25},... | collective-permute-start | bytes 393224 | tf_op jit(solution)/shard_map/ppermute | solution.py:273
  38.8 2.0 %collective-permute-done.13 = f32[2,128,128]{2,1,0:T(8,128)S(1)} collective-permute-done((f32[2,128,128]{2,1,0:T(8,128)S(1)}, f32[2,128,128]{2,1,0:T(8,128)S(1)}, u32[]{:S(2)}, u32[]{:S(2)}) %collective-permute-start.13) | collective-permute-done | bytes 131104 | tf_op jit(solution)/shard_map/ppermute | solution.py:273
  41.7 1.9 %shard_map.98 = (bf16[1024,256]{1,0:T(8,128)(2,1)S(1)}, bf16[1024,256]{1,0:T(8,128)(2,1)S(1)}, f32[1024,256]{1,0:T(8,128)S(1)}, f32[1024,256]{1,0:T(8,128)S(1)}) custom-call(bf16[1024,1024]{1,0:T(8,128)(2,1)S(1)} %copy-done, bf16[1024,256]{1,0:T(8,128)(2,1)S(1)} %get-tuple-element.115.k_ref, bf16[1024,256]{1,0:T(8,128)(2,1)S(1)} %get-tuple-element.116.v_ref, ...), custom_call_target="tpu_custom_call" | custom-call | flops 603979776 | bytes 5902336 | tf_op jit(solution)/shard_map/pallas_call | solution.py:215
  44.3 2.7 %shard_map.99 = (bf16[1024,256]{1,0:T(8,128)(2,1)S(1)}, bf16[1024,256]{1,0:T(8,128)(2,1)S(1)}, f32[1024,256]{1,0:T(8,128)S(1)}, f32[1024,256]{1,0:T(8,128)S(1)},...) custom-call(bf16[1024,1024]{1,0:T(8,128)(2,1)S(1)} %copy-done, bf16[1024,256]{1,0:T(8,128)(2,1)S(1)} %get-tuple-element.196.k_ref, ...), custom_call_target="tpu_custom_call" | custom-call | flops 603979776 | bytes 6950912 | tf_op jit(solution)/shard_map/pallas_call | solution.py:215
  48.5 2.8 %shard_map.100 = (bf16[1024,256]{1,0:T(8,128)(2,1)S(1)}, bf16[1024,256]{1,0:T(8,128)(2,1)S(1)}, f32[1024,256]{1,0:T(8,128)S(1)}, f32[1024,256]{1,0:T(8,128)S(1)}...) custom-call(bf16[1024,1024]{1,0:T(8,128)(2,1)S(1)} %copy-done, ...), custom_call_target="tpu_custom_call", output_to_operand_aliasing={{4}: (11, {}), {5}: (12, {})} | custom-call | flops 603979776 | bytes 11145216 | tf_op jit(solution)/shard_map/pallas_call | solution.py:215
  51.3 2.8 %shard_map.101 = (bf16[1024,256]{1,0:T(8,128)(2,1)S(1)}, bf16[1024,256]{1,0:T(8,128)(2,1)S(1)}, f32[1024,256]{1,0:T(8,128)S(1)}, f32[1024,256]{1,0:T(8,128)S(1)}...) custom-call(bf16[1024,1024]{1,0:T(8,128)(2,1)S(1)} %copy-done, ...), custom_call_target="tpu_custom_call", output_to_operand_aliasing={{4}: (11, {}), {5}: (12, {})} | custom-call | flops 603979776 | bytes 11145216 | tf_op jit(solution)/shard_map/pallas_call | solution.py:215
  55.1 1.3 %collective-permute-start.20 = (f32[2,128,128]{2,1,0:T(8,128)S(1)}, f32[2,128,128]{2,1,0:T(8,128)S(1)}, u32[]{:S(2)}, u32[]{:S(2)}) collective-permute-start(f32[2,128,128]{2,1,0:T(8,128)S(1)} %add.132), channel_id=1, source_target_pairs={{12,4},{8,0},{13,5},{9,1},{14,6},{10,2},{15,7},{11,3}} | collective-permute-start | bytes 393224 | tf_op jit(solution)/shard_map/ppermute | solution.py:273
  56.5 1.3 %collective-permute-start.16 = (f32[2,128,128]{2,1,0:T(8,128)S(1)}, f32[2,128,128]{2,1,0:T(8,128)S(1)}, u32[]{:S(2)}, u32[]{:S(2)}) collective-permute-start(f32[2,128,128]{2,1,0:T(8,128)S(1)} %add.127), channel_id=1, source_target_pairs={{12,4},{8,0},{13,5},{9,1},{14,6},{10,2},{15,7},{11,3}} | collective-permute-start | bytes 393224 | tf_op jit(solution)/shard_map/ppermute | solution.py:273
  57.8 7.8 %collective-permute-done.20 = f32[2,128,128]{2,1,0:T(8,128)S(1)} collective-permute-done((f32[2,128,128]{2,1,0:T(8,128)S(1)}, f32[2,128,128]{2,1,0:T(8,128)S(1)}, u32[]{:S(2)}, u32[]{:S(2)}) %collective-permute-start.20) | collective-permute-done | bytes 131104 | tf_op jit(solution)/shard_map/ppermute | solution.py:273
  65.6 1.6 %collective-permute-start.21 = (f32[2,128,128]{2,1,0:T(8,128)S(1)}, f32[2,128,128]{2,1,0:T(8,128)S(1)}, u32[]{:S(2)}, u32[]{:S(2)}) collective-permute-start(f32[2,128,128]{2,1,0:T(8,128)S(1)} %get-tuple-element.211), channel_id=1, source_target_pairs={{28,24},{24,28},{20,16},{16,20},{12,8},{8,12},{4,0},{0,4},{29,25},... | collective-permute-start | bytes 393224 | tf_op jit(solution)/shard_map/ppermute | solution.py:273
  69.2 1.3 %shard_map.103 = (bf16[1024,1024]{1,0:T(8,128)(2,1)}, bf16[1024,1024]{1,0:T(8,128)(2,1)}) custom-call(bf16[1024,256]{1,0:T(8,128)(2,1)S(1)} %get-tuple-element.196.k_ref, bf16[1024,256]{1,0:T(8,128)(2,1)S(1)} %get-tuple-element.122.v_ref, f32[2,128,128]{2,1,0:T(8,128)S(1)} %get-tuple-element.210.s_ref, f32[1024,256]{1,0:T(8,128)S(1)} %get-tuple-element.192.rest_0_, ...), custom_call_target="tpu_custom_call" | custom-call | flops 134217728 | bytes 3276800 | tf_op jit(solution)/shard_map/pallas_call | solution.py:215
  70.5 1.3 %shard_map.104 = (bf16[1024,1024]{1,0:T(8,128)(2,1)}, bf16[1024,1024]{1,0:T(8,128)(2,1)}) custom-call(bf16[1024,256]{1,0:T(8,128)(2,1)S(1)} %get-tuple-element.199.k_ref, bf16[1024,256]{1,0:T(8,128)(2,1)S(1)} %get-tuple-element.134.v_ref, f32[2,128,128]{2,1,0:T(8,128)S(1)} %get-tuple-element.208.s_ref, ...), custom_call_target="tpu_custom_call", output_to_operand_aliasing={{0}: (5, {}), {1}: (6, {})} | custom-call | flops 134217728 | bytes 7471104 | tf_op jit(solution)/shard_map/pallas_call | solution.py:215
  71.8 1.3 %shard_map.105 = (bf16[1024,1024]{1,0:T(8,128)(2,1)}, bf16[1024,1024]{1,0:T(8,128)(2,1)}) custom-call(bf16[1024,256]{1,0:T(8,128)(2,1)S(1)} %get-tuple-element.115.k_ref, bf16[1024,256]{1,0:T(8,128)(2,1)S(1)} %get-tuple-element.116.v_ref, f32[2,128,128]{2,1,0:T(8,128)S(1)} %collective-permute-done.21.s_ref, ...), custom_call_target="tpu_custom_call", output_to_operand_aliasing={{0}: (5, {}), {1}: (6, {})} | custom-call | flops 134217728 | bytes 7471104 | tf_op jit(solution)/shard_map/pallas_call | solution.py:215
  73.2 1.3 %shard_map.106 = (bf16[1024,1024]{1,0:T(8,128)(2,1)}, bf16[1024,1024]{1,0:T(8,128)(2,1)}) custom-call(bf16[1024,256]{1,0:T(8,128)(2,1)S(1)} %get-tuple-element.127.k_ref, bf16[1024,256]{1,0:T(8,128)(2,1)S(1)} %get-tuple-element.128.v_ref, f32[2,128,128]{2,1,0:T(8,128)S(1)} %collective-permute-done.17.s_ref, ...), custom_call_target="tpu_custom_call", output_to_operand_aliasing={{0}: (5, {}), {1}: (6, {})} | custom-call | flops 134217728 | bytes 7471104 | tf_op jit(solution)/shard_map/pallas_call | solution.py:215
  (68 shorter events, 21.6 us)
Async XLA Ops:
  2.2 10.3 %copy-start = (bf16[1024,1024]{1,0:T(8,128)(2,1)S(1)}, bf16[1024,1024]{1,0:T(8,128)(2,1)}, u32[]{:S(2)}) copy-start(bf16[1024,1024]{1,0:T(8,128)(2,1)} %q_ref.18) | copy-start | bytes 6291460
  2.2 6.5 %collective-permute-start.1 = (f32[2,128,128]{2,1,0:T(8,128)S(1)}, f32[2,128,128]{2,1,0:T(8,128)S(1)}, u32[]{:S(2)}, u32[]{:S(2)}) collective-permute-start(f32[2,128,128]{2,1,0:T(8,128)S(1)} %get-tuple-element.108), channel_id=1, source_target_pairs={{0,4},{4,0},{8,12},{12,8},{16,20},{20,16},{24,28},{28,24},{1,5},{5... | collective-permute-start | bytes 393224 | tf_op jit(solution)/shard_map/ppermute | solution.py:273
  7.5 5.9 %collective-permute-start = (f32[2,128,128]{2,1,0:T(8,128)S(1)}, f32[2,128,128]{2,1,0:T(8,128)S(1)}, u32[]{:S(2)}, u32[]{:S(2)}) collective-permute-start(f32[2,128,128]{2,1,0:T(8,128)S(1)} %get-tuple-element.112), channel_id=1, source_target_pairs={{0,4},{4,0},{8,12},{12,8},{16,20},{20,16},{24,28},{28,24},{1,5},{5... | collective-permute-start | bytes 393224 | tf_op jit(solution)/shard_map/ppermute | solution.py:273
  8.8 8.2 %collective-permute-start.3 = (f32[2,128,128]{2,1,0:T(8,128)S(1)}, f32[2,128,128]{2,1,0:T(8,128)S(1)}, u32[]{:S(2)}, u32[]{:S(2)}) collective-permute-start(f32[2,128,128]{2,1,0:T(8,128)S(1)} %add.104), channel_id=1, source_target_pairs={{0,8},{4,12},{1,9},{5,13},{2,10},{6,14},{3,11},{7,15}} | collective-permute-start | bytes 393224 | tf_op jit(solution)/shard_map/ppermute | solution.py:273
  13.4 5.2 %collective-permute-start.2 = (f32[2,128,128]{2,1,0:T(8,128)S(1)}, f32[2,128,128]{2,1,0:T(8,128)S(1)}, u32[]{:S(2)}, u32[]{:S(2)}) collective-permute-start(f32[2,128,128]{2,1,0:T(8,128)S(1)} %add.105), channel_id=1, source_target_pairs={{0,8},{4,12},{1,9},{5,13},{2,10},{6,14},{3,11},{7,15}} | collective-permute-start | bytes 393224 | tf_op jit(solution)/shard_map/ppermute | solution.py:273
  17.0 3.3 %collective-permute-start.6 = (f32[2,128,128]{2,1,0:T(8,128)S(1)}, f32[2,128,128]{2,1,0:T(8,128)S(1)}, u32[]{:S(2)}, u32[]{:S(2)}) collective-permute-start(f32[2,128,128]{2,1,0:T(8,128)S(1)} %add.106), channel_id=1, source_target_pairs={{8,16},{12,20},{9,17},{13,21},{10,18},{14,22},{11,19},{15,23}} | collective-permute-start | bytes 393224 | tf_op jit(solution)/shard_map/ppermute | solution.py:273
  18.7 2.5 %collective-permute-start.4 = (f32[2,128,128]{2,1,0:T(8,128)S(1)}, f32[2,128,128]{2,1,0:T(8,128)S(1)}, u32[]{:S(2)}, u32[]{:S(2)}) collective-permute-start(f32[2,128,128]{2,1,0:T(8,128)S(1)} %add.107), channel_id=1, source_target_pairs={{8,16},{12,20},{9,17},{13,21},{10,18},{14,22},{11,19},{15,23}} | collective-permute-start | bytes 393224 | tf_op jit(solution)/shard_map/ppermute | solution.py:273
  20.3 3.8 %copy-start.1 = (bf16[1024,1024]{1,0:T(8,128)(2,1)S(1)}, bf16[1024,1024]{1,0:T(8,128)(2,1)}, u32[]{:S(2)}) copy-start(bf16[1024,1024]{1,0:T(8,128)(2,1)} %og_ref.15) | copy-start | bytes 6291460
  20.3 1.5 %collective-permute-start.7 = (f32[2,128,128]{2,1,0:T(8,128)S(1)}, f32[2,128,128]{2,1,0:T(8,128)S(1)}, u32[]{:S(2)}, u32[]{:S(2)}) collective-permute-start(f32[2,128,128]{2,1,0:T(8,128)S(1)} %add.113), channel_id=1, source_target_pairs={{16,24},{20,28},{17,25},{21,29},{18,26},{22,30},{19,27},{23,31}} | collective-permute-start | bytes 393224 | tf_op jit(solution)/shard_map/ppermute | solution.py:273
  21.2 1.5 %collective-permute-start.5 = (f32[2,128,128]{2,1,0:T(8,128)S(1)}, f32[2,128,128]{2,1,0:T(8,128)S(1)}, u32[]{:S(2)}, u32[]{:S(2)}) collective-permute-start(f32[2,128,128]{2,1,0:T(8,128)S(1)} %add.109), channel_id=1, source_target_pairs={{16,24},{20,28},{17,25},{21,29},{18,26},{22,30},{19,27},{23,31}} | collective-permute-start | bytes 393224 | tf_op jit(solution)/shard_map/ppermute | solution.py:273
  21.9 5.0 %collective-permute-start.9 = (f32[2,128,128]{2,1,0:T(8,128)S(1)}, f32[2,128,128]{2,1,0:T(8,128)S(1)}, u32[]{:S(2)}, u32[]{:S(2)}) collective-permute-start(f32[2,128,128]{2,1,0:T(8,128)S(1)} %get-tuple-element.212), channel_id=1, source_target_pairs={{0,4},{4,0},{8,12},{12,8},{16,20},{20,16},{24,28},{28,24},{1,5},{5... | collective-permute-start | bytes 393224 | tf_op jit(solution)/shard_map/ppermute | solution.py:273
  22.7 5.6 %collective-permute-start.8 = (f32[2,128,128]{2,1,0:T(8,128)S(1)}, f32[2,128,128]{2,1,0:T(8,128)S(1)}, u32[]{:S(2)}, u32[]{:S(2)}) collective-permute-start(f32[2,128,128]{2,1,0:T(8,128)S(1)} %get-tuple-element.215), channel_id=1, source_target_pairs={{0,4},{4,0},{8,12},{12,8},{16,20},{20,16},{24,28},{28,24},{1,5},{5... | collective-permute-start | bytes 393224 | tf_op jit(solution)/shard_map/ppermute | solution.py:273
  29.0 1.2 %collective-permute-start.10 = (f32[2,1024]{1,0:T(2,128)S(1)}, f32[2,1024]{1,0:T(2,128)S(1)}, u32[]{:S(2)}, u32[]{:S(2)}) collective-permute-start(f32[2,1024]{1,0:T(2,128)S(1)} %add_add_fusion.4), channel_id=1, source_target_pairs={{0,1},{1,0},{2,3},{3,2},{4,5},{5,4},{6,7},{7,6},{8,9},{9,8},{10,11... | collective-permute-start | bytes 24584 | tf_op jit(solution)/shard_map/ppermute | solution.py:294
  30.2 3.7 %collective-permute-start.11 = (f32[2,1024]{1,0:T(2,128)S(1)}, f32[2,1024]{1,0:T(2,128)S(1)}, u32[]{:S(2)}, u32[]{:S(2)}) collective-permute-start(f32[2,1024]{1,0:T(2,128)S(1)} %add.121), channel_id=1, source_target_pairs={{0,2},{1,3},{2,0},{3,1},{4,6},{5,7},{6,4},{7,5},{8,10},{9,11},{10,... | collective-permute-start | bytes 24584 | tf_op jit(solution)/shard_map/ppermute | solution.py:294
  34.7 6.1 %collective-permute-start.13 = (f32[2,128,128]{2,1,0:T(8,128)S(1)}, f32[2,128,128]{2,1,0:T(8,128)S(1)}, u32[]{:S(2)}, u32[]{:S(2)}) collective-permute-start(f32[2,128,128]{2,1,0:T(8,128)S(1)} %get-tuple-element.150), channel_id=1, source_target_pairs={{28,24},{24,28},{20,16},{16,20},{12,8},{8,12},{4,0},{0,4},{29,25},... | collective-permute-start | bytes 393224 | tf_op jit(solution)/shard_map/ppermute | solution.py:273
  36.6 7.0 %collective-permute-start.12 = (f32[2,128,128]{2,1,0:T(8,128)S(1)}, f32[2,128,128]{2,1,0:T(8,128)S(1)}, u32[]{:S(2)}, u32[]{:S(2)}) collective-permute-start(f32[2,128,128]{2,1,0:T(8,128)S(1)} %get-tuple-element.154), channel_id=1, source_target_pairs={{28,24},{24,28},{20,16},{16,20},{12,8},{8,12},{4,0},{0,4},{29,25},... | collective-permute-start | bytes 393224 | tf_op jit(solution)/shard_map/ppermute | solution.py:273
  40.8 6.3 %collective-permute-start.18 = (f32[2,128,128]{2,1,0:T(8,128)S(1)}, f32[2,128,128]{2,1,0:T(8,128)S(1)}, u32[]{:S(2)}, u32[]{:S(2)}) collective-permute-start(f32[2,128,128]{2,1,0:T(8,128)S(1)} %add.123), channel_id=1, source_target_pairs={{28,20},{24,16},{29,21},{25,17},{30,22},{26,18},{31,23},{27,19}} | collective-permute-start | bytes 393224 | tf_op jit(solution)/shard_map/ppermute | solution.py:273
  43.7 4.1 %collective-permute-start.14 = (f32[2,128,128]{2,1,0:T(8,128)S(1)}, f32[2,128,128]{2,1,0:T(8,128)S(1)}, u32[]{:S(2)}, u32[]{:S(2)}) collective-permute-start(f32[2,128,128]{2,1,0:T(8,128)S(1)} %add.124), channel_id=1, source_target_pairs={{28,20},{24,16},{29,21},{25,17},{30,22},{26,18},{31,23},{27,19}} | collective-permute-start | bytes 393224 | tf_op jit(solution)/shard_map/ppermute | solution.py:273
  47.1 8.0 %collective-permute-start.19 = (f32[2,128,128]{2,1,0:T(8,128)S(1)}, f32[2,128,128]{2,1,0:T(8,128)S(1)}, u32[]{:S(2)}, u32[]{:S(2)}) collective-permute-start(f32[2,128,128]{2,1,0:T(8,128)S(1)} %add.130), channel_id=1, source_target_pairs={{20,12},{16,8},{21,13},{17,9},{22,14},{18,10},{23,15},{19,11}} | collective-permute-start | bytes 393224 | tf_op jit(solution)/shard_map/ppermute | solution.py:273
  47.8 8.6 %collective-permute-start.15 = (f32[2,128,128]{2,1,0:T(8,128)S(1)}, f32[2,128,128]{2,1,0:T(8,128)S(1)}, u32[]{:S(2)}, u32[]{:S(2)}) collective-permute-start(f32[2,128,128]{2,1,0:T(8,128)S(1)} %add.125), channel_id=1, source_target_pairs={{20,12},{16,8},{21,13},{17,9},{22,14},{18,10},{23,15},{19,11}} | collective-permute-start | bytes 393224 | tf_op jit(solution)/shard_map/ppermute | solution.py:273
  55.1 10.5 %collective-permute-start.20 = (f32[2,128,128]{2,1,0:T(8,128)S(1)}, f32[2,128,128]{2,1,0:T(8,128)S(1)}, u32[]{:S(2)}, u32[]{:S(2)}) collective-permute-start(f32[2,128,128]{2,1,0:T(8,128)S(1)} %add.132), channel_id=1, source_target_pairs={{12,4},{8,0},{13,5},{9,1},{14,6},{10,2},{15,7},{11,3}} | collective-permute-start | bytes 393224 | tf_op jit(solution)/shard_map/ppermute | solution.py:273
  56.5 11.6 %collective-permute-start.16 = (f32[2,128,128]{2,1,0:T(8,128)S(1)}, f32[2,128,128]{2,1,0:T(8,128)S(1)}, u32[]{:S(2)}, u32[]{:S(2)}) collective-permute-start(f32[2,128,128]{2,1,0:T(8,128)S(1)} %add.127), channel_id=1, source_target_pairs={{12,4},{8,0},{13,5},{9,1},{14,6},{10,2},{15,7},{11,3}} | collective-permute-start | bytes 393224 | tf_op jit(solution)/shard_map/ppermute | solution.py:273
  65.6 6.1 %collective-permute-start.21 = (f32[2,128,128]{2,1,0:T(8,128)S(1)}, f32[2,128,128]{2,1,0:T(8,128)S(1)}, u32[]{:S(2)}, u32[]{:S(2)}) collective-permute-start(f32[2,128,128]{2,1,0:T(8,128)S(1)} %get-tuple-element.211), channel_id=1, source_target_pairs={{28,24},{24,28},{20,16},{16,20},{12,8},{8,12},{4,0},{0,4},{29,25},... | collective-permute-start | bytes 393224 | tf_op jit(solution)/shard_map/ppermute | solution.py:273
  68.1 5.0 %collective-permute-start.17 = (f32[2,128,128]{2,1,0:T(8,128)S(1)}, f32[2,128,128]{2,1,0:T(8,128)S(1)}, u32[]{:S(2)}, u32[]{:S(2)}) collective-permute-start(f32[2,128,128]{2,1,0:T(8,128)S(1)} %get-tuple-element.209), channel_id=1, source_target_pairs={{28,24},{24,28},{20,16},{16,20},{12,8},{8,12},{4,0},{0,4},{29,25},... | collective-permute-start | bytes 393224 | tf_op jit(solution)/shard_map/ppermute | solution.py:273
  (1 other events, 3.8 us)

commit v9 on v8

--- a/solution.py
+++ b/solution.py
@@ -133,11 +133,11 @@
 def back_kernel(here, before, size, blocks, q_ref, k_ref, v_ref, w_ref, g_ref, p_ref, a_ref, gain_ref, inv_ref, *rest):
     at = places(size)
     copies = []
-    if before is not None:
-        old_m, old_q = rest[:2]
+    if before:
         m_ref, qg_ref, kl_ref, vl_ref, m_hbm, q_hbm, bw, plow, slow, sems = rest[-10:]
-        there = at(*before)
-        copies = flush([(old_m, m_hbm.at[:, there]), (old_q, q_hbm.at[:, there])], sems)
+        for n, where in enumerate(before):
+            there = at(*where)
+            copies += flush([(rest[2 * n], m_hbm.at[:, there]), (rest[2 * n + 1], q_hbm.at[:, there])], sems.at[n])
     else:
         m_ref, qg_ref, kl_ref, vl_ref, bw, plow, slow = rest
     causal = causal_mask()
@@ -357,10 +357,8 @@
         [lambda i=i: scan_stages(states[2 * i], lambda: states[2 * i + 1], seq_size, low, False) for i in range(2)],
         in_events({
             0: [functools.partial(piece_load, [1, 2, 3])],
-            2: [functools.partial(piece_local, 0)],
-            3: [functools.partial(piece_local, 1)],
-            4: [functools.partial(piece_local, 2)],
-            5: [functools.partial(piece_local, 3)],
+            3: [functools.partial(piece_local, 0), functools.partial(piece_local, 1)],
+            5: [functools.partial(piece_local, 2), functools.partial(piece_local, 3)],
             last: [functools.partial(piece_stats, 1), functools.partial(piece_stats, 3)],
         }),
         lambda i, answer: prefixes.update({2 * i + 1: answer}),
@@ -368,7 +366,7 @@
     )
     total = head_sum(sum(sums[g] for g in range(1, 4)) + sums[0], head_size)
 
-    factors, inner, made, fresh, before, suffixes, results = [], {}, [], [], [None], {}, []
+    factors, inner, made, fresh, suffixes, results = [], {}, [], [], {}, []
 
     def piece_grad(g, tied):
         (q,) = after(tied, queries)
@@ -381,19 +379,21 @@
         factors.extend(new)
         return (backs[g],)
 
-    def piece_back(g, first, count, tied):
+    def piece_back(g, first, count, out, tied):
         (q,) = after(tied, queries)
-        ins = [q, ks[g], vs[g], weights[g], grads[g], prefixes[g], atts[g], gain, factors[0], *fresh]
+        old = list(fresh) if out else []
+        ins = [q, ks[g], vs[g], weights[g], grads[g], prefixes[g], atts[g], gain, factors[0]]
+        ins += [a for _, *pair in old for a in pair]
         own = (rows, count * HEAD_DIM)
         specs, outs, aliases = [VMEM] * len(ins), [(own, BF16)] * 2 + [(own, F32)] * 2, {}
         out_specs, scratch = [VMEM] * 4, [pltpu.VMEM(own, BF16)] * 3
-        if fresh:
+        if old:
             aliases = {len(ins) + n: 4 + n for n in range(len(made))}
             ins, specs = ins + made, specs + [HBM] * len(made)
             outs, out_specs = outs + [whole] * 2, out_specs + [HBM] * 2
-            scratch.append(pltpu.SemaphoreType.DMA((2,)))
+            scratch.append(pltpu.SemaphoreType.DMA((len(old), 2)))
         m, q, *others = call(
-            functools.partial(back_kernel, (g, first, count), before[0], size, blocks),
+            functools.partial(back_kernel, (g, first, count), [where for where, _, _ in old], size, blocks),
             ins,
             outs,
             in_specs=specs,
@@ -402,14 +402,18 @@
             aliases=aliases,
             flops=9 * unit * count,
         )
-        inner[g, first], made[:] = (count, *others[:2]), others[2:]
-        fresh[:], before[0] = [m, q], (g, first, count)
+        inner[g, first] = (count, *others[:2])
+        if old:
+            made[:] = others[2:]
+            fresh.clear()
+        fresh.append(((g, first, count), m, q))
         return tuple(others[:2])
 
     def piece_flush(tied):
-        ins, into = [*after(tied, fresh[0]), fresh[1]], list(made)
+        ((where, m, q),) = fresh
+        ins, into = [*after(tied, m), q], list(made)
         made[:] = call(
-            functools.partial(flush_kernel, before[0], size),
+            functools.partial(flush_kernel, where, size),
             ins + into,
             [whole] * 2,
             in_specs=[VMEM] * 2 + [HBM] * len(into),
@@ -442,11 +446,10 @@
     drive(
         [lambda i=i: scan_stages(backs[2 * i], lambda: backs[2 * i + 1], seq_size, low, True) for i in range(2)],
         in_events({
-            0: [functools.partial(piece_grad, 2)],
-            1: [functools.partial(piece_grad, 1), functools.partial(piece_grad, 3)],
-            2: [functools.partial(piece_back, 0, 0, size)],
-            3: [functools.partial(piece_back, 1, 0, size)],
-            5: [functools.partial(piece_back, 2, 0, size), functools.partial(piece_back, 3, 0, size), piece_flush],
+            0: [functools.partial(piece_grad, 2), functools.partial(piece_grad, 1)],
+            1: [functools.partial(piece_grad, 3)],
+            3: [functools.partial(piece_back, 0, 0, size, False), functools.partial(piece_back, 1, 0, size, False)],
+            5: [functools.partial(piece_back, 2, 0, size, True), functools.partial(piece_back, 3, 0, size, True), piece_flush],
             last: [functools.partial(piece_last, 1), functools.partial(piece_last, 3)],
         }),
         lambda i, answer: suffixes.update({2 * i + 1: answer}),

time: 74.9 us -> 73.7 us (0.984)
  transfers between devices with their start and end apart: 22 -> 22, of which waited for: 9 -> 12; matrix products, arithmetic and copies ran while one was open for 1% -> 1% of each run, Pallas kernels for 33% -> 33%
where the time goes in v9:
time: 73.7 us; the launch traced here: 73.3 us
  Pallas kernels  28.5 us (39%)
  starting transfers between devices  26.1 us (35%)
  waiting for transfers between devices  17.1 us (23%)
  between operations  1.26 us (2%)
    pallas_call x23, Pallas kernels, call(): pl.pallas_call(kernel, in_specs=in_specs or [VMEM] * len(ins), out_specs=...  28.5 us
    ppermute x20, starting transfers between devices, drive(): live.append((name, scan, lax.ppermute(operand, 'seq', pairs)))  24.5 us
    ppermute x20, waiting for transfers between devices, drive(): live.append((name, scan, lax.ppermute(operand, 'seq', pairs)))  13.8 us
    ppermute x2, waiting for transfers between devices, head_sum(): a = a + lax.ppermute(a, 'head', [(i, i ^ step) for i in range(size)])  3.3 us
    ppermute x2, starting transfers between devices, head_sum(): a = a + lax.ppermute(a, 'head', [(i, i ^ step) for i in range(size)])  1.58 us
  transfers between devices with their start and end apart: 22, of which 12 were waited for; matrix products, arithmetic and copies ran while one was open for 1% of the time, Pallas kernels for 33%

profile of v9, /device:TPU:0, one launch (start us, length us, event | category | flops | bytes accessed | tf_op | source)
XLA Modules:
  0.0 73.3 jit_solution(749976877043831803)
XLA Ops:
  0.6 1.6 %shard_map.84 = (bf16[1024,256]{1,0:T(8,128)(2,1)S(1)}, bf16[1024,256]{1,0:T(8,128)(2,1)S(1)}, f32[2,128,128]{2,1,0:T(8,128)S(1)}) custom-call(bf16[1024,1024]{1,0:T(8,128)(2,1)} %k_hbm.1, bf16[1024,1024]{1,0:T(8,128)(2,1)} %v_hbm.1), custom_call_target="tpu_custom_call" | custom-call | flops 67108864 | bytes 4194304 | tf_op jit(solution)/shard_map/pallas_call | solution.py:215
  2.2 3.0 %collective-permute-start.4 = (f32[2,128,128]{2,1,0:T(8,128)S(1)}, f32[2,128,128]{2,1,0:T(8,128)S(1)}, u32[]{:S(2)}, u32[]{:S(2)}) collective-permute-start(f32[2,128,128]{2,1,0:T(8,128)S(1)} %get-tuple-element.102), channel_id=1, source_target_pairs={{0,4},{4,0},{8,12},{12,8},{16,20},{20,16},{24,28},{28,24},{1,5},{5... | collective-permute-start | bytes 393224 | tf_op jit(solution)/shard_map/ppermute | solution.py:273
  5.2 2.3 %shard_map.85 = (bf16[1024,256]{1,0:T(8,128)(2,1)S(1)}, bf16[1024,256]{1,0:T(8,128)(2,1)S(1)}, bf16[1024,256]{1,0:T(8,128)(2,1)S(1)}, bf16[1024,256]{1,0:T(8,128...) custom-call(bf16[1024,1024]{1,0:T(8,128)(2,1)} %k_hbm.1, ...), custom_call_target="tpu_custom_call" | custom-call | flops 201326592 | bytes 4194304 | tf_op jit(solution)/shard_map/pallas_call | solution.py:215
  8.8 3.7 %collective-permute-start.5 = (f32[2,128,128]{2,1,0:T(8,128)S(1)}, f32[2,128,128]{2,1,0:T(8,128)S(1)}, u32[]{:S(2)}, u32[]{:S(2)}) collective-permute-start(f32[2,128,128]{2,1,0:T(8,128)S(1)} %add.110), channel_id=1, source_target_pairs={{0,8},{4,12},{1,9},{5,13},{2,10},{6,14},{3,11},{7,15}} | collective-permute-start | bytes 393224 | tf_op jit(solution)/shard_map/ppermute | solution.py:273
  12.6 3.5 %collective-permute-start.1 = (f32[2,128,128]{2,1,0:T(8,128)S(1)}, f32[2,128,128]{2,1,0:T(8,128)S(1)}, u32[]{:S(2)}, u32[]{:S(2)}) collective-permute-start(f32[2,128,128]{2,1,0:T(8,128)S(1)} %add.104), channel_id=1, source_target_pairs={{0,8},{4,12},{1,9},{5,13},{2,10},{6,14},{3,11},{7,15}} | collective-permute-start | bytes 393224 | tf_op jit(solution)/shard_map/ppermute | solution.py:273
  23.6 1.4 %collective-permute-start.8 = (f32[2,128,128]{2,1,0:T(8,128)S(1)}, f32[2,128,128]{2,1,0:T(8,128)S(1)}, u32[]{:S(2)}, u32[]{:S(2)}) collective-permute-start(f32[2,128,128]{2,1,0:T(8,128)S(1)} %get-tuple-element.203), channel_id=1, source_target_pairs={{0,4},{4,0},{8,12},{12,8},{16,20},{20,16},{24,28},{28,24},{1,5},{5... | collective-permute-start | bytes 393224 | tf_op jit(solution)/shard_map/ppermute | solution.py:273
  26.2 1.6 %collective-permute-done.9.p_ref = f32[2,128,128]{2,1,0:T(8,128)S(1)} collective-permute-done((f32[2,128,128]{2,1,0:T(8,128)S(1)}, f32[2,128,128]{2,1,0:T(8,128)S(1)}, u32[]{:S(2)}, u32[]{:S(2)}) %collective-permute-start.9) | collective-permute-done | bytes 131104 | tf_op jit(solution)/shard_map/ppermute | solution.py:273
  30.0 1.2 %collective-permute-done.10 = f32[2,1024]{1,0:T(2,128)S(1)} collective-permute-done((f32[2,1024]{1,0:T(2,128)S(1)}, f32[2,1024]{1,0:T(2,128)S(1)}, u32[]{:S(2)}, u32[]{:S(2)}) %collective-permute-start.10) | collective-permute-done | bytes 8224 | tf_op jit(solution)/shard_map/ppermute | solution.py:294
  31.1 1.5 %collective-permute-start.11 = (f32[2,1024]{1,0:T(2,128)S(1)}, f32[2,1024]{1,0:T(2,128)S(1)}, u32[]{:S(2)}, u32[]{:S(2)}) collective-permute-start(f32[2,1024]{1,0:T(2,128)S(1)} %add.121), channel_id=1, source_target_pairs={{0,2},{1,3},{2,0},{3,1},{4,6},{5,7},{6,4},{7,5},{8,10},{9,11},{10,... | collective-permute-start | bytes 24584 | tf_op jit(solution)/shard_map/ppermute | solution.py:294
  32.6 2.1 %collective-permute-done.11 = f32[2,1024]{1,0:T(2,128)S(1)} collective-permute-done((f32[2,1024]{1,0:T(2,128)S(1)}, f32[2,1024]{1,0:T(2,128)S(1)}, u32[]{:S(2)}, u32[]{:S(2)}) %collective-permute-start.11) | collective-permute-done | bytes 8224 | tf_op jit(solution)/shard_map/ppermute | solution.py:294
  35.6 1.3 %collective-permute-start.17 = (f32[2,128,128]{2,1,0:T(8,128)S(1)}, f32[2,128,128]{2,1,0:T(8,128)S(1)}, u32[]{:S(2)}, u32[]{:S(2)}) collective-permute-start(f32[2,128,128]{2,1,0:T(8,128)S(1)} %get-tuple-element.142), channel_id=1, source_target_pairs={{28,24},{24,28},{20,16},{16,20},{12,8},{8,12},{4,0},{0,4},{29,25},... | collective-permute-start | bytes 393224 | tf_op jit(solution)/shard_map/ppermute | solution.py:273
  39.7 2.1 %collective-permute-done.17 = f32[2,128,128]{2,1,0:T(8,128)S(1)} collective-permute-done((f32[2,128,128]{2,1,0:T(8,128)S(1)}, f32[2,128,128]{2,1,0:T(8,128)S(1)}, u32[]{:S(2)}, u32[]{:S(2)}) %collective-permute-start.17) | collective-permute-done | bytes 131104 | tf_op jit(solution)/shard_map/ppermute | solution.py:273
  44.0 1.9 %shard_map.97 = (bf16[1024,256]{1,0:T(8,128)(2,1)S(1)}, bf16[1024,256]{1,0:T(8,128)(2,1)S(1)}, f32[1024,256]{1,0:T(8,128)S(1)}, f32[1024,256]{1,0:T(8,128)S(1)}) custom-call(bf16[1024,1024]{1,0:T(8,128)(2,1)S(1)} %copy-done, bf16[1024,256]{1,0:T(8,128)(2,1)S(1)} %get-tuple-element.117.k_ref, bf16[1024,256]{1,0:T(8,128)(2,1)S(1)} %get-tuple-element.118.v_ref, ...), custom_call_target="tpu_custom_call" | custom-call | flops 603979776 | bytes 5902336 | tf_op jit(solution)/shard_map/pallas_call | solution.py:215
  46.0 1.9 %shard_map.99 = (bf16[1024,256]{1,0:T(8,128)(2,1)S(1)}, bf16[1024,256]{1,0:T(8,128)(2,1)S(1)}, f32[1024,256]{1,0:T(8,128)S(1)}, f32[1024,256]{1,0:T(8,128)S(1)}) custom-call(bf16[1024,1024]{1,0:T(8,128)(2,1)S(1)} %copy-done, bf16[1024,256]{1,0:T(8,128)(2,1)S(1)} %get-tuple-element.184.k_ref, bf16[1024,256]{1,0:T(8,128)(2,1)S(1)} %get-tuple-element.123.v_ref, ...), custom_call_target="tpu_custom_call" | custom-call | flops 603979776 | bytes 5902336 | tf_op jit(solution)/shard_map/pallas_call | solution.py:215
  49.3 3.1 %shard_map.100 = (bf16[1024,256]{1,0:T(8,128)(2,1)S(1)}, bf16[1024,256]{1,0:T(8,128)(2,1)S(1)}, f32[1024,256]{1,0:T(8,128)S(1)}, f32[1024,256]{1,0:T(8,128)S(1)}...) custom-call(bf16[1024,1024]{1,0:T(8,128)(2,1)S(1)} %copy-done, bf16[1024,256]{1,0:T(8,128)(2,1)S(1)} %get-tuple-element.108.k_ref, ...), custom_call_target="tpu_custom_call" | custom-call | flops 603979776 | bytes 7999488 | tf_op jit(solution)/shard_map/pallas_call | solution.py:215
  52.4 2.8 %shard_map.101 = (bf16[1024,256]{1,0:T(8,128)(2,1)S(1)}, bf16[1024,256]{1,0:T(8,128)(2,1)S(1)}, f32[1024,256]{1,0:T(8,128)S(1)}, f32[1024,256]{1,0:T(8,128)S(1)}...) custom-call(bf16[1024,1024]{1,0:T(8,128)(2,1)S(1)} %copy-done, ...), custom_call_target="tpu_custom_call", output_to_operand_aliasing={{4}: (11, {}), {5}: (12, {})} | custom-call | flops 603979776 | bytes 11145216 | tf_op jit(solution)/shard_map/pallas_call | solution.py:215
  55.2 1.0 %shard_map.102 = (bf16[1024,1024]{1,0:T(8,128)(2,1)}, bf16[1024,1024]{1,0:T(8,128)(2,1)}) custom-call(bf16[1024,256]{1,0:T(8,128)(2,1)S(1)} %get-tuple-element.172.a_ref, bf16[1024,256]{1,0:T(8,128)(2,1)S(1)} %get-tuple-element.173.b_ref, bf16[1024,1024]{1,0:T(8,128)(2,1)} %get-tuple-element.174.rest_0_, ...), custom_call_target="tpu_custom_call", output_to_operand_aliasing={{0}: (2, {}), {1}: (3, {})} | custom-call | bytes 5242880 | tf_op jit(solution)/shard_map/pallas_call | solution.py:215
  56.3 1.3 %collective-permute-start.20 = (f32[2,128,128]{2,1,0:T(8,128)S(1)}, f32[2,128,128]{2,1,0:T(8,128)S(1)}, u32[]{:S(2)}, u32[]{:S(2)}) collective-permute-start(f32[2,128,128]{2,1,0:T(8,128)S(1)} %add.132), channel_id=1, source_target_pairs={{12,4},{8,0},{13,5},{9,1},{14,6},{10,2},{15,7},{11,3}} | collective-permute-start | bytes 393224 | tf_op jit(solution)/shard_map/ppermute | solution.py:273
  57.6 1.3 %collective-permute-start.15 = (f32[2,128,128]{2,1,0:T(8,128)S(1)}, f32[2,128,128]{2,1,0:T(8,128)S(1)}, u32[]{:S(2)}, u32[]{:S(2)}) collective-permute-start(f32[2,128,128]{2,1,0:T(8,128)S(1)} %add.126), channel_id=1, source_target_pairs={{12,4},{8,0},{13,5},{9,1},{14,6},{10,2},{15,7},{11,3}} | collective-permute-start | bytes 393224 | tf_op jit(solution)/shard_map/ppermute | solution.py:273
  58.9 6.5 %collective-permute-done.20 = f32[2,128,128]{2,1,0:T(8,128)S(1)} collective-permute-done((f32[2,128,128]{2,1,0:T(8,128)S(1)}, f32[2,128,128]{2,1,0:T(8,128)S(1)}, u32[]{:S(2)}, u32[]{:S(2)}) %collective-permute-start.20) | collective-permute-done | bytes 131104 | tf_op jit(solution)/shard_map/ppermute | solution.py:273
  67.6 1.3 %shard_map.103 = (bf16[1024,1024]{1,0:T(8,128)(2,1)}, bf16[1024,1024]{1,0:T(8,128)(2,1)}) custom-call(bf16[1024,256]{1,0:T(8,128)(2,1)S(1)} %get-tuple-element.184.k_ref, bf16[1024,256]{1,0:T(8,128)(2,1)S(1)} %get-tuple-element.123.v_ref, f32[2,128,128]{2,1,0:T(8,128)S(1)} %get-tuple-element.198.s_ref, f32[1024,256]{1,0:T(8,128)S(1)} %get-tuple-element.180.rest_0_, ...), custom_call_target="tpu_custom_call" | custom-call | flops 134217728 | bytes 3276800 | tf_op jit(solution)/shard_map/pallas_call | solution.py:215
  69.0 1.3 %shard_map.104 = (bf16[1024,1024]{1,0:T(8,128)(2,1)}, bf16[1024,1024]{1,0:T(8,128)(2,1)}) custom-call(bf16[1024,256]{1,0:T(8,128)(2,1)S(1)} %get-tuple-element.187.k_ref, bf16[1024,256]{1,0:T(8,128)(2,1)S(1)} %get-tuple-element.114.v_ref, f32[2,128,128]{2,1,0:T(8,128)S(1)} %get-tuple-element.196.s_ref, ...), custom_call_target="tpu_custom_call", output_to_operand_aliasing={{0}: (5, {}), {1}: (6, {})} | custom-call | flops 134217728 | bytes 7471104 | tf_op jit(solution)/shard_map/pallas_call | solution.py:215
  70.5 1.3 %shard_map.105 = (bf16[1024,1024]{1,0:T(8,128)(2,1)}, bf16[1024,1024]{1,0:T(8,128)(2,1)}) custom-call(bf16[1024,256]{1,0:T(8,128)(2,1)S(1)} %get-tuple-element.117.k_ref, bf16[1024,256]{1,0:T(8,128)(2,1)S(1)} %get-tuple-element.118.v_ref, f32[2,128,128]{2,1,0:T(8,128)S(1)} %collective-permute-done.21.s_ref, ...), custom_call_target="tpu_custom_call", output_to_operand_aliasing={{0}: (5, {}), {1}: (6, {})} | custom-call | flops 134217728 | bytes 7471104 | tf_op jit(solution)/shard_map/pallas_call | solution.py:215
  71.9 1.3 %shard_map.106 = (bf16[1024,1024]{1,0:T(8,128)(2,1)}, bf16[1024,1024]{1,0:T(8,128)(2,1)}) custom-call(bf16[1024,256]{1,0:T(8,128)(2,1)S(1)} %get-tuple-element.108.k_ref, bf16[1024,256]{1,0:T(8,128)(2,1)S(1)} %get-tuple-element.109.v_ref, f32[2,128,128]{2,1,0:T(8,128)S(1)} %collective-permute-done.16.s_ref, ...), custom_call_target="tpu_custom_call", output_to_operand_aliasing={{0}: (5, {}), {1}: (6, {})} | custom-call | flops 134217728 | bytes 7471104 | tf_op jit(solution)/shard_map/pallas_call | solution.py:215
  (68 shorter events, 21.8 us)
Async XLA Ops:
  2.2 13.9 %copy-start = (bf16[1024,1024]{1,0:T(8,128)(2,1)S(1)}, bf16[1024,1024]{1,0:T(8,128)(2,1)}, u32[]{:S(2)}) copy-start(bf16[1024,1024]{1,0:T(8,128)(2,1)} %q_ref.18) | copy-start | bytes 6291460
  2.2 6.5 %collective-permute-start.4 = (f32[2,128,128]{2,1,0:T(8,128)S(1)}, f32[2,128,128]{2,1,0:T(8,128)S(1)}, u32[]{:S(2)}, u32[]{:S(2)}) collective-permute-start(f32[2,128,128]{2,1,0:T(8,128)S(1)} %get-tuple-element.102), channel_id=1, source_target_pairs={{0,4},{4,0},{8,12},{12,8},{16,20},{20,16},{24,28},{28,24},{1,5},{5... | collective-permute-start | bytes 393224 | tf_op jit(solution)/shard_map/ppermute | solution.py:273
  7.5 5.0 %collective-permute-start = (f32[2,128,128]{2,1,0:T(8,128)S(1)}, f32[2,128,128]{2,1,0:T(8,128)S(1)}, u32[]{:S(2)}, u32[]{:S(2)}) collective-permute-start(f32[2,128,128]{2,1,0:T(8,128)S(1)} %get-tuple-element.106), channel_id=1, source_target_pairs={{0,4},{4,0},{8,12},{12,8},{16,20},{20,16},{24,28},{28,24},{1,5},{5... | collective-permute-start | bytes 393224 | tf_op jit(solution)/shard_map/ppermute | solution.py:273
  8.8 9.1 %collective-permute-start.5 = (f32[2,128,128]{2,1,0:T(8,128)S(1)}, f32[2,128,128]{2,1,0:T(8,128)S(1)}, u32[]{:S(2)}, u32[]{:S(2)}) collective-permute-start(f32[2,128,128]{2,1,0:T(8,128)S(1)} %add.110), channel_id=1, source_target_pairs={{0,8},{4,12},{1,9},{5,13},{2,10},{6,14},{3,11},{7,15}} | collective-permute-start | bytes 393224 | tf_op jit(solution)/shard_map/ppermute | solution.py:273
  12.6 6.0 %collective-permute-start.1 = (f32[2,128,128]{2,1,0:T(8,128)S(1)}, f32[2,128,128]{2,1,0:T(8,128)S(1)}, u32[]{:S(2)}, u32[]{:S(2)}) collective-permute-start(f32[2,128,128]{2,1,0:T(8,128)S(1)} %add.104), channel_id=1, source_target_pairs={{0,8},{4,12},{1,9},{5,13},{2,10},{6,14},{3,11},{7,15}} | collective-permute-start | bytes 393224 | tf_op jit(solution)/shard_map/ppermute | solution.py:273
  17.9 3.3 %collective-permute-start.6 = (f32[2,128,128]{2,1,0:T(8,128)S(1)}, f32[2,128,128]{2,1,0:T(8,128)S(1)}, u32[]{:S(2)}, u32[]{:S(2)}) collective-permute-start(f32[2,128,128]{2,1,0:T(8,128)S(1)} %add.111), channel_id=1, source_target_pairs={{8,16},{12,20},{9,17},{13,21},{10,18},{14,22},{11,19},{15,23}} | collective-permute-start | bytes 393224 | tf_op jit(solution)/shard_map/ppermute | solution.py:273
  18.7 3.4 %collective-permute-start.2 = (f32[2,128,128]{2,1,0:T(8,128)S(1)}, f32[2,128,128]{2,1,0:T(8,128)S(1)}, u32[]{:S(2)}, u32[]{:S(2)}) collective-permute-start(f32[2,128,128]{2,1,0:T(8,128)S(1)} %add.105), channel_id=1, source_target_pairs={{8,16},{12,20},{9,17},{13,21},{10,18},{14,22},{11,19},{15,23}} | collective-permute-start | bytes 393224 | tf_op jit(solution)/shard_map/ppermute | solution.py:273
  21.2 3.8 %copy-start.1 = (bf16[1024,1024]{1,0:T(8,128)(2,1)S(1)}, bf16[1024,1024]{1,0:T(8,128)(2,1)}, u32[]{:S(2)}) copy-start(bf16[1024,1024]{1,0:T(8,128)(2,1)} %og_ref.15) | copy-start | bytes 6291460
  21.2 1.5 %collective-permute-start.7 = (f32[2,128,128]{2,1,0:T(8,128)S(1)}, f32[2,128,128]{2,1,0:T(8,128)S(1)}, u32[]{:S(2)}, u32[]{:S(2)}) collective-permute-start(f32[2,128,128]{2,1,0:T(8,128)S(1)} %add.113), channel_id=1, source_target_pairs={{16,24},{20,28},{17,25},{21,29},{18,26},{22,30},{19,27},{23,31}} | collective-permute-start | bytes 393224 | tf_op jit(solution)/shard_map/ppermute | solution.py:273
  22.1 1.5 %collective-permute-start.3 = (f32[2,128,128]{2,1,0:T(8,128)S(1)}, f32[2,128,128]{2,1,0:T(8,128)S(1)}, u32[]{:S(2)}, u32[]{:S(2)}) collective-permute-start(f32[2,128,128]{2,1,0:T(8,128)S(1)} %add.107), channel_id=1, source_target_pairs={{16,24},{20,28},{17,25},{21,29},{18,26},{22,30},{19,27},{23,31}} | collective-permute-start | bytes 393224 | tf_op jit(solution)/shard_map/ppermute | solution.py:273
  22.8 5.0 %collective-permute-start.9 = (f32[2,128,128]{2,1,0:T(8,128)S(1)}, f32[2,128,128]{2,1,0:T(8,128)S(1)}, u32[]{:S(2)}, u32[]{:S(2)}) collective-permute-start(f32[2,128,128]{2,1,0:T(8,128)S(1)} %get-tuple-element.200), channel_id=1, source_target_pairs={{0,4},{4,0},{8,12},{12,8},{16,20},{20,16},{24,28},{28,24},{1,5},{5... | collective-permute-start | bytes 393224 | tf_op jit(solution)/shard_map/ppermute | solution.py:273
  23.6 5.6 %collective-permute-start.8 = (f32[2,128,128]{2,1,0:T(8,128)S(1)}, f32[2,128,128]{2,1,0:T(8,128)S(1)}, u32[]{:S(2)}, u32[]{:S(2)}) collective-permute-start(f32[2,128,128]{2,1,0:T(8,128)S(1)} %get-tuple-element.203), channel_id=1, source_target_pairs={{0,4},{4,0},{8,12},{12,8},{16,20},{20,16},{24,28},{28,24},{1,5},{5... | collective-permute-start | bytes 393224 | tf_op jit(solution)/shard_map/ppermute | solution.py:273
  29.9 1.2 %collective-permute-start.10 = (f32[2,1024]{1,0:T(2,128)S(1)}, f32[2,1024]{1,0:T(2,128)S(1)}, u32[]{:S(2)}, u32[]{:S(2)}) collective-permute-start(f32[2,1024]{1,0:T(2,128)S(1)} %add_add_fusion.4), channel_id=1, source_target_pairs={{0,1},{1,0},{2,3},{3,2},{4,5},{5,4},{6,7},{7,6},{8,9},{9,8},{10,11... | collective-permute-start | bytes 24584 | tf_op jit(solution)/shard_map/ppermute | solution.py:294
  31.1 3.7 %collective-permute-start.11 = (f32[2,1024]{1,0:T(2,128)S(1)}, f32[2,1024]{1,0:T(2,128)S(1)}, u32[]{:S(2)}, u32[]{:S(2)}) collective-permute-start(f32[2,1024]{1,0:T(2,128)S(1)} %add.121), channel_id=1, source_target_pairs={{0,2},{1,3},{2,0},{3,1},{4,6},{5,7},{6,4},{7,5},{8,10},{9,11},{10,... | collective-permute-start | bytes 24584 | tf_op jit(solution)/shard_map/ppermute | solution.py:294
  35.6 6.1 %collective-permute-start.17 = (f32[2,128,128]{2,1,0:T(8,128)S(1)}, f32[2,128,128]{2,1,0:T(8,128)S(1)}, u32[]{:S(2)}, u32[]{:S(2)}) collective-permute-start(f32[2,128,128]{2,1,0:T(8,128)S(1)} %get-tuple-element.142), channel_id=1, source_target_pairs={{28,24},{24,28},{20,16},{16,20},{12,8},{8,12},{4,0},{0,4},{29,25},... | collective-permute-start | bytes 393224 | tf_op jit(solution)/shard_map/ppermute | solution.py:273
  37.5 5.6 %collective-permute-start.12 = (f32[2,128,128]{2,1,0:T(8,128)S(1)}, f32[2,128,128]{2,1,0:T(8,128)S(1)}, u32[]{:S(2)}, u32[]{:S(2)}) collective-permute-start(f32[2,128,128]{2,1,0:T(8,128)S(1)} %get-tuple-element.146), channel_id=1, source_target_pairs={{28,24},{24,28},{20,16},{16,20},{12,8},{8,12},{4,0},{0,4},{29,25},... | collective-permute-start | bytes 393224 | tf_op jit(solution)/shard_map/ppermute | solution.py:273
  41.8 6.1 %collective-permute-start.18 = (f32[2,128,128]{2,1,0:T(8,128)S(1)}, f32[2,128,128]{2,1,0:T(8,128)S(1)}, u32[]{:S(2)}, u32[]{:S(2)}) collective-permute-start(f32[2,128,128]{2,1,0:T(8,128)S(1)} %add.129), channel_id=1, source_target_pairs={{28,20},{24,16},{29,21},{25,17},{30,22},{26,18},{31,23},{27,19}} | collective-permute-start | bytes 393224 | tf_op jit(solution)/shard_map/ppermute | solution.py:273
  43.2 5.4 %collective-permute-start.13 = (f32[2,128,128]{2,1,0:T(8,128)S(1)}, f32[2,128,128]{2,1,0:T(8,128)S(1)}, u32[]{:S(2)}, u32[]{:S(2)}) collective-permute-start(f32[2,128,128]{2,1,0:T(8,128)S(1)} %add.123), channel_id=1, source_target_pairs={{28,20},{24,16},{29,21},{25,17},{30,22},{26,18},{31,23},{27,19}} | collective-permute-start | bytes 393224 | tf_op jit(solution)/shard_map/ppermute | solution.py:273
  47.9 8.3 %collective-permute-start.19 = (f32[2,128,128]{2,1,0:T(8,128)S(1)}, f32[2,128,128]{2,1,0:T(8,128)S(1)}, u32[]{:S(2)}, u32[]{:S(2)}) collective-permute-start(f32[2,128,128]{2,1,0:T(8,128)S(1)} %add.130), channel_id=1, source_target_pairs={{20,12},{16,8},{21,13},{17,9},{22,14},{18,10},{23,15},{19,11}} | collective-permute-start | bytes 393224 | tf_op jit(solution)/shard_map/ppermute | solution.py:273
  48.6 9.0 %collective-permute-start.14 = (f32[2,128,128]{2,1,0:T(8,128)S(1)}, f32[2,128,128]{2,1,0:T(8,128)S(1)}, u32[]{:S(2)}, u32[]{:S(2)}) collective-permute-start(f32[2,128,128]{2,1,0:T(8,128)S(1)} %add.124), channel_id=1, source_target_pairs={{20,12},{16,8},{21,13},{17,9},{22,14},{18,10},{23,15},{19,11}} | collective-permute-start | bytes 393224 | tf_op jit(solution)/shard_map/ppermute | solution.py:273
  56.3 9.1 %collective-permute-start.20 = (f32[2,128,128]{2,1,0:T(8,128)S(1)}, f32[2,128,128]{2,1,0:T(8,128)S(1)}, u32[]{:S(2)}, u32[]{:S(2)}) collective-permute-start(f32[2,128,128]{2,1,0:T(8,128)S(1)} %add.132), channel_id=1, source_target_pairs={{12,4},{8,0},{13,5},{9,1},{14,6},{10,2},{15,7},{11,3}} | collective-permute-start | bytes 393224 | tf_op jit(solution)/shard_map/ppermute | solution.py:273
  57.6 9.2 %collective-permute-start.15 = (f32[2,128,128]{2,1,0:T(8,128)S(1)}, f32[2,128,128]{2,1,0:T(8,128)S(1)}, u32[]{:S(2)}, u32[]{:S(2)}) collective-permute-start(f32[2,128,128]{2,1,0:T(8,128)S(1)} %add.126), channel_id=1, source_target_pairs={{12,4},{8,0},{13,5},{9,1},{14,6},{10,2},{15,7},{11,3}} | collective-permute-start | bytes 393224 | tf_op jit(solution)/shard_map/ppermute | solution.py:273
  65.4 5.0 %collective-permute-start.21 = (f32[2,128,128]{2,1,0:T(8,128)S(1)}, f32[2,128,128]{2,1,0:T(8,128)S(1)}, u32[]{:S(2)}, u32[]{:S(2)}) collective-permute-start(f32[2,128,128]{2,1,0:T(8,128)S(1)} %get-tuple-element.199), channel_id=1, source_target_pairs={{28,24},{24,28},{20,16},{16,20},{12,8},{8,12},{4,0},{0,4},{29,25},... | collective-permute-start | bytes 393224 | tf_op jit(solution)/shard_map/ppermute | solution.py:273
  66.9 5.0 %collective-permute-start.16 = (f32[2,128,128]{2,1,0:T(8,128)S(1)}, f32[2,128,128]{2,1,0:T(8,128)S(1)}, u32[]{:S(2)}, u32[]{:S(2)}) collective-permute-start(f32[2,128,128]{2,1,0:T(8,128)S(1)} %get-tuple-element.197), channel_id=1, source_target_pairs={{28,24},{24,28},{20,16},{16,20},{12,8},{8,12},{4,0},{0,4},{29,25},... | collective-permute-start | bytes 393224 | tf_op jit(solution)/shard_map/ppermute | solution.py:273
  (1 other events, 3.8 us)

commit v10 on v9

--- a/solution.py
+++ b/solution.py
@@ -446,8 +446,8 @@
     drive(
         [lambda i=i: scan_stages(backs[2 * i], lambda: backs[2 * i + 1], seq_size, low, True) for i in range(2)],
         in_events({
-            0: [functools.partial(piece_grad, 2), functools.partial(piece_grad, 1)],
-            1: [functools.partial(piece_grad, 3)],
+            0: [functools.partial(piece_grad, 2)],
+            1: [functools.partial(piece_grad, 1), functools.partial(piece_grad, 3)],
             3: [functools.partial(piece_back, 0, 0, size, False), functools.partial(piece_back, 1, 0, size, False)],
             5: [functools.partial(piece_back, 2, 0, size, True), functools.partial(piece_back, 3, 0, size, True), piece_flush],
             last: [functools.partial(piece_last, 1), functools.partial(piece_last, 3)],

time: 73.7 us -> 73.7 us (level)
  no operation moved by 1% of the time
where the time goes in v10:
time: 73.7 us; the launch traced here: 73.3 us
  Pallas kernels  28.5 us (39%)
  starting transfers between devices  26.1 us (35%)
  waiting for transfers between devices  17.1 us (23%)
  between operations  1.26 us (2%)
    pallas_call x23, Pallas kernels, call(): pl.pallas_call(kernel, in_specs=in_specs or [VMEM] * len(ins), out_specs=...  28.5 us
    ppermute x20, starting transfers between devices, drive(): live.append((name, scan, lax.ppermute(operand, 'seq', pairs)))  24.5 us
    ppermute x20, waiting for transfers between devices, drive(): live.append((name, scan, lax.ppermute(operand, 'seq', pairs)))  13.8 us
    ppermute x2, waiting for transfers between devices, head_sum(): a = a + lax.ppermute(a, 'head', [(i, i ^ step) for i in range(size)])  3.3 us
    ppermute x2, starting transfers between devices, head_sum(): a = a + lax.ppermute(a, 'head', [(i, i ^ step) for i in range(size)])  1.58 us
  transfers between devices with their start and end apart: 22, of which 12 were waited for; matrix products, arithmetic and copies ran while one was open for 1% of the time, Pallas kernels for 33%

profile of v10, /device:TPU:0, one launch (start us, length us, event | category | flops | bytes accessed | tf_op | source)
XLA Modules:
  0.0 73.3 jit_solution(749976877043831803)
XLA Ops:
  0.6 1.6 %shard_map.84 = (bf16[1024,256]{1,0:T(8,128)(2,1)S(1)}, bf16[1024,256]{1,0:T(8,128)(2,1)S(1)}, f32[2,128,128]{2,1,0:T(8,128)S(1)}) custom-call(bf16[1024,1024]{1,0:T(8,128)(2,1)} %k_hbm.1, bf16[1024,1024]{1,0:T(8,128)(2,1)} %v_hbm.1), custom_call_target="tpu_custom_call" | custom-call | flops 67108864 | bytes 4194304 | tf_op jit(solution)/shard_map/pallas_call | solution.py:215
  2.2 3.0 %collective-permute-start.4 = (f32[2,128,128]{2,1,0:T(8,128)S(1)}, f32[2,128,128]{2,1,0:T(8,128)S(1)}, u32[]{:S(2)}, u32[]{:S(2)}) collective-permute-start(f32[2,128,128]{2,1,0:T(8,128)S(1)} %get-tuple-element.103), channel_id=1, source_target_pairs={{0,4},{4,0},{8,12},{12,8},{16,20},{20,16},{24,28},{28,24},{1,5},{5... | collective-permute-start | bytes 393224 | tf_op jit(solution)/shard_map/ppermute | solution.py:273
  5.2 2.3 %shard_map.85 = (bf16[1024,256]{1,0:T(8,128)(2,1)S(1)}, bf16[1024,256]{1,0:T(8,128)(2,1)S(1)}, bf16[1024,256]{1,0:T(8,128)(2,1)S(1)}, bf16[1024,256]{1,0:T(8,128...) custom-call(bf16[1024,1024]{1,0:T(8,128)(2,1)} %k_hbm.1, ...), custom_call_target="tpu_custom_call" | custom-call | flops 201326592 | bytes 4194304 | tf_op jit(solution)/shard_map/pallas_call | solution.py:215
  8.8 3.7 %collective-permute-start.5 = (f32[2,128,128]{2,1,0:T(8,128)S(1)}, f32[2,128,128]{2,1,0:T(8,128)S(1)}, u32[]{:S(2)}, u32[]{:S(2)}) collective-permute-start(f32[2,128,128]{2,1,0:T(8,128)S(1)} %add.110), channel_id=1, source_target_pairs={{0,8},{4,12},{1,9},{5,13},{2,10},{6,14},{3,11},{7,15}} | collective-permute-start | bytes 393224 | tf_op jit(solution)/shard_map/ppermute | solution.py:273
  12.6 3.5 %collective-permute-start.1 = (f32[2,128,128]{2,1,0:T(8,128)S(1)}, f32[2,128,128]{2,1,0:T(8,128)S(1)}, u32[]{:S(2)}, u32[]{:S(2)}) collective-permute-start(f32[2,128,128]{2,1,0:T(8,128)S(1)} %add.104), channel_id=1, source_target_pairs={{0,8},{4,12},{1,9},{5,13},{2,10},{6,14},{3,11},{7,15}} | collective-permute-start | bytes 393224 | tf_op jit(solution)/shard_map/ppermute | solution.py:273
  23.6 1.4 %collective-permute-start.8 = (f32[2,128,128]{2,1,0:T(8,128)S(1)}, f32[2,128,128]{2,1,0:T(8,128)S(1)}, u32[]{:S(2)}, u32[]{:S(2)}) collective-permute-start(f32[2,128,128]{2,1,0:T(8,128)S(1)} %get-tuple-element.205), channel_id=1, source_target_pairs={{0,4},{4,0},{8,12},{12,8},{16,20},{20,16},{24,28},{28,24},{1,5},{5... | collective-permute-start | bytes 393224 | tf_op jit(solution)/shard_map/ppermute | solution.py:273
  26.2 1.6 %collective-permute-done.9.p_ref = f32[2,128,128]{2,1,0:T(8,128)S(1)} collective-permute-done((f32[2,128,128]{2,1,0:T(8,128)S(1)}, f32[2,128,128]{2,1,0:T(8,128)S(1)}, u32[]{:S(2)}, u32[]{:S(2)}) %collective-permute-start.9) | collective-permute-done | bytes 131104 | tf_op jit(solution)/shard_map/ppermute | solution.py:273
  30.0 1.2 %collective-permute-done.10 = f32[2,1024]{1,0:T(2,128)S(1)} collective-permute-done((f32[2,1024]{1,0:T(2,128)S(1)}, f32[2,1024]{1,0:T(2,128)S(1)}, u32[]{:S(2)}, u32[]{:S(2)}) %collective-permute-start.10) | collective-permute-done | bytes 8224 | tf_op jit(solution)/shard_map/ppermute | solution.py:294
  31.1 1.5 %collective-permute-start.11 = (f32[2,1024]{1,0:T(2,128)S(1)}, f32[2,1024]{1,0:T(2,128)S(1)}, u32[]{:S(2)}, u32[]{:S(2)}) collective-permute-start(f32[2,1024]{1,0:T(2,128)S(1)} %add.121), channel_id=1, source_target_pairs={{0,2},{1,3},{2,0},{3,1},{4,6},{5,7},{6,4},{7,5},{8,10},{9,11},{10,... | collective-permute-start | bytes 24584 | tf_op jit(solution)/shard_map/ppermute | solution.py:294
  32.6 2.1 %collective-permute-done.11 = f32[2,1024]{1,0:T(2,128)S(1)} collective-permute-done((f32[2,1024]{1,0:T(2,128)S(1)}, f32[2,1024]{1,0:T(2,128)S(1)}, u32[]{:S(2)}, u32[]{:S(2)}) %collective-permute-start.11) | collective-permute-done | bytes 8224 | tf_op jit(solution)/shard_map/ppermute | solution.py:294
  35.6 1.3 %collective-permute-start.17 = (f32[2,128,128]{2,1,0:T(8,128)S(1)}, f32[2,128,128]{2,1,0:T(8,128)S(1)}, u32[]{:S(2)}, u32[]{:S(2)}) collective-permute-start(f32[2,128,128]{2,1,0:T(8,128)S(1)} %get-tuple-element.143), channel_id=1, source_target_pairs={{28,24},{24,28},{20,16},{16,20},{12,8},{8,12},{4,0},{0,4},{29,25},... | collective-permute-start | bytes 393224 | tf_op jit(solution)/shard_map/ppermute | solution.py:273
  39.7 2.1 %collective-permute-done.17 = f32[2,128,128]{2,1,0:T(8,128)S(1)} collective-permute-done((f32[2,128,128]{2,1,0:T(8,128)S(1)}, f32[2,128,128]{2,1,0:T(8,128)S(1)}, u32[]{:S(2)}, u32[]{:S(2)}) %collective-permute-start.17) | collective-permute-done | bytes 131104 | tf_op jit(solution)/shard_map/ppermute | solution.py:273
  44.0 1.9 %shard_map.98 = (bf16[1024,256]{1,0:T(8,128)(2,1)S(1)}, bf16[1024,256]{1,0:T(8,128)(2,1)S(1)}, f32[1024,256]{1,0:T(8,128)S(1)}, f32[1024,256]{1,0:T(8,128)S(1)}) custom-call(bf16[1024,1024]{1,0:T(8,128)(2,1)S(1)} %copy-done, bf16[1024,256]{1,0:T(8,128)(2,1)S(1)} %get-tuple-element.118.k_ref, bf16[1024,256]{1,0:T(8,128)(2,1)S(1)} %get-tuple-element.119.v_ref, ...), custom_call_target="tpu_custom_call" | custom-call | flops 603979776 | bytes 5902336 | tf_op jit(solution)/shard_map/pallas_call | solution.py:215
  46.0 1.9 %shard_map.99 = (bf16[1024,256]{1,0:T(8,128)(2,1)S(1)}, bf16[1024,256]{1,0:T(8,128)(2,1)S(1)}, f32[1024,256]{1,0:T(8,128)S(1)}, f32[1024,256]{1,0:T(8,128)S(1)}) custom-call(bf16[1024,1024]{1,0:T(8,128)(2,1)S(1)} %copy-done, bf16[1024,256]{1,0:T(8,128)(2,1)S(1)} %get-tuple-element.186.k_ref, bf16[1024,256]{1,0:T(8,128)(2,1)S(1)} %get-tuple-element.124.v_ref, ...), custom_call_target="tpu_custom_call" | custom-call | flops 603979776 | bytes 5902336 | tf_op jit(solution)/shard_map/pallas_call | solution.py:215
  49.3 3.1 %shard_map.100 = (bf16[1024,256]{1,0:T(8,128)(2,1)S(1)}, bf16[1024,256]{1,0:T(8,128)(2,1)S(1)}, f32[1024,256]{1,0:T(8,128)S(1)}, f32[1024,256]{1,0:T(8,128)S(1)}...) custom-call(bf16[1024,1024]{1,0:T(8,128)(2,1)S(1)} %copy-done, bf16[1024,256]{1,0:T(8,128)(2,1)S(1)} %get-tuple-element.109.k_ref, ...), custom_call_target="tpu_custom_call" | custom-call | flops 603979776 | bytes 7999488 | tf_op jit(solution)/shard_map/pallas_call | solution.py:215
  52.4 2.8 %shard_map.101 = (bf16[1024,256]{1,0:T(8,128)(2,1)S(1)}, bf16[1024,256]{1,0:T(8,128)(2,1)S(1)}, f32[1024,256]{1,0:T(8,128)S(1)}, f32[1024,256]{1,0:T(8,128)S(1)}...) custom-call(bf16[1024,1024]{1,0:T(8,128)(2,1)S(1)} %copy-done, ...), custom_call_target="tpu_custom_call", output_to_operand_aliasing={{4}: (11, {}), {5}: (12, {})} | custom-call | flops 603979776 | bytes 11145216 | tf_op jit(solution)/shard_map/pallas_call | solution.py:215
  55.2 1.0 %shard_map.102 = (bf16[1024,1024]{1,0:T(8,128)(2,1)}, bf16[1024,1024]{1,0:T(8,128)(2,1)}) custom-call(bf16[1024,256]{1,0:T(8,128)(2,1)S(1)} %get-tuple-element.175.a_ref, bf16[1024,256]{1,0:T(8,128)(2,1)S(1)} %get-tuple-element.176.b_ref, bf16[1024,1024]{1,0:T(8,128)(2,1)} %get-tuple-element.177.rest_0_, ...), custom_call_target="tpu_custom_call", output_to_operand_aliasing={{0}: (2, {}), {1}: (3, {})} | custom-call | bytes 5242880 | tf_op jit(solution)/shard_map/pallas_call | solution.py:215
  56.3 1.3 %collective-permute-start.20 = (f32[2,128,128]{2,1,0:T(8,128)S(1)}, f32[2,128,128]{2,1,0:T(8,128)S(1)}, u32[]{:S(2)}, u32[]{:S(2)}) collective-permute-start(f32[2,128,128]{2,1,0:T(8,128)S(1)} %add.132), channel_id=1, source_target_pairs={{12,4},{8,0},{13,5},{9,1},{14,6},{10,2},{15,7},{11,3}} | collective-permute-start | bytes 393224 | tf_op jit(solution)/shard_map/ppermute | solution.py:273
  57.6 1.3 %collective-permute-start.15 = (f32[2,128,128]{2,1,0:T(8,128)S(1)}, f32[2,128,128]{2,1,0:T(8,128)S(1)}, u32[]{:S(2)}, u32[]{:S(2)}) collective-permute-start(f32[2,128,128]{2,1,0:T(8,128)S(1)} %add.126), channel_id=1, source_target_pairs={{12,4},{8,0},{13,5},{9,1},{14,6},{10,2},{15,7},{11,3}} | collective-permute-start | bytes 393224 | tf_op jit(solution)/shard_map/ppermute | solution.py:273
  58.9 6.5 %collective-permute-done.20 = f32[2,128,128]{2,1,0:T(8,128)S(1)} collective-permute-done((f32[2,128,128]{2,1,0:T(8,128)S(1)}, f32[2,128,128]{2,1,0:T(8,128)S(1)}, u32[]{:S(2)}, u32[]{:S(2)}) %collective-permute-start.20) | collective-permute-done | bytes 131104 | tf_op jit(solution)/shard_map/ppermute | solution.py:273
  67.6 1.3 %shard_map.103 = (bf16[1024,1024]{1,0:T(8,128)(2,1)}, bf16[1024,1024]{1,0:T(8,128)(2,1)}) custom-call(bf16[1024,256]{1,0:T(8,128)(2,1)S(1)} %get-tuple-element.186.k_ref, bf16[1024,256]{1,0:T(8,128)(2,1)S(1)} %get-tuple-element.124.v_ref, f32[2,128,128]{2,1,0:T(8,128)S(1)} %get-tuple-element.200.s_ref, f32[1024,256]{1,0:T(8,128)S(1)} %get-tuple-element.182.rest_0_, ...), custom_call_target="tpu_custom_call" | custom-call | flops 134217728 | bytes 3276800 | tf_op jit(solution)/shard_map/pallas_call | solution.py:215
  69.0 1.3 %shard_map.104 = (bf16[1024,1024]{1,0:T(8,128)(2,1)}, bf16[1024,1024]{1,0:T(8,128)(2,1)}) custom-call(bf16[1024,256]{1,0:T(8,128)(2,1)S(1)} %get-tuple-element.189.k_ref, bf16[1024,256]{1,0:T(8,128)(2,1)S(1)} %get-tuple-element.115.v_ref, f32[2,128,128]{2,1,0:T(8,128)S(1)} %get-tuple-element.198.s_ref, ...), custom_call_target="tpu_custom_call", output_to_operand_aliasing={{0}: (5, {}), {1}: (6, {})} | custom-call | flops 134217728 | bytes 7471104 | tf_op jit(solution)/shard_map/pallas_call | solution.py:215
  70.5 1.3 %shard_map.105 = (bf16[1024,1024]{1,0:T(8,128)(2,1)}, bf16[1024,1024]{1,0:T(8,128)(2,1)}) custom-call(bf16[1024,256]{1,0:T(8,128)(2,1)S(1)} %get-tuple-element.118.k_ref, bf16[1024,256]{1,0:T(8,128)(2,1)S(1)} %get-tuple-element.119.v_ref, f32[2,128,128]{2,1,0:T(8,128)S(1)} %collective-permute-done.21.s_ref, ...), custom_call_target="tpu_custom_call", output_to_operand_aliasing={{0}: (5, {}), {1}: (6, {})} | custom-call | flops 134217728 | bytes 7471104 | tf_op jit(solution)/shard_map/pallas_call | solution.py:215
  71.9 1.3 %shard_map.106 = (bf16[1024,1024]{1,0:T(8,128)(2,1)}, bf16[1024,1024]{1,0:T(8,128)(2,1)}) custom-call(bf16[1024,256]{1,0:T(8,128)(2,1)S(1)} %get-tuple-element.109.k_ref, bf16[1024,256]{1,0:T(8,128)(2,1)S(1)} %get-tuple-element.110.v_ref, f32[2,128,128]{2,1,0:T(8,128)S(1)} %collective-permute-done.16.s_ref, ...), custom_call_target="tpu_custom_call", output_to_operand_aliasing={{0}: (5, {}), {1}: (6, {})} | custom-call | flops 134217728 | bytes 7471104 | tf_op jit(solution)/shard_map/pallas_call | solution.py:215
  (68 shorter events, 21.8 us)
Async XLA Ops:
  2.2 13.9 %copy-start = (bf16[1024,1024]{1,0:T(8,128)(2,1)S(1)}, bf16[1024,1024]{1,0:T(8,128)(2,1)}, u32[]{:S(2)}) copy-start(bf16[1024,1024]{1,0:T(8,128)(2,1)} %q_ref.18) | copy-start | bytes 6291460
  2.2 6.5 %collective-permute-start.4 = (f32[2,128,128]{2,1,0:T(8,128)S(1)}, f32[2,128,128]{2,1,0:T(8,128)S(1)}, u32[]{:S(2)}, u32[]{:S(2)}) collective-permute-start(f32[2,128,128]{2,1,0:T(8,128)S(1)} %get-tuple-element.103), channel_id=1, source_target_pairs={{0,4},{4,0},{8,12},{12,8},{16,20},{20,16},{24,28},{28,24},{1,5},{5... | collective-permute-start | bytes 393224 | tf_op jit(solution)/shard_map/ppermute | solution.py:273
  7.5 5.0 %collective-permute-start = (f32[2,128,128]{2,1,0:T(8,128)S(1)}, f32[2,128,128]{2,1,0:T(8,128)S(1)}, u32[]{:S(2)}, u32[]{:S(2)}) collective-permute-start(f32[2,128,128]{2,1,0:T(8,128)S(1)} %get-tuple-element.107), channel_id=1, source_target_pairs={{0,4},{4,0},{8,12},{12,8},{16,20},{20,16},{24,28},{28,24},{1,5},{5... | collective-permute-start | bytes 393224 | tf_op jit(solution)/shard_map/ppermute | solution.py:273
  8.8 9.1 %collective-permute-start.5 = (f32[2,128,128]{2,1,0:T(8,128)S(1)}, f32[2,128,128]{2,1,0:T(8,128)S(1)}, u32[]{:S(2)}, u32[]{:S(2)}) collective-permute-start(f32[2,128,128]{2,1,0:T(8,128)S(1)} %add.110), channel_id=1, source_target_pairs={{0,8},{4,12},{1,9},{5,13},{2,10},{6,14},{3,11},{7,15}} | collective-permute-start | bytes 393224 | tf_op jit(solution)/shard_map/ppermute | solution.py:273
  12.6 6.0 %collective-permute-start.1 = (f32[2,128,128]{2,1,0:T(8,128)S(1)}, f32[2,128,128]{2,1,0:T(8,128)S(1)}, u32[]{:S(2)}, u32[]{:S(2)}) collective-permute-start(f32[2,128,128]{2,1,0:T(8,128)S(1)} %add.104), channel_id=1, source_target_pairs={{0,8},{4,12},{1,9},{5,13},{2,10},{6,14},{3,11},{7,15}} | collective-permute-start | bytes 393224 | tf_op jit(solution)/shard_map/ppermute | solution.py:273
  17.9 3.3 %collective-permute-start.6 = (f32[2,128,128]{2,1,0:T(8,128)S(1)}, f32[2,128,128]{2,1,0:T(8,128)S(1)}, u32[]{:S(2)}, u32[]{:S(2)}) collective-permute-start(f32[2,128,128]{2,1,0:T(8,128)S(1)} %add.111), channel_id=1, source_target_pairs={{8,16},{12,20},{9,17},{13,21},{10,18},{14,22},{11,19},{15,23}} | collective-permute-start | bytes 393224 | tf_op jit(solution)/shard_map/ppermute | solution.py:273
  18.7 3.4 %collective-permute-start.2 = (f32[2,128,128]{2,1,0:T(8,128)S(1)}, f32[2,128,128]{2,1,0:T(8,128)S(1)}, u32[]{:S(2)}, u32[]{:S(2)}) collective-permute-start(f32[2,128,128]{2,1,0:T(8,128)S(1)} %add.105), channel_id=1, source_target_pairs={{8,16},{12,20},{9,17},{13,21},{10,18},{14,22},{11,19},{15,23}} | collective-permute-start | bytes 393224 | tf_op jit(solution)/shard_map/ppermute | solution.py:273
  21.2 3.8 %copy-start.1 = (bf16[1024,1024]{1,0:T(8,128)(2,1)S(1)}, bf16[1024,1024]{1,0:T(8,128)(2,1)}, u32[]{:S(2)}) copy-start(bf16[1024,1024]{1,0:T(8,128)(2,1)} %og_ref.15) | copy-start | bytes 6291460
  21.2 1.5 %collective-permute-start.7 = (f32[2,128,128]{2,1,0:T(8,128)S(1)}, f32[2,128,128]{2,1,0:T(8,128)S(1)}, u32[]{:S(2)}, u32[]{:S(2)}) collective-permute-start(f32[2,128,128]{2,1,0:T(8,128)S(1)} %add.113), channel_id=1, source_target_pairs={{16,24},{20,28},{17,25},{21,29},{18,26},{22,30},{19,27},{23,31}} | collective-permute-start | bytes 393224 | tf_op jit(solution)/shard_map/ppermute | solution.py:273
  22.1 1.5 %collective-permute-start.3 = (f32[2,128,128]{2,1,0:T(8,128)S(1)}, f32[2,128,128]{2,1,0:T(8,128)S(1)}, u32[]{:S(2)}, u32[]{:S(2)}) collective-permute-start(f32[2,128,128]{2,1,0:T(8,128)S(1)} %add.107), channel_id=1, source_target_pairs={{16,24},{20,28},{17,25},{21,29},{18,26},{22,30},{19,27},{23,31}} | collective-permute-start | bytes 393224 | tf_op jit(solution)/shard_map/ppermute | solution.py:273
  22.8 5.0 %collective-permute-start.9 = (f32[2,128,128]{2,1,0:T(8,128)S(1)}, f32[2,128,128]{2,1,0:T(8,128)S(1)}, u32[]{:S(2)}, u32[]{:S(2)}) collective-permute-start(f32[2,128,128]{2,1,0:T(8,128)S(1)} %get-tuple-element.202), channel_id=1, source_target_pairs={{0,4},{4,0},{8,12},{12,8},{16,20},{20,16},{24,28},{28,24},{1,5},{5... | collective-permute-start | bytes 393224 | tf_op jit(solution)/shard_map/ppermute | solution.py:273
  23.6 5.6 %collective-permute-start.8 = (f32[2,128,128]{2,1,0:T(8,128)S(1)}, f32[2,128,128]{2,1,0:T(8,128)S(1)}, u32[]{:S(2)}, u32[]{:S(2)}) collective-permute-start(f32[2,128,128]{2,1,0:T(8,128)S(1)} %get-tuple-element.205), channel_id=1, source_target_pairs={{0,4},{4,0},{8,12},{12,8},{16,20},{20,16},{24,28},{28,24},{1,5},{5... | collective-permute-start | bytes 393224 | tf_op jit(solution)/shard_map/ppermute | solution.py:273
  29.9 1.2 %collective-permute-start.10 = (f32[2,1024]{1,0:T(2,128)S(1)}, f32[2,1024]{1,0:T(2,128)S(1)}, u32[]{:S(2)}, u32[]{:S(2)}) collective-permute-start(f32[2,1024]{1,0:T(2,128)S(1)} %add_add_fusion.4), channel_id=1, source_target_pairs={{0,1},{1,0},{2,3},{3,2},{4,5},{5,4},{6,7},{7,6},{8,9},{9,8},{10,11... | collective-permute-start | bytes 24584 | tf_op jit(solution)/shard_map/ppermute | solution.py:294
  31.1 3.7 %collective-permute-start.11 = (f32[2,1024]{1,0:T(2,128)S(1)}, f32[2,1024]{1,0:T(2,128)S(1)}, u32[]{:S(2)}, u32[]{:S(2)}) collective-permute-start(f32[2,1024]{1,0:T(2,128)S(1)} %add.121), channel_id=1, source_target_pairs={{0,2},{1,3},{2,0},{3,1},{4,6},{5,7},{6,4},{7,5},{8,10},{9,11},{10,... | collective-permute-start | bytes 24584 | tf_op jit(solution)/shard_map/ppermute | solution.py:294
  35.6 6.1 %collective-permute-start.17 = (f32[2,128,128]{2,1,0:T(8,128)S(1)}, f32[2,128,128]{2,1,0:T(8,128)S(1)}, u32[]{:S(2)}, u32[]{:S(2)}) collective-permute-start(f32[2,128,128]{2,1,0:T(8,128)S(1)} %get-tuple-element.143), channel_id=1, source_target_pairs={{28,24},{24,28},{20,16},{16,20},{12,8},{8,12},{4,0},{0,4},{29,25},... | collective-permute-start | bytes 393224 | tf_op jit(solution)/shard_map/ppermute | solution.py:273
  37.5 5.6 %collective-permute-start.12 = (f32[2,128,128]{2,1,0:T(8,128)S(1)}, f32[2,128,128]{2,1,0:T(8,128)S(1)}, u32[]{:S(2)}, u32[]{:S(2)}) collective-permute-start(f32[2,128,128]{2,1,0:T(8,128)S(1)} %get-tuple-element.147), channel_id=1, source_target_pairs={{28,24},{24,28},{20,16},{16,20},{12,8},{8,12},{4,0},{0,4},{29,25},... | collective-permute-start | bytes 393224 | tf_op jit(solution)/shard_map/ppermute | solution.py:273
  41.8 6.1 %collective-permute-start.18 = (f32[2,128,128]{2,1,0:T(8,128)S(1)}, f32[2,128,128]{2,1,0:T(8,128)S(1)}, u32[]{:S(2)}, u32[]{:S(2)}) collective-permute-start(f32[2,128,128]{2,1,0:T(8,128)S(1)} %add.129), channel_id=1, source_target_pairs={{28,20},{24,16},{29,21},{25,17},{30,22},{26,18},{31,23},{27,19}} | collective-permute-start | bytes 393224 | tf_op jit(solution)/shard_map/ppermute | solution.py:273
  43.2 5.4 %collective-permute-start.13 = (f32[2,128,128]{2,1,0:T(8,128)S(1)}, f32[2,128,128]{2,1,0:T(8,128)S(1)}, u32[]{:S(2)}, u32[]{:S(2)}) collective-permute-start(f32[2,128,128]{2,1,0:T(8,128)S(1)} %add.123), channel_id=1, source_target_pairs={{28,20},{24,16},{29,21},{25,17},{30,22},{26,18},{31,23},{27,19}} | collective-permute-start | bytes 393224 | tf_op jit(solution)/shard_map/ppermute | solution.py:273
  47.9 8.3 %collective-permute-start.19 = (f32[2,128,128]{2,1,0:T(8,128)S(1)}, f32[2,128,128]{2,1,0:T(8,128)S(1)}, u32[]{:S(2)}, u32[]{:S(2)}) collective-permute-start(f32[2,128,128]{2,1,0:T(8,128)S(1)} %add.130), channel_id=1, source_target_pairs={{20,12},{16,8},{21,13},{17,9},{22,14},{18,10},{23,15},{19,11}} | collective-permute-start | bytes 393224 | tf_op jit(solution)/shard_map/ppermute | solution.py:273
  48.6 9.0 %collective-permute-start.14 = (f32[2,128,128]{2,1,0:T(8,128)S(1)}, f32[2,128,128]{2,1,0:T(8,128)S(1)}, u32[]{:S(2)}, u32[]{:S(2)}) collective-permute-start(f32[2,128,128]{2,1,0:T(8,128)S(1)} %add.124), channel_id=1, source_target_pairs={{20,12},{16,8},{21,13},{17,9},{22,14},{18,10},{23,15},{19,11}} | collective-permute-start | bytes 393224 | tf_op jit(solution)/shard_map/ppermute | solution.py:273
  56.3 9.1 %collective-permute-start.20 = (f32[2,128,128]{2,1,0:T(8,128)S(1)}, f32[2,128,128]{2,1,0:T(8,128)S(1)}, u32[]{:S(2)}, u32[]{:S(2)}) collective-permute-start(f32[2,128,128]{2,1,0:T(8,128)S(1)} %add.132), channel_id=1, source_target_pairs={{12,4},{8,0},{13,5},{9,1},{14,6},{10,2},{15,7},{11,3}} | collective-permute-start | bytes 393224 | tf_op jit(solution)/shard_map/ppermute | solution.py:273
  57.6 9.2 %collective-permute-start.15 = (f32[2,128,128]{2,1,0:T(8,128)S(1)}, f32[2,128,128]{2,1,0:T(8,128)S(1)}, u32[]{:S(2)}, u32[]{:S(2)}) collective-permute-start(f32[2,128,128]{2,1,0:T(8,128)S(1)} %add.126), channel_id=1, source_target_pairs={{12,4},{8,0},{13,5},{9,1},{14,6},{10,2},{15,7},{11,3}} | collective-permute-start | bytes 393224 | tf_op jit(solution)/shard_map/ppermute | solution.py:273
  65.4 5.0 %collective-permute-start.21 = (f32[2,128,128]{2,1,0:T(8,128)S(1)}, f32[2,128,128]{2,1,0:T(8,128)S(1)}, u32[]{:S(2)}, u32[]{:S(2)}) collective-permute-start(f32[2,128,128]{2,1,0:T(8,128)S(1)} %get-tuple-element.201), channel_id=1, source_target_pairs={{28,24},{24,28},{20,16},{16,20},{12,8},{8,12},{4,0},{0,4},{29,25},... | collective-permute-start | bytes 393224 | tf_op jit(solution)/shard_map/ppermute | solution.py:273
  66.9 5.0 %collective-permute-start.16 = (f32[2,128,128]{2,1,0:T(8,128)S(1)}, f32[2,128,128]{2,1,0:T(8,128)S(1)}, u32[]{:S(2)}, u32[]{:S(2)}) collective-permute-start(f32[2,128,128]{2,1,0:T(8,128)S(1)} %get-tuple-element.199), channel_id=1, source_target_pairs={{28,24},{24,28},{20,16},{16,20},{12,8},{8,12},{4,0},{0,4},{29,25},... | collective-permute-start | bytes 393224 | tf_op jit(solution)/shard_map/ppermute | solution.py:273
  (1 other events, 3.8 us)
